TPU v7x, 256 devices: a whole 4x4x8 slice. The times are simulated.
256 devices in a mesh: lev: 8 (over z_lo, x), hor: 32 (over z_hi, y, core).
Axes of the slice: x: 4, y: 4, z: 8 (z_hi: 4, z_lo: 2; z = z_hi * 2 + z_lo), core: 2. Of those that a mesh axis runs over, the one named last changes fastest.
Arguments:
- slab_fields: float32 [4, 32, 524288], P(None, 'lev', 'hor'), may hold values from -6 to 6
- sample_index: int32 [32, 1024], P('hor', 'lev'), may hold values from 0 to 2047
- thickness: float32 [32], replicated, may hold values from 0.3 to 3
- level_cuts: int32 [31], replicated, may hold values 0 or 1
Outputs:
- gram: float32 [2176, 2176], P('hor', 'lev')
Inputs may be any that keep to these rules, and one draw needn't show every extreme that they name: sample_index[j, k] indexes a column among the 2048 columns that start at j * 16384 + (k // 128) * 2048.
All inputs are finite; a program needn't handle non-finite values.
Results may differ from a plain program's by a relative error of at most 0.00068.
Values may be sent and summed in bfloat16 or wider, within the bound.
No kernel may reach another device: no remote copies, remote signals or barrier semaphores. Data moves between devices by JAX's collectives and lax.ppermute only.
A program may use at most 128 MiB of HBM per device.

v0:
```python
import jax
import jax.numpy as jnp
from jax import lax
from jax.sharding import PartitionSpec as P


def vertical_filter(values, thickness, level_cuts):
    link = 1.0 - level_cuts.astype(jnp.float32)
    zero_one = jnp.zeros((1,), jnp.float32)
    lower_link = jnp.concatenate([zero_one, link])
    upper_link = jnp.concatenate([link, zero_one])
    lower_weight = jnp.concatenate([zero_one, thickness[:-1]]) * lower_link
    upper_weight = jnp.concatenate([thickness[1:], zero_one]) * upper_link
    zero_row = jnp.zeros_like(values[:, :1, :])
    below = jnp.concatenate([zero_row, values[:, :-1, :]], axis=1)
    above = jnp.concatenate([values[:, 1:, :], zero_row], axis=1)
    numer = (
        2.0 * thickness[None, :, None] * values
        + lower_weight[None, :, None] * below
        + upper_weight[None, :, None] * above
    )
    denom = 2.0 * thickness + lower_weight + upper_weight
    return numer / denom[None, :, None]


def quadratic_features(smooth):
    count = smooth.shape[2]
    later = jnp.concatenate([smooth[2], smooth[3]], axis=0)
    earlier = jnp.concatenate([smooth[0], smooth[1]], axis=0)
    product = (later[:, None, :] * smooth[0][None, :, :]).reshape(-1, count)
    return jnp.concatenate([later, earlier, product], axis=0).astype(jnp.bfloat16)


def on_device(slab_fields, sample_index, thickness, level_cuts):
    samp_count = sample_index.shape[1]
    lev_count = lax.axis_size("lev")
    hor_count = lax.axis_size("hor")
    all_lists = lax.all_gather(sample_index, "lev", axis=1, tiled=True)[0]
    group_cols = slab_fields.shape[2] // lev_count
    offsets = jnp.arange(all_lists.shape[0]) // samp_count * group_cols + all_lists
    chosen = jnp.take(slab_fields, offsets, axis=2)
    picked_cols = lax.all_to_all(chosen, "lev", split_axis=2, concat_axis=1, tiled=True)
    smooth = vertical_filter(picked_cols, thickness, level_cuts)
    feat_count = 4 * smooth.shape[1] + 2 * smooth.shape[1] * smooth.shape[1]
    col_count = feat_count // lev_count
    col_start = lax.axis_index("lev") * col_count
    features_bf = quadratic_features(smooth)
    block_features_bf = lax.all_gather(features_bf, "lev", axis=1, tiled=True)
    chosen_rows = lax.dynamic_slice_in_dim(block_features_bf, col_start, col_count, 0)
    column_block = lax.dot_general(
        block_features_bf, chosen_rows, (((1,), (1,)), ((), ())), preferred_element_type=jnp.float32
    )
    gram_block = lax.psum_scatter(column_block, "hor", scatter_dimension=0, tiled=True)
    count_all = samp_count * lev_count * hor_count
    return gram_block / count_all


def solution(mesh):
    in_specs = (P(None, "lev", "hor"), P("hor", "lev"), P(), P())
    out_specs = P("hor", "lev")
    return jax.shard_map(
        on_device, mesh=mesh, in_specs=in_specs, out_specs=out_specs, check_vma=False
    )
```

profile of v0, /device:TPU:26, one launch (start us, length us, event | category | flops | bytes accessed | tf_op | source)
XLA Modules:
  0.0 281.2 jit_solution(17869697223792710759)
XLA Ops:
  6.5 21.7 %copy.7 = f32[4,4,16384]{1,0,2:T(4,128)} copy(f32[4,4,16384]{2,1,0:T(4,128)} %param.4) | data formatting | bytes 2097152 | tf_op args[0]
  28.3 16.4 %all_gather.6 = s32[1,1024]{1,0:T(1,128)S(1)} all-gather(s32[1,128]{1,0:T(1,128)S(1)} %copy-done.2), channel_id=1, replica_groups=mesh['lev'=8,'hor'=32] {'lev'}, dimensions={1}, use_global_device_ids=true | all-gather | bytes 4608 | tf_op jit(solution)/shard_map/all_gather | solution.py:38
  44.7 16.8 %gather_fusion = f32[1024,4,4]{2,1,0:T(4,128)} fusion(f32[4,4,16384]{1,0,2:T(4,128)} %copy.7, s32[1024]{0:T(1024)S(1)} %broadcast_clamp_fusion), kind=kCustom, calls=%fused_computation | custom fusion | bytes 135168 | tf_op jit(solution)/shard_map/jit(_take)/gather | solution.py:41
  61.6 5.5 %fusion.18 = f32[1024,4,4]{2,1,0:T(4,128)S(1)} fusion(f32[1024,4,4]{2,1,0:T(4,128)} %gather_fusion, pred[1024]{0:T(1024)(128)(4,1)S(1)} %compare_and_fusion), kind=kLoop, calls=%fused_computation.49 | loop fusion | flops 16384 | bytes 132096
  67.0 3.0 %reshape.135 = f32[8,1,2048]{2,1,0:T(1,128)} reshape(f32[1024,4,4]{2,1,0:T(4,128)S(1)} %fusion.18) | data formatting | bytes 131072
  70.1 6.6 %all-to-all-start = ((f32[8,1,2048]{2,1,0:T(1,128)}), f32[8,1,2048]{2,1,0:T(1,128)S(1)}, u32[]{:S(2)}, u32[]{:S(2)}) async-start(f32[8,1,2048]{2,1,0:T(1,128)} %reshape.135), calls=%async_computation | async-start | bytes 131072 | tf_op jit(solution)/shard_map/all_to_all | solution.py:42
  76.7 0.1 fusion.17
  76.7 0.1 add_add_fusion
  76.8 4.8 %all-to-all-done = f32[8,1,2048]{2,1,0:T(1,128)S(1)} async-done(((f32[8,1,2048]{2,1,0:T(1,128)}), f32[8,1,2048]{2,1,0:T(1,128)S(1)}, u32[]{:S(2)}, u32[]{:S(2)}) %all-to-all-start) | async-done | bytes 65568 | tf_op jit(solution)/shard_map/all_to_all | solution.py:42
  81.6 0.5 broadcast.122
  82.1 0.8 reduce
  82.9 2.7 reshape.136
  85.6 0.8 copy.8
  86.5 0.1 add_divide_fusion
  86.6 0.1 multiply_convert_fusion
  86.7 0.1 constant_dynamic-update-slice_fusion
  86.8 0.8 copy-done
  87.6 0.0 all-gather.2.cloned.1.call-update
  87.7 64.5 %all-gather.2.cloned.1.call-done = bf16[2176,1024]{1,0:T(8,128)(2,1)} async-done(((bf16[2176,128]{1,0:T(8,128)(2,1)}), bf16[2176,1024]{1,0:T(8,128)(2,1)}) %all-gather.2.cloned.1.call-update) | async-done | bytes 4456464 | tf_op jit(solution)/shard_map/all_gather | solution.py:48
  152.2 4.9 %fusion.1 = f32[2176,272]{1,0:T(8,128)S(1)} fusion(bf16[2176,1024]{1,0:T(8,128)(2,1)} %all-gather.2.cloned.1.call-done, s32[]{:T(128)S(6)} %select_n.43), kind=kOutput, calls=%fused_computation.3 | convolution fusion | flops 1212153856 | bytes 7380996 | tf_op jit(solution)/shard_map/dot_general | solution.py:50
  157.1 0.0 copy-start.4
  157.1 75.4 %fusion = f32[80,272]{1,0:T(8,128)S(1)} fusion(f32[2176,272]{1,0:T(8,128)S(1)} %fusion.1), kind=kCustom, calls=%all-reduce-scatter | all-reduce-scatter fusion | flops 696321 | bytes 2455552
  232.5 4.4 %collective-permute-start.3 = (f32[80,272]{1,0:T(8,128)S(1)}, f32[80,272]{1,0:T(8,128)S(1)}, u32[]{:S(2)}, u32[]{:S(2)}) collective-permute-start(f32[80,272]{1,0:T(8,128)S(1)} %fusion), channel_id=1, source_target_pairs={{0,4},{1,5},{2,6},{3,7},{4,8},{5,9},{6,10},{7,11},{8,12},{9,13},{1... | collective-permute-start | bytes 261128
  236.9 8.4 %collective-permute-start.2 = (f32[80,272]{1,0:T(8,128)S(1)}, f32[80,272]{1,0:T(8,128)S(1)}, u32[]{:S(2)}, u32[]{:S(2)}) collective-permute-start(f32[80,272]{1,0:T(8,128)S(1)} %fusion), channel_id=1, source_target_pairs={{0,3},{1,4},{2,5},{3,6},{4,7},{5,8},{6,9},{7,10},{8,11},{9,12},{10... | collective-permute-start | bytes 261128
  245.3 10.9 %collective-permute-start.1 = (f32[80,272]{1,0:T(8,128)S(1)}, f32[80,272]{1,0:T(8,128)S(1)}, u32[]{:S(2)}, u32[]{:S(2)}) collective-permute-start(f32[80,272]{1,0:T(8,128)S(1)} %fusion), channel_id=1, source_target_pairs={{0,2},{1,3},{2,4},{3,5},{4,6},{5,7},{6,8},{7,9},{8,10},{9,11},{10,... | collective-permute-start | bytes 261128
  256.2 8.4 %collective-permute-start = (f32[80,272]{1,0:T(8,128)S(1)}, f32[80,272]{1,0:T(8,128)S(1)}, u32[]{:S(2)}, u32[]{:S(2)}) collective-permute-start(f32[80,272]{1,0:T(8,128)S(1)} %fusion), channel_id=1, source_target_pairs={{0,1},{1,2},{2,3},{3,4},{4,5},{5,6},{6,7},{7,8},{8,9},{9,10},{10,1... | collective-permute-start | bytes 261128
  264.7 1.9 collective-permute-start.4
  266.6 0.6 dynamic-slice.4
  267.8 4.8 %collective-permute-done.4 = f32[52,272]{1,0:T(8,128)S(1)} collective-permute-done((f32[52,272]{1,0:T(8,128)S(1)}, f32[52,272]{1,0:T(8,128)S(1)}, u32[]{:S(2)}, u32[]{:S(2)}) %collective-permute-start.4) | collective-permute-done | bytes 56608
  272.6 0.0 collective-permute-done.3
  272.6 1.0 concatenate.50
  273.7 0.7 dynamic-slice_multiply_fusion
  (23 shorter events, 0.1 us)
Async XLA Ops:
  6.5 21.7 %copy-start.2 = (s32[1,128]{1,0:T(1,128)S(1)}, s32[1,128]{1,0:T(1,128)}, u32[]{:S(2)}) copy-start(s32[1,128]{1,0:T(1,128)} %param.5) | copy-start | bytes 1540
  28.2 48.4 %copy-start.1 = (f32[32]{0:T(128)S(1)}, f32[32]{0:T(128)}, u32[]{:S(2)}) copy-start(f32[32]{0:T(128)} %param.6) | copy-start | bytes 388
  28.2 48.4 %copy-start.3 = (s32[31]{0:T(128)S(1)}, s32[31]{0:T(128)}, u32[]{:S(2)}) copy-start(s32[31]{0:T(128)} %param.7) | copy-start | bytes 376
  70.1 11.5 %all-to-all-start = ((f32[8,1,2048]{2,1,0:T(1,128)}), f32[8,1,2048]{2,1,0:T(1,128)S(1)}, u32[]{:S(2)}, u32[]{:S(2)}) async-start(f32[8,1,2048]{2,1,0:T(1,128)} %reshape.135), calls=%async_computation | async-start | bytes 131072 | tf_op jit(solution)/shard_map/all_to_all | solution.py:42
  76.6 75.5 %all-gather.2.cloned.1.call-start = ((), (), s32[]{:S(2)}) async-start(), calls=%async_computation.1 | async-start | bytes 5013504 | tf_op jit(solution)/shard_map/all_gather | solution.py:48
  86.8 0.8 copy-start
  157.1 109.5 %copy-start.4 = (u32[256]{0:T(256)S(1)}, u32[256]{0:T(256)}, u32[]{:S(2)}) copy-start(u32[256]{0:T(256)} %constant.76) | copy-start | bytes 3076
  232.5 40.1 %collective-permute-start.3 = (f32[80,272]{1,0:T(8,128)S(1)}, f32[80,272]{1,0:T(8,128)S(1)}, u32[]{:S(2)}, u32[]{:S(2)}) collective-permute-start(f32[80,272]{1,0:T(8,128)S(1)} %fusion), channel_id=1, source_target_pairs={{0,4},{1,5},{2,6},{3,7},{4,8},{5,9},{6,10},{7,11},{8,12},{9,13},{1... | collective-permute-start | bytes 261128
  236.9 35.7 %collective-permute-start.2 = (f32[80,272]{1,0:T(8,128)S(1)}, f32[80,272]{1,0:T(8,128)S(1)}, u32[]{:S(2)}, u32[]{:S(2)}) collective-permute-start(f32[80,272]{1,0:T(8,128)S(1)} %fusion), channel_id=1, source_target_pairs={{0,3},{1,4},{2,5},{3,6},{4,7},{5,8},{6,9},{7,10},{8,11},{9,12},{10... | collective-permute-start | bytes 261128
  245.3 27.3 %collective-permute-start.1 = (f32[80,272]{1,0:T(8,128)S(1)}, f32[80,272]{1,0:T(8,128)S(1)}, u32[]{:S(2)}, u32[]{:S(2)}) collective-permute-start(f32[80,272]{1,0:T(8,128)S(1)} %fusion), channel_id=1, source_target_pairs={{0,2},{1,3},{2,4},{3,5},{4,6},{5,7},{6,8},{7,9},{8,10},{9,11},{10,... | collective-permute-start | bytes 261128
  256.2 16.4 %collective-permute-start = (f32[80,272]{1,0:T(8,128)S(1)}, f32[80,272]{1,0:T(8,128)S(1)}, u32[]{:S(2)}, u32[]{:S(2)}) collective-permute-start(f32[80,272]{1,0:T(8,128)S(1)} %fusion), channel_id=1, source_target_pairs={{0,1},{1,2},{2,3},{3,4},{4,5},{5,6},{6,7},{7,8},{8,9},{9,10},{10,1... | collective-permute-start | bytes 261128
  264.7 7.9 %collective-permute-start.4 = (f32[52,272]{1,0:T(8,128)S(1)}, f32[52,272]{1,0:T(8,128)S(1)}, u32[]{:S(2)}, u32[]{:S(2)}) collective-permute-start(f32[52,272]{1,0:T(8,128)S(1)} %slice.42), channel_id=1, source_target_pairs={{0,5},{1,6},{2,7},{3,8},{4,9},{5,10},{6,11},{7,12},{8,13},{9,14},{... | collective-permute-start | bytes 169736
Sparse Core Ops, SparseCore 0:
  87.8 64.3 all-gather.1
where the time goes:
time: 284 us; the launch traced here: 281 us
  blocking collectives  91.9 us (32%)
  waiting for transfers between devices  74 us (26%)
  local copies, waits for them, and re-layouts  48.2 us (17%)
  starting transfers between devices  40.6 us (14%)
  between operations  14.3 us (5%)
  other arithmetic  7.31 us (3%)
  matrix products  4.9 us (2%)
    unnamed x1, blocking collectives  75.4 us
    all_gather x1, waiting for transfers between devices, on_device(): block_features_bf = lax.all_gather(features_bf, 'lev', axis=1, tiled=True)  64.5 us
    unnamed x5, starting transfers between devices  34 us
    unnamed x20, local copies, waits for them, and re-layouts  30 us
    gather x1, local copies, waits for them, and re-layouts, on_device(): chosen = jnp.take(slab_fields, offsets, axis=2)  16.8 us
    all_gather x1, blocking collectives, on_device(): all_lists = lax.all_gather(sample_index, 'lev', axis=1, tiled=True)[0]  16.4 us
    all_to_all x1, starting transfers between devices, on_device(): lax.all_to_all(chosen, 'lev', split_axis=2, concat_axis=1, tiled=True)  6.56 us
  transfers between devices with their start and end apart: 7, of which 3 were waited for; matrix products, arithmetic and copies ran while one was open for 0% of the time, Pallas kernels for 0%

commit v1 on v0

v1 whole, which is shorter than its diff:
```python
import jax
import jax.numpy as jnp
from jax import lax
from jax.experimental import pallas as pl
from jax.experimental.pallas import tpu as pltpu
from jax.sharding import PartitionSpec as P

LEV, SLOTS, LANES = 32, 4, 128
N_X, N_ZLO, N_Y, N_ZHI = 4, 2, 4, 4
N_LEV, N_HOR = N_X * N_ZLO, N_ZHI * N_Y * 2
GROUP, SAMP = 2048, 128
BLOCK = N_LEV * SAMP
FEAT = 4 * LEV + 2 * LEV * LEV
ROWS_OUT, COLS_OUT = FEAT // N_HOR, FEAT // N_LEV
CHUNK, WINDOW = 72, 80
PIECE = N_ZHI * 2 * CHUNK
SENT = PIECE + CHUNK
VMEM = pl.BlockSpec(memory_space=pltpu.VMEM)


def params(mib):
    return pltpu.CompilerParams(vmem_limit_bytes=mib << 20)


def shift_lev(value, step_zlo, step_x):
    pairs = [(i, (i // N_X ^ step_zlo) * N_X + (i + step_x) % N_X) for i in range(N_LEV)]
    return lax.ppermute(value, "lev", pairs)


def shift_hor(value, step_zhi, step_y, step_core):
    pairs = []
    for i in range(N_HOR):
        zhi, y, core = i // (2 * N_Y), i // 2 % N_Y, i % 2
        to = (zhi + step_zhi) % N_ZHI * 2 * N_Y + (y + step_y) % N_Y * 2 + (core ^ step_core)
        pairs.append((i, to))
    return lax.ppermute(value, "hor", pairs)


def pick_kernel(index_ref, slab_ref, out_ref):
    for group in range(N_LEV):
        index = jnp.broadcast_to(index_ref[group : group + 1, :], (8, LANES))
        lane, tile = index % LANES, index // LANES
        hits = [tile == t for t in range(GROUP // LANES)]
        for pair in range(2):
            total = jnp.zeros((8, LANES), jnp.float32)
            for t in range(GROUP // LANES):
                at = pl.ds(group * GROUP + t * LANES, LANES)
                both = jnp.concatenate([slab_ref[2 * pair, :, at], slab_ref[2 * pair + 1, :, at]], axis=0)
                total = jnp.where(hits[t], jnp.take_along_axis(both, lane, axis=1), total)
            out_ref[8 * pair : 8 * pair + 8, group * SAMP : (group + 1) * SAMP] = total


def smooth_kernel(coef_ref, w0_ref, w1_ref, w2_ref, w3_ref, out_ref, raw_ref):
    x = lax.axis_index("lev") % N_X
    for step, ref in enumerate((w0_ref, w1_ref, w2_ref, w3_ref)):
        source = lax.rem(x - step + N_X, N_X)
        for zlo in range(N_ZLO):
            raw_ref[zlo * N_X + source] = ref[zlo]

    def tile(t, carry):
        at = pl.ds(pl.multiple_of(t * LANES, LANES), LANES)
        for slot in range(SLOTS):
            rows = [raw_ref[lev, 4 * slot : 4 * slot + 4, at] for lev in range(N_LEV)]
            value = jnp.concatenate(rows, axis=0)
            below, above = pltpu.roll(value, 1, 0), pltpu.roll(value, LEV - 1, 0)
            out_ref[slot * LEV : (slot + 1) * LEV, at] = (
                coef_ref[0:LEV] * value + coef_ref[LEV : 2 * LEV] * below + coef_ref[2 * LEV :] * above
            )
        return carry

    lax.fori_loop(0, BLOCK // LANES, tile, 0)


def gram_kernel(own_ref, other_ref, s0_ref, s1_ref, s2_ref, s3_ref, feat_ref, left_ref, prod_ref):
    hor, lev = lax.axis_index("hor"), lax.axis_index("lev")
    zhi, y, core = hor // (2 * N_Y), hor // 2 % N_Y, hor % 2
    for block, ref in enumerate((own_ref, other_ref)):

        def tile(t, carry):
            at = pl.ds(pl.multiple_of(t * LANES, LANES), LANES)
            to = pl.ds(pl.multiple_of(block * BLOCK + t * LANES, LANES), LANES)
            early = ref[0 : 2 * LEV, at]
            feat_ref[0 : 2 * LEV, to] = ref[2 * LEV : 4 * LEV, at].astype(jnp.bfloat16)
            feat_ref[2 * LEV : 4 * LEV, to] = early.astype(jnp.bfloat16)
            first = early[0:LEV]
            for m in range(2 * LEV):
                row = jnp.broadcast_to(ref[pl.ds(2 * LEV + m, 1), at], (LEV, LANES))
                feat_ref[4 * LEV + m * LEV : 4 * LEV + (m + 1) * LEV, to] = (row * first).astype(jnp.bfloat16)
            return carry

        lax.fori_loop(0, BLOCK // LANES, tile, 0)

    right = pl.ds(pl.multiple_of(lev * COLS_OUT, 16), COLS_OUT)
    for step_y, out_ref in enumerate((s0_ref, s1_ref, s2_ref, s3_ref)):
        to_y = lax.rem(y + step_y, N_Y)
        skip = 8 * lax.rem(to_y, 2)
        for step_z in range(N_ZHI):
            to_z = lax.rem(zhi + step_z, N_ZHI)
            start = (to_z * N_Y + to_y) * 2 * ROWS_OUT + core * 64 - skip
            left_ref[step_z * WINDOW : (step_z + 1) * WINDOW, :] = feat_ref[pl.ds(pl.multiple_of(start, 16), WINDOW), :]
        prod_ref[...] = lax.dot_general(
            left_ref[...], feat_ref[right, :], (((1,), (1,)), ((), ())), preferred_element_type=jnp.float32
        )
        for step_z in range(N_ZHI):
            rows = pl.ds(pl.multiple_of(step_z * WINDOW + skip, 8), CHUNK)
            for half in range(2):
                place = (2 * step_z + half) * CHUNK
                out_ref[place : place + CHUNK, :] = prod_ref[rows, half * LANES : (half + 1) * LANES]
            out_ref[PIECE:SENT, 16 * step_z : 16 * step_z + 16] = prod_ref[rows, 2 * LANES : COLS_OUT]


def add_kernel(s0_ref, s1_ref, s2_ref, s3_ref, t0_ref, t1_ref, t2_ref, t3_ref):
    def total(rows):
        return (s0_ref[rows, :] + s1_ref[rows, :]) + (s2_ref[rows, :] + s3_ref[rows, :])

    rest = total(slice(PIECE, SENT))
    for step_z, ref in enumerate((t0_ref, t1_ref, t2_ref, t3_ref)):
        ref[0 : 2 * CHUNK, :] = total(slice(step_z * 2 * CHUNK, (step_z + 1) * 2 * CHUNK))
        ref[2 * CHUNK :, :] = rest


def final_kernel(t0_ref, t1_ref, t2_ref, t3_ref, out_ref):
    odd = lax.axis_index("hor") % 2 == 1
    refs = (t0_ref, t1_ref, t2_ref, t3_ref)
    scale = 1.0 / (BLOCK * N_HOR)

    def place(value):
        return jnp.where(odd, value[CHUNK - ROWS_OUT : CHUNK], value[0:ROWS_OUT]) * scale

    for half in range(2):
        rows = slice(half * CHUNK, (half + 1) * CHUNK)
        value = (t0_ref[rows, :] + t1_ref[rows, :]) + (t2_ref[rows, :] + t3_ref[rows, :])
        out_ref[:, half * LANES : (half + 1) * LANES] = place(value)
    rest = [ref[2 * CHUNK :, 16 * k : 16 * k + 16] for k, ref in enumerate(refs)]
    out_ref[:, 2 * LANES :] = place((rest[0] + rest[1]) + (rest[2] + rest[3]))


def filter_coefficients(thickness, level_cuts):
    link = 1.0 - level_cuts.astype(jnp.float32)
    zero_one = jnp.zeros((1,), jnp.float32)
    lower = jnp.concatenate([zero_one, thickness[:-1] * link])
    upper = jnp.concatenate([thickness[1:] * link, zero_one])
    denom = 2.0 * thickness + lower + upper
    coef = jnp.concatenate([2.0 * thickness / denom, lower / denom, upper / denom])
    return jnp.broadcast_to(coef[:, None], (3 * LEV, LANES))


def on_device(slab_fields, sample_index, thickness, level_cuts):
    f32 = jnp.float32
    coef = filter_coefficients(thickness, level_cuts)
    lists = lax.all_to_all(jnp.broadcast_to(sample_index, (N_LEV, SAMP)), "lev", 0, 0, tiled=True)
    picked = pl.pallas_call(
        pick_kernel,
        out_shape=jax.ShapeDtypeStruct((4 * SLOTS, BLOCK), f32),
        in_specs=[VMEM] * 2,
        out_specs=VMEM,
        compiler_params=params(16),
        name="pick",
    )(lists, slab_fields)
    across = shift_lev(picked, 1, 0)
    up = lax.axis_index("lev") // N_X == 1
    near = jnp.stack([jnp.where(up, across, picked), jnp.where(up, picked, across)])
    far = {k: shift_lev(near, 0, k) for k in (2, 1, 3)}
    own = pl.pallas_call(
        smooth_kernel,
        out_shape=jax.ShapeDtypeStruct((SLOTS * LEV, BLOCK), f32),
        in_specs=[VMEM] * 5,
        out_specs=VMEM,
        scratch_shapes=[pltpu.VMEM((N_LEV, 4 * SLOTS, BLOCK), f32)],
        compiler_params=params(16),
        name="smooth",
    )(coef, near, far[1], far[2], far[3])
    other = shift_hor(own, 0, 0, 1)
    parts = pl.pallas_call(
        gram_kernel,
        out_shape=[jax.ShapeDtypeStruct((SENT, LANES), f32)] * N_Y,
        in_specs=[VMEM] * 2,
        out_specs=[VMEM] * N_Y,
        scratch_shapes=[
            pltpu.VMEM((FEAT, 2 * BLOCK), jnp.bfloat16),
            pltpu.VMEM((N_ZHI * WINDOW, 2 * BLOCK), jnp.bfloat16),
            pltpu.VMEM((N_ZHI * WINDOW, COLS_OUT), f32),
        ],
        compiler_params=params(32),
        name="gram",
    )(own, other)
    from_y = {k: shift_hor(parts[k], 0, k, 0) for k in (2, 1, 3)}
    sums = pl.pallas_call(
        add_kernel,
        out_shape=[jax.ShapeDtypeStruct((3 * CHUNK, LANES), f32)] * N_ZHI,
        in_specs=[VMEM] * N_Y,
        out_specs=[VMEM] * N_ZHI,
        compiler_params=params(8),
        name="add",
    )(parts[0], from_y[1], from_y[2], from_y[3])
    from_z = {k: shift_hor(sums[k], k, 0, 0) for k in (2, 1, 3)}
    return pl.pallas_call(
        final_kernel,
        out_shape=jax.ShapeDtypeStruct((ROWS_OUT, COLS_OUT), f32),
        in_specs=[VMEM] * N_ZHI,
        out_specs=VMEM,
        compiler_params=params(8),
        name="final",
    )(sums[0], from_z[1], from_z[2], from_z[3])


def solution(mesh):
    in_specs = (P(None, "lev", "hor"), P("hor", "lev"), P(), P())
    out_specs = P("hor", "lev")
    return jax.shard_map(on_device, mesh=mesh, in_specs=in_specs, out_specs=out_specs, check_vma=False)
```

time: 284 us -> 75.4 us (0.27)
  the two profiles are of different devices: /device:TPU:26 before, /device:TPU:1 now
where the time goes in v1:
time: 75.4 us; the launch traced here: 75.2 us
  waiting for transfers between devices  36.4 us (48%)
  starting transfers between devices  28.3 us (38%)
  Pallas kernels  7.48 us (10%)
  local copies, waits for them, and re-layouts  2.55 us (3%)
    ppermute x7, waiting for transfers between devices, shift_hor(): return lax.ppermute(value, 'hor', pairs)  23.5 us
    ppermute x7, starting transfers between devices, shift_hor(): return lax.ppermute(value, 'hor', pairs)  19.5 us
    ppermute x4, waiting for transfers between devices, shift_lev(): return lax.ppermute(value, 'lev', pairs)  8.14 us
    all_to_all x1, starting transfers between devices, on_device(): lax.all_to_all(jnp.broadcast_to(sample_index, (N_LEV, SAMP)), 'lev', 0, 0...  6.33 us
    pallas_call x1, Pallas kernels, on_device(): pl.pallas_call(gram_kernel, out_shape=[jax.ShapeDtypeStruct((SENT, LANES)...  5.88 us
    all_to_all x1, waiting for transfers between devices, on_device(): lax.all_to_all(jnp.broadcast_to(sample_index, (N_LEV, SAMP)), 'lev', 0, 0...  4.84 us
    ppermute x4, starting transfers between devices, shift_lev(): return lax.ppermute(value, 'lev', pairs)  2.52 us
    unnamed x8, local copies, waits for them, and re-layouts  1.89 us
  transfers between devices with their start and end apart: 12, of which 10 were waited for; matrix products, arithmetic and copies ran while one was open for 0% of the time, Pallas kernels for 0%

profile of v1, /device:TPU:1, one launch (start us, length us, event | category | flops | bytes accessed | tf_op | source)
XLA Modules:
  0.0 75.2 jit_solution(11972105012457698173)
XLA Ops:
  0.0 0.7 copy-done.2
  0.7 0.6 broadcast_in_dim.5
  1.3 6.3 %all-to-all-start = ((s32[8,1,128]{2,1,0:T(1,128)}), s32[8,1,128]{2,1,0:T(1,128)S(1)}, u32[]{:S(2)}, u32[]{:S(2)}) async-start(s32[8,1,128]{2,1,0:T(1,128)} %broadcast_in_dim.5), calls=%async_computation | async-start | bytes 8192 | tf_op jit(solution)/shard_map/all_to_all | solution.py:151
  7.7 4.8 %all-to-all-done = s32[8,1,128]{2,1,0:T(1,128)S(1)} async-done(((s32[8,1,128]{2,1,0:T(1,128)}), s32[8,1,128]{2,1,0:T(1,128)S(1)}, u32[]{:S(2)}, u32[]{:S(2)}) %all-to-all-start) | async-done | bytes 4128 | tf_op jit(solution)/shard_map/all_to_all | solution.py:151
  12.5 1.2 %copy-done = f32[4,4,16384]{2,1,0:T(4,128)S(1)} copy-done((f32[4,4,16384]{2,1,0:T(4,128)S(1)}, f32[4,4,16384]{2,1,0:T(4,128)}, u32[]{:S(2)}) %copy-start) | copy-done | bytes 1048600
  13.7 0.4 pick.1
  14.1 0.4 collective-permute-start
  14.5 0.1 multiply_divide_fusion
  14.6 2.8 %collective-permute-done = f32[16,1024]{1,0:T(8,128)S(1)} collective-permute-done((f32[16,1024]{1,0:T(8,128)S(1)}, f32[16,1024]{1,0:T(8,128)S(1)}, u32[]{:S(2)}, u32[]{:S(2)}) %collective-permute-start) | collective-permute-done | bytes 65568 | tf_op jit(solution)/shard_map/ppermute | solution.py:27
  17.4 1.0 %collective-permute-start.3 = (f32[2,16,1024]{2,1,0:T(8,128)S(1)}, f32[2,16,1024]{2,1,0:T(8,128)S(1)}, u32[]{:S(2)}, u32[]{:S(2)}) collective-permute-start(f32[2,16,1024]{2,1,0:T(8,128)S(1)} %pad_maximum_fusion.w0_ref), channel_id=1, source_target_pairs={{0,96},{32,0},{64,32},{96,64},{128,224},{160,128},{192,160},{224,1... | collective-permute-start | bytes 393224 | tf_op jit(solution)/shard_map/ppermute | solution.py:27
  18.3 1.2 %collective-permute-start.2 = (f32[2,16,1024]{2,1,0:T(8,128)S(1)}, f32[2,16,1024]{2,1,0:T(8,128)S(1)}, u32[]{:S(2)}, u32[]{:S(2)}) collective-permute-start(f32[2,16,1024]{2,1,0:T(8,128)S(1)} %pad_maximum_fusion.w0_ref), channel_id=1, source_target_pairs={{0,64},{32,96},{64,0},{96,32},{128,192},{160,224},{192,128},{224,1... | collective-permute-start | bytes 393224 | tf_op jit(solution)/shard_map/ppermute | solution.py:27
  19.5 0.1 fusion.1
  19.6 0.1 pad_maximum_fusion.3
  19.7 1.6 %collective-permute-done.3.w3_ref = f32[2,16,1024]{2,1,0:T(8,128)S(1)} collective-permute-done((f32[2,16,1024]{2,1,0:T(8,128)S(1)}, f32[2,16,1024]{2,1,0:T(8,128)S(1)}, u32[]{:S(2)}, u32[]{:S(2)}) %collective-permute-start.3) | collective-permute-done | bytes 131104 | tf_op jit(solution)/shard_map/ppermute | solution.py:27
  21.3 2.4 %collective-permute-done.2.w2_ref = f32[2,16,1024]{2,1,0:T(8,128)S(1)} collective-permute-done((f32[2,16,1024]{2,1,0:T(8,128)S(1)}, f32[2,16,1024]{2,1,0:T(8,128)S(1)}, u32[]{:S(2)}, u32[]{:S(2)}) %collective-permute-start.2) | collective-permute-done | bytes 131104 | tf_op jit(solution)/shard_map/ppermute | solution.py:27
  23.7 1.3 %collective-permute-done.1.w1_ref = f32[2,16,1024]{2,1,0:T(8,128)S(1)} collective-permute-done((f32[2,16,1024]{2,1,0:T(8,128)S(1)}, f32[2,16,1024]{2,1,0:T(8,128)S(1)}, u32[]{:S(2)}, u32[]{:S(2)}) %collective-permute-start.1) | collective-permute-done | bytes 131104 | tf_op jit(solution)/shard_map/ppermute | solution.py:27
  25.1 0.3 smooth.1.own_ref
  25.4 4.8 %collective-permute-start.4 = (f32[128,1024]{1,0:T(8,128)S(1)}, f32[128,1024]{1,0:T(8,128)S(1)}, u32[]{:S(2)}, u32[]{:S(2)}) collective-permute-start(f32[128,1024]{1,0:T(8,128)S(1)} %smooth.1.own_ref), channel_id=1, source_target_pairs={{0,1},{1,0},{2,3},{3,2},{4,5},{5,4},{6,7},{7,6},{8,9},{9,8},{10,11... | collective-permute-start | bytes 1572872 | tf_op jit(solution)/shard_map/ppermute | solution.py:36
  30.2 1.5 %collective-permute-done.4.other_ref = f32[128,1024]{1,0:T(8,128)S(1)} collective-permute-done((f32[128,1024]{1,0:T(8,128)S(1)}, f32[128,1024]{1,0:T(8,128)S(1)}, u32[]{:S(2)}, u32[]{:S(2)}) %collective-permute-start.4) | collective-permute-done | bytes 524320 | tf_op jit(solution)/shard_map/ppermute | solution.py:36
  31.8 5.9 %gram.1 = (f32[648,128]{1,0:T(8,128)S(1)}, f32[648,128]{1,0:T(8,128)S(1)}, f32[648,128]{1,0:T(8,128)S(1)}, f32[648,128]{1,0:T(8,128)S(1)}) custom-call(f32[128,1024]{1,0:T(8,128)S(1)} %smooth.1.own_ref, f32[128,1024]{1,0:T(8,128)S(1)} %collective-permute-done.4.other_ref), custom_call_target="tpu_custom_call" | custom-call | tf_op jit(solution)/shard_map/gram/pallas_call | solution.py:174
  37.6 1.4 %collective-permute-start.5 = (f32[648,128]{1,0:T(8,128)S(1)}, f32[648,128]{1,0:T(8,128)S(1)}, u32[]{:S(2)}, u32[]{:S(2)}) collective-permute-start(f32[648,128]{1,0:T(8,128)S(1)} %get-tuple-element.14), channel_id=1, source_target_pairs={{0,2},{1,3},{2,4},{3,5},{4,6},{5,7},{6,0},{7,1},{8,10},{9,11},{10,... | collective-permute-start | bytes 995336 | tf_op jit(solution)/shard_map/ppermute | solution.py:36
  39.0 2.6 %collective-permute-start.6 = (f32[648,128]{1,0:T(8,128)S(1)}, f32[648,128]{1,0:T(8,128)S(1)}, u32[]{:S(2)}, u32[]{:S(2)}) collective-permute-start(f32[648,128]{1,0:T(8,128)S(1)} %get-tuple-element.15), channel_id=1, source_target_pairs={{0,4},{1,5},{2,6},{3,7},{4,0},{5,1},{6,2},{7,3},{8,12},{9,13},{10,... | collective-permute-start | bytes 995336 | tf_op jit(solution)/shard_map/ppermute | solution.py:36
  41.6 1.1 %collective-permute-start.7 = (f32[648,128]{1,0:T(8,128)S(1)}, f32[648,128]{1,0:T(8,128)S(1)}, u32[]{:S(2)}, u32[]{:S(2)}) collective-permute-start(f32[648,128]{1,0:T(8,128)S(1)} %get-tuple-element.16), channel_id=1, source_target_pairs={{0,6},{1,7},{2,0},{3,1},{4,2},{5,3},{6,4},{7,5},{8,14},{9,15},{10,... | collective-permute-start | bytes 995336 | tf_op jit(solution)/shard_map/ppermute | solution.py:36
  42.7 5.4 %collective-permute-done.5.s1_ref = f32[648,128]{1,0:T(8,128)S(1)} collective-permute-done((f32[648,128]{1,0:T(8,128)S(1)}, f32[648,128]{1,0:T(8,128)S(1)}, u32[]{:S(2)}, u32[]{:S(2)}) %collective-permute-start.5) | collective-permute-done | bytes 331808 | tf_op jit(solution)/shard_map/ppermute | solution.py:36
  48.0 8.2 %collective-permute-done.6.s2_ref = f32[648,128]{1,0:T(8,128)S(1)} collective-permute-done((f32[648,128]{1,0:T(8,128)S(1)}, f32[648,128]{1,0:T(8,128)S(1)}, u32[]{:S(2)}, u32[]{:S(2)}) %collective-permute-start.6) | collective-permute-done | bytes 331808 | tf_op jit(solution)/shard_map/ppermute | solution.py:36
  56.3 0.1 add.14
  56.4 3.0 %collective-permute-start.8 = (f32[216,128]{1,0:T(8,128)S(1)}, f32[216,128]{1,0:T(8,128)S(1)}, u32[]{:S(2)}, u32[]{:S(2)}) collective-permute-start(f32[216,128]{1,0:T(8,128)S(1)} %get-tuple-element.18), channel_id=1, source_target_pairs={{0,8},{1,9},{2,10},{3,11},{4,12},{5,13},{6,14},{7,15},{8,16},{9,17... | collective-permute-start | bytes 331784 | tf_op jit(solution)/shard_map/ppermute | solution.py:36
  59.4 4.2 %collective-permute-start.9 = (f32[216,128]{1,0:T(8,128)S(1)}, f32[216,128]{1,0:T(8,128)S(1)}, u32[]{:S(2)}, u32[]{:S(2)}) collective-permute-start(f32[216,128]{1,0:T(8,128)S(1)} %get-tuple-element.19), channel_id=1, source_target_pairs={{0,16},{1,17},{2,18},{3,19},{4,20},{5,21},{6,22},{7,23},{8,24},{9,... | collective-permute-start | bytes 331784 | tf_op jit(solution)/shard_map/ppermute | solution.py:36
  63.7 2.4 %collective-permute-start.10 = (f32[216,128]{1,0:T(8,128)S(1)}, f32[216,128]{1,0:T(8,128)S(1)}, u32[]{:S(2)}, u32[]{:S(2)}) collective-permute-start(f32[216,128]{1,0:T(8,128)S(1)} %get-tuple-element.20), channel_id=1, source_target_pairs={{0,24},{1,25},{2,26},{3,27},{4,28},{5,29},{6,30},{7,31},{8,0},{9,1... | collective-permute-start | bytes 331784 | tf_op jit(solution)/shard_map/ppermute | solution.py:36
  66.1 4.0 %collective-permute-done.9.t2_ref = f32[216,128]{1,0:T(8,128)S(1)} collective-permute-done((f32[216,128]{1,0:T(8,128)S(1)}, f32[216,128]{1,0:T(8,128)S(1)}, u32[]{:S(2)}, u32[]{:S(2)}) %collective-permute-start.9) | collective-permute-done | bytes 110624 | tf_op jit(solution)/shard_map/ppermute | solution.py:36
  70.1 4.3 %collective-permute-done.10.t3_ref = f32[216,128]{1,0:T(8,128)S(1)} collective-permute-done((f32[216,128]{1,0:T(8,128)S(1)}, f32[216,128]{1,0:T(8,128)S(1)}, u32[]{:S(2)}, u32[]{:S(2)}) %collective-permute-start.10) | collective-permute-done | bytes 110624 | tf_op jit(solution)/shard_map/ppermute | solution.py:36
  74.4 0.8 %final.1 = f32[68,272]{1,0:T(8,128)} custom-call(f32[216,128]{1,0:T(8,128)S(1)} %get-tuple-element.17.t0_ref, f32[216,128]{1,0:T(8,128)S(1)} %collective-permute-done.8.t1_ref, f32[216,128]{1,0:T(8,128)S(1)} %collective-permute-done.9.t2_ref, f32[216,128]{1,0:T(8,128)S(1)} %collective-permute-done.10.t3_ref), custom_call_target="tpu_custom_call" | custom-call | tf_op jit(solution)/shard_map/final/pallas_call | solution.py:197
  (13 shorter events, 0.2 us)
Async XLA Ops:
  0.0 0.7 copy-start.2
  1.3 6.3 %copy-start.1 = (f32[32]{0:T(128)S(1)}, f32[32]{0:T(128)}, u32[]{:S(2)}) copy-start(f32[32]{0:T(128)} %param.6) | copy-start | bytes 388
  1.3 6.3 %copy-start.3 = (s32[31]{0:T(128)S(1)}, s32[31]{0:T(128)}, u32[]{:S(2)}) copy-start(s32[31]{0:T(128)} %param.7) | copy-start | bytes 376
  1.3 11.3 %all-to-all-start = ((s32[8,1,128]{2,1,0:T(1,128)}), s32[8,1,128]{2,1,0:T(1,128)S(1)}, u32[]{:S(2)}, u32[]{:S(2)}) async-start(s32[8,1,128]{2,1,0:T(1,128)} %broadcast_in_dim.5), calls=%async_computation | async-start | bytes 8192 | tf_op jit(solution)/shard_map/all_to_all | solution.py:151
  12.5 1.2 %copy-start = (f32[4,4,16384]{2,1,0:T(4,128)S(1)}, f32[4,4,16384]{2,1,0:T(4,128)}, u32[]{:S(2)}) copy-start(f32[4,4,16384]{2,1,0:T(4,128)} %slab_ref.1) | copy-start | bytes 3145732
  14.1 3.2 %collective-permute-start = (f32[16,1024]{1,0:T(8,128)S(1)}, f32[16,1024]{1,0:T(8,128)S(1)}, u32[]{:S(2)}, u32[]{:S(2)}) collective-permute-start(f32[16,1024]{1,0:T(8,128)S(1)} %pick.1), channel_id=1, source_target_pairs={{0,128},{32,160},{64,192},{96,224},{128,0},{160,32},{192,64},{224,... | collective-permute-start | bytes 196616 | tf_op jit(solution)/shard_map/ppermute | solution.py:27
  17.4 3.9 %collective-permute-start.3 = (f32[2,16,1024]{2,1,0:T(8,128)S(1)}, f32[2,16,1024]{2,1,0:T(8,128)S(1)}, u32[]{:S(2)}, u32[]{:S(2)}) collective-permute-start(f32[2,16,1024]{2,1,0:T(8,128)S(1)} %pad_maximum_fusion.w0_ref), channel_id=1, source_target_pairs={{0,96},{32,0},{64,32},{96,64},{128,224},{160,128},{192,160},{224,1... | collective-permute-start | bytes 393224 | tf_op jit(solution)/shard_map/ppermute | solution.py:27
  18.3 5.4 %collective-permute-start.2 = (f32[2,16,1024]{2,1,0:T(8,128)S(1)}, f32[2,16,1024]{2,1,0:T(8,128)S(1)}, u32[]{:S(2)}, u32[]{:S(2)}) collective-permute-start(f32[2,16,1024]{2,1,0:T(8,128)S(1)} %pad_maximum_fusion.w0_ref), channel_id=1, source_target_pairs={{0,64},{32,96},{64,0},{96,32},{128,192},{160,224},{192,128},{224,1... | collective-permute-start | bytes 393224 | tf_op jit(solution)/shard_map/ppermute | solution.py:27
  19.5 5.5 %collective-permute-start.1 = (f32[2,16,1024]{2,1,0:T(8,128)S(1)}, f32[2,16,1024]{2,1,0:T(8,128)S(1)}, u32[]{:S(2)}, u32[]{:S(2)}) collective-permute-start(f32[2,16,1024]{2,1,0:T(8,128)S(1)} %pad_maximum_fusion.w0_ref), channel_id=1, source_target_pairs={{0,32},{32,64},{64,96},{96,0},{128,160},{160,192},{192,224},{224,1... | collective-permute-start | bytes 393224 | tf_op jit(solution)/shard_map/ppermute | solution.py:27
  25.4 6.3 %collective-permute-start.4 = (f32[128,1024]{1,0:T(8,128)S(1)}, f32[128,1024]{1,0:T(8,128)S(1)}, u32[]{:S(2)}, u32[]{:S(2)}) collective-permute-start(f32[128,1024]{1,0:T(8,128)S(1)} %smooth.1.own_ref), channel_id=1, source_target_pairs={{0,1},{1,0},{2,3},{3,2},{4,5},{5,4},{6,7},{7,6},{8,9},{9,8},{10,11... | collective-permute-start | bytes 1572872 | tf_op jit(solution)/shard_map/ppermute | solution.py:36
  37.6 10.4 %collective-permute-start.5 = (f32[648,128]{1,0:T(8,128)S(1)}, f32[648,128]{1,0:T(8,128)S(1)}, u32[]{:S(2)}, u32[]{:S(2)}) collective-permute-start(f32[648,128]{1,0:T(8,128)S(1)} %get-tuple-element.14), channel_id=1, source_target_pairs={{0,2},{1,3},{2,4},{3,5},{4,6},{5,7},{6,0},{7,1},{8,10},{9,11},{10,... | collective-permute-start | bytes 995336 | tf_op jit(solution)/shard_map/ppermute | solution.py:36
  39.0 17.3 %collective-permute-start.6 = (f32[648,128]{1,0:T(8,128)S(1)}, f32[648,128]{1,0:T(8,128)S(1)}, u32[]{:S(2)}, u32[]{:S(2)}) collective-permute-start(f32[648,128]{1,0:T(8,128)S(1)} %get-tuple-element.15), channel_id=1, source_target_pairs={{0,4},{1,5},{2,6},{3,7},{4,0},{5,1},{6,2},{7,3},{8,12},{9,13},{10,... | collective-permute-start | bytes 995336 | tf_op jit(solution)/shard_map/ppermute | solution.py:36
  41.6 14.7 %collective-permute-start.7 = (f32[648,128]{1,0:T(8,128)S(1)}, f32[648,128]{1,0:T(8,128)S(1)}, u32[]{:S(2)}, u32[]{:S(2)}) collective-permute-start(f32[648,128]{1,0:T(8,128)S(1)} %get-tuple-element.16), channel_id=1, source_target_pairs={{0,6},{1,7},{2,0},{3,1},{4,2},{5,3},{6,4},{7,5},{8,14},{9,15},{10,... | collective-permute-start | bytes 995336 | tf_op jit(solution)/shard_map/ppermute | solution.py:36
  56.4 9.7 %collective-permute-start.8 = (f32[216,128]{1,0:T(8,128)S(1)}, f32[216,128]{1,0:T(8,128)S(1)}, u32[]{:S(2)}, u32[]{:S(2)}) collective-permute-start(f32[216,128]{1,0:T(8,128)S(1)} %get-tuple-element.18), channel_id=1, source_target_pairs={{0,8},{1,9},{2,10},{3,11},{4,12},{5,13},{6,14},{7,15},{8,16},{9,17... | collective-permute-start | bytes 331784 | tf_op jit(solution)/shard_map/ppermute | solution.py:36
  59.4 10.6 %collective-permute-start.9 = (f32[216,128]{1,0:T(8,128)S(1)}, f32[216,128]{1,0:T(8,128)S(1)}, u32[]{:S(2)}, u32[]{:S(2)}) collective-permute-start(f32[216,128]{1,0:T(8,128)S(1)} %get-tuple-element.19), channel_id=1, source_target_pairs={{0,16},{1,17},{2,18},{3,19},{4,20},{5,21},{6,22},{7,23},{8,24},{9,... | collective-permute-start | bytes 331784 | tf_op jit(solution)/shard_map/ppermute | solution.py:36
  63.7 10.7 %collective-permute-start.10 = (f32[216,128]{1,0:T(8,128)S(1)}, f32[216,128]{1,0:T(8,128)S(1)}, u32[]{:S(2)}, u32[]{:S(2)}) collective-permute-start(f32[216,128]{1,0:T(8,128)S(1)} %get-tuple-element.20), channel_id=1, source_target_pairs={{0,24},{1,25},{2,26},{3,27},{4,28},{5,29},{6,30},{7,31},{8,0},{9,1... | collective-permute-start | bytes 331784 | tf_op jit(solution)/shard_map/ppermute | solution.py:36

commit v2 on v1

v2 whole, which is shorter than its diff:
```python
import functools

import jax
import jax.numpy as jnp
from jax import lax
from jax.experimental import pallas as pl
from jax.experimental.pallas import tpu as pltpu
from jax.sharding import PartitionSpec as P

LEV, SLOTS, LANES = 32, 4, 128
N_X, N_ZLO, N_Y, N_ZHI = 4, 2, 4, 4
N_LEV, N_HOR = N_X * N_ZLO, N_ZHI * N_Y * 2
GROUP, SAMP = 2048, 128
BLOCK = N_LEV * SAMP
FEAT = 4 * LEV + 2 * LEV * LEV
ROWS_OUT, COLS_OUT = FEAT // N_HOR, FEAT // N_LEV
CHUNK, WINDOW = 72, 80
PIECE = N_ZHI * 2 * CHUNK
SENT = PIECE + CHUNK
LAST = 2 * CHUNK + 16
SHARE = 1 << 18
VMEM = pl.BlockSpec(memory_space=pltpu.VMEM)


def params(mib):
    return pltpu.CompilerParams(vmem_limit_bytes=mib << 20)


def cost(flops, moved):
    return pl.CostEstimate(flops=flops, bytes_accessed=moved, transcendentals=0)


def shift_lev(value, step_zlo, step_x):
    pairs = [(i, (i // N_X ^ step_zlo) * N_X + (i + step_x) % N_X) for i in range(N_LEV)]
    return lax.ppermute(value, "lev", pairs)


def shift_hor(value, step_zhi, step_y, step_core):
    pairs = []
    for i in range(N_HOR):
        zhi, y, core = i // (2 * N_Y), i // 2 % N_Y, i % 2
        to = (zhi + step_zhi) % N_ZHI * 2 * N_Y + (y + step_y) % N_Y * 2 + (core ^ step_core)
        pairs.append((i, to))
    return lax.ppermute(value, "hor", pairs)


def repeat_kernel(index_ref, out_ref):
    for lev in range(N_LEV):
        out_ref[lev] = index_ref[...]


def stage_kernel(slab_ref, out_ref):
    for slot in range(SLOTS):
        out_ref[4 * slot : 4 * slot + 4, :] = slab_ref[slot]


def pick_kernel(index_ref, slab_ref, out_ref):
    for group in range(N_LEV):
        index = jnp.broadcast_to(index_ref[group], (8, LANES))
        lane, tile = index % LANES, index // LANES
        hits = [tile == t for t in range(GROUP // LANES)]
        for pair in range(2):
            rows = slice(8 * pair, 8 * pair + 8)
            total = jnp.zeros((8, LANES), jnp.float32)
            for t in range(GROUP // LANES):
                at = slice(group * GROUP + t * LANES, group * GROUP + (t + 1) * LANES)
                total = jnp.where(hits[t], jnp.take_along_axis(slab_ref[rows, at], lane, axis=1), total)
            out_ref[rows, group * SAMP : (group + 1) * SAMP] = total


def smooth_kernel(coef_ref, w0_ref, w1_ref, w2_ref, w3_ref, out_ref, raw_ref):
    x = lax.axis_index("lev") % N_X
    for step, ref in enumerate((w0_ref, w1_ref, w2_ref, w3_ref)):
        source = lax.rem(x - step + N_X, N_X)
        for zlo in range(N_ZLO):
            raw_ref[zlo * N_X + source] = ref[zlo]

    def tile(t, carry):
        at = pl.ds(pl.multiple_of(t * LANES, LANES), LANES)
        for slot in range(SLOTS):
            rows = [raw_ref[lev, 4 * slot : 4 * slot + 4, at] for lev in range(N_LEV)]
            value = jnp.concatenate(rows, axis=0)
            below, above = pltpu.roll(value, 1, 0), pltpu.roll(value, LEV - 1, 0)
            out_ref[slot * LEV : (slot + 1) * LEV, at] = (
                coef_ref[0:LEV] * value + coef_ref[LEV : 2 * LEV] * below + coef_ref[2 * LEV :] * above
            )
        return carry

    lax.fori_loop(0, BLOCK // LANES, tile, 0)


def feature_kernel(smooth_ref, feat_ref):
    def tile(t, carry):
        at = pl.ds(pl.multiple_of(t * LANES, LANES), LANES)
        early = smooth_ref[0 : 2 * LEV, at]
        feat_ref[0 : 2 * LEV, at] = smooth_ref[2 * LEV : 4 * LEV, at].astype(jnp.bfloat16)
        feat_ref[2 * LEV : 4 * LEV, at] = early.astype(jnp.bfloat16)
        first = early[0:LEV]
        for m in range(2 * LEV):
            row = jnp.broadcast_to(smooth_ref[pl.ds(2 * LEV + m, 1), at], (LEV, LANES))
            feat_ref[4 * LEV + m * LEV : 4 * LEV + (m + 1) * LEV, at] = (row * first).astype(jnp.bfloat16)
        return carry

    lax.fori_loop(0, BLOCK // LANES, tile, 0)


def gram_kernel(step_y, own_ref, other_ref, out_ref, left_ref, prod_ref):
    hor, lev = lax.axis_index("hor"), lax.axis_index("lev")
    zhi, y, core = hor // (2 * N_Y), hor // 2 % N_Y, hor % 2
    right = pl.ds(pl.multiple_of(lev * COLS_OUT, 16), COLS_OUT)
    to_y = lax.rem(y + step_y, N_Y)
    skip = 8 * lax.rem(to_y, 2)
    for block, ref in enumerate((own_ref, other_ref)):
        for step_z in range(N_ZHI):
            to_z = lax.rem(zhi + step_z, N_ZHI)
            start = (to_z * N_Y + to_y) * 2 * ROWS_OUT + core * 64 - skip
            rows = pl.ds(pl.multiple_of(start, 16), WINDOW)
            left_ref[step_z * WINDOW : (step_z + 1) * WINDOW, :] = ref[rows, :]
        part = lax.dot_general(
            left_ref[...], ref[right, :], (((1,), (1,)), ((), ())), preferred_element_type=jnp.float32
        )
        prod_ref[...] = part + prod_ref[...] if block else part
    for step_z in range(N_ZHI):
        rows = pl.ds(pl.multiple_of(step_z * WINDOW + skip, 8), CHUNK)
        for half in range(2):
            place = (2 * step_z + half) * CHUNK
            out_ref[place : place + CHUNK, :] = prod_ref[rows, half * LANES : (half + 1) * LANES]
        out_ref[PIECE:SENT, 16 * step_z : 16 * step_z + 16] = prod_ref[rows, 2 * LANES : COLS_OUT]


def add_kernel(a_ref, b_ref, out_ref):
    out_ref[...] = a_ref[...] + b_ref[...]


def split_kernel(a_ref, b_ref, t0_ref, t1_ref, t2_ref, t3_ref):
    rest = a_ref[PIECE:SENT, :] + b_ref[PIECE:SENT, :]
    strip = lax.broadcasted_iota(jnp.int32, (8, LANES), 1) // 16
    for step_z, ref in enumerate((t0_ref, t1_ref, t2_ref, t3_ref)):
        rows = slice(step_z * 2 * CHUNK, (step_z + 1) * 2 * CHUNK)
        ref[0 : 2 * CHUNK, :] = a_ref[rows, :] + b_ref[rows, :]
        packed = jnp.zeros((8, LANES), jnp.float32)
        for group in range(8):
            moved = pltpu.roll(rest[8 * group : 8 * group + 8], 16 * (group - step_z) % LANES, 1)
            packed = jnp.where(strip == group, moved, packed)
        ref[2 * CHUNK : 2 * CHUNK + 8, :] = packed
        ref[2 * CHUNK + 8 : LAST, :] = pltpu.roll(rest[64:CHUNK], -16 * step_z % LANES, 1)


def final_kernel(t0_ref, t1_ref, t2_ref, t3_ref, out_ref):
    odd = lax.axis_index("hor") % 2 == 1
    scale = 1.0 / (BLOCK * N_HOR)

    def total(rows):
        return (t0_ref[rows, :] + t1_ref[rows, :]) + (t2_ref[rows, :] + t3_ref[rows, :])

    def place(value):
        return jnp.where(odd, value[CHUNK - ROWS_OUT : CHUNK], value[0:ROWS_OUT]) * scale

    for half in range(2):
        value = total(slice(half * CHUNK, (half + 1) * CHUNK))
        out_ref[:, half * LANES : (half + 1) * LANES] = place(value)
    packed = total(slice(2 * CHUNK, 2 * CHUNK + 8))
    rest = [pltpu.roll(packed, -16 * group % LANES, 1) for group in range(8)]
    rest.append(total(slice(2 * CHUNK + 8, LAST)))
    out_ref[:, 2 * LANES :] = place(jnp.concatenate(rest, axis=0))[:, :16]


def filter_coefficients(thickness, level_cuts):
    link = 1.0 - level_cuts.astype(jnp.float32)
    zero_one = jnp.zeros((1,), jnp.float32)
    lower = jnp.concatenate([zero_one, thickness[:-1] * link])
    upper = jnp.concatenate([thickness[1:] * link, zero_one])
    denom = 2.0 * thickness + lower + upper
    coef = jnp.concatenate([2.0 * thickness / denom, lower / denom, upper / denom])
    return jnp.broadcast_to(coef[:, None], (3 * LEV, LANES))


def features(smoothed):
    return pl.pallas_call(
        feature_kernel,
        out_shape=jax.ShapeDtypeStruct((FEAT, BLOCK), jnp.bfloat16),
        in_specs=[VMEM],
        out_specs=VMEM,
        compiler_params=params(12),
        cost_estimate=cost(FEAT * BLOCK, 5 << 20),
        name="features",
    )(smoothed)


def on_device(slab_fields, sample_index, thickness, level_cuts):
    f32 = jnp.float32
    coef = filter_coefficients(thickness, level_cuts)
    repeated = pl.pallas_call(
        repeat_kernel,
        out_shape=jax.ShapeDtypeStruct((N_LEV, 1, SAMP), jnp.int32),
        in_specs=[VMEM],
        out_specs=VMEM,
        compiler_params=params(1),
        name="repeat",
    )(sample_index)
    lists = lax.all_to_all(repeated, "lev", 0, 0, tiled=True)
    staged = pl.pallas_call(
        stage_kernel,
        out_shape=jax.ShapeDtypeStruct((4 * SLOTS, N_LEV * GROUP), f32),
        in_specs=[VMEM],
        out_specs=VMEM,
        compiler_params=params(8),
        cost_estimate=cost(0, 2 << 20),
        name="stage",
    )(slab_fields)
    picked = pl.pallas_call(
        pick_kernel,
        out_shape=jax.ShapeDtypeStruct((4 * SLOTS, BLOCK), f32),
        in_specs=[VMEM] * 2,
        out_specs=VMEM,
        compiler_params=params(8),
        name="pick",
    )(lists, staged)
    across = shift_lev(picked, 1, 0)
    up = lax.axis_index("lev") // N_X == 1
    near = jnp.stack([jnp.where(up, across, picked), jnp.where(up, picked, across)])
    far = {k: shift_lev(near, 0, k) for k in (2, 1, 3)}
    own = pl.pallas_call(
        smooth_kernel,
        out_shape=jax.ShapeDtypeStruct((SLOTS * LEV, BLOCK), f32),
        in_specs=[VMEM] * 5,
        out_specs=VMEM,
        scratch_shapes=[pltpu.VMEM((N_LEV, 4 * SLOTS, BLOCK), f32)],
        compiler_params=params(16),
        name="smooth",
    )(coef, near, far[1], far[2], far[3])
    other = shift_hor(own, 0, 0, 1)
    feats = [features(own), features(other)]
    parts = {}
    for k in (2, 1, 3, 0):
        parts[k] = pl.pallas_call(
            functools.partial(gram_kernel, k),
            out_shape=jax.ShapeDtypeStruct((SENT, LANES), f32),
            in_specs=[VMEM] * 2,
            out_specs=VMEM,
            scratch_shapes=[
                pltpu.VMEM((N_ZHI * WINDOW, BLOCK), jnp.bfloat16),
                pltpu.VMEM((N_ZHI * WINDOW, COLS_OUT), f32),
            ],
            compiler_params=params(16),
            cost_estimate=cost(1, SHARE),
            name="gram",
        )(*feats)
    from_y = {k: shift_hor(parts[k], 0, k, 0) for k in (2, 1, 3)}
    total = parts[0]
    for k in (2, 1):
        total = pl.pallas_call(
            add_kernel,
            out_shape=jax.ShapeDtypeStruct((SENT, LANES), f32),
            in_specs=[VMEM] * 2,
            out_specs=VMEM,
            compiler_params=params(8),
            cost_estimate=cost(1, SHARE),
            name="add",
        )(total, from_y[k])
    sums = pl.pallas_call(
        split_kernel,
        out_shape=[jax.ShapeDtypeStruct((LAST, LANES), f32)] * N_ZHI,
        in_specs=[VMEM] * 2,
        out_specs=[VMEM] * N_ZHI,
        compiler_params=params(8),
        cost_estimate=cost(1, SHARE),
        name="split",
    )(total, from_y[3])
    from_z = {k: shift_hor(sums[k], k, 0, 0) for k in (2, 1, 3)}
    return pl.pallas_call(
        final_kernel,
        out_shape=jax.ShapeDtypeStruct((ROWS_OUT, COLS_OUT), f32),
        in_specs=[VMEM] * N_ZHI,
        out_specs=VMEM,
        compiler_params=params(8),
        name="final",
    )(sums[0], from_z[1], from_z[2], from_z[3])


def solution(mesh):
    in_specs = (P(None, "lev", "hor"), P("hor", "lev"), P(), P())
    out_specs = P("hor", "lev")
    return jax.shard_map(on_device, mesh=mesh, in_specs=in_specs, out_specs=out_specs, check_vma=False)
```

time: 75.4 us -> 67.2 us (0.89)
  the two profiles are of different devices: /device:TPU:1 before, /device:TPU:6 now
where the time goes in v2:
time: 67.2 us; the launch traced here: 65.9 us
  starting transfers between devices  27.6 us (41%)
  waiting for transfers between devices  25.8 us (38%)
  Pallas kernels  8.82 us (13%)
  local copies, waits for them, and re-layouts  1.95 us (3%)
  other arithmetic  1.71 us (3%)
    ppermute x7, starting transfers between devices, shift_hor(): return lax.ppermute(value, 'hor', pairs)  17.2 us
    ppermute x7, waiting for transfers between devices, shift_hor(): return lax.ppermute(value, 'hor', pairs)  14.7 us
    ppermute x4, waiting for transfers between devices, shift_lev(): return lax.ppermute(value, 'lev', pairs)  9.26 us
    all_to_all x1, starting transfers between devices, on_device(): lists = lax.all_to_all(repeated, 'lev', 0, 0, tiled=True)  6.13 us
    ppermute x4, starting transfers between devices, shift_lev(): return lax.ppermute(value, 'lev', pairs)  4.23 us
    pallas_call x4, Pallas kernels, on_device(): pl.pallas_call(functools.partial(gram_kernel, k), out_shape=jax.ShapeDtyp...  4.16 us
    pallas_call x2, Pallas kernels, features(): pl.pallas_call(feature_kernel, out_shape=jax.ShapeDtypeStruct((FEAT, BLOC...  2.32 us
    unnamed x4, local copies, waits for them, and re-layouts  1.88 us
  transfers between devices with their start and end apart: 12, of which 11 were waited for; matrix products, arithmetic and copies ran while one was open for 3% of the time, Pallas kernels for 7%

profile of v2, /device:TPU:6, one launch (start us, length us, event | category | flops | bytes accessed | tf_op | source)
XLA Modules:
  0.0 65.9 jit_solution(828621744328225789)
XLA Ops:
  0.0 0.7 copy-done.1
  0.7 0.6 repeat.1
  1.3 6.1 %all-to-all-start = ((s32[8,1,128]{2,1,0:T(1,128)}), s32[8,1,128]{2,1,0:T(1,128)S(1)}, u32[]{:S(2)}, u32[]{:S(2)}) async-start(s32[8,1,128]{2,1,0:T(1,128)} %repeat.1), calls=%async_computation | async-start | bytes 8192 | tf_op jit(solution)/shard_map/all_to_all | solution.py:201
  7.4 0.8 %slice_multiply_fusion.1 = (f32[31]{0:T(128)S(1)}, f32[31]{0:T(128)S(1)}) fusion(f32[32]{0:T(128)} %param.6, s32[31]{0:T(128)} %param.7), kind=kLoop, calls=%fused_computation.9 | loop fusion | flops 124 | bytes 620 | tf_op jit(solution)/shard_map/mul | solution.py:171
  8.2 1.2 %copy-done = f32[4,4,16384]{2,1,0:T(4,128)S(1)} copy-done((f32[4,4,16384]{2,1,0:T(4,128)S(1)}, f32[4,4,16384]{2,1,0:T(4,128)}, u32[]{:S(2)}) %copy-start) | copy-done | bytes 1048600
  9.5 1.8 %all-to-all-done.index_ref = s32[8,1,128]{2,1,0:T(1,128)S(1)} async-done(((s32[8,1,128]{2,1,0:T(1,128)}), s32[8,1,128]{2,1,0:T(1,128)S(1)}, u32[]{:S(2)}, u32[]{:S(2)}) %all-to-all-start) | async-done | bytes 4128 | tf_op jit(solution)/shard_map/all_to_all | solution.py:201
  11.8 0.7 collective-permute-start
  12.4 0.7 %multiply_divide_fusion = (f32[32]{0:T(128)S(1)}, f32[32]{0:T(128)S(1)}) fusion(f32[32]{0:T(128)} %param.6, f32[1]{0:T(128)} %constant.20.clone.1, f32[31]{0:T(128)S(1)} %get-tuple-element.18, f32[31]{0:T(128)S(1)} %get-tuple-element.17), kind=kLoop, calls=%fused_computation.10 | loop fusion | flops 192 | bytes 636 | tf_op jit(solution)/shard_map/div | solution.py:174
  13.2 3.0 %collective-permute-done = f32[16,1024]{1,0:T(8,128)S(1)} collective-permute-done((f32[16,1024]{1,0:T(8,128)S(1)}, f32[16,1024]{1,0:T(8,128)S(1)}, u32[]{:S(2)}, u32[]{:S(2)}) %collective-permute-start) | collective-permute-done | bytes 65568 | tf_op jit(solution)/shard_map/ppermute | solution.py:35
  16.2 2.1 %collective-permute-start.1 = (f32[2,16,1024]{2,1,0:T(8,128)S(1)}, f32[2,16,1024]{2,1,0:T(8,128)S(1)}, u32[]{:S(2)}, u32[]{:S(2)}) collective-permute-start(f32[2,16,1024]{2,1,0:T(8,128)S(1)} %pad_maximum_fusion.w0_ref), channel_id=1, source_target_pairs={{0,32},{32,64},{64,96},{96,0},{128,160},{160,192},{192,224},{224,1... | collective-permute-start | bytes 393224 | tf_op jit(solution)/shard_map/ppermute | solution.py:35
  18.9 0.9 %collective-permute-start.3 = (f32[2,16,1024]{2,1,0:T(8,128)S(1)}, f32[2,16,1024]{2,1,0:T(8,128)S(1)}, u32[]{:S(2)}, u32[]{:S(2)}) collective-permute-start(f32[2,16,1024]{2,1,0:T(8,128)S(1)} %pad_maximum_fusion.w0_ref), channel_id=1, source_target_pairs={{0,96},{32,0},{64,32},{96,64},{128,224},{160,128},{192,160},{224,1... | collective-permute-start | bytes 393224 | tf_op jit(solution)/shard_map/ppermute | solution.py:35
  19.9 2.3 %collective-permute-done.1.w1_ref = f32[2,16,1024]{2,1,0:T(8,128)S(1)} collective-permute-done((f32[2,16,1024]{2,1,0:T(8,128)S(1)}, f32[2,16,1024]{2,1,0:T(8,128)S(1)}, u32[]{:S(2)}, u32[]{:S(2)}) %collective-permute-start.1) | collective-permute-done | bytes 131104 | tf_op jit(solution)/shard_map/ppermute | solution.py:35
  22.2 2.7 %collective-permute-done.2.w2_ref = f32[2,16,1024]{2,1,0:T(8,128)S(1)} collective-permute-done((f32[2,16,1024]{2,1,0:T(8,128)S(1)}, f32[2,16,1024]{2,1,0:T(8,128)S(1)}, u32[]{:S(2)}, u32[]{:S(2)}) %collective-permute-start.2) | collective-permute-done | bytes 131104 | tf_op jit(solution)/shard_map/ppermute | solution.py:35
  24.9 1.3 %collective-permute-done.3.w3_ref = f32[2,16,1024]{2,1,0:T(8,128)S(1)} collective-permute-done((f32[2,16,1024]{2,1,0:T(8,128)S(1)}, f32[2,16,1024]{2,1,0:T(8,128)S(1)}, u32[]{:S(2)}, u32[]{:S(2)}) %collective-permute-start.3) | collective-permute-done | bytes 131104 | tf_op jit(solution)/shard_map/ppermute | solution.py:35
  26.7 1.2 %features.2.own_ref = bf16[2176,1024]{1,0:T(8,128)(2,1)S(1)} custom-call(f32[128,1024]{1,0:T(8,128)S(1)} %smooth.1.smooth_ref), custom_call_target="tpu_custom_call" | custom-call | flops 2228224 | bytes 5242880 | tf_op jit(solution)/shard_map/features/pallas_call | solution.py:179
  27.8 0.7 %collective-permute-done.4.smooth_ref = f32[128,1024]{1,0:T(8,128)S(1)} collective-permute-done((f32[128,1024]{1,0:T(8,128)S(1)}, f32[128,1024]{1,0:T(8,128)S(1)}, u32[]{:S(2)}, u32[]{:S(2)}) %collective-permute-start.4) | collective-permute-done | bytes 524320 | tf_op jit(solution)/shard_map/ppermute | solution.py:44
  28.6 1.2 %features.3.other_ref = bf16[2176,1024]{1,0:T(8,128)(2,1)S(1)} custom-call(f32[128,1024]{1,0:T(8,128)S(1)} %collective-permute-done.4.smooth_ref), custom_call_target="tpu_custom_call" | custom-call | flops 2228224 | bytes 5242880 | tf_op jit(solution)/shard_map/features/pallas_call | solution.py:179
  29.7 1.0 %gram.5 = f32[648,128]{1,0:T(8,128)S(1)} custom-call(bf16[2176,1024]{1,0:T(8,128)(2,1)S(1)} %features.2.own_ref, bf16[2176,1024]{1,0:T(8,128)(2,1)S(1)} %features.3.other_ref), custom_call_target="tpu_custom_call" | custom-call | flops 1 | bytes 262144 | tf_op jit(solution)/shard_map/gram/pallas_call | solution.py:236
  30.8 3.3 %collective-permute-start.5 = (f32[648,128]{1,0:T(8,128)S(1)}, f32[648,128]{1,0:T(8,128)S(1)}, u32[]{:S(2)}, u32[]{:S(2)}) collective-permute-start(f32[648,128]{1,0:T(8,128)S(1)} %gram.5), channel_id=1, source_target_pairs={{0,4},{1,5},{2,6},{3,7},{4,0},{5,1},{6,2},{7,3},{8,12},{9,13},{10,... | collective-permute-start | bytes 995336 | tf_op jit(solution)/shard_map/ppermute | solution.py:44
  34.0 1.0 %gram.6 = f32[648,128]{1,0:T(8,128)S(1)} custom-call(bf16[2176,1024]{1,0:T(8,128)(2,1)S(1)} %features.2.own_ref, bf16[2176,1024]{1,0:T(8,128)(2,1)S(1)} %features.3.other_ref), custom_call_target="tpu_custom_call" | custom-call | flops 1 | bytes 262144 | tf_op jit(solution)/shard_map/gram/pallas_call | solution.py:236
  35.1 0.7 %collective-permute-start.6 = (f32[648,128]{1,0:T(8,128)S(1)}, f32[648,128]{1,0:T(8,128)S(1)}, u32[]{:S(2)}, u32[]{:S(2)}) collective-permute-start(f32[648,128]{1,0:T(8,128)S(1)} %gram.6), channel_id=1, source_target_pairs={{0,2},{1,3},{2,4},{3,5},{4,6},{5,7},{6,0},{7,1},{8,10},{9,11},{10,... | collective-permute-start | bytes 995336 | tf_op jit(solution)/shard_map/ppermute | solution.py:44
  35.8 1.0 %gram.7 = f32[648,128]{1,0:T(8,128)S(1)} custom-call(bf16[2176,1024]{1,0:T(8,128)(2,1)S(1)} %features.2.own_ref, bf16[2176,1024]{1,0:T(8,128)(2,1)S(1)} %features.3.other_ref), custom_call_target="tpu_custom_call" | custom-call | flops 1 | bytes 262144 | tf_op jit(solution)/shard_map/gram/pallas_call | solution.py:236
  36.9 2.6 %collective-permute-start.7 = (f32[648,128]{1,0:T(8,128)S(1)}, f32[648,128]{1,0:T(8,128)S(1)}, u32[]{:S(2)}, u32[]{:S(2)}) collective-permute-start(f32[648,128]{1,0:T(8,128)S(1)} %gram.7), channel_id=1, source_target_pairs={{0,6},{1,7},{2,0},{3,1},{4,2},{5,3},{6,4},{7,5},{8,14},{9,15},{10,... | collective-permute-start | bytes 995336 | tf_op jit(solution)/shard_map/ppermute | solution.py:44
  39.5 1.0 %gram.4.a_ref = f32[648,128]{1,0:T(8,128)S(1)} custom-call(bf16[2176,1024]{1,0:T(8,128)(2,1)S(1)} %features.2.own_ref, bf16[2176,1024]{1,0:T(8,128)(2,1)S(1)} %features.3.other_ref), custom_call_target="tpu_custom_call" | custom-call | flops 1 | bytes 262144 | tf_op jit(solution)/shard_map/gram/pallas_call | solution.py:236
  40.5 2.5 %collective-permute-done.5.b_ref = f32[648,128]{1,0:T(8,128)S(1)} collective-permute-done((f32[648,128]{1,0:T(8,128)S(1)}, f32[648,128]{1,0:T(8,128)S(1)}, u32[]{:S(2)}, u32[]{:S(2)}) %collective-permute-start.5) | collective-permute-done | bytes 331808 | tf_op jit(solution)/shard_map/ppermute | solution.py:44
  43.1 6.2 %collective-permute-done.6.b_ref = f32[648,128]{1,0:T(8,128)S(1)} collective-permute-done((f32[648,128]{1,0:T(8,128)S(1)}, f32[648,128]{1,0:T(8,128)S(1)}, u32[]{:S(2)}, u32[]{:S(2)}) %collective-permute-start.6) | collective-permute-done | bytes 331808 | tf_op jit(solution)/shard_map/ppermute | solution.py:44
  49.8 3.3 %collective-permute-start.8 = (f32[160,128]{1,0:T(8,128)S(1)}, f32[160,128]{1,0:T(8,128)S(1)}, u32[]{:S(2)}, u32[]{:S(2)}) collective-permute-start(f32[160,128]{1,0:T(8,128)S(1)} %get-tuple-element.10), channel_id=1, source_target_pairs={{0,8},{1,9},{2,10},{3,11},{4,12},{5,13},{6,14},{7,15},{8,16},{9,17... | collective-permute-start | bytes 245768 | tf_op jit(solution)/shard_map/ppermute | solution.py:44
  53.1 4.5 %collective-permute-start.9 = (f32[160,128]{1,0:T(8,128)S(1)}, f32[160,128]{1,0:T(8,128)S(1)}, u32[]{:S(2)}, u32[]{:S(2)}) collective-permute-start(f32[160,128]{1,0:T(8,128)S(1)} %get-tuple-element.11), channel_id=1, source_target_pairs={{0,16},{1,17},{2,18},{3,19},{4,20},{5,21},{6,22},{7,23},{8,24},{9,... | collective-permute-start | bytes 245768 | tf_op jit(solution)/shard_map/ppermute | solution.py:44
  57.6 2.7 %collective-permute-start.10 = (f32[160,128]{1,0:T(8,128)S(1)}, f32[160,128]{1,0:T(8,128)S(1)}, u32[]{:S(2)}, u32[]{:S(2)}) collective-permute-start(f32[160,128]{1,0:T(8,128)S(1)} %get-tuple-element.12), channel_id=1, source_target_pairs={{0,24},{1,25},{2,26},{3,27},{4,28},{5,29},{6,30},{7,31},{8,0},{9,1... | collective-permute-start | bytes 245768 | tf_op jit(solution)/shard_map/ppermute | solution.py:44
  60.3 3.4 %collective-permute-done.9.t2_ref = f32[160,128]{1,0:T(8,128)S(1)} collective-permute-done((f32[160,128]{1,0:T(8,128)S(1)}, f32[160,128]{1,0:T(8,128)S(1)}, u32[]{:S(2)}, u32[]{:S(2)}) %collective-permute-start.9) | collective-permute-done | bytes 81952 | tf_op jit(solution)/shard_map/ppermute | solution.py:44
  63.6 1.6 %collective-permute-done.10.t3_ref = f32[160,128]{1,0:T(8,128)S(1)} collective-permute-done((f32[160,128]{1,0:T(8,128)S(1)}, f32[160,128]{1,0:T(8,128)S(1)}, u32[]{:S(2)}, u32[]{:S(2)}) %collective-permute-start.10) | collective-permute-done | bytes 81952 | tf_op jit(solution)/shard_map/ppermute | solution.py:44
  65.2 0.7 %final.1 = f32[68,272]{1,0:T(8,128)} custom-call(f32[160,128]{1,0:T(8,128)S(1)} %get-tuple-element.9.t0_ref, f32[160,128]{1,0:T(8,128)S(1)} %collective-permute-done.8.t1_ref, f32[160,128]{1,0:T(8,128)S(1)} %collective-permute-done.9.t2_ref, f32[160,128]{1,0:T(8,128)S(1)} %collective-permute-done.10.t3_ref), custom_call_target="tpu_custom_call" | custom-call | tf_op jit(solution)/shard_map/final/pallas_call | solution.py:271
  (17 shorter events, 2.2 us)
Async XLA Ops:
  0.0 0.7 copy-start.1
  1.3 10.1 %all-to-all-start = ((s32[8,1,128]{2,1,0:T(1,128)}), s32[8,1,128]{2,1,0:T(1,128)S(1)}, u32[]{:S(2)}, u32[]{:S(2)}) async-start(s32[8,1,128]{2,1,0:T(1,128)} %repeat.1), calls=%async_computation | async-start | bytes 8192 | tf_op jit(solution)/shard_map/all_to_all | solution.py:201
  8.2 1.2 %copy-start = (f32[4,4,16384]{2,1,0:T(4,128)S(1)}, f32[4,4,16384]{2,1,0:T(4,128)}, u32[]{:S(2)}) copy-start(f32[4,4,16384]{2,1,0:T(4,128)} %slab_ref.1) | copy-start | bytes 3145732
  11.8 4.4 %collective-permute-start = (f32[16,1024]{1,0:T(8,128)S(1)}, f32[16,1024]{1,0:T(8,128)S(1)}, u32[]{:S(2)}, u32[]{:S(2)}) collective-permute-start(f32[16,1024]{1,0:T(8,128)S(1)} %pick.1), channel_id=1, source_target_pairs={{0,128},{32,160},{64,192},{96,224},{128,0},{160,32},{192,64},{224,... | collective-permute-start | bytes 196616 | tf_op jit(solution)/shard_map/ppermute | solution.py:35
  16.2 6.1 %collective-permute-start.1 = (f32[2,16,1024]{2,1,0:T(8,128)S(1)}, f32[2,16,1024]{2,1,0:T(8,128)S(1)}, u32[]{:S(2)}, u32[]{:S(2)}) collective-permute-start(f32[2,16,1024]{2,1,0:T(8,128)S(1)} %pad_maximum_fusion.w0_ref), channel_id=1, source_target_pairs={{0,32},{32,64},{64,96},{96,0},{128,160},{160,192},{192,224},{224,1... | collective-permute-start | bytes 393224 | tf_op jit(solution)/shard_map/ppermute | solution.py:35
  18.3 6.6 %collective-permute-start.2 = (f32[2,16,1024]{2,1,0:T(8,128)S(1)}, f32[2,16,1024]{2,1,0:T(8,128)S(1)}, u32[]{:S(2)}, u32[]{:S(2)}) collective-permute-start(f32[2,16,1024]{2,1,0:T(8,128)S(1)} %pad_maximum_fusion.w0_ref), channel_id=1, source_target_pairs={{0,64},{32,96},{64,0},{96,32},{128,192},{160,224},{192,128},{224,1... | collective-permute-start | bytes 393224 | tf_op jit(solution)/shard_map/ppermute | solution.py:35
  18.9 7.3 %collective-permute-start.3 = (f32[2,16,1024]{2,1,0:T(8,128)S(1)}, f32[2,16,1024]{2,1,0:T(8,128)S(1)}, u32[]{:S(2)}, u32[]{:S(2)}) collective-permute-start(f32[2,16,1024]{2,1,0:T(8,128)S(1)} %pad_maximum_fusion.w0_ref), channel_id=1, source_target_pairs={{0,96},{32,0},{64,32},{96,64},{128,224},{160,128},{192,160},{224,1... | collective-permute-start | bytes 393224 | tf_op jit(solution)/shard_map/ppermute | solution.py:35
  26.6 2.0 %collective-permute-start.4 = (f32[128,1024]{1,0:T(8,128)S(1)}, f32[128,1024]{1,0:T(8,128)S(1)}, u32[]{:S(2)}, u32[]{:S(2)}) collective-permute-start(f32[128,1024]{1,0:T(8,128)S(1)} %smooth.1.smooth_ref), channel_id=1, source_target_pairs={{0,1},{1,0},{2,3},{3,2},{4,5},{5,4},{6,7},{7,6},{8,9},{9,8},{10,11... | collective-permute-start | bytes 1572872 | tf_op jit(solution)/shard_map/ppermute | solution.py:44
  30.8 12.3 %collective-permute-start.5 = (f32[648,128]{1,0:T(8,128)S(1)}, f32[648,128]{1,0:T(8,128)S(1)}, u32[]{:S(2)}, u32[]{:S(2)}) collective-permute-start(f32[648,128]{1,0:T(8,128)S(1)} %gram.5), channel_id=1, source_target_pairs={{0,4},{1,5},{2,6},{3,7},{4,0},{5,1},{6,2},{7,3},{8,12},{9,13},{10,... | collective-permute-start | bytes 995336 | tf_op jit(solution)/shard_map/ppermute | solution.py:44
  35.1 14.2 %collective-permute-start.6 = (f32[648,128]{1,0:T(8,128)S(1)}, f32[648,128]{1,0:T(8,128)S(1)}, u32[]{:S(2)}, u32[]{:S(2)}) collective-permute-start(f32[648,128]{1,0:T(8,128)S(1)} %gram.6), channel_id=1, source_target_pairs={{0,2},{1,3},{2,4},{3,5},{4,6},{5,7},{6,0},{7,1},{8,10},{9,11},{10,... | collective-permute-start | bytes 995336 | tf_op jit(solution)/shard_map/ppermute | solution.py:44
  36.9 12.8 %collective-permute-start.7 = (f32[648,128]{1,0:T(8,128)S(1)}, f32[648,128]{1,0:T(8,128)S(1)}, u32[]{:S(2)}, u32[]{:S(2)}) collective-permute-start(f32[648,128]{1,0:T(8,128)S(1)} %gram.7), channel_id=1, source_target_pairs={{0,6},{1,7},{2,0},{3,1},{4,2},{5,3},{6,4},{7,5},{8,14},{9,15},{10,... | collective-permute-start | bytes 995336 | tf_op jit(solution)/shard_map/ppermute | solution.py:44
  49.8 10.5 %collective-permute-start.8 = (f32[160,128]{1,0:T(8,128)S(1)}, f32[160,128]{1,0:T(8,128)S(1)}, u32[]{:S(2)}, u32[]{:S(2)}) collective-permute-start(f32[160,128]{1,0:T(8,128)S(1)} %get-tuple-element.10), channel_id=1, source_target_pairs={{0,8},{1,9},{2,10},{3,11},{4,12},{5,13},{6,14},{7,15},{8,16},{9,17... | collective-permute-start | bytes 245768 | tf_op jit(solution)/shard_map/ppermute | solution.py:44
  53.1 10.5 %collective-permute-start.9 = (f32[160,128]{1,0:T(8,128)S(1)}, f32[160,128]{1,0:T(8,128)S(1)}, u32[]{:S(2)}, u32[]{:S(2)}) collective-permute-start(f32[160,128]{1,0:T(8,128)S(1)} %get-tuple-element.11), channel_id=1, source_target_pairs={{0,16},{1,17},{2,18},{3,19},{4,20},{5,21},{6,22},{7,23},{8,24},{9,... | collective-permute-start | bytes 245768 | tf_op jit(solution)/shard_map/ppermute | solution.py:44
  57.6 7.6 %collective-permute-start.10 = (f32[160,128]{1,0:T(8,128)S(1)}, f32[160,128]{1,0:T(8,128)S(1)}, u32[]{:S(2)}, u32[]{:S(2)}) collective-permute-start(f32[160,128]{1,0:T(8,128)S(1)} %get-tuple-element.12), channel_id=1, source_target_pairs={{0,24},{1,25},{2,26},{3,27},{4,28},{5,29},{6,30},{7,31},{8,0},{9,1... | collective-permute-start | bytes 245768 | tf_op jit(solution)/shard_map/ppermute | solution.py:44

commit v3 on v2

--- a/solution.py
+++ b/solution.py
@@ -14,8 +14,8 @@
 BLOCK = N_LEV * SAMP
 FEAT = 4 * LEV + 2 * LEV * LEV
 ROWS_OUT, COLS_OUT = FEAT // N_HOR, FEAT // N_LEV
-CHUNK, WINDOW = 72, 80
-PIECE = N_ZHI * 2 * CHUNK
+CHUNK, WINDOW, CHUNKS = 72, 80, 4
+PIECE = CHUNKS * 2 * CHUNK
 SENT = PIECE + CHUNK
 LAST = 2 * CHUNK + 16
 SHARE = 1 << 18
@@ -35,12 +35,20 @@
     return lax.ppermute(value, "lev", pairs)
 
 
-def shift_hor(value, step_zhi, step_y, step_core):
+def swap_cores(value):
+    return lax.ppermute(value, "hor", [(i, i ^ 1) for i in range(N_HOR)])
+
+
+def hop(value, axis, cross):
     pairs = []
     for i in range(N_HOR):
         zhi, y, core = i // (2 * N_Y), i // 2 % N_Y, i % 2
-        to = (zhi + step_zhi) % N_ZHI * 2 * N_Y + (y + step_y) % N_Y * 2 + (core ^ step_core)
-        pairs.append((i, to))
+        ahead = 1 - 2 * core
+        if axis == "y":
+            y = (y + ahead) % N_Y
+        else:
+            zhi = (zhi + ahead) % N_ZHI
+        pairs.append((i, zhi * 2 * N_Y + y * 2 + (core ^ cross)))
     return lax.ppermute(value, "hor", pairs)
 
 
@@ -104,28 +112,31 @@
     lax.fori_loop(0, BLOCK // LANES, tile, 0)
 
 
-def gram_kernel(step_y, own_ref, other_ref, out_ref, left_ref, prod_ref):
+def gram_kernel(place, own_ref, other_ref, out_ref, left_ref, prod_ref):
     hor, lev = lax.axis_index("hor"), lax.axis_index("lev")
     zhi, y, core = hor // (2 * N_Y), hor // 2 % N_Y, hor % 2
     right = pl.ds(pl.multiple_of(lev * COLS_OUT, 16), COLS_OUT)
-    to_y = lax.rem(y + step_y, N_Y)
+    to_y = {"far": y + 2, "cross": y + 5 - 2 * core, "near": y + 5 - 2 * core, "own": y}[place]
+    to_y = lax.rem(to_y, N_Y)
+    to_core = 1 - core if place == "cross" else core
+    next_z = lax.rem(zhi + 5 - 2 * to_core, N_ZHI)
+    chunks = ((zhi, to_core), (next_z, to_core), (next_z, 1 - to_core), (lax.rem(zhi + 2, N_ZHI), to_core))
     skip = 8 * lax.rem(to_y, 2)
     for block, ref in enumerate((own_ref, other_ref)):
-        for step_z in range(N_ZHI):
-            to_z = lax.rem(zhi + step_z, N_ZHI)
-            start = (to_z * N_Y + to_y) * 2 * ROWS_OUT + core * 64 - skip
+        for chunk, (to_z, row_core) in enumerate(chunks):
+            start = (to_z * N_Y + to_y) * 2 * ROWS_OUT + row_core * 64 - skip
             rows = pl.ds(pl.multiple_of(start, 16), WINDOW)
-            left_ref[step_z * WINDOW : (step_z + 1) * WINDOW, :] = ref[rows, :]
+            left_ref[chunk * WINDOW : (chunk + 1) * WINDOW, :] = ref[rows, :]
         part = lax.dot_general(
             left_ref[...], ref[right, :], (((1,), (1,)), ((), ())), preferred_element_type=jnp.float32
         )
         prod_ref[...] = part + prod_ref[...] if block else part
-    for step_z in range(N_ZHI):
-        rows = pl.ds(pl.multiple_of(step_z * WINDOW + skip, 8), CHUNK)
+    for chunk in range(CHUNKS):
+        rows = pl.ds(pl.multiple_of(chunk * WINDOW + skip, 8), CHUNK)
         for half in range(2):
-            place = (2 * step_z + half) * CHUNK
-            out_ref[place : place + CHUNK, :] = prod_ref[rows, half * LANES : (half + 1) * LANES]
-        out_ref[PIECE:SENT, 16 * step_z : 16 * step_z + 16] = prod_ref[rows, 2 * LANES : COLS_OUT]
+            base = (2 * chunk + half) * CHUNK
+            out_ref[base : base + CHUNK, :] = prod_ref[rows, half * LANES : (half + 1) * LANES]
+        out_ref[PIECE:SENT, 16 * chunk : 16 * chunk + 16] = prod_ref[rows, 2 * LANES : COLS_OUT]
 
 
 def add_kernel(a_ref, b_ref, out_ref):
@@ -135,23 +146,23 @@
 def split_kernel(a_ref, b_ref, t0_ref, t1_ref, t2_ref, t3_ref):
     rest = a_ref[PIECE:SENT, :] + b_ref[PIECE:SENT, :]
     strip = lax.broadcasted_iota(jnp.int32, (8, LANES), 1) // 16
-    for step_z, ref in enumerate((t0_ref, t1_ref, t2_ref, t3_ref)):
-        rows = slice(step_z * 2 * CHUNK, (step_z + 1) * 2 * CHUNK)
+    for chunk, ref in enumerate((t0_ref, t1_ref, t2_ref, t3_ref)):
+        rows = slice(chunk * 2 * CHUNK, (chunk + 1) * 2 * CHUNK)
         ref[0 : 2 * CHUNK, :] = a_ref[rows, :] + b_ref[rows, :]
         packed = jnp.zeros((8, LANES), jnp.float32)
         for group in range(8):
-            moved = pltpu.roll(rest[8 * group : 8 * group + 8], 16 * (group - step_z) % LANES, 1)
+            moved = pltpu.roll(rest[8 * group : 8 * group + 8], 16 * (group - chunk) % LANES, 1)
             packed = jnp.where(strip == group, moved, packed)
         ref[2 * CHUNK : 2 * CHUNK + 8, :] = packed
-        ref[2 * CHUNK + 8 : LAST, :] = pltpu.roll(rest[64:CHUNK], -16 * step_z % LANES, 1)
-
-
-def final_kernel(t0_ref, t1_ref, t2_ref, t3_ref, out_ref):
+        ref[2 * CHUNK + 8 : LAST, :] = pltpu.roll(rest[64:CHUNK], -16 * chunk % LANES, 1)
+
+
+def final_kernel(t0_ref, t1_ref, t2_ref, out_ref):
     odd = lax.axis_index("hor") % 2 == 1
     scale = 1.0 / (BLOCK * N_HOR)
 
     def total(rows):
-        return (t0_ref[rows, :] + t1_ref[rows, :]) + (t2_ref[rows, :] + t3_ref[rows, :])
+        return (t0_ref[rows, :] + t1_ref[rows, :]) + t2_ref[rows, :]
 
     def place(value):
         return jnp.where(odd, value[CHUNK - ROWS_OUT : CHUNK], value[0:ROWS_OUT]) * scale
@@ -185,6 +196,18 @@
         cost_estimate=cost(FEAT * BLOCK, 5 << 20),
         name="features",
     )(smoothed)
+
+
+def add(a, b):
+    return pl.pallas_call(
+        add_kernel,
+        out_shape=jax.ShapeDtypeStruct(a.shape, a.dtype),
+        in_specs=[VMEM] * 2,
+        out_specs=VMEM,
+        compiler_params=params(4),
+        cost_estimate=cost(1, SHARE),
+        name="add",
+    )(a, b)
 
 
 def on_device(slab_fields, sample_index, thickness, level_cuts):
@@ -229,53 +252,49 @@
         compiler_params=params(16),
         name="smooth",
     )(coef, near, far[1], far[2], far[3])
-    other = shift_hor(own, 0, 0, 1)
+    other = swap_cores(own)
     feats = [features(own), features(other)]
     parts = {}
-    for k in (2, 1, 3, 0):
+    for k in ("far", "cross", "near", "own"):
         parts[k] = pl.pallas_call(
             functools.partial(gram_kernel, k),
             out_shape=jax.ShapeDtypeStruct((SENT, LANES), f32),
             in_specs=[VMEM] * 2,
             out_specs=VMEM,
             scratch_shapes=[
-                pltpu.VMEM((N_ZHI * WINDOW, BLOCK), jnp.bfloat16),
-                pltpu.VMEM((N_ZHI * WINDOW, COLS_OUT), f32),
+                pltpu.VMEM((CHUNKS * WINDOW, BLOCK), jnp.bfloat16),
+                pltpu.VMEM((CHUNKS * WINDOW, COLS_OUT), f32),
             ],
             compiler_params=params(16),
             cost_estimate=cost(1, SHARE),
             name="gram",
         )(*feats)
-    from_y = {k: shift_hor(parts[k], 0, k, 0) for k in (2, 1, 3)}
-    total = parts[0]
-    for k in (2, 1):
-        total = pl.pallas_call(
-            add_kernel,
-            out_shape=jax.ShapeDtypeStruct((SENT, LANES), f32),
-            in_specs=[VMEM] * 2,
-            out_specs=VMEM,
-            compiler_params=params(8),
-            cost_estimate=cost(1, SHARE),
-            name="add",
-        )(total, from_y[k])
+        if k == "cross":
+            feats, parts[k] = lax.optimization_barrier((feats, parts[k]))
+    two_back = hop(parts["far"], "y", 0)
+    from_cross = hop(parts["cross"], "y", 1)
+    from_near = hop(add(parts["near"], two_back), "y", 0)
     sums = pl.pallas_call(
         split_kernel,
-        out_shape=[jax.ShapeDtypeStruct((LAST, LANES), f32)] * N_ZHI,
+        out_shape=[jax.ShapeDtypeStruct((LAST, LANES), f32)] * CHUNKS,
         in_specs=[VMEM] * 2,
-        out_specs=[VMEM] * N_ZHI,
+        out_specs=[VMEM] * CHUNKS,
         compiler_params=params(8),
         cost_estimate=cost(1, SHARE),
         name="split",
-    )(total, from_y[3])
-    from_z = {k: shift_hor(sums[k], k, 0, 0) for k in (2, 1, 3)}
+    )(add(parts["own"], from_cross), from_near)
+    two_back = hop(sums[3], "z_hi", 0)
+    from_cross = hop(sums[2], "z_hi", 1)
+    from_near = hop(add(sums[1], two_back), "z_hi", 0)
     return pl.pallas_call(
         final_kernel,
         out_shape=jax.ShapeDtypeStruct((ROWS_OUT, COLS_OUT), f32),
-        in_specs=[VMEM] * N_ZHI,
+        in_specs=[VMEM] * 3,
         out_specs=VMEM,
         compiler_params=params(8),
+        cost_estimate=cost(1, SHARE),
         name="final",
-    )(sums[0], from_z[1], from_z[2], from_z[3])
+    )(sums[0], from_cross, from_near)
 
 
 def solution(mesh):

time: 67.2 us -> 64.2 us (0.955); the launches traced: 65.9 us -> 64 us
  starting transfers between devices: 27.6 us -> 17.6 us
  waiting for transfers between devices: 25.8 us -> 33.8 us
    ppermute x7, starting transfers between devices: 17.2 us -> 7.28 us  [the longest x6 7.19 us: hop(): return lax.ppermute(value, 'hor', pairs)]
    ppermute x7, waiting for transfers between devices: 14.7 us -> 22.7 us  [the longest x6 21.9 us: hop(): return lax.ppermute(value, 'hor', pairs)]
  transfers between devices with their start and end apart: 12 -> 12, of which waited for: 11 -> 10; matrix products, arithmetic and copies ran while one was open for 3% -> 3% of each run, Pallas kernels for 7% -> 7%
where the time goes in v3:
time: 64.2 us; the launch traced here: 64 us
  waiting for transfers between devices  33.8 us (53%)
  starting transfers between devices  17.6 us (27%)
  Pallas kernels  8.8 us (14%)
  local copies, waits for them, and re-layouts  1.95 us (3%)
  other arithmetic  1.71 us (3%)
    ppermute x6, waiting for transfers between devices, hop(): return lax.ppermute(value, 'hor', pairs)  21.9 us
    ppermute x4, waiting for transfers between devices, shift_lev(): return lax.ppermute(value, 'lev', pairs)  9.26 us
    ppermute x6, starting transfers between devices, hop(): return lax.ppermute(value, 'hor', pairs)  7.19 us
    all_to_all x1, starting transfers between devices, on_device(): lists = lax.all_to_all(repeated, 'lev', 0, 0, tiled=True)  6.13 us
    ppermute x4, starting transfers between devices, shift_lev(): return lax.ppermute(value, 'lev', pairs)  4.23 us
    pallas_call x4, Pallas kernels, on_device(): pl.pallas_call(functools.partial(gram_kernel, k), out_shape=jax.ShapeDtyp...  4.14 us
    pallas_call x2, Pallas kernels, features(): pl.pallas_call(feature_kernel, out_shape=jax.ShapeDtypeStruct((FEAT, BLOC...  2.32 us
    unnamed x4, local copies, waits for them, and re-layouts  1.88 us
  transfers between devices with their start and end apart: 12, of which 10 were waited for; matrix products, arithmetic and copies ran while one was open for 3% of the time, Pallas kernels for 7%

profile of v3, /device:TPU:6, one launch (start us, length us, event | category | flops | bytes accessed | tf_op | source)
XLA Modules:
  0.0 64.0 jit_solution(16674754920094548048)
XLA Ops:
  0.0 0.7 %copy-done.1 = s32[1,128]{1,0:T(1,128)S(1)} copy-done((s32[1,128]{1,0:T(1,128)S(1)}, s32[1,128]{1,0:T(1,128)}, u32[]{:S(2)}) %copy-start.1) | copy-done | bytes 536
  0.7 0.6 repeat.1
  1.3 6.1 %all-to-all-start = ((s32[8,1,128]{2,1,0:T(1,128)}), s32[8,1,128]{2,1,0:T(1,128)S(1)}, u32[]{:S(2)}, u32[]{:S(2)}) async-start(s32[8,1,128]{2,1,0:T(1,128)} %repeat.1), calls=%async_computation | async-start | bytes 8192 | tf_op jit(solution)/shard_map/all_to_all | solution.py:224
  7.4 0.8 %slice_multiply_fusion.1 = (f32[31]{0:T(128)S(1)}, f32[31]{0:T(128)S(1)}) fusion(f32[32]{0:T(128)} %param.6, s32[31]{0:T(128)} %param.7), kind=kLoop, calls=%fused_computation.9 | loop fusion | flops 124 | bytes 620 | tf_op jit(solution)/shard_map/mul | solution.py:182
  8.2 1.2 %copy-done = f32[4,4,16384]{2,1,0:T(4,128)S(1)} copy-done((f32[4,4,16384]{2,1,0:T(4,128)S(1)}, f32[4,4,16384]{2,1,0:T(4,128)}, u32[]{:S(2)}) %copy-start) | copy-done | bytes 1048600
  9.5 1.8 %all-to-all-done.index_ref = s32[8,1,128]{2,1,0:T(1,128)S(1)} async-done(((s32[8,1,128]{2,1,0:T(1,128)}), s32[8,1,128]{2,1,0:T(1,128)S(1)}, u32[]{:S(2)}, u32[]{:S(2)}) %all-to-all-start) | async-done | bytes 4128 | tf_op jit(solution)/shard_map/all_to_all | solution.py:224
  11.4 0.4 pick.1
  11.8 0.7 %collective-permute-start = (f32[16,1024]{1,0:T(8,128)S(1)}, f32[16,1024]{1,0:T(8,128)S(1)}, u32[]{:S(2)}, u32[]{:S(2)}) collective-permute-start(f32[16,1024]{1,0:T(8,128)S(1)} %pick.1), channel_id=1, source_target_pairs={{0,128},{32,160},{64,192},{96,224},{128,0},{160,32},{192,64},{224,... | collective-permute-start | bytes 196616 | tf_op jit(solution)/shard_map/ppermute | solution.py:35
  12.4 0.7 %multiply_divide_fusion = (f32[32]{0:T(128)S(1)}, f32[32]{0:T(128)S(1)}) fusion(f32[32]{0:T(128)} %param.6, f32[1]{0:T(128)} %constant.20.clone.1, f32[31]{0:T(128)S(1)} %get-tuple-element.24, f32[31]{0:T(128)S(1)} %get-tuple-element.23), kind=kLoop, calls=%fused_computation.10 | loop fusion | flops 192 | bytes 636 | tf_op jit(solution)/shard_map/div | solution.py:185
  13.2 3.0 %collective-permute-done = f32[16,1024]{1,0:T(8,128)S(1)} collective-permute-done((f32[16,1024]{1,0:T(8,128)S(1)}, f32[16,1024]{1,0:T(8,128)S(1)}, u32[]{:S(2)}, u32[]{:S(2)}) %collective-permute-start) | collective-permute-done | bytes 65568 | tf_op jit(solution)/shard_map/ppermute | solution.py:35
  16.2 2.1 %collective-permute-start.1 = (f32[2,16,1024]{2,1,0:T(8,128)S(1)}, f32[2,16,1024]{2,1,0:T(8,128)S(1)}, u32[]{:S(2)}, u32[]{:S(2)}) collective-permute-start(f32[2,16,1024]{2,1,0:T(8,128)S(1)} %pad_maximum_fusion.w0_ref), channel_id=1, source_target_pairs={{0,32},{32,64},{64,96},{96,0},{128,160},{160,192},{192,224},{224,1... | collective-permute-start | bytes 393224 | tf_op jit(solution)/shard_map/ppermute | solution.py:35
  18.3 0.6 collective-permute-start.2
  18.9 0.9 %collective-permute-start.3 = (f32[2,16,1024]{2,1,0:T(8,128)S(1)}, f32[2,16,1024]{2,1,0:T(8,128)S(1)}, u32[]{:S(2)}, u32[]{:S(2)}) collective-permute-start(f32[2,16,1024]{2,1,0:T(8,128)S(1)} %pad_maximum_fusion.w0_ref), channel_id=1, source_target_pairs={{0,96},{32,0},{64,32},{96,64},{128,224},{160,128},{192,160},{224,1... | collective-permute-start | bytes 393224 | tf_op jit(solution)/shard_map/ppermute | solution.py:35
  19.9 2.3 %collective-permute-done.1.w1_ref = f32[2,16,1024]{2,1,0:T(8,128)S(1)} collective-permute-done((f32[2,16,1024]{2,1,0:T(8,128)S(1)}, f32[2,16,1024]{2,1,0:T(8,128)S(1)}, u32[]{:S(2)}, u32[]{:S(2)}) %collective-permute-start.1) | collective-permute-done | bytes 131104 | tf_op jit(solution)/shard_map/ppermute | solution.py:35
  22.2 2.7 %collective-permute-done.2.w2_ref = f32[2,16,1024]{2,1,0:T(8,128)S(1)} collective-permute-done((f32[2,16,1024]{2,1,0:T(8,128)S(1)}, f32[2,16,1024]{2,1,0:T(8,128)S(1)}, u32[]{:S(2)}, u32[]{:S(2)}) %collective-permute-start.2) | collective-permute-done | bytes 131104 | tf_op jit(solution)/shard_map/ppermute | solution.py:35
  24.9 1.3 %collective-permute-done.3.w3_ref = f32[2,16,1024]{2,1,0:T(8,128)S(1)} collective-permute-done((f32[2,16,1024]{2,1,0:T(8,128)S(1)}, f32[2,16,1024]{2,1,0:T(8,128)S(1)}, u32[]{:S(2)}, u32[]{:S(2)}) %collective-permute-start.3) | collective-permute-done | bytes 131104 | tf_op jit(solution)/shard_map/ppermute | solution.py:35
  26.7 1.2 %features.2.own_ref = bf16[2176,1024]{1,0:T(8,128)(2,1)S(1)} custom-call(f32[128,1024]{1,0:T(8,128)S(1)} %smooth.1.smooth_ref), custom_call_target="tpu_custom_call" | custom-call | flops 2228224 | bytes 5242880 | tf_op jit(solution)/shard_map/features/pallas_call | solution.py:190
  27.8 0.7 %collective-permute-done.4.smooth_ref = f32[128,1024]{1,0:T(8,128)S(1)} collective-permute-done((f32[128,1024]{1,0:T(8,128)S(1)}, f32[128,1024]{1,0:T(8,128)S(1)}, u32[]{:S(2)}, u32[]{:S(2)}) %collective-permute-start.4) | collective-permute-done | bytes 524320 | tf_op jit(solution)/shard_map/ppermute | solution.py:39
  28.6 1.2 %features.3.other_ref = bf16[2176,1024]{1,0:T(8,128)(2,1)S(1)} custom-call(f32[128,1024]{1,0:T(8,128)S(1)} %collective-permute-done.4.smooth_ref), custom_call_target="tpu_custom_call" | custom-call | flops 2228224 | bytes 5242880 | tf_op jit(solution)/shard_map/features/pallas_call | solution.py:190
  29.7 1.0 %gram.7 = f32[648,128]{1,0:T(8,128)S(1)} custom-call(bf16[2176,1024]{1,0:T(8,128)(2,1)S(1)} %features.2.own_ref, bf16[2176,1024]{1,0:T(8,128)(2,1)S(1)} %features.3.other_ref), custom_call_target="tpu_custom_call" | custom-call | flops 1 | bytes 262144 | tf_op jit(solution)/shard_map/gram/pallas_call | solution.py:259
  30.8 1.7 %collective-permute-start.6 = (f32[648,128]{1,0:T(8,128)S(1)}, f32[648,128]{1,0:T(8,128)S(1)}, u32[]{:S(2)}, u32[]{:S(2)}) collective-permute-start(f32[648,128]{1,0:T(8,128)S(1)} %gram.7), channel_id=1, source_target_pairs={{0,2},{1,7},{2,4},{3,1},{4,6},{5,3},{6,0},{7,5},{8,10},{9,15},{10,... | collective-permute-start | bytes 995336 | tf_op jit(solution)/shard_map/ppermute | solution.py:52
  32.4 1.0 %gram.4 = f32[648,128]{1,0:T(8,128)S(1)} custom-call(bf16[2176,1024]{1,0:T(8,128)(2,1)S(1)} %features.2.own_ref, bf16[2176,1024]{1,0:T(8,128)(2,1)S(1)} %features.3.other_ref), custom_call_target="tpu_custom_call" | custom-call | flops 1 | bytes 262144 | tf_op jit(solution)/shard_map/gram/pallas_call | solution.py:259
  33.5 1.0 %gram.6.a_ref = f32[648,128]{1,0:T(8,128)S(1)} custom-call(bf16[2176,1024]{1,0:T(8,128)(2,1)S(1)} %features.2.own_ref, bf16[2176,1024]{1,0:T(8,128)(2,1)S(1)} %features.3.other_ref), custom_call_target="tpu_custom_call" | custom-call | flops 1 | bytes 262144 | tf_op jit(solution)/shard_map/gram/pallas_call | solution.py:259
  34.6 4.6 %collective-permute-done.6.b_ref = f32[648,128]{1,0:T(8,128)S(1)} collective-permute-done((f32[648,128]{1,0:T(8,128)S(1)}, f32[648,128]{1,0:T(8,128)S(1)}, u32[]{:S(2)}, u32[]{:S(2)}) %collective-permute-start.6) | collective-permute-done | bytes 331808 | tf_op jit(solution)/shard_map/ppermute | solution.py:52
  39.2 0.5 collective-permute-start.7
  39.7 1.0 %gram.5.a_ref = f32[648,128]{1,0:T(8,128)S(1)} custom-call(bf16[2176,1024]{1,0:T(8,128)(2,1)S(1)} %features.2.own_ref, bf16[2176,1024]{1,0:T(8,128)(2,1)S(1)} %features.3.other_ref), custom_call_target="tpu_custom_call" | custom-call | flops 1 | bytes 262144 | tf_op jit(solution)/shard_map/gram/pallas_call | solution.py:259
  40.7 6.9 %collective-permute-done.7.b_ref = f32[648,128]{1,0:T(8,128)S(1)} collective-permute-done((f32[648,128]{1,0:T(8,128)S(1)}, f32[648,128]{1,0:T(8,128)S(1)}, u32[]{:S(2)}, u32[]{:S(2)}) %collective-permute-start.7) | collective-permute-done | bytes 331808 | tf_op jit(solution)/shard_map/ppermute | solution.py:52
  47.7 3.3 %collective-permute-start.9 = (f32[160,128]{1,0:T(8,128)S(1)}, f32[160,128]{1,0:T(8,128)S(1)}, u32[]{:S(2)}, u32[]{:S(2)}) collective-permute-start(f32[160,128]{1,0:T(8,128)S(1)} %get-tuple-element.18), channel_id=1, source_target_pairs={{0,8},{1,25},{2,10},{3,27},{4,12},{5,29},{6,14},{7,31},{8,16},{9,1... | collective-permute-start | bytes 245768 | tf_op jit(solution)/shard_map/ppermute | solution.py:52
  51.1 4.6 %collective-permute-done.9.b_ref = f32[160,128]{1,0:T(8,128)S(1)} collective-permute-done((f32[160,128]{1,0:T(8,128)S(1)}, f32[160,128]{1,0:T(8,128)S(1)}, u32[]{:S(2)}, u32[]{:S(2)}) %collective-permute-start.9) | collective-permute-done | bytes 81952 | tf_op jit(solution)/shard_map/ppermute | solution.py:52
  55.7 1.7 %collective-permute-start.10 = (f32[160,128]{1,0:T(8,128)S(1)}, f32[160,128]{1,0:T(8,128)S(1)}, u32[]{:S(2)}, u32[]{:S(2)}) collective-permute-start(f32[160,128]{1,0:T(8,128)S(1)} %add.18), channel_id=1, source_target_pairs={{0,8},{1,25},{2,10},{3,27},{4,12},{5,29},{6,14},{7,31},{8,16},{9,1... | collective-permute-start | bytes 245768 | tf_op jit(solution)/shard_map/ppermute | solution.py:52
  57.4 5.8 %collective-permute-done.10.t2_ref = f32[160,128]{1,0:T(8,128)S(1)} collective-permute-done((f32[160,128]{1,0:T(8,128)S(1)}, f32[160,128]{1,0:T(8,128)S(1)}, u32[]{:S(2)}, u32[]{:S(2)}) %collective-permute-start.10) | collective-permute-done | bytes 81952 | tf_op jit(solution)/shard_map/ppermute | solution.py:52
  63.2 0.7 %final.1 = f32[68,272]{1,0:T(8,128)} custom-call(f32[160,128]{1,0:T(8,128)S(1)} %get-tuple-element.15.t0_ref, f32[160,128]{1,0:T(8,128)S(1)} %collective-permute-done.8.t1_ref, f32[160,128]{1,0:T(8,128)S(1)} %collective-permute-done.10.t2_ref), custom_call_target="tpu_custom_call" | custom-call | flops 1 | bytes 262144 | tf_op jit(solution)/shard_map/final/pallas_call | solution.py:289
  (18 shorter events, 1.1 us)
Async XLA Ops:
  0.0 0.7 %copy-start.1 = (s32[1,128]{1,0:T(1,128)S(1)}, s32[1,128]{1,0:T(1,128)}, u32[]{:S(2)}) copy-start(s32[1,128]{1,0:T(1,128)} %index_ref.1) | copy-start | bytes 1540
  1.3 10.1 %all-to-all-start = ((s32[8,1,128]{2,1,0:T(1,128)}), s32[8,1,128]{2,1,0:T(1,128)S(1)}, u32[]{:S(2)}, u32[]{:S(2)}) async-start(s32[8,1,128]{2,1,0:T(1,128)} %repeat.1), calls=%async_computation | async-start | bytes 8192 | tf_op jit(solution)/shard_map/all_to_all | solution.py:224
  8.2 1.2 %copy-start = (f32[4,4,16384]{2,1,0:T(4,128)S(1)}, f32[4,4,16384]{2,1,0:T(4,128)}, u32[]{:S(2)}) copy-start(f32[4,4,16384]{2,1,0:T(4,128)} %slab_ref.1) | copy-start | bytes 3145732
  11.8 4.4 %collective-permute-start = (f32[16,1024]{1,0:T(8,128)S(1)}, f32[16,1024]{1,0:T(8,128)S(1)}, u32[]{:S(2)}, u32[]{:S(2)}) collective-permute-start(f32[16,1024]{1,0:T(8,128)S(1)} %pick.1), channel_id=1, source_target_pairs={{0,128},{32,160},{64,192},{96,224},{128,0},{160,32},{192,64},{224,... | collective-permute-start | bytes 196616 | tf_op jit(solution)/shard_map/ppermute | solution.py:35
  16.2 6.1 %collective-permute-start.1 = (f32[2,16,1024]{2,1,0:T(8,128)S(1)}, f32[2,16,1024]{2,1,0:T(8,128)S(1)}, u32[]{:S(2)}, u32[]{:S(2)}) collective-permute-start(f32[2,16,1024]{2,1,0:T(8,128)S(1)} %pad_maximum_fusion.w0_ref), channel_id=1, source_target_pairs={{0,32},{32,64},{64,96},{96,0},{128,160},{160,192},{192,224},{224,1... | collective-permute-start | bytes 393224 | tf_op jit(solution)/shard_map/ppermute | solution.py:35
  18.3 6.6 %collective-permute-start.2 = (f32[2,16,1024]{2,1,0:T(8,128)S(1)}, f32[2,16,1024]{2,1,0:T(8,128)S(1)}, u32[]{:S(2)}, u32[]{:S(2)}) collective-permute-start(f32[2,16,1024]{2,1,0:T(8,128)S(1)} %pad_maximum_fusion.w0_ref), channel_id=1, source_target_pairs={{0,64},{32,96},{64,0},{96,32},{128,192},{160,224},{192,128},{224,1... | collective-permute-start | bytes 393224 | tf_op jit(solution)/shard_map/ppermute | solution.py:35
  18.9 7.3 %collective-permute-start.3 = (f32[2,16,1024]{2,1,0:T(8,128)S(1)}, f32[2,16,1024]{2,1,0:T(8,128)S(1)}, u32[]{:S(2)}, u32[]{:S(2)}) collective-permute-start(f32[2,16,1024]{2,1,0:T(8,128)S(1)} %pad_maximum_fusion.w0_ref), channel_id=1, source_target_pairs={{0,96},{32,0},{64,32},{96,64},{128,224},{160,128},{192,160},{224,1... | collective-permute-start | bytes 393224 | tf_op jit(solution)/shard_map/ppermute | solution.py:35
  26.6 2.0 %collective-permute-start.4 = (f32[128,1024]{1,0:T(8,128)S(1)}, f32[128,1024]{1,0:T(8,128)S(1)}, u32[]{:S(2)}, u32[]{:S(2)}) collective-permute-start(f32[128,1024]{1,0:T(8,128)S(1)} %smooth.1.smooth_ref), channel_id=1, source_target_pairs={{0,1},{1,0},{2,3},{3,2},{4,5},{5,4},{6,7},{7,6},{8,9},{9,8},{10,11... | collective-permute-start | bytes 1572872 | tf_op jit(solution)/shard_map/ppermute | solution.py:39
  30.8 8.4 %collective-permute-start.6 = (f32[648,128]{1,0:T(8,128)S(1)}, f32[648,128]{1,0:T(8,128)S(1)}, u32[]{:S(2)}, u32[]{:S(2)}) collective-permute-start(f32[648,128]{1,0:T(8,128)S(1)} %gram.7), channel_id=1, source_target_pairs={{0,2},{1,7},{2,4},{3,1},{4,6},{5,3},{6,0},{7,5},{8,10},{9,15},{10,... | collective-permute-start | bytes 995336 | tf_op jit(solution)/shard_map/ppermute | solution.py:52
  33.5 7.2 %collective-permute-start.5 = (f32[648,128]{1,0:T(8,128)S(1)}, f32[648,128]{1,0:T(8,128)S(1)}, u32[]{:S(2)}, u32[]{:S(2)}) collective-permute-start(f32[648,128]{1,0:T(8,128)S(1)} %gram.4), channel_id=1, source_target_pairs={{0,3},{1,6},{2,5},{3,0},{4,7},{5,2},{6,1},{7,4},{8,11},{9,14},{10,... | collective-permute-start | bytes 995336 | tf_op jit(solution)/shard_map/ppermute | solution.py:52
  39.2 8.4 %collective-permute-start.7 = (f32[648,128]{1,0:T(8,128)S(1)}, f32[648,128]{1,0:T(8,128)S(1)}, u32[]{:S(2)}, u32[]{:S(2)}) collective-permute-start(f32[648,128]{1,0:T(8,128)S(1)} %add.17), channel_id=1, source_target_pairs={{0,2},{1,7},{2,4},{3,1},{4,6},{5,3},{6,0},{7,5},{8,10},{9,15},{10,... | collective-permute-start | bytes 995336 | tf_op jit(solution)/shard_map/ppermute | solution.py:52
  47.7 8.0 %collective-permute-start.9 = (f32[160,128]{1,0:T(8,128)S(1)}, f32[160,128]{1,0:T(8,128)S(1)}, u32[]{:S(2)}, u32[]{:S(2)}) collective-permute-start(f32[160,128]{1,0:T(8,128)S(1)} %get-tuple-element.18), channel_id=1, source_target_pairs={{0,8},{1,25},{2,10},{3,27},{4,12},{5,29},{6,14},{7,31},{8,16},{9,1... | collective-permute-start | bytes 245768 | tf_op jit(solution)/shard_map/ppermute | solution.py:52
  51.1 6.3 %collective-permute-start.8 = (f32[160,128]{1,0:T(8,128)S(1)}, f32[160,128]{1,0:T(8,128)S(1)}, u32[]{:S(2)}, u32[]{:S(2)}) collective-permute-start(f32[160,128]{1,0:T(8,128)S(1)} %get-tuple-element.16), channel_id=1, source_target_pairs={{0,9},{1,24},{2,11},{3,26},{4,13},{5,28},{6,15},{7,30},{8,17},{9,0... | collective-permute-start | bytes 245768 | tf_op jit(solution)/shard_map/ppermute | solution.py:52
  55.7 7.5 %collective-permute-start.10 = (f32[160,128]{1,0:T(8,128)S(1)}, f32[160,128]{1,0:T(8,128)S(1)}, u32[]{:S(2)}, u32[]{:S(2)}) collective-permute-start(f32[160,128]{1,0:T(8,128)S(1)} %add.18), channel_id=1, source_target_pairs={{0,8},{1,25},{2,10},{3,27},{4,12},{5,29},{6,14},{7,31},{8,16},{9,1... | collective-permute-start | bytes 245768 | tf_op jit(solution)/shard_map/ppermute | solution.py:52

commit v4 on v3

--- a/solution.py
+++ b/solution.py
@@ -52,9 +52,12 @@
     return lax.ppermute(value, "hor", pairs)
 
 
-def repeat_kernel(index_ref, out_ref):
-    for lev in range(N_LEV):
-        out_ref[lev] = index_ref[...]
+def repeat_kernel(index_ref, out_ref, sems):
+    copies = [pltpu.make_async_copy(index_ref, out_ref.at[lev], sems.at[lev]) for lev in range(N_LEV)]
+    for copy in copies:
+        copy.start()
+    for copy in copies:
+        copy.wait()
 
 
 def stage_kernel(slab_ref, out_ref):
@@ -143,26 +146,27 @@
     out_ref[...] = a_ref[...] + b_ref[...]
 
 
-def split_kernel(a_ref, b_ref, t0_ref, t1_ref, t2_ref, t3_ref):
+def split_kernel(a_ref, b_ref, own_ref, next_ref, far_ref):
     rest = a_ref[PIECE:SENT, :] + b_ref[PIECE:SENT, :]
     strip = lax.broadcasted_iota(jnp.int32, (8, LANES), 1) // 16
-    for chunk, ref in enumerate((t0_ref, t1_ref, t2_ref, t3_ref)):
+    places = ((own_ref, 0), (next_ref, 0), (next_ref, LAST), (far_ref, 0))
+    for chunk, (ref, base) in enumerate(places):
         rows = slice(chunk * 2 * CHUNK, (chunk + 1) * 2 * CHUNK)
-        ref[0 : 2 * CHUNK, :] = a_ref[rows, :] + b_ref[rows, :]
+        ref[base : base + 2 * CHUNK, :] = a_ref[rows, :] + b_ref[rows, :]
         packed = jnp.zeros((8, LANES), jnp.float32)
         for group in range(8):
             moved = pltpu.roll(rest[8 * group : 8 * group + 8], 16 * (group - chunk) % LANES, 1)
             packed = jnp.where(strip == group, moved, packed)
-        ref[2 * CHUNK : 2 * CHUNK + 8, :] = packed
-        ref[2 * CHUNK + 8 : LAST, :] = pltpu.roll(rest[64:CHUNK], -16 * chunk % LANES, 1)
-
-
-def final_kernel(t0_ref, t1_ref, t2_ref, out_ref):
+        ref[base + 2 * CHUNK : base + 2 * CHUNK + 8, :] = packed
+        ref[base + 2 * CHUNK + 8 : base + LAST, :] = pltpu.roll(rest[64:CHUNK], -16 * chunk % LANES, 1)
+
+
+def final_kernel(own_ref, next_ref, swapped_ref, far_ref, out_ref):
     odd = lax.axis_index("hor") % 2 == 1
     scale = 1.0 / (BLOCK * N_HOR)
 
     def total(rows):
-        return (t0_ref[rows, :] + t1_ref[rows, :]) + t2_ref[rows, :]
+        return (own_ref[rows, :] + next_ref[rows, :]) + (swapped_ref[rows, :] + far_ref[rows, :])
 
     def place(value):
         return jnp.where(odd, value[CHUNK - ROWS_OUT : CHUNK], value[0:ROWS_OUT]) * scale
@@ -216,9 +220,10 @@
     repeated = pl.pallas_call(
         repeat_kernel,
         out_shape=jax.ShapeDtypeStruct((N_LEV, 1, SAMP), jnp.int32),
-        in_specs=[VMEM],
-        out_specs=VMEM,
-        compiler_params=params(1),
+        in_specs=[pl.BlockSpec(memory_space=pltpu.HBM)],
+        out_specs=pl.BlockSpec(memory_space=pl.ANY),
+        scratch_shapes=[pltpu.SemaphoreType.DMA((N_LEV,))],
+        compiler_params=params(60),
         name="repeat",
     )(sample_index)
     lists = lax.all_to_all(repeated, "lev", 0, 0, tiled=True)
@@ -274,27 +279,28 @@
     two_back = hop(parts["far"], "y", 0)
     from_cross = hop(parts["cross"], "y", 1)
     from_near = hop(add(parts["near"], two_back), "y", 0)
-    sums = pl.pallas_call(
+    chunk = jax.ShapeDtypeStruct((LAST, LANES), f32)
+    kept, beside, beyond = pl.pallas_call(
         split_kernel,
-        out_shape=[jax.ShapeDtypeStruct((LAST, LANES), f32)] * CHUNKS,
+        out_shape=[chunk, jax.ShapeDtypeStruct((2 * LAST, LANES), f32), chunk],
         in_specs=[VMEM] * 2,
-        out_specs=[VMEM] * CHUNKS,
+        out_specs=[VMEM] * 3,
         compiler_params=params(8),
         cost_estimate=cost(1, SHARE),
         name="split",
     )(add(parts["own"], from_cross), from_near)
-    two_back = hop(sums[3], "z_hi", 0)
-    from_cross = hop(sums[2], "z_hi", 1)
-    from_near = hop(add(sums[1], two_back), "z_hi", 0)
+    from_next = hop(beside, "z_hi", 0)
+    from_far = lax.ppermute(beyond, "hor", [(i, (i + N_HOR // 2) % N_HOR) for i in range(N_HOR)])
+    swapped = swap_cores(from_next[LAST:])
     return pl.pallas_call(
         final_kernel,
         out_shape=jax.ShapeDtypeStruct((ROWS_OUT, COLS_OUT), f32),
-        in_specs=[VMEM] * 3,
+        in_specs=[VMEM] * 4,
         out_specs=VMEM,
         compiler_params=params(8),
         cost_estimate=cost(1, SHARE),
         name="final",
-    )(sums[0], from_cross, from_near)
+    )(kept, from_next, swapped, from_far)
 
 
 def solution(mesh):

time: 64.2 us -> 63.6 us (level)
  waiting for transfers between devices: 33.8 us -> 30.2 us
  starting transfers between devices: 17.6 us -> 20.5 us
  Pallas kernels: 8.8 us -> 9.63 us
  local copies, waits for them, and re-layouts: 1.95 us -> 1.3 us
    ppermute x6 -> x4, waiting for transfers between devices: 21.9 us -> 13.7 us  [hop(): return lax.ppermute(value, 'hor', pairs)]
    ppermute x0 -> x1, waiting for transfers between devices: none -> 4.62 us  [on_device(): lax.ppermute(beyond, 'hor', [(i, (i + N_HOR // 2) % N_HOR) for i in range...]
    ppermute x0 -> x1, starting transfers between devices: none -> 4.49 us  [on_device(): lax.ppermute(beyond, 'hor', [(i, (i + N_HOR // 2) % N_HOR) for i in range...]
    ppermute x6 -> x4, starting transfers between devices: 7.19 us -> 5.52 us  [hop(): return lax.ppermute(value, 'hor', pairs)]
    pallas_call x1, Pallas kernels: 0.59 us -> 1.43 us  [on_device(): pl.pallas_call(repeat_kernel, out_shape=jax.ShapeDtypeStruct((N_LEV, 1, S...]
    unnamed x4 -> x2, local copies, waits for them, and re-layouts: 1.88 us -> 1.22 us
where the time goes in v4:
time: 63.6 us; the launch traced here: 63.4 us
  waiting for transfers between devices  30.2 us (47%)
  starting transfers between devices  20.5 us (32%)
  Pallas kernels  9.63 us (15%)
  other arithmetic  1.71 us (3%)
  local copies, waits for them, and re-layouts  1.3 us (2%)
    ppermute x4, waiting for transfers between devices, hop(): return lax.ppermute(value, 'hor', pairs)  13.7 us
    ppermute x4, waiting for transfers between devices, shift_lev(): return lax.ppermute(value, 'lev', pairs)  9.26 us
    all_to_all x1, starting transfers between devices, on_device(): lists = lax.all_to_all(repeated, 'lev', 0, 0, tiled=True)  6.14 us
    ppermute x4, starting transfers between devices, hop(): return lax.ppermute(value, 'hor', pairs)  5.52 us
    ppermute x1, waiting for transfers between devices, on_device(): lax.ppermute(beyond, 'hor', [(i, (i + N_HOR // 2) % N_HOR) for i in range...  4.62 us
    ppermute x1, starting transfers between devices, on_device(): lax.ppermute(beyond, 'hor', [(i, (i + N_HOR // 2) % N_HOR) for i in range...  4.49 us
    ppermute x4, starting transfers between devices, shift_lev(): return lax.ppermute(value, 'lev', pairs)  4.23 us
    pallas_call x4, Pallas kernels, on_device(): pl.pallas_call(functools.partial(gram_kernel, k), out_shape=jax.ShapeDtyp...  4.14 us
  transfers between devices with their start and end apart: 12, of which 10 were waited for; matrix products, arithmetic and copies ran while one was open for 3% of the time, Pallas kernels for 7%

profile of v4, /device:TPU:6, one launch (start us, length us, event | category | flops | bytes accessed | tf_op | source)
XLA Modules:
  0.0 63.4 jit_solution(6766490205155796592)
XLA Ops:
  0.0 1.4 %repeat.1 = s32[8,1,128]{2,1,0:T(1,128)} custom-call(s32[1,128]{1,0:T(1,128)} %index_ref.1), custom_call_target="tpu_custom_call" | custom-call | tf_op jit(solution)/shard_map/repeat/pallas_call | solution.py:220
  1.4 6.1 %all-to-all-start = ((s32[8,1,128]{2,1,0:T(1,128)}), s32[8,1,128]{2,1,0:T(1,128)S(1)}, u32[]{:S(2)}, u32[]{:S(2)}) async-start(s32[8,1,128]{2,1,0:T(1,128)} %repeat.1), calls=%async_computation | async-start | bytes 8192 | tf_op jit(solution)/shard_map/all_to_all | solution.py:229
  7.6 0.8 %slice_multiply_fusion.1 = (f32[31]{0:T(128)S(1)}, f32[31]{0:T(128)S(1)}) fusion(f32[32]{0:T(128)} %param.6, s32[31]{0:T(128)} %param.7), kind=kLoop, calls=%fused_computation.9 | loop fusion | flops 124 | bytes 620 | tf_op jit(solution)/shard_map/mul | solution.py:186
  8.4 1.2 %copy-done = f32[4,4,16384]{2,1,0:T(4,128)S(1)} copy-done((f32[4,4,16384]{2,1,0:T(4,128)S(1)}, f32[4,4,16384]{2,1,0:T(4,128)}, u32[]{:S(2)}) %copy-start) | copy-done | bytes 1048600
  9.8 1.8 %all-to-all-done.index_ref = s32[8,1,128]{2,1,0:T(1,128)S(1)} async-done(((s32[8,1,128]{2,1,0:T(1,128)}), s32[8,1,128]{2,1,0:T(1,128)S(1)}, u32[]{:S(2)}, u32[]{:S(2)}) %all-to-all-start) | async-done | bytes 4128 | tf_op jit(solution)/shard_map/all_to_all | solution.py:229
  11.6 0.4 pick.1
  12.0 0.7 %collective-permute-start = (f32[16,1024]{1,0:T(8,128)S(1)}, f32[16,1024]{1,0:T(8,128)S(1)}, u32[]{:S(2)}, u32[]{:S(2)}) collective-permute-start(f32[16,1024]{1,0:T(8,128)S(1)} %pick.1), channel_id=1, source_target_pairs={{0,128},{32,160},{64,192},{96,224},{128,0},{160,32},{192,64},{224,... | collective-permute-start | bytes 196616 | tf_op jit(solution)/shard_map/ppermute | solution.py:35
  12.6 0.7 %multiply_divide_fusion = (f32[32]{0:T(128)S(1)}, f32[32]{0:T(128)S(1)}) fusion(f32[32]{0:T(128)} %param.6, f32[1]{0:T(128)} %constant.20.clone.1, f32[31]{0:T(128)S(1)} %get-tuple-element.22, f32[31]{0:T(128)S(1)} %get-tuple-element.21), kind=kLoop, calls=%fused_computation.10 | loop fusion | flops 192 | bytes 636 | tf_op jit(solution)/shard_map/div | solution.py:189
  13.4 3.0 %collective-permute-done = f32[16,1024]{1,0:T(8,128)S(1)} collective-permute-done((f32[16,1024]{1,0:T(8,128)S(1)}, f32[16,1024]{1,0:T(8,128)S(1)}, u32[]{:S(2)}, u32[]{:S(2)}) %collective-permute-start) | collective-permute-done | bytes 65568 | tf_op jit(solution)/shard_map/ppermute | solution.py:35
  16.4 2.1 %collective-permute-start.1 = (f32[2,16,1024]{2,1,0:T(8,128)S(1)}, f32[2,16,1024]{2,1,0:T(8,128)S(1)}, u32[]{:S(2)}, u32[]{:S(2)}) collective-permute-start(f32[2,16,1024]{2,1,0:T(8,128)S(1)} %pad_maximum_fusion.w0_ref), channel_id=1, source_target_pairs={{0,32},{32,64},{64,96},{96,0},{128,160},{160,192},{192,224},{224,1... | collective-permute-start | bytes 393224 | tf_op jit(solution)/shard_map/ppermute | solution.py:35
  18.5 0.6 collective-permute-start.2
  19.1 0.9 %collective-permute-start.3 = (f32[2,16,1024]{2,1,0:T(8,128)S(1)}, f32[2,16,1024]{2,1,0:T(8,128)S(1)}, u32[]{:S(2)}, u32[]{:S(2)}) collective-permute-start(f32[2,16,1024]{2,1,0:T(8,128)S(1)} %pad_maximum_fusion.w0_ref), channel_id=1, source_target_pairs={{0,96},{32,0},{64,32},{96,64},{128,224},{160,128},{192,160},{224,1... | collective-permute-start | bytes 393224 | tf_op jit(solution)/shard_map/ppermute | solution.py:35
  20.1 2.3 %collective-permute-done.1.w1_ref = f32[2,16,1024]{2,1,0:T(8,128)S(1)} collective-permute-done((f32[2,16,1024]{2,1,0:T(8,128)S(1)}, f32[2,16,1024]{2,1,0:T(8,128)S(1)}, u32[]{:S(2)}, u32[]{:S(2)}) %collective-permute-start.1) | collective-permute-done | bytes 131104 | tf_op jit(solution)/shard_map/ppermute | solution.py:35
  22.4 2.7 %collective-permute-done.2.w2_ref = f32[2,16,1024]{2,1,0:T(8,128)S(1)} collective-permute-done((f32[2,16,1024]{2,1,0:T(8,128)S(1)}, f32[2,16,1024]{2,1,0:T(8,128)S(1)}, u32[]{:S(2)}, u32[]{:S(2)}) %collective-permute-start.2) | collective-permute-done | bytes 131104 | tf_op jit(solution)/shard_map/ppermute | solution.py:35
  25.1 1.3 %collective-permute-done.3.w3_ref = f32[2,16,1024]{2,1,0:T(8,128)S(1)} collective-permute-done((f32[2,16,1024]{2,1,0:T(8,128)S(1)}, f32[2,16,1024]{2,1,0:T(8,128)S(1)}, u32[]{:S(2)}, u32[]{:S(2)}) %collective-permute-start.3) | collective-permute-done | bytes 131104 | tf_op jit(solution)/shard_map/ppermute | solution.py:35
  26.5 0.3 smooth.1.smooth_ref
  26.9 1.2 %features.2.own_ref = bf16[2176,1024]{1,0:T(8,128)(2,1)S(1)} custom-call(f32[128,1024]{1,0:T(8,128)S(1)} %smooth.1.smooth_ref), custom_call_target="tpu_custom_call" | custom-call | flops 2228224 | bytes 5242880 | tf_op jit(solution)/shard_map/features/pallas_call | solution.py:194
  28.0 0.7 %collective-permute-done.4.smooth_ref = f32[128,1024]{1,0:T(8,128)S(1)} collective-permute-done((f32[128,1024]{1,0:T(8,128)S(1)}, f32[128,1024]{1,0:T(8,128)S(1)}, u32[]{:S(2)}, u32[]{:S(2)}) %collective-permute-start.4) | collective-permute-done | bytes 524320 | tf_op jit(solution)/shard_map/ppermute | solution.py:39
  28.8 1.2 %features.3.other_ref = bf16[2176,1024]{1,0:T(8,128)(2,1)S(1)} custom-call(f32[128,1024]{1,0:T(8,128)S(1)} %collective-permute-done.4.smooth_ref), custom_call_target="tpu_custom_call" | custom-call | flops 2228224 | bytes 5242880 | tf_op jit(solution)/shard_map/features/pallas_call | solution.py:194
  29.9 1.0 %gram.7 = f32[648,128]{1,0:T(8,128)S(1)} custom-call(bf16[2176,1024]{1,0:T(8,128)(2,1)S(1)} %features.2.own_ref, bf16[2176,1024]{1,0:T(8,128)(2,1)S(1)} %features.3.other_ref), custom_call_target="tpu_custom_call" | custom-call | flops 1 | bytes 262144 | tf_op jit(solution)/shard_map/gram/pallas_call | solution.py:264
  31.0 1.7 %collective-permute-start.6 = (f32[648,128]{1,0:T(8,128)S(1)}, f32[648,128]{1,0:T(8,128)S(1)}, u32[]{:S(2)}, u32[]{:S(2)}) collective-permute-start(f32[648,128]{1,0:T(8,128)S(1)} %gram.7), channel_id=1, source_target_pairs={{0,2},{1,7},{2,4},{3,1},{4,6},{5,3},{6,0},{7,5},{8,10},{9,15},{10,... | collective-permute-start | bytes 995336 | tf_op jit(solution)/shard_map/ppermute | solution.py:52
  32.6 1.0 %gram.4 = f32[648,128]{1,0:T(8,128)S(1)} custom-call(bf16[2176,1024]{1,0:T(8,128)(2,1)S(1)} %features.2.own_ref, bf16[2176,1024]{1,0:T(8,128)(2,1)S(1)} %features.3.other_ref), custom_call_target="tpu_custom_call" | custom-call | flops 1 | bytes 262144 | tf_op jit(solution)/shard_map/gram/pallas_call | solution.py:264
  33.7 1.0 %gram.6.a_ref = f32[648,128]{1,0:T(8,128)S(1)} custom-call(bf16[2176,1024]{1,0:T(8,128)(2,1)S(1)} %features.2.own_ref, bf16[2176,1024]{1,0:T(8,128)(2,1)S(1)} %features.3.other_ref), custom_call_target="tpu_custom_call" | custom-call | flops 1 | bytes 262144 | tf_op jit(solution)/shard_map/gram/pallas_call | solution.py:264
  34.8 4.6 %collective-permute-done.6.b_ref = f32[648,128]{1,0:T(8,128)S(1)} collective-permute-done((f32[648,128]{1,0:T(8,128)S(1)}, f32[648,128]{1,0:T(8,128)S(1)}, u32[]{:S(2)}, u32[]{:S(2)}) %collective-permute-start.6) | collective-permute-done | bytes 331808 | tf_op jit(solution)/shard_map/ppermute | solution.py:52
  39.4 0.5 collective-permute-start.7
  39.9 1.0 %gram.5.a_ref = f32[648,128]{1,0:T(8,128)S(1)} custom-call(bf16[2176,1024]{1,0:T(8,128)(2,1)S(1)} %features.2.own_ref, bf16[2176,1024]{1,0:T(8,128)(2,1)S(1)} %features.3.other_ref), custom_call_target="tpu_custom_call" | custom-call | flops 1 | bytes 262144 | tf_op jit(solution)/shard_map/gram/pallas_call | solution.py:264
  40.9 6.9 %collective-permute-done.7.b_ref = f32[648,128]{1,0:T(8,128)S(1)} collective-permute-done((f32[648,128]{1,0:T(8,128)S(1)}, f32[648,128]{1,0:T(8,128)S(1)}, u32[]{:S(2)}, u32[]{:S(2)}) %collective-permute-start.7) | collective-permute-done | bytes 331808 | tf_op jit(solution)/shard_map/ppermute | solution.py:52
  47.9 3.3 %collective-permute-start.8 = (f32[320,128]{1,0:T(8,128)S(1)}, f32[320,128]{1,0:T(8,128)S(1)}, u32[]{:S(2)}, u32[]{:S(2)}) collective-permute-start(f32[320,128]{1,0:T(8,128)S(1)} %get-tuple-element.15), channel_id=1, source_target_pairs={{0,8},{1,25},{2,10},{3,27},{4,12},{5,29},{6,14},{7,31},{8,16},{9,1... | collective-permute-start | bytes 491528 | tf_op jit(solution)/shard_map/ppermute | solution.py:52
  51.3 4.5 %collective-permute-start.10 = (f32[160,128]{1,0:T(8,128)S(1)}, f32[160,128]{1,0:T(8,128)S(1)}, u32[]{:S(2)}, u32[]{:S(2)}) collective-permute-start(f32[160,128]{1,0:T(8,128)S(1)} %get-tuple-element.16), channel_id=1, source_target_pairs={{0,16},{1,17},{2,18},{3,19},{4,20},{5,21},{6,22},{7,23},{8,24},{9,... | collective-permute-start | bytes 245768 | tf_op jit(solution)/shard_map/ppermute | solution.py:293
  55.8 2.3 %collective-permute-done.8.next_ref = f32[320,128]{1,0:T(8,128)S(1)} collective-permute-done((f32[320,128]{1,0:T(8,128)S(1)}, f32[320,128]{1,0:T(8,128)S(1)}, u32[]{:S(2)}, u32[]{:S(2)}) %collective-permute-start.8) | collective-permute-done | bytes 163872 | tf_op jit(solution)/shard_map/ppermute | solution.py:52
  58.1 4.6 %collective-permute-done.10.far_ref = f32[160,128]{1,0:T(8,128)S(1)} collective-permute-done((f32[160,128]{1,0:T(8,128)S(1)}, f32[160,128]{1,0:T(8,128)S(1)}, u32[]{:S(2)}, u32[]{:S(2)}) %collective-permute-start.10) | collective-permute-done | bytes 81952 | tf_op jit(solution)/shard_map/ppermute | solution.py:293
  62.7 0.7 %final.1 = f32[68,272]{1,0:T(8,128)} custom-call(f32[160,128]{1,0:T(8,128)S(1)} %get-tuple-element.14.own_ref, f32[320,128]{1,0:T(8,128)S(1)} %collective-permute-done.8.next_ref, f32[160,128]{1,0:T(8,128)S(1)} %collective-permute-done.9.swapped_ref, f32[160,128]{1,0:T(8,128)S(1)} %collective-permute-done.10.far_ref), custom_call_target="tpu_custom_call" | custom-call | flops 1 | bytes 262144 | tf_op jit(solution)/shard_map/final/pallas_call | solution.py:295
  (16 shorter events, 0.8 us)
Async XLA Ops:
  1.4 10.2 %all-to-all-start = ((s32[8,1,128]{2,1,0:T(1,128)}), s32[8,1,128]{2,1,0:T(1,128)S(1)}, u32[]{:S(2)}, u32[]{:S(2)}) async-start(s32[8,1,128]{2,1,0:T(1,128)} %repeat.1), calls=%async_computation | async-start | bytes 8192 | tf_op jit(solution)/shard_map/all_to_all | solution.py:229
  8.4 1.2 %copy-start = (f32[4,4,16384]{2,1,0:T(4,128)S(1)}, f32[4,4,16384]{2,1,0:T(4,128)}, u32[]{:S(2)}) copy-start(f32[4,4,16384]{2,1,0:T(4,128)} %slab_ref.1) | copy-start | bytes 3145732
  12.0 4.4 %collective-permute-start = (f32[16,1024]{1,0:T(8,128)S(1)}, f32[16,1024]{1,0:T(8,128)S(1)}, u32[]{:S(2)}, u32[]{:S(2)}) collective-permute-start(f32[16,1024]{1,0:T(8,128)S(1)} %pick.1), channel_id=1, source_target_pairs={{0,128},{32,160},{64,192},{96,224},{128,0},{160,32},{192,64},{224,... | collective-permute-start | bytes 196616 | tf_op jit(solution)/shard_map/ppermute | solution.py:35
  16.4 6.1 %collective-permute-start.1 = (f32[2,16,1024]{2,1,0:T(8,128)S(1)}, f32[2,16,1024]{2,1,0:T(8,128)S(1)}, u32[]{:S(2)}, u32[]{:S(2)}) collective-permute-start(f32[2,16,1024]{2,1,0:T(8,128)S(1)} %pad_maximum_fusion.w0_ref), channel_id=1, source_target_pairs={{0,32},{32,64},{64,96},{96,0},{128,160},{160,192},{192,224},{224,1... | collective-permute-start | bytes 393224 | tf_op jit(solution)/shard_map/ppermute | solution.py:35
  18.5 6.6 %collective-permute-start.2 = (f32[2,16,1024]{2,1,0:T(8,128)S(1)}, f32[2,16,1024]{2,1,0:T(8,128)S(1)}, u32[]{:S(2)}, u32[]{:S(2)}) collective-permute-start(f32[2,16,1024]{2,1,0:T(8,128)S(1)} %pad_maximum_fusion.w0_ref), channel_id=1, source_target_pairs={{0,64},{32,96},{64,0},{96,32},{128,192},{160,224},{192,128},{224,1... | collective-permute-start | bytes 393224 | tf_op jit(solution)/shard_map/ppermute | solution.py:35
  19.1 7.3 %collective-permute-start.3 = (f32[2,16,1024]{2,1,0:T(8,128)S(1)}, f32[2,16,1024]{2,1,0:T(8,128)S(1)}, u32[]{:S(2)}, u32[]{:S(2)}) collective-permute-start(f32[2,16,1024]{2,1,0:T(8,128)S(1)} %pad_maximum_fusion.w0_ref), channel_id=1, source_target_pairs={{0,96},{32,0},{64,32},{96,64},{128,224},{160,128},{192,160},{224,1... | collective-permute-start | bytes 393224 | tf_op jit(solution)/shard_map/ppermute | solution.py:35
  26.8 2.0 %collective-permute-start.4 = (f32[128,1024]{1,0:T(8,128)S(1)}, f32[128,1024]{1,0:T(8,128)S(1)}, u32[]{:S(2)}, u32[]{:S(2)}) collective-permute-start(f32[128,1024]{1,0:T(8,128)S(1)} %smooth.1.smooth_ref), channel_id=1, source_target_pairs={{0,1},{1,0},{2,3},{3,2},{4,5},{5,4},{6,7},{7,6},{8,9},{9,8},{10,11... | collective-permute-start | bytes 1572872 | tf_op jit(solution)/shard_map/ppermute | solution.py:39
  31.0 8.4 %collective-permute-start.6 = (f32[648,128]{1,0:T(8,128)S(1)}, f32[648,128]{1,0:T(8,128)S(1)}, u32[]{:S(2)}, u32[]{:S(2)}) collective-permute-start(f32[648,128]{1,0:T(8,128)S(1)} %gram.7), channel_id=1, source_target_pairs={{0,2},{1,7},{2,4},{3,1},{4,6},{5,3},{6,0},{7,5},{8,10},{9,15},{10,... | collective-permute-start | bytes 995336 | tf_op jit(solution)/shard_map/ppermute | solution.py:52
  33.7 7.2 %collective-permute-start.5 = (f32[648,128]{1,0:T(8,128)S(1)}, f32[648,128]{1,0:T(8,128)S(1)}, u32[]{:S(2)}, u32[]{:S(2)}) collective-permute-start(f32[648,128]{1,0:T(8,128)S(1)} %gram.4), channel_id=1, source_target_pairs={{0,3},{1,6},{2,5},{3,0},{4,7},{5,2},{6,1},{7,4},{8,11},{9,14},{10,... | collective-permute-start | bytes 995336 | tf_op jit(solution)/shard_map/ppermute | solution.py:52
  39.4 8.4 %collective-permute-start.7 = (f32[648,128]{1,0:T(8,128)S(1)}, f32[648,128]{1,0:T(8,128)S(1)}, u32[]{:S(2)}, u32[]{:S(2)}) collective-permute-start(f32[648,128]{1,0:T(8,128)S(1)} %add.16), channel_id=1, source_target_pairs={{0,2},{1,7},{2,4},{3,1},{4,6},{5,3},{6,0},{7,5},{8,10},{9,15},{10,... | collective-permute-start | bytes 995336 | tf_op jit(solution)/shard_map/ppermute | solution.py:52
  47.9 10.1 %collective-permute-start.8 = (f32[320,128]{1,0:T(8,128)S(1)}, f32[320,128]{1,0:T(8,128)S(1)}, u32[]{:S(2)}, u32[]{:S(2)}) collective-permute-start(f32[320,128]{1,0:T(8,128)S(1)} %get-tuple-element.15), channel_id=1, source_target_pairs={{0,8},{1,25},{2,10},{3,27},{4,12},{5,29},{6,14},{7,31},{8,16},{9,1... | collective-permute-start | bytes 491528 | tf_op jit(solution)/shard_map/ppermute | solution.py:52
  51.3 11.4 %collective-permute-start.10 = (f32[160,128]{1,0:T(8,128)S(1)}, f32[160,128]{1,0:T(8,128)S(1)}, u32[]{:S(2)}, u32[]{:S(2)}) collective-permute-start(f32[160,128]{1,0:T(8,128)S(1)} %get-tuple-element.16), channel_id=1, source_target_pairs={{0,16},{1,17},{2,18},{3,19},{4,20},{5,21},{6,22},{7,23},{8,24},{9,... | collective-permute-start | bytes 245768 | tf_op jit(solution)/shard_map/ppermute | solution.py:293
  58.1 4.6 %collective-permute-start.9 = (f32[160,128]{1,0:T(8,128)S(1)}, f32[160,128]{1,0:T(8,128)S(1)}, u32[]{:S(2)}, u32[]{:S(2)}) collective-permute-start(f32[160,128]{1,0:T(8,128)S(1)} %slice.12), channel_id=1, source_target_pairs={{0,1},{1,0},{2,3},{3,2},{4,5},{5,4},{6,7},{7,6},{8,9},{9,8},{10,11... | collective-permute-start | bytes 245768 | tf_op jit(solution)/shard_map/ppermute | solution.py:39

commit v5 on v3

--- a/solution.py
+++ b/solution.py
@@ -14,9 +14,11 @@
 BLOCK = N_LEV * SAMP
 FEAT = 4 * LEV + 2 * LEV * LEV
 ROWS_OUT, COLS_OUT = FEAT // N_HOR, FEAT // N_LEV
-CHUNK, WINDOW, CHUNKS = 72, 80, 4
-PIECE = CHUNKS * 2 * CHUNK
-SENT = PIECE + CHUNK
+CHUNK, BOTH, HALF = 72, 2 * ROWS_OUT, 16
+WINDOWS = (CHUNK, BOTH, CHUNK)
+BUILT = sum(WINDOWS) + 8 * len(WINDOWS)
+MAIN = 2 * sum(WINDOWS)
+SENT = MAIN + 40
 LAST = 2 * CHUNK + 16
 SHARE = 1 << 18
 VMEM = pl.BlockSpec(memory_space=pltpu.VMEM)
@@ -97,64 +99,106 @@
     lax.fori_loop(0, BLOCK // LANES, tile, 0)
 
 
-def feature_kernel(smooth_ref, feat_ref):
-    def tile(t, carry):
-        at = pl.ds(pl.multiple_of(t * LANES, LANES), LANES)
-        early = smooth_ref[0 : 2 * LEV, at]
-        feat_ref[0 : 2 * LEV, at] = smooth_ref[2 * LEV : 4 * LEV, at].astype(jnp.bfloat16)
-        feat_ref[2 * LEV : 4 * LEV, at] = early.astype(jnp.bfloat16)
-        first = early[0:LEV]
-        for m in range(2 * LEV):
-            row = jnp.broadcast_to(smooth_ref[pl.ds(2 * LEV + m, 1), at], (LEV, LANES))
-            feat_ref[4 * LEV + m * LEV : 4 * LEV + (m + 1) * LEV, at] = (row * first).astype(jnp.bfloat16)
-        return carry
-
-    lax.fori_loop(0, BLOCK // LANES, tile, 0)
-
-
-def gram_kernel(place, own_ref, other_ref, out_ref, left_ref, prod_ref):
-    hor, lev = lax.axis_index("hor"), lax.axis_index("lev")
+def build_rows(smooth_ref, half, out_ref, at):
+    late = 2 * LEV
+    m = jnp.maximum(half - 4 * LEV // HALF, 0) // 2
+    product = smooth_ref[pl.ds(late + m, 1), :] * smooth_ref[pl.ds(pl.multiple_of(half % 2 * HALF, HALF), HALF), :]
+    linear = smooth_ref[pl.ds(pl.multiple_of((late + half * HALF) % (4 * LEV), HALF), HALF), :]
+    rows = jnp.where(half < 4 * LEV // HALF, linear, product)
+    out_ref[at : at + HALF, :] = rows.astype(jnp.bfloat16)
+
+
+def right_kernel(smooth_ref, out_ref):
+    lev = lax.axis_index("lev")
+    for i in range(COLS_OUT // HALF):
+        build_rows(smooth_ref, lev * (COLS_OUT // HALF) + i, out_ref, i * HALF)
+
+
+def windows_of(place):
+    hor = lax.axis_index("hor")
     zhi, y, core = hor // (2 * N_Y), hor // 2 % N_Y, hor % 2
-    right = pl.ds(pl.multiple_of(lev * COLS_OUT, 16), COLS_OUT)
     to_y = {"far": y + 2, "cross": y + 5 - 2 * core, "near": y + 5 - 2 * core, "own": y}[place]
     to_y = lax.rem(to_y, N_Y)
     to_core = 1 - core if place == "cross" else core
-    next_z = lax.rem(zhi + 5 - 2 * to_core, N_ZHI)
-    chunks = ((zhi, to_core), (next_z, to_core), (next_z, 1 - to_core), (lax.rem(zhi + 2, N_ZHI), to_core))
     skip = 8 * lax.rem(to_y, 2)
-    for block, ref in enumerate((own_ref, other_ref)):
-        for chunk, (to_z, row_core) in enumerate(chunks):
-            start = (to_z * N_Y + to_y) * 2 * ROWS_OUT + row_core * 64 - skip
-            rows = pl.ds(pl.multiple_of(start, 16), WINDOW)
-            left_ref[chunk * WINDOW : (chunk + 1) * WINDOW, :] = ref[rows, :]
-        part = lax.dot_general(
-            left_ref[...], ref[right, :], (((1,), (1,)), ((), ())), preferred_element_type=jnp.float32
-        )
-        prod_ref[...] = part + prod_ref[...] if block else part
-    for chunk in range(CHUNKS):
-        rows = pl.ds(pl.multiple_of(chunk * WINDOW + skip, 8), CHUNK)
+
+    def start(to_z, offset):
+        return (lax.rem(to_z, N_ZHI) * N_Y + to_y) * BOTH + offset - skip
+
+    return (start(zhi, 64 * to_core), start(zhi + 5 - 2 * to_core, 0), start(zhi + 2, 64 * to_core)), skip
+
+
+def product(place, smooth_ref, right_ref, left_ref):
+    at = 0
+    for first, size in zip(windows_of(place)[0], WINDOWS):
+        for i in range((size + 8) // HALF):
+            build_rows(smooth_ref, first // HALF + i, left_ref, at)
+            at += HALF
+    return lax.dot_general(
+        left_ref[...], right_ref[...], (((1,), (1,)), ((), ())), preferred_element_type=jnp.float32
+    )
+
+
+def emit(place, prod_ref, out_ref):
+    skip = windows_of(place)[1]
+    at, base, group = 0, 0, 0
+    for size in WINDOWS:
         for half in range(2):
-            base = (2 * chunk + half) * CHUNK
-            out_ref[base : base + CHUNK, :] = prod_ref[rows, half * LANES : (half + 1) * LANES]
-        out_ref[PIECE:SENT, 16 * chunk : 16 * chunk + 16] = prod_ref[rows, 2 * LANES : COLS_OUT]
+            rows = pl.ds(pl.multiple_of(at + skip, 8), size)
+            out_ref[base : base + size, :] = prod_ref[rows, half * LANES : (half + 1) * LANES]
+            base += size
+        for i in range(size // 8):
+            rows = pl.ds(pl.multiple_of(at + 8 * i + skip, 8), 8)
+            to = MAIN + 8 * (group // 8)
+            strip = 16 * (group % 8)
+            out_ref[to : to + 8, strip : strip + 16] = prod_ref[rows, 2 * LANES : COLS_OUT]
+            group += 1
+        at += size + 8
+
+
+def begin_kernel(place, smooth_ref, right_ref, out_ref, left_ref):
+    out_ref[...] = product(place, smooth_ref, right_ref, left_ref)
+
+
+def finish_kernel(place, part_ref, smooth_ref, right_ref, out_ref, left_ref, prod_ref):
+    prod_ref[...] = part_ref[...] + product(place, smooth_ref, right_ref, left_ref)
+    emit(place, prod_ref, out_ref)
+
+
+def gram_kernel(place, own_ref, own_right_ref, other_ref, other_right_ref, out_ref, left_ref, prod_ref):
+    prod_ref[...] = product(place, own_ref, own_right_ref, left_ref)
+    prod_ref[...] += product(place, other_ref, other_right_ref, left_ref)
+    emit(place, prod_ref, out_ref)
 
 
 def add_kernel(a_ref, b_ref, out_ref):
     out_ref[...] = a_ref[...] + b_ref[...]
 
 
-def split_kernel(a_ref, b_ref, t0_ref, t1_ref, t2_ref, t3_ref):
-    rest = a_ref[PIECE:SENT, :] + b_ref[PIECE:SENT, :]
-    strip = lax.broadcasted_iota(jnp.int32, (8, LANES), 1) // 16
-    for chunk, ref in enumerate((t0_ref, t1_ref, t2_ref, t3_ref)):
-        rows = slice(chunk * 2 * CHUNK, (chunk + 1) * 2 * CHUNK)
-        ref[0 : 2 * CHUNK, :] = a_ref[rows, :] + b_ref[rows, :]
-        packed = jnp.zeros((8, LANES), jnp.float32)
-        for group in range(8):
-            moved = pltpu.roll(rest[8 * group : 8 * group + 8], 16 * (group - chunk) % LANES, 1)
-            packed = jnp.where(strip == group, moved, packed)
-        ref[2 * CHUNK : 2 * CHUNK + 8, :] = packed
-        ref[2 * CHUNK + 8 : LAST, :] = pltpu.roll(rest[64:CHUNK], -16 * chunk % LANES, 1)
+def split_kernel(a_ref, b_ref, own_ref, near_ref, cross_ref, far_ref):
+    core = lax.axis_index("hor") % 2
+    lane = lax.broadcasted_iota(jnp.int32, (8, LANES), 1)
+
+    def total(start, size):
+        rows = pl.ds(start if isinstance(start, int) else pl.multiple_of(start, 8), size)
+        return a_ref[rows, :] + b_ref[rows, :]
+
+    ahead = 2 * CHUNK
+    places = (
+        (own_ref, 0, CHUNK, 0, 0),
+        (near_ref, ahead + 64 * core, BOTH, 1 + core, 1),
+        (cross_ref, ahead + 64 * (1 - core), BOTH, 2 - core, 1),
+        (far_ref, ahead + 2 * BOTH, CHUNK, 3, 2),
+    )
+    for ref, start, stride, tile, strip in places:
+        ref[0:CHUNK, :] = total(start, CHUNK)
+        ref[CHUNK : 2 * CHUNK, :] = total(start + stride, CHUNK)
+        one, two = total(MAIN + 8 * tile, 8), total(MAIN + 8 * tile + 8, 8)
+        if strip:
+            one, two = pltpu.roll(one, LANES - 16 * strip, 1), pltpu.roll(two, LANES - 16 * strip, 1)
+            one = jnp.where(lane < LANES - 16 * strip, one, two)
+        ref[2 * CHUNK : 2 * CHUNK + 8, :] = one
+        ref[2 * CHUNK + 8 : LAST, :] = two
 
 
 def final_kernel(t0_ref, t1_ref, t2_ref, out_ref):
@@ -186,16 +230,30 @@
     return jnp.broadcast_to(coef[:, None], (3 * LEV, LANES))
 
 
-def features(smoothed):
+def right_of(smoothed):
     return pl.pallas_call(
-        feature_kernel,
-        out_shape=jax.ShapeDtypeStruct((FEAT, BLOCK), jnp.bfloat16),
+        right_kernel,
+        out_shape=jax.ShapeDtypeStruct((COLS_OUT, BLOCK), jnp.bfloat16),
         in_specs=[VMEM],
         out_specs=VMEM,
+        compiler_params=params(4),
+        cost_estimate=cost(1, SHARE),
+        name="right",
+    )(smoothed)
+
+
+def gram(kernel, place, out_shape, *operands):
+    scratch = [pltpu.VMEM((BUILT, BLOCK), jnp.bfloat16), pltpu.VMEM((BUILT, COLS_OUT), jnp.float32)]
+    return pl.pallas_call(
+        functools.partial(kernel, place),
+        out_shape=jax.ShapeDtypeStruct(out_shape, jnp.float32),
+        in_specs=[VMEM] * len(operands),
+        out_specs=VMEM,
+        scratch_shapes=scratch[:1] if kernel is begin_kernel else scratch,
         compiler_params=params(12),
-        cost_estimate=cost(FEAT * BLOCK, 5 << 20),
-        name="features",
-    )(smoothed)
+        cost_estimate=cost(1, SHARE),
+        name="gram_" + place,
+    )(*operands)
 
 
 def add(a, b):
@@ -253,39 +311,31 @@
         name="smooth",
     )(coef, near, far[1], far[2], far[3])
     other = swap_cores(own)
-    feats = [features(own), features(other)]
-    parts = {}
-    for k in ("far", "cross", "near", "own"):
-        parts[k] = pl.pallas_call(
-            functools.partial(gram_kernel, k),
-            out_shape=jax.ShapeDtypeStruct((SENT, LANES), f32),
-            in_specs=[VMEM] * 2,
-            out_specs=VMEM,
-            scratch_shapes=[
-                pltpu.VMEM((CHUNKS * WINDOW, BLOCK), jnp.bfloat16),
-                pltpu.VMEM((CHUNKS * WINDOW, COLS_OUT), f32),
-            ],
-            compiler_params=params(16),
-            cost_estimate=cost(1, SHARE),
-            name="gram",
-        )(*feats)
-        if k == "cross":
-            feats, parts[k] = lax.optimization_barrier((feats, parts[k]))
+    own_right = right_of(own)
+    begun = gram(begin_kernel, "far", (BUILT, COLS_OUT), own, own_right)
+    other_right = right_of(other)
+    sent = (SENT, LANES)
+    parts = {"far": gram(finish_kernel, "far", sent, begun, other, other_right)}
+    both = (own, own_right, other, other_right)
+    parts["cross"] = gram(gram_kernel, "cross", sent, *both)
+    both, parts["cross"] = lax.optimization_barrier((both, parts["cross"]))
+    parts["near"] = gram(gram_kernel, "near", sent, *both)
+    parts["own"] = gram(gram_kernel, "own", sent, *both)
     two_back = hop(parts["far"], "y", 0)
     from_cross = hop(parts["cross"], "y", 1)
     from_near = hop(add(parts["near"], two_back), "y", 0)
-    sums = pl.pallas_call(
+    kept, near, cross, far = pl.pallas_call(
         split_kernel,
-        out_shape=[jax.ShapeDtypeStruct((LAST, LANES), f32)] * CHUNKS,
+        out_shape=[jax.ShapeDtypeStruct((LAST, LANES), f32)] * 4,
         in_specs=[VMEM] * 2,
-        out_specs=[VMEM] * CHUNKS,
+        out_specs=[VMEM] * 4,
         compiler_params=params(8),
         cost_estimate=cost(1, SHARE),
         name="split",
     )(add(parts["own"], from_cross), from_near)
-    two_back = hop(sums[3], "z_hi", 0)
-    from_cross = hop(sums[2], "z_hi", 1)
-    from_near = hop(add(sums[1], two_back), "z_hi", 0)
+    two_back = hop(far, "z_hi", 0)
+    from_cross = hop(cross, "z_hi", 1)
+    from_near = hop(add(near, two_back), "z_hi", 0)
     return pl.pallas_call(
         final_kernel,
         out_shape=jax.ShapeDtypeStruct((ROWS_OUT, COLS_OUT), f32),
@@ -294,7 +344,7 @@
         compiler_params=params(8),
         cost_estimate=cost(1, SHARE),
         name="final",
-    )(sums[0], from_cross, from_near)
+    )(kept, from_cross, from_near)
 
 
 def solution(mesh):

time: 64.2 us -> 62.5 us (0.974)
  other arithmetic: 1.71 us -> 0.33 us
  Pallas kernels: 8.8 us -> 8 us
    ppermute x6, waiting for transfers between devices: 21.9 us -> 20.8 us  [hop(): return lax.ppermute(value, 'hor', pairs)]
    pallas_call x6 -> x7, Pallas kernels: 6.47 us -> 5.68 us  [the longest x5 5.23 us: gram(): pl.pallas_call(functools.partial(kernel, place), out_shape=jax.ShapeDtype...]
    mul x1, other arithmetic: 0.8 us -> 0.07 us  [filter_coefficients(): lower = jnp.concatenate([zero_one, thickness[:-1] * link])]
    all_to_all x1, waiting for transfers between devices: 1.85 us -> 2.57 us  [on_device(): lists = lax.all_to_all(repeated, 'lev', 0, 0, tiled=True)]
    ppermute x4, waiting for transfers between devices: 9.26 us -> 9.91 us  [shift_lev(): return lax.ppermute(value, 'lev', pairs)]
    div x1, other arithmetic: 0.73 us -> 0.08 us  [filter_coefficients(): 2.0 * thickness / denom]
    unnamed x4 -> x8, local copies, waits for them, and re-layouts: 1.88 us -> 1.89 us
  transfers between devices with their start and end apart: 12 -> 12, of which waited for: 10 -> 10; matrix products, arithmetic and copies ran while one was open for 3% -> 0% of each run, Pallas kernels for 7% -> 8%
where the time goes in v5:
time: 62.5 us; the launch traced here: 62.4 us
  waiting for transfers between devices  34.3 us (55%)
  starting transfers between devices  17.7 us (28%)
  Pallas kernels  8 us (13%)
  local copies, waits for them, and re-layouts  1.96 us (3%)
    ppermute x6, waiting for transfers between devices, hop(): return lax.ppermute(value, 'hor', pairs)  20.8 us
    ppermute x4, waiting for transfers between devices, shift_lev(): return lax.ppermute(value, 'lev', pairs)  9.91 us
    ppermute x6, starting transfers between devices, hop(): return lax.ppermute(value, 'hor', pairs)  7.11 us
    all_to_all x1, starting transfers between devices, on_device(): lists = lax.all_to_all(repeated, 'lev', 0, 0, tiled=True)  6.26 us
    pallas_call x5, Pallas kernels, gram(): pl.pallas_call(functools.partial(kernel, place), out_shape=jax.ShapeDtype...  5.23 us
    ppermute x4, starting transfers between devices, shift_lev(): return lax.ppermute(value, 'lev', pairs)  4.23 us
    all_to_all x1, waiting for transfers between devices, on_device(): lists = lax.all_to_all(repeated, 'lev', 0, 0, tiled=True)  2.57 us
    unnamed x8, local copies, waits for them, and re-layouts  1.89 us
  transfers between devices with their start and end apart: 12, of which 10 were waited for; matrix products, arithmetic and copies ran while one was open for 0% of the time, Pallas kernels for 8%

profile of v5, /device:TPU:6, one launch (start us, length us, event | category | flops | bytes accessed | tf_op | source)
XLA Modules:
  0.0 62.4 jit_solution(17152506055401447577)
XLA Ops:
  0.0 0.7 %copy-done.1 = s32[1,128]{1,0:T(1,128)S(1)} copy-done((s32[1,128]{1,0:T(1,128)S(1)}, s32[1,128]{1,0:T(1,128)}, u32[]{:S(2)}) %copy-start.1) | copy-done | bytes 536
  0.7 0.6 repeat.1
  1.3 6.3 %all-to-all-start = ((s32[8,1,128]{2,1,0:T(1,128)}), s32[8,1,128]{2,1,0:T(1,128)S(1)}, u32[]{:S(2)}, u32[]{:S(2)}) async-start(s32[8,1,128]{2,1,0:T(1,128)} %repeat.1), calls=%async_computation | async-start | bytes 8192 | tf_op jit(solution)/shard_map/all_to_all | solution.py:282
  7.6 1.2 %copy-done = f32[4,4,16384]{2,1,0:T(4,128)S(1)} copy-done((f32[4,4,16384]{2,1,0:T(4,128)S(1)}, f32[4,4,16384]{2,1,0:T(4,128)}, u32[]{:S(2)}) %copy-start) | copy-done | bytes 1048600
  9.0 2.6 %all-to-all-done.index_ref = s32[8,1,128]{2,1,0:T(1,128)S(1)} async-done(((s32[8,1,128]{2,1,0:T(1,128)}), s32[8,1,128]{2,1,0:T(1,128)S(1)}, u32[]{:S(2)}, u32[]{:S(2)}) %all-to-all-start) | async-done | bytes 4128 | tf_op jit(solution)/shard_map/all_to_all | solution.py:282
  11.5 0.4 pick.1
  11.9 0.7 %collective-permute-start = (f32[16,1024]{1,0:T(8,128)S(1)}, f32[16,1024]{1,0:T(8,128)S(1)}, u32[]{:S(2)}, u32[]{:S(2)}) collective-permute-start(f32[16,1024]{1,0:T(8,128)S(1)} %pick.1), channel_id=1, source_target_pairs={{0,128},{32,160},{64,192},{96,224},{128,0},{160,32},{192,64},{224,... | collective-permute-start | bytes 196616 | tf_op jit(solution)/shard_map/ppermute | solution.py:37
  12.6 3.6 %collective-permute-done = f32[16,1024]{1,0:T(8,128)S(1)} collective-permute-done((f32[16,1024]{1,0:T(8,128)S(1)}, f32[16,1024]{1,0:T(8,128)S(1)}, u32[]{:S(2)}, u32[]{:S(2)}) %collective-permute-start) | collective-permute-done | bytes 65568 | tf_op jit(solution)/shard_map/ppermute | solution.py:37
  16.3 2.1 %collective-permute-start.1 = (f32[2,16,1024]{2,1,0:T(8,128)S(1)}, f32[2,16,1024]{2,1,0:T(8,128)S(1)}, u32[]{:S(2)}, u32[]{:S(2)}) collective-permute-start(f32[2,16,1024]{2,1,0:T(8,128)S(1)} %pad_maximum_fusion.w0_ref), channel_id=1, source_target_pairs={{0,32},{32,64},{64,96},{96,0},{128,160},{160,192},{192,224},{224,1... | collective-permute-start | bytes 393224 | tf_op jit(solution)/shard_map/ppermute | solution.py:37
  18.4 0.6 collective-permute-start.2
  19.0 0.9 %collective-permute-start.3 = (f32[2,16,1024]{2,1,0:T(8,128)S(1)}, f32[2,16,1024]{2,1,0:T(8,128)S(1)}, u32[]{:S(2)}, u32[]{:S(2)}) collective-permute-start(f32[2,16,1024]{2,1,0:T(8,128)S(1)} %pad_maximum_fusion.w0_ref), channel_id=1, source_target_pairs={{0,96},{32,0},{64,32},{96,64},{128,224},{160,128},{192,160},{224,1... | collective-permute-start | bytes 393224 | tf_op jit(solution)/shard_map/ppermute | solution.py:37
  20.0 2.3 %collective-permute-done.1.w1_ref = f32[2,16,1024]{2,1,0:T(8,128)S(1)} collective-permute-done((f32[2,16,1024]{2,1,0:T(8,128)S(1)}, f32[2,16,1024]{2,1,0:T(8,128)S(1)}, u32[]{:S(2)}, u32[]{:S(2)}) %collective-permute-start.1) | collective-permute-done | bytes 131104 | tf_op jit(solution)/shard_map/ppermute | solution.py:37
  22.4 2.7 %collective-permute-done.2.w2_ref = f32[2,16,1024]{2,1,0:T(8,128)S(1)} collective-permute-done((f32[2,16,1024]{2,1,0:T(8,128)S(1)}, f32[2,16,1024]{2,1,0:T(8,128)S(1)}, u32[]{:S(2)}, u32[]{:S(2)}) %collective-permute-start.2) | collective-permute-done | bytes 131104 | tf_op jit(solution)/shard_map/ppermute | solution.py:37
  25.0 1.3 %collective-permute-done.3.w3_ref = f32[2,16,1024]{2,1,0:T(8,128)S(1)} collective-permute-done((f32[2,16,1024]{2,1,0:T(8,128)S(1)}, f32[2,16,1024]{2,1,0:T(8,128)S(1)}, u32[]{:S(2)}, u32[]{:S(2)}) %collective-permute-start.3) | collective-permute-done | bytes 131104 | tf_op jit(solution)/shard_map/ppermute | solution.py:37
  26.4 0.3 smooth.1.smooth_ref.own_ref
  26.8 0.2 right.2.own_right_ref.right_ref
  27.0 0.7 %gram_far.2.part_ref = f32[304,272]{1,0:T(8,128)S(1)} custom-call(f32[128,1024]{1,0:T(8,128)S(1)} %smooth.1.smooth_ref.own_ref, bf16[272,1024]{1,0:T(8,128)(2,1)S(1)} %right.2.own_right_ref.right_ref), custom_call_target="tpu_custom_call" | custom-call | flops 1 | bytes 262144 | tf_op jit(solution)/shard_map/gram_far/pallas_call | solution.py:247
  27.7 1.0 %collective-permute-done.4.smooth_ref.other_ref = f32[128,1024]{1,0:T(8,128)S(1)} collective-permute-done((f32[128,1024]{1,0:T(8,128)S(1)}, f32[128,1024]{1,0:T(8,128)S(1)}, u32[]{:S(2)}, u32[]{:S(2)}) %collective-permute-start.4) | collective-permute-done | bytes 524320 | tf_op jit(solution)/shard_map/ppermute | solution.py:41
  28.7 0.2 right.3.other_right_ref.right_ref
  28.9 0.9 %gram_far.3 = f32[600,128]{1,0:T(8,128)S(1)} custom-call(f32[304,272]{1,0:T(8,128)S(1)} %gram_far.2.part_ref, f32[128,1024]{1,0:T(8,128)S(1)} %collective-permute-done.4.smooth_ref.other_ref, bf16[272,1024]{1,0:T(8,128)(2,1)S(1)} %right.3.other_right_ref.right_ref), custom_call_target="tpu_custom_call" | custom-call | flops 1 | bytes 262144 | tf_op jit(solution)/shard_map/gram_far/pallas_call | solution.py:247
  29.8 1.6 %collective-permute-start.6 = (f32[600,128]{1,0:T(8,128)S(1)}, f32[600,128]{1,0:T(8,128)S(1)}, u32[]{:S(2)}, u32[]{:S(2)}) collective-permute-start(f32[600,128]{1,0:T(8,128)S(1)} %gram_far.3), channel_id=1, source_target_pairs={{0,2},{1,7},{2,4},{3,1},{4,6},{5,3},{6,0},{7,5},{8,10},{9,15},{10,... | collective-permute-start | bytes 921608 | tf_op jit(solution)/shard_map/ppermute | solution.py:54
  31.4 1.2 %gram_cross.1 = f32[600,128]{1,0:T(8,128)S(1)} custom-call(f32[128,1024]{1,0:T(8,128)S(1)} %smooth.1.smooth_ref.own_ref, bf16[272,1024]{1,0:T(8,128)(2,1)S(1)} %right.2.own_right_ref.right_ref, f32[128,1024]{1,0:T(8,128)S(1)} %collective-permute-done.4.smooth_ref.other_ref, bf16[272,1024]{1,0:T(8,128)(2,1)S(1)} %right.3.other_right_ref.right_ref), custom_call_target="tpu_custom_call" | custom-call | flops 1 | bytes 262144 | tf_op jit(solution)/shard_map/gram_cross/pallas_call | solution.py:247
  32.7 1.2 %gram_near.1.a_ref = f32[600,128]{1,0:T(8,128)S(1)} custom-call(f32[128,1024]{1,0:T(8,128)S(1)} %smooth.1.smooth_ref.own_ref, bf16[272,1024]{1,0:T(8,128)(2,1)S(1)} %right.2.own_right_ref.right_ref, f32[128,1024]{1,0:T(8,128)S(1)} %collective-permute-done.4.smooth_ref.other_ref, bf16[272,1024]{1,0:T(8,128)(2,1)S(1)} %right.3.other_right_ref.right_ref), custom_call_target="tpu_custom_call" | custom-call | flops 1 | bytes 262144 | tf_op jit(solution)/shard_map/gram_near/pallas_call | solution.py:247
  34.0 3.9 %collective-permute-done.6.b_ref = f32[600,128]{1,0:T(8,128)S(1)} collective-permute-done((f32[600,128]{1,0:T(8,128)S(1)}, f32[600,128]{1,0:T(8,128)S(1)}, u32[]{:S(2)}, u32[]{:S(2)}) %collective-permute-start.6) | collective-permute-done | bytes 307232 | tf_op jit(solution)/shard_map/ppermute | solution.py:54
  37.9 0.5 collective-permute-start.7
  38.4 1.2 %gram_own.1.a_ref = f32[600,128]{1,0:T(8,128)S(1)} custom-call(f32[128,1024]{1,0:T(8,128)S(1)} %smooth.1.smooth_ref.own_ref, bf16[272,1024]{1,0:T(8,128)(2,1)S(1)} %right.2.own_right_ref.right_ref, f32[128,1024]{1,0:T(8,128)S(1)} %collective-permute-done.4.smooth_ref.other_ref, bf16[272,1024]{1,0:T(8,128)(2,1)S(1)} %right.3.other_right_ref.right_ref), custom_call_target="tpu_custom_call" | custom-call | flops 1 | bytes 262144 | tf_op jit(solution)/shard_map/gram_own/pallas_call | solution.py:247
  39.6 6.4 %collective-permute-done.7.b_ref = f32[600,128]{1,0:T(8,128)S(1)} collective-permute-done((f32[600,128]{1,0:T(8,128)S(1)}, f32[600,128]{1,0:T(8,128)S(1)}, u32[]{:S(2)}, u32[]{:S(2)}) %collective-permute-start.7) | collective-permute-done | bytes 307232 | tf_op jit(solution)/shard_map/ppermute | solution.py:54
  46.2 3.3 %collective-permute-start.9 = (f32[160,128]{1,0:T(8,128)S(1)}, f32[160,128]{1,0:T(8,128)S(1)}, u32[]{:S(2)}, u32[]{:S(2)}) collective-permute-start(f32[160,128]{1,0:T(8,128)S(1)} %get-tuple-element.22), channel_id=1, source_target_pairs={{0,8},{1,25},{2,10},{3,27},{4,12},{5,29},{6,14},{7,31},{8,16},{9,1... | collective-permute-start | bytes 245768 | tf_op jit(solution)/shard_map/ppermute | solution.py:54
  49.5 4.6 %collective-permute-done.9.b_ref = f32[160,128]{1,0:T(8,128)S(1)} collective-permute-done((f32[160,128]{1,0:T(8,128)S(1)}, f32[160,128]{1,0:T(8,128)S(1)}, u32[]{:S(2)}, u32[]{:S(2)}) %collective-permute-start.9) | collective-permute-done | bytes 81952 | tf_op jit(solution)/shard_map/ppermute | solution.py:54
  54.1 1.7 %collective-permute-start.10 = (f32[160,128]{1,0:T(8,128)S(1)}, f32[160,128]{1,0:T(8,128)S(1)}, u32[]{:S(2)}, u32[]{:S(2)}) collective-permute-start(f32[160,128]{1,0:T(8,128)S(1)} %add.18), channel_id=1, source_target_pairs={{0,8},{1,25},{2,10},{3,27},{4,12},{5,29},{6,14},{7,31},{8,16},{9,1... | collective-permute-start | bytes 245768 | tf_op jit(solution)/shard_map/ppermute | solution.py:54
  55.8 5.8 %collective-permute-done.10.t2_ref = f32[160,128]{1,0:T(8,128)S(1)} collective-permute-done((f32[160,128]{1,0:T(8,128)S(1)}, f32[160,128]{1,0:T(8,128)S(1)}, u32[]{:S(2)}, u32[]{:S(2)}) %collective-permute-start.10) | collective-permute-done | bytes 81952 | tf_op jit(solution)/shard_map/ppermute | solution.py:54
  61.6 0.7 %final.1 = f32[68,272]{1,0:T(8,128)} custom-call(f32[160,128]{1,0:T(8,128)S(1)} %get-tuple-element.19.t0_ref, f32[160,128]{1,0:T(8,128)S(1)} %collective-permute-done.8.t1_ref, f32[160,128]{1,0:T(8,128)S(1)} %collective-permute-done.10.t2_ref), custom_call_target="tpu_custom_call" | custom-call | flops 1 | bytes 262144 | tf_op jit(solution)/shard_map/final/pallas_call | solution.py:339
  (23 shorter events, 0.9 us)
Async XLA Ops:
  0.0 0.7 %copy-start.1 = (s32[1,128]{1,0:T(1,128)S(1)}, s32[1,128]{1,0:T(1,128)}, u32[]{:S(2)}) copy-start(s32[1,128]{1,0:T(1,128)} %index_ref.1) | copy-start | bytes 1540
  1.3 6.3 %copy-start.2 = (f32[32]{0:T(128)S(1)}, f32[32]{0:T(128)}, u32[]{:S(2)}) copy-start(f32[32]{0:T(128)} %param.6) | copy-start | bytes 388
  1.3 6.3 %copy-start.3 = (s32[31]{0:T(128)S(1)}, s32[31]{0:T(128)}, u32[]{:S(2)}) copy-start(s32[31]{0:T(128)} %param.7) | copy-start | bytes 376
  1.3 10.3 %all-to-all-start = ((s32[8,1,128]{2,1,0:T(1,128)}), s32[8,1,128]{2,1,0:T(1,128)S(1)}, u32[]{:S(2)}, u32[]{:S(2)}) async-start(s32[8,1,128]{2,1,0:T(1,128)} %repeat.1), calls=%async_computation | async-start | bytes 8192 | tf_op jit(solution)/shard_map/all_to_all | solution.py:282
  7.6 1.2 %copy-start = (f32[4,4,16384]{2,1,0:T(4,128)S(1)}, f32[4,4,16384]{2,1,0:T(4,128)}, u32[]{:S(2)}) copy-start(f32[4,4,16384]{2,1,0:T(4,128)} %slab_ref.1) | copy-start | bytes 3145732
  11.9 4.4 %collective-permute-start = (f32[16,1024]{1,0:T(8,128)S(1)}, f32[16,1024]{1,0:T(8,128)S(1)}, u32[]{:S(2)}, u32[]{:S(2)}) collective-permute-start(f32[16,1024]{1,0:T(8,128)S(1)} %pick.1), channel_id=1, source_target_pairs={{0,128},{32,160},{64,192},{96,224},{128,0},{160,32},{192,64},{224,... | collective-permute-start | bytes 196616 | tf_op jit(solution)/shard_map/ppermute | solution.py:37
  16.3 6.1 %collective-permute-start.1 = (f32[2,16,1024]{2,1,0:T(8,128)S(1)}, f32[2,16,1024]{2,1,0:T(8,128)S(1)}, u32[]{:S(2)}, u32[]{:S(2)}) collective-permute-start(f32[2,16,1024]{2,1,0:T(8,128)S(1)} %pad_maximum_fusion.w0_ref), channel_id=1, source_target_pairs={{0,32},{32,64},{64,96},{96,0},{128,160},{160,192},{192,224},{224,1... | collective-permute-start | bytes 393224 | tf_op jit(solution)/shard_map/ppermute | solution.py:37
  18.4 6.6 %collective-permute-start.2 = (f32[2,16,1024]{2,1,0:T(8,128)S(1)}, f32[2,16,1024]{2,1,0:T(8,128)S(1)}, u32[]{:S(2)}, u32[]{:S(2)}) collective-permute-start(f32[2,16,1024]{2,1,0:T(8,128)S(1)} %pad_maximum_fusion.w0_ref), channel_id=1, source_target_pairs={{0,64},{32,96},{64,0},{96,32},{128,192},{160,224},{192,128},{224,1... | collective-permute-start | bytes 393224 | tf_op jit(solution)/shard_map/ppermute | solution.py:37
  19.0 7.3 %collective-permute-start.3 = (f32[2,16,1024]{2,1,0:T(8,128)S(1)}, f32[2,16,1024]{2,1,0:T(8,128)S(1)}, u32[]{:S(2)}, u32[]{:S(2)}) collective-permute-start(f32[2,16,1024]{2,1,0:T(8,128)S(1)} %pad_maximum_fusion.w0_ref), channel_id=1, source_target_pairs={{0,96},{32,0},{64,32},{96,64},{128,224},{160,128},{192,160},{224,1... | collective-permute-start | bytes 393224 | tf_op jit(solution)/shard_map/ppermute | solution.py:37
  26.7 2.0 %collective-permute-start.4 = (f32[128,1024]{1,0:T(8,128)S(1)}, f32[128,1024]{1,0:T(8,128)S(1)}, u32[]{:S(2)}, u32[]{:S(2)}) collective-permute-start(f32[128,1024]{1,0:T(8,128)S(1)} %smooth.1.smooth_ref.own_ref), channel_id=1, source_target_pairs={{0,1},{1,0},{2,3},{3,2},{4,5},{5,4},{6,7},{7,6},{8,9},{9,8},{10,11... | collective-permute-start | bytes 1572872 | tf_op jit(solution)/shard_map/ppermute | solution.py:41
  29.8 8.1 %collective-permute-start.6 = (f32[600,128]{1,0:T(8,128)S(1)}, f32[600,128]{1,0:T(8,128)S(1)}, u32[]{:S(2)}, u32[]{:S(2)}) collective-permute-start(f32[600,128]{1,0:T(8,128)S(1)} %gram_far.3), channel_id=1, source_target_pairs={{0,2},{1,7},{2,4},{3,1},{4,6},{5,3},{6,0},{7,5},{8,10},{9,15},{10,... | collective-permute-start | bytes 921608 | tf_op jit(solution)/shard_map/ppermute | solution.py:54
  32.6 6.9 %collective-permute-start.5 = (f32[600,128]{1,0:T(8,128)S(1)}, f32[600,128]{1,0:T(8,128)S(1)}, u32[]{:S(2)}, u32[]{:S(2)}) collective-permute-start(f32[600,128]{1,0:T(8,128)S(1)} %gram_cross.1), channel_id=1, source_target_pairs={{0,3},{1,6},{2,5},{3,0},{4,7},{5,2},{6,1},{7,4},{8,11},{9,14},{10,... | collective-permute-start | bytes 921608 | tf_op jit(solution)/shard_map/ppermute | solution.py:54
  37.9 8.1 %collective-permute-start.7 = (f32[600,128]{1,0:T(8,128)S(1)}, f32[600,128]{1,0:T(8,128)S(1)}, u32[]{:S(2)}, u32[]{:S(2)}) collective-permute-start(f32[600,128]{1,0:T(8,128)S(1)} %add.17), channel_id=1, source_target_pairs={{0,2},{1,7},{2,4},{3,1},{4,6},{5,3},{6,0},{7,5},{8,10},{9,15},{10,... | collective-permute-start | bytes 921608 | tf_op jit(solution)/shard_map/ppermute | solution.py:54
  46.2 7.9 %collective-permute-start.9 = (f32[160,128]{1,0:T(8,128)S(1)}, f32[160,128]{1,0:T(8,128)S(1)}, u32[]{:S(2)}, u32[]{:S(2)}) collective-permute-start(f32[160,128]{1,0:T(8,128)S(1)} %get-tuple-element.22), channel_id=1, source_target_pairs={{0,8},{1,25},{2,10},{3,27},{4,12},{5,29},{6,14},{7,31},{8,16},{9,1... | collective-permute-start | bytes 245768 | tf_op jit(solution)/shard_map/ppermute | solution.py:54
  49.5 6.3 %collective-permute-start.8 = (f32[160,128]{1,0:T(8,128)S(1)}, f32[160,128]{1,0:T(8,128)S(1)}, u32[]{:S(2)}, u32[]{:S(2)}) collective-permute-start(f32[160,128]{1,0:T(8,128)S(1)} %get-tuple-element.20), channel_id=1, source_target_pairs={{0,9},{1,24},{2,11},{3,26},{4,13},{5,28},{6,15},{7,30},{8,17},{9,0... | collective-permute-start | bytes 245768 | tf_op jit(solution)/shard_map/ppermute | solution.py:54
  54.1 7.5 %collective-permute-start.10 = (f32[160,128]{1,0:T(8,128)S(1)}, f32[160,128]{1,0:T(8,128)S(1)}, u32[]{:S(2)}, u32[]{:S(2)}) collective-permute-start(f32[160,128]{1,0:T(8,128)S(1)} %add.18), channel_id=1, source_target_pairs={{0,8},{1,25},{2,10},{3,27},{4,12},{5,29},{6,14},{7,31},{8,16},{9,1... | collective-permute-start | bytes 245768 | tf_op jit(solution)/shard_map/ppermute | solution.py:54

commit v6 on v5

--- a/solution.py
+++ b/solution.py
@@ -15,11 +15,11 @@
 FEAT = 4 * LEV + 2 * LEV * LEV
 ROWS_OUT, COLS_OUT = FEAT // N_HOR, FEAT // N_LEV
 CHUNK, BOTH, HALF = 72, 2 * ROWS_OUT, 16
-WINDOWS = (CHUNK, BOTH, CHUNK)
+WINDOWS = (CHUNK, CHUNK, BOTH)
 BUILT = sum(WINDOWS) + 8 * len(WINDOWS)
-MAIN = 2 * sum(WINDOWS)
-SENT = MAIN + 40
 LAST = 2 * CHUNK + 16
+REST = 2 * (CHUNK + BOTH)
+SENT = LAST + REST + 32
 SHARE = 1 << 18
 VMEM = pl.BlockSpec(memory_space=pltpu.VMEM)
 
@@ -125,7 +125,7 @@
     def start(to_z, offset):
         return (lax.rem(to_z, N_ZHI) * N_Y + to_y) * BOTH + offset - skip
 
-    return (start(zhi, 64 * to_core), start(zhi + 5 - 2 * to_core, 0), start(zhi + 2, 64 * to_core)), skip
+    return (start(zhi + 2, 64 * to_core), start(zhi, 64 * to_core), start(zhi + 5 - 2 * to_core, 0)), skip
 
 
 def product(place, smooth_ref, right_ref, left_ref):
@@ -141,15 +141,17 @@
 
 def emit(place, prod_ref, out_ref):
     skip = windows_of(place)[1]
-    at, base, group = 0, 0, 0
-    for size in WINDOWS:
+    at, base, group, tail = 0, 0, 0, 2 * CHUNK
+    for number, size in enumerate(WINDOWS):
+        if number == 1:
+            base, group, tail = LAST, 0, LAST + REST
         for half in range(2):
             rows = pl.ds(pl.multiple_of(at + skip, 8), size)
             out_ref[base : base + size, :] = prod_ref[rows, half * LANES : (half + 1) * LANES]
             base += size
         for i in range(size // 8):
             rows = pl.ds(pl.multiple_of(at + 8 * i + skip, 8), 8)
-            to = MAIN + 8 * (group // 8)
+            to = tail + 8 * (group // 8)
             strip = 16 * (group % 8)
             out_ref[to : to + 8, strip : strip + 16] = prod_ref[rows, 2 * LANES : COLS_OUT]
             group += 1
@@ -175,7 +177,12 @@
     out_ref[...] = a_ref[...] + b_ref[...]
 
 
-def split_kernel(a_ref, b_ref, own_ref, near_ref, cross_ref, far_ref):
+def cut_kernel(a_ref, b_ref, far_ref, rest_ref):
+    far_ref[...] = a_ref[0:LAST, :] + b_ref[0:LAST, :]
+    rest_ref[...] = a_ref[LAST:SENT, :] + b_ref[LAST:SENT, :]
+
+
+def split_kernel(a_ref, b_ref, own_ref, near_ref, cross_ref):
     core = lax.axis_index("hor") % 2
     lane = lax.broadcasted_iota(jnp.int32, (8, LANES), 1)
 
@@ -185,15 +192,14 @@
 
     ahead = 2 * CHUNK
     places = (
-        (own_ref, 0, CHUNK, 0, 0),
         (near_ref, ahead + 64 * core, BOTH, 1 + core, 1),
         (cross_ref, ahead + 64 * (1 - core), BOTH, 2 - core, 1),
-        (far_ref, ahead + 2 * BOTH, CHUNK, 3, 2),
+        (own_ref, 0, CHUNK, 0, 0),
     )
     for ref, start, stride, tile, strip in places:
         ref[0:CHUNK, :] = total(start, CHUNK)
         ref[CHUNK : 2 * CHUNK, :] = total(start + stride, CHUNK)
-        one, two = total(MAIN + 8 * tile, 8), total(MAIN + 8 * tile + 8, 8)
+        one, two = total(REST + 8 * tile, 8), total(REST + 8 * tile + 8, 8)
         if strip:
             one, two = pltpu.roll(one, LANES - 16 * strip, 1), pltpu.roll(two, LANES - 16 * strip, 1)
             one = jnp.where(lane < LANES - 16 * strip, one, two)
@@ -256,15 +262,28 @@
     )(*operands)
 
 
-def add(a, b):
+def add(a, b, share=1):
     return pl.pallas_call(
         add_kernel,
         out_shape=jax.ShapeDtypeStruct(a.shape, a.dtype),
         in_specs=[VMEM] * 2,
         out_specs=VMEM,
         compiler_params=params(4),
-        cost_estimate=cost(1, SHARE),
+        cost_estimate=cost(share, SHARE),
         name="add",
+    )(a, b)
+
+
+def cut(a, b):
+    shapes = ((LAST, LANES), (SENT - LAST, LANES))
+    return pl.pallas_call(
+        cut_kernel,
+        out_shape=[jax.ShapeDtypeStruct(shape, a.dtype) for shape in shapes],
+        in_specs=[VMEM] * 2,
+        out_specs=[VMEM] * 2,
+        compiler_params=params(4),
+        cost_estimate=cost(1, SHARE),
+        name="cut",
     )(a, b)
 
 
@@ -323,17 +342,19 @@
     parts["own"] = gram(gram_kernel, "own", sent, *both)
     two_back = hop(parts["far"], "y", 0)
     from_cross = hop(parts["cross"], "y", 1)
-    from_near = hop(add(parts["near"], two_back), "y", 0)
-    kept, near, cross, far = pl.pallas_call(
+    near_far, near_rest = cut(parts["near"], two_back)
+    from_near_far, from_near_rest = hop(near_far, "y", 0), hop(near_rest, "y", 0)
+    sum_far, sum_rest = cut(parts["own"], from_cross)
+    two_back = hop(add(sum_far, from_near_far, 1 << 30), "z_hi", 0)
+    kept, near, cross = pl.pallas_call(
         split_kernel,
-        out_shape=[jax.ShapeDtypeStruct((LAST, LANES), f32)] * 4,
+        out_shape=[jax.ShapeDtypeStruct((LAST, LANES), f32)] * 3,
         in_specs=[VMEM] * 2,
-        out_specs=[VMEM] * 4,
+        out_specs=[VMEM] * 3,
         compiler_params=params(8),
         cost_estimate=cost(1, SHARE),
         name="split",
-    )(add(parts["own"], from_cross), from_near)
-    two_back = hop(far, "z_hi", 0)
+    )(sum_rest, from_near_rest)
     from_cross = hop(cross, "z_hi", 1)
     from_near = hop(add(near, two_back), "z_hi", 0)
     return pl.pallas_call(

time: 62.5 us -> 60 us (0.960)
  waiting for transfers between devices: 34.3 us -> 29.4 us
  starting transfers between devices: 17.7 us -> 20.2 us
    ppermute x6 -> x7, waiting for transfers between devices: 20.8 us -> 15.9 us  [hop(): return lax.ppermute(value, 'hor', pairs)]
    ppermute x6 -> x7, starting transfers between devices: 7.11 us -> 9.6 us  [hop(): return lax.ppermute(value, 'hor', pairs)]
  transfers between devices with their start and end apart: 12 -> 13, of which waited for: 10 -> 10; matrix products, arithmetic and copies ran while one was open for 0% -> 1% of each run, Pallas kernels for 8% -> 8%
where the time goes in v6:
time: 60 us; the launch traced here: 59.8 us
  waiting for transfers between devices  29.4 us (49%)
  starting transfers between devices  20.2 us (34%)
  Pallas kernels  7.89 us (13%)
  local copies, waits for them, and re-layouts  1.96 us (3%)
    ppermute x7, waiting for transfers between devices, hop(): return lax.ppermute(value, 'hor', pairs)  15.9 us
    ppermute x4, waiting for transfers between devices, shift_lev(): return lax.ppermute(value, 'lev', pairs)  9.91 us
    ppermute x7, starting transfers between devices, hop(): return lax.ppermute(value, 'hor', pairs)  9.6 us
    all_to_all x1, starting transfers between devices, on_device(): lists = lax.all_to_all(repeated, 'lev', 0, 0, tiled=True)  6.26 us
    pallas_call x5, Pallas kernels, gram(): pl.pallas_call(functools.partial(kernel, place), out_shape=jax.ShapeDtype...  5.12 us
    ppermute x4, starting transfers between devices, shift_lev(): return lax.ppermute(value, 'lev', pairs)  4.23 us
    all_to_all x1, waiting for transfers between devices, on_device(): lists = lax.all_to_all(repeated, 'lev', 0, 0, tiled=True)  2.57 us
    unnamed x8, local copies, waits for them, and re-layouts  1.89 us
  transfers between devices with their start and end apart: 13, of which 10 were waited for; matrix products, arithmetic and copies ran while one was open for 1% of the time, Pallas kernels for 8%

profile of v6, /device:TPU:6, one launch (start us, length us, event | category | flops | bytes accessed | tf_op | source)
XLA Modules:
  0.0 59.8 jit_solution(8346778075131340425)
XLA Ops:
  0.0 0.7 %copy-done.1 = s32[1,128]{1,0:T(1,128)S(1)} copy-done((s32[1,128]{1,0:T(1,128)S(1)}, s32[1,128]{1,0:T(1,128)}, u32[]{:S(2)}) %copy-start.1) | copy-done | bytes 536
  0.7 0.6 repeat.1
  1.3 6.3 %all-to-all-start = ((s32[8,1,128]{2,1,0:T(1,128)}), s32[8,1,128]{2,1,0:T(1,128)S(1)}, u32[]{:S(2)}, u32[]{:S(2)}) async-start(s32[8,1,128]{2,1,0:T(1,128)} %repeat.1), calls=%async_computation | async-start | bytes 8192 | tf_op jit(solution)/shard_map/all_to_all | solution.py:301
  7.6 1.2 %copy-done = f32[4,4,16384]{2,1,0:T(4,128)S(1)} copy-done((f32[4,4,16384]{2,1,0:T(4,128)S(1)}, f32[4,4,16384]{2,1,0:T(4,128)}, u32[]{:S(2)}) %copy-start) | copy-done | bytes 1048600
  9.0 2.6 %all-to-all-done.index_ref = s32[8,1,128]{2,1,0:T(1,128)S(1)} async-done(((s32[8,1,128]{2,1,0:T(1,128)}), s32[8,1,128]{2,1,0:T(1,128)S(1)}, u32[]{:S(2)}, u32[]{:S(2)}) %all-to-all-start) | async-done | bytes 4128 | tf_op jit(solution)/shard_map/all_to_all | solution.py:301
  11.5 0.4 pick.1
  11.9 0.7 %collective-permute-start = (f32[16,1024]{1,0:T(8,128)S(1)}, f32[16,1024]{1,0:T(8,128)S(1)}, u32[]{:S(2)}, u32[]{:S(2)}) collective-permute-start(f32[16,1024]{1,0:T(8,128)S(1)} %pick.1), channel_id=1, source_target_pairs={{0,128},{32,160},{64,192},{96,224},{128,0},{160,32},{192,64},{224,... | collective-permute-start | bytes 196616 | tf_op jit(solution)/shard_map/ppermute | solution.py:37
  12.6 3.6 %collective-permute-done = f32[16,1024]{1,0:T(8,128)S(1)} collective-permute-done((f32[16,1024]{1,0:T(8,128)S(1)}, f32[16,1024]{1,0:T(8,128)S(1)}, u32[]{:S(2)}, u32[]{:S(2)}) %collective-permute-start) | collective-permute-done | bytes 65568 | tf_op jit(solution)/shard_map/ppermute | solution.py:37
  16.3 2.1 %collective-permute-start.1 = (f32[2,16,1024]{2,1,0:T(8,128)S(1)}, f32[2,16,1024]{2,1,0:T(8,128)S(1)}, u32[]{:S(2)}, u32[]{:S(2)}) collective-permute-start(f32[2,16,1024]{2,1,0:T(8,128)S(1)} %pad_maximum_fusion.w0_ref), channel_id=1, source_target_pairs={{0,32},{32,64},{64,96},{96,0},{128,160},{160,192},{192,224},{224,1... | collective-permute-start | bytes 393224 | tf_op jit(solution)/shard_map/ppermute | solution.py:37
  18.4 0.6 collective-permute-start.2
  19.0 0.9 %collective-permute-start.3 = (f32[2,16,1024]{2,1,0:T(8,128)S(1)}, f32[2,16,1024]{2,1,0:T(8,128)S(1)}, u32[]{:S(2)}, u32[]{:S(2)}) collective-permute-start(f32[2,16,1024]{2,1,0:T(8,128)S(1)} %pad_maximum_fusion.w0_ref), channel_id=1, source_target_pairs={{0,96},{32,0},{64,32},{96,64},{128,224},{160,128},{192,160},{224,1... | collective-permute-start | bytes 393224 | tf_op jit(solution)/shard_map/ppermute | solution.py:37
  20.0 2.3 %collective-permute-done.1.w1_ref = f32[2,16,1024]{2,1,0:T(8,128)S(1)} collective-permute-done((f32[2,16,1024]{2,1,0:T(8,128)S(1)}, f32[2,16,1024]{2,1,0:T(8,128)S(1)}, u32[]{:S(2)}, u32[]{:S(2)}) %collective-permute-start.1) | collective-permute-done | bytes 131104 | tf_op jit(solution)/shard_map/ppermute | solution.py:37
  22.4 2.7 %collective-permute-done.2.w2_ref = f32[2,16,1024]{2,1,0:T(8,128)S(1)} collective-permute-done((f32[2,16,1024]{2,1,0:T(8,128)S(1)}, f32[2,16,1024]{2,1,0:T(8,128)S(1)}, u32[]{:S(2)}, u32[]{:S(2)}) %collective-permute-start.2) | collective-permute-done | bytes 131104 | tf_op jit(solution)/shard_map/ppermute | solution.py:37
  25.0 1.3 %collective-permute-done.3.w3_ref = f32[2,16,1024]{2,1,0:T(8,128)S(1)} collective-permute-done((f32[2,16,1024]{2,1,0:T(8,128)S(1)}, f32[2,16,1024]{2,1,0:T(8,128)S(1)}, u32[]{:S(2)}, u32[]{:S(2)}) %collective-permute-start.3) | collective-permute-done | bytes 131104 | tf_op jit(solution)/shard_map/ppermute | solution.py:37
  26.4 0.3 smooth.1.smooth_ref.own_ref
  27.0 0.7 %gram_far.2.part_ref = f32[304,272]{1,0:T(8,128)S(1)} custom-call(f32[128,1024]{1,0:T(8,128)S(1)} %smooth.1.smooth_ref.own_ref, bf16[272,1024]{1,0:T(8,128)(2,1)S(1)} %right.2.own_right_ref.right_ref), custom_call_target="tpu_custom_call" | custom-call | flops 1 | bytes 262144 | tf_op jit(solution)/shard_map/gram_far/pallas_call | solution.py:253
  27.7 1.0 %collective-permute-done.4.smooth_ref.other_ref = f32[128,1024]{1,0:T(8,128)S(1)} collective-permute-done((f32[128,1024]{1,0:T(8,128)S(1)}, f32[128,1024]{1,0:T(8,128)S(1)}, u32[]{:S(2)}, u32[]{:S(2)}) %collective-permute-start.4) | collective-permute-done | bytes 524320 | tf_op jit(solution)/shard_map/ppermute | solution.py:41
  28.9 0.8 %gram_far.3 = f32[608,128]{1,0:T(8,128)S(1)} custom-call(f32[304,272]{1,0:T(8,128)S(1)} %gram_far.2.part_ref, f32[128,1024]{1,0:T(8,128)S(1)} %collective-permute-done.4.smooth_ref.other_ref, bf16[272,1024]{1,0:T(8,128)(2,1)S(1)} %right.3.other_right_ref.right_ref), custom_call_target="tpu_custom_call" | custom-call | flops 1 | bytes 262144 | tf_op jit(solution)/shard_map/gram_far/pallas_call | solution.py:253
  29.8 1.6 %collective-permute-start.6 = (f32[608,128]{1,0:T(8,128)S(1)}, f32[608,128]{1,0:T(8,128)S(1)}, u32[]{:S(2)}, u32[]{:S(2)}) collective-permute-start(f32[608,128]{1,0:T(8,128)S(1)} %gram_far.3), channel_id=1, source_target_pairs={{0,2},{1,7},{2,4},{3,1},{4,6},{5,3},{6,0},{7,5},{8,10},{9,15},{10,... | collective-permute-start | bytes 933896 | tf_op jit(solution)/shard_map/ppermute | solution.py:54
  31.4 1.2 %gram_cross.1 = f32[608,128]{1,0:T(8,128)S(1)} custom-call(f32[128,1024]{1,0:T(8,128)S(1)} %smooth.1.smooth_ref.own_ref, bf16[272,1024]{1,0:T(8,128)(2,1)S(1)} %right.2.own_right_ref.right_ref, f32[128,1024]{1,0:T(8,128)S(1)} %collective-permute-done.4.smooth_ref.other_ref, bf16[272,1024]{1,0:T(8,128)(2,1)S(1)} %right.3.other_right_ref.right_ref), custom_call_target="tpu_custom_call" | custom-call | flops 1 | bytes 262144 | tf_op jit(solution)/shard_map/gram_cross/pallas_call | solution.py:253
  32.7 1.2 %gram_near.1.a_ref = f32[608,128]{1,0:T(8,128)S(1)} custom-call(f32[128,1024]{1,0:T(8,128)S(1)} %smooth.1.smooth_ref.own_ref, bf16[272,1024]{1,0:T(8,128)(2,1)S(1)} %right.2.own_right_ref.right_ref, f32[128,1024]{1,0:T(8,128)S(1)} %collective-permute-done.4.smooth_ref.other_ref, bf16[272,1024]{1,0:T(8,128)(2,1)S(1)} %right.3.other_right_ref.right_ref), custom_call_target="tpu_custom_call" | custom-call | flops 1 | bytes 262144 | tf_op jit(solution)/shard_map/gram_near/pallas_call | solution.py:253
  33.9 4.0 %collective-permute-done.6.b_ref = f32[608,128]{1,0:T(8,128)S(1)} collective-permute-done((f32[608,128]{1,0:T(8,128)S(1)}, f32[608,128]{1,0:T(8,128)S(1)}, u32[]{:S(2)}, u32[]{:S(2)}) %collective-permute-start.6) | collective-permute-done | bytes 311328 | tf_op jit(solution)/shard_map/ppermute | solution.py:54
  38.0 0.4 collective-permute-start.9
  38.4 1.6 %collective-permute-start.7 = (f32[448,128]{1,0:T(8,128)S(1)}, f32[448,128]{1,0:T(8,128)S(1)}, u32[]{:S(2)}, u32[]{:S(2)}) collective-permute-start(f32[448,128]{1,0:T(8,128)S(1)} %get-tuple-element.23), channel_id=1, source_target_pairs={{0,2},{1,7},{2,4},{3,1},{4,6},{5,3},{6,0},{7,5},{8,10},{9,15},{10,... | collective-permute-start | bytes 688136 | tf_op jit(solution)/shard_map/ppermute | solution.py:54
  40.0 1.2 %gram_own.1.a_ref = f32[608,128]{1,0:T(8,128)S(1)} custom-call(f32[128,1024]{1,0:T(8,128)S(1)} %smooth.1.smooth_ref.own_ref, bf16[272,1024]{1,0:T(8,128)(2,1)S(1)} %right.2.own_right_ref.right_ref, f32[128,1024]{1,0:T(8,128)S(1)} %collective-permute-done.4.smooth_ref.other_ref, bf16[272,1024]{1,0:T(8,128)(2,1)S(1)} %right.3.other_right_ref.right_ref), custom_call_target="tpu_custom_call" | custom-call | flops 1 | bytes 262144 | tf_op jit(solution)/shard_map/gram_own/pallas_call | solution.py:253
  41.2 2.5 %collective-permute-done.9.b_ref = f32[160,128]{1,0:T(8,128)S(1)} collective-permute-done((f32[160,128]{1,0:T(8,128)S(1)}, f32[160,128]{1,0:T(8,128)S(1)}, u32[]{:S(2)}, u32[]{:S(2)}) %collective-permute-start.9) | collective-permute-done | bytes 81952 | tf_op jit(solution)/shard_map/ppermute | solution.py:54
  43.7 3.4 %collective-permute-start.10 = (f32[160,128]{1,0:T(8,128)S(1)}, f32[160,128]{1,0:T(8,128)S(1)}, u32[]{:S(2)}, u32[]{:S(2)}) collective-permute-start(f32[160,128]{1,0:T(8,128)S(1)} %add.15), channel_id=1, source_target_pairs={{0,8},{1,25},{2,10},{3,27},{4,12},{5,29},{6,14},{7,31},{8,16},{9,1... | collective-permute-start | bytes 245768 | tf_op jit(solution)/shard_map/ppermute | solution.py:54
  47.1 0.8 %collective-permute-start.8 = (f32[160,128]{1,0:T(8,128)S(1)}, f32[160,128]{1,0:T(8,128)S(1)}, u32[]{:S(2)}, u32[]{:S(2)}) collective-permute-start(f32[160,128]{1,0:T(8,128)S(1)} %get-tuple-element.25), channel_id=1, source_target_pairs={{0,9},{1,24},{2,11},{3,26},{4,13},{5,28},{6,15},{7,30},{8,17},{9,0... | collective-permute-start | bytes 245768 | tf_op jit(solution)/shard_map/ppermute | solution.py:54
  47.9 3.7 %collective-permute-done.10.b_ref = f32[160,128]{1,0:T(8,128)S(1)} collective-permute-done((f32[160,128]{1,0:T(8,128)S(1)}, f32[160,128]{1,0:T(8,128)S(1)}, u32[]{:S(2)}, u32[]{:S(2)}) %collective-permute-start.10) | collective-permute-done | bytes 81952 | tf_op jit(solution)/shard_map/ppermute | solution.py:54
  51.6 1.8 %collective-permute-start.11 = (f32[160,128]{1,0:T(8,128)S(1)}, f32[160,128]{1,0:T(8,128)S(1)}, u32[]{:S(2)}, u32[]{:S(2)}) collective-permute-start(f32[160,128]{1,0:T(8,128)S(1)} %add.16), channel_id=1, source_target_pairs={{0,8},{1,25},{2,10},{3,27},{4,12},{5,29},{6,14},{7,31},{8,16},{9,1... | collective-permute-start | bytes 245768 | tf_op jit(solution)/shard_map/ppermute | solution.py:54
  53.4 5.7 %collective-permute-done.11.t2_ref = f32[160,128]{1,0:T(8,128)S(1)} collective-permute-done((f32[160,128]{1,0:T(8,128)S(1)}, f32[160,128]{1,0:T(8,128)S(1)}, u32[]{:S(2)}, u32[]{:S(2)}) %collective-permute-start.11) | collective-permute-done | bytes 81952 | tf_op jit(solution)/shard_map/ppermute | solution.py:54
  59.1 0.7 %final.1 = f32[68,272]{1,0:T(8,128)} custom-call(f32[160,128]{1,0:T(8,128)S(1)} %get-tuple-element.24.t0_ref, f32[160,128]{1,0:T(8,128)S(1)} %collective-permute-done.8.t1_ref, f32[160,128]{1,0:T(8,128)S(1)} %collective-permute-done.11.t2_ref), custom_call_target="tpu_custom_call" | custom-call | flops 1 | bytes 262144 | tf_op jit(solution)/shard_map/final/pallas_call | solution.py:360
  (26 shorter events, 1.4 us)
Async XLA Ops:
  0.0 0.7 %copy-start.1 = (s32[1,128]{1,0:T(1,128)S(1)}, s32[1,128]{1,0:T(1,128)}, u32[]{:S(2)}) copy-start(s32[1,128]{1,0:T(1,128)} %index_ref.1) | copy-start | bytes 1540
  1.3 6.3 %copy-start.2 = (f32[32]{0:T(128)S(1)}, f32[32]{0:T(128)}, u32[]{:S(2)}) copy-start(f32[32]{0:T(128)} %param.6) | copy-start | bytes 388
  1.3 6.3 %copy-start.3 = (s32[31]{0:T(128)S(1)}, s32[31]{0:T(128)}, u32[]{:S(2)}) copy-start(s32[31]{0:T(128)} %param.7) | copy-start | bytes 376
  1.3 10.3 %all-to-all-start = ((s32[8,1,128]{2,1,0:T(1,128)}), s32[8,1,128]{2,1,0:T(1,128)S(1)}, u32[]{:S(2)}, u32[]{:S(2)}) async-start(s32[8,1,128]{2,1,0:T(1,128)} %repeat.1), calls=%async_computation | async-start | bytes 8192 | tf_op jit(solution)/shard_map/all_to_all | solution.py:301
  7.6 1.2 %copy-start = (f32[4,4,16384]{2,1,0:T(4,128)S(1)}, f32[4,4,16384]{2,1,0:T(4,128)}, u32[]{:S(2)}) copy-start(f32[4,4,16384]{2,1,0:T(4,128)} %slab_ref.1) | copy-start | bytes 3145732
  11.9 4.4 %collective-permute-start = (f32[16,1024]{1,0:T(8,128)S(1)}, f32[16,1024]{1,0:T(8,128)S(1)}, u32[]{:S(2)}, u32[]{:S(2)}) collective-permute-start(f32[16,1024]{1,0:T(8,128)S(1)} %pick.1), channel_id=1, source_target_pairs={{0,128},{32,160},{64,192},{96,224},{128,0},{160,32},{192,64},{224,... | collective-permute-start | bytes 196616 | tf_op jit(solution)/shard_map/ppermute | solution.py:37
  16.3 6.1 %collective-permute-start.1 = (f32[2,16,1024]{2,1,0:T(8,128)S(1)}, f32[2,16,1024]{2,1,0:T(8,128)S(1)}, u32[]{:S(2)}, u32[]{:S(2)}) collective-permute-start(f32[2,16,1024]{2,1,0:T(8,128)S(1)} %pad_maximum_fusion.w0_ref), channel_id=1, source_target_pairs={{0,32},{32,64},{64,96},{96,0},{128,160},{160,192},{192,224},{224,1... | collective-permute-start | bytes 393224 | tf_op jit(solution)/shard_map/ppermute | solution.py:37
  18.4 6.6 %collective-permute-start.2 = (f32[2,16,1024]{2,1,0:T(8,128)S(1)}, f32[2,16,1024]{2,1,0:T(8,128)S(1)}, u32[]{:S(2)}, u32[]{:S(2)}) collective-permute-start(f32[2,16,1024]{2,1,0:T(8,128)S(1)} %pad_maximum_fusion.w0_ref), channel_id=1, source_target_pairs={{0,64},{32,96},{64,0},{96,32},{128,192},{160,224},{192,128},{224,1... | collective-permute-start | bytes 393224 | tf_op jit(solution)/shard_map/ppermute | solution.py:37
  19.0 7.3 %collective-permute-start.3 = (f32[2,16,1024]{2,1,0:T(8,128)S(1)}, f32[2,16,1024]{2,1,0:T(8,128)S(1)}, u32[]{:S(2)}, u32[]{:S(2)}) collective-permute-start(f32[2,16,1024]{2,1,0:T(8,128)S(1)} %pad_maximum_fusion.w0_ref), channel_id=1, source_target_pairs={{0,96},{32,0},{64,32},{96,64},{128,224},{160,128},{192,160},{224,1... | collective-permute-start | bytes 393224 | tf_op jit(solution)/shard_map/ppermute | solution.py:37
  26.7 2.0 %collective-permute-start.4 = (f32[128,1024]{1,0:T(8,128)S(1)}, f32[128,1024]{1,0:T(8,128)S(1)}, u32[]{:S(2)}, u32[]{:S(2)}) collective-permute-start(f32[128,1024]{1,0:T(8,128)S(1)} %smooth.1.smooth_ref.own_ref), channel_id=1, source_target_pairs={{0,1},{1,0},{2,3},{3,2},{4,5},{5,4},{6,7},{7,6},{8,9},{9,8},{10,11... | collective-permute-start | bytes 1572872 | tf_op jit(solution)/shard_map/ppermute | solution.py:41
  29.8 8.1 %collective-permute-start.6 = (f32[608,128]{1,0:T(8,128)S(1)}, f32[608,128]{1,0:T(8,128)S(1)}, u32[]{:S(2)}, u32[]{:S(2)}) collective-permute-start(f32[608,128]{1,0:T(8,128)S(1)} %gram_far.3), channel_id=1, source_target_pairs={{0,2},{1,7},{2,4},{3,1},{4,6},{5,3},{6,0},{7,5},{8,10},{9,15},{10,... | collective-permute-start | bytes 933896 | tf_op jit(solution)/shard_map/ppermute | solution.py:54
  32.6 8.6 %collective-permute-start.5 = (f32[608,128]{1,0:T(8,128)S(1)}, f32[608,128]{1,0:T(8,128)S(1)}, u32[]{:S(2)}, u32[]{:S(2)}) collective-permute-start(f32[608,128]{1,0:T(8,128)S(1)} %gram_cross.1), channel_id=1, source_target_pairs={{0,3},{1,6},{2,5},{3,0},{4,7},{5,2},{6,1},{7,4},{8,11},{9,14},{10,... | collective-permute-start | bytes 933896 | tf_op jit(solution)/shard_map/ppermute | solution.py:54
  38.0 5.7 %collective-permute-start.9 = (f32[160,128]{1,0:T(8,128)S(1)}, f32[160,128]{1,0:T(8,128)S(1)}, u32[]{:S(2)}, u32[]{:S(2)}) collective-permute-start(f32[160,128]{1,0:T(8,128)S(1)} %get-tuple-element.28), channel_id=1, source_target_pairs={{0,2},{1,7},{2,4},{3,1},{4,6},{5,3},{6,0},{7,5},{8,10},{9,15},{10,... | collective-permute-start | bytes 245768 | tf_op jit(solution)/shard_map/ppermute | solution.py:54
  38.4 8.7 %collective-permute-start.7 = (f32[448,128]{1,0:T(8,128)S(1)}, f32[448,128]{1,0:T(8,128)S(1)}, u32[]{:S(2)}, u32[]{:S(2)}) collective-permute-start(f32[448,128]{1,0:T(8,128)S(1)} %get-tuple-element.23), channel_id=1, source_target_pairs={{0,2},{1,7},{2,4},{3,1},{4,6},{5,3},{6,0},{7,5},{8,10},{9,15},{10,... | collective-permute-start | bytes 688136 | tf_op jit(solution)/shard_map/ppermute | solution.py:54
  43.7 7.9 %collective-permute-start.10 = (f32[160,128]{1,0:T(8,128)S(1)}, f32[160,128]{1,0:T(8,128)S(1)}, u32[]{:S(2)}, u32[]{:S(2)}) collective-permute-start(f32[160,128]{1,0:T(8,128)S(1)} %add.15), channel_id=1, source_target_pairs={{0,8},{1,25},{2,10},{3,27},{4,12},{5,29},{6,14},{7,31},{8,16},{9,1... | collective-permute-start | bytes 245768 | tf_op jit(solution)/shard_map/ppermute | solution.py:54
  47.1 6.2 %collective-permute-start.8 = (f32[160,128]{1,0:T(8,128)S(1)}, f32[160,128]{1,0:T(8,128)S(1)}, u32[]{:S(2)}, u32[]{:S(2)}) collective-permute-start(f32[160,128]{1,0:T(8,128)S(1)} %get-tuple-element.25), channel_id=1, source_target_pairs={{0,9},{1,24},{2,11},{3,26},{4,13},{5,28},{6,15},{7,30},{8,17},{9,0... | collective-permute-start | bytes 245768 | tf_op jit(solution)/shard_map/ppermute | solution.py:54
  51.6 7.5 %collective-permute-start.11 = (f32[160,128]{1,0:T(8,128)S(1)}, f32[160,128]{1,0:T(8,128)S(1)}, u32[]{:S(2)}, u32[]{:S(2)}) collective-permute-start(f32[160,128]{1,0:T(8,128)S(1)} %add.16), channel_id=1, source_target_pairs={{0,8},{1,25},{2,10},{3,27},{4,12},{5,29},{6,14},{7,31},{8,16},{9,1... | collective-permute-start | bytes 245768 | tf_op jit(solution)/shard_map/ppermute | solution.py:54

commit v7 on v6

--- a/solution.py
+++ b/solution.py
@@ -15,11 +15,11 @@
 FEAT = 4 * LEV + 2 * LEV * LEV
 ROWS_OUT, COLS_OUT = FEAT // N_HOR, FEAT // N_LEV
 CHUNK, BOTH, HALF = 72, 2 * ROWS_OUT, 16
-WINDOWS = (CHUNK, CHUNK, BOTH)
-BUILT = sum(WINDOWS) + 8 * len(WINDOWS)
+PLACES = ("far", "cross", "near", "own")
+BUILT_A, BUILT_B = 4 * (CHUNK + 8), CHUNK + BOTH + 16
 LAST = 2 * CHUNK + 16
 REST = 2 * (CHUNK + BOTH)
-SENT = LAST + REST + 32
+SENT = REST + 32
 SHARE = 1 << 18
 VMEM = pl.BlockSpec(memory_space=pltpu.VMEM)
 
@@ -128,9 +128,17 @@
     return (start(zhi + 2, 64 * to_core), start(zhi, 64 * to_core), start(zhi + 5 - 2 * to_core, 0)), skip
 
 
-def product(place, smooth_ref, right_ref, left_ref):
+def pieces_a():
+    return [(windows_of(place)[0][0], CHUNK) for place in PLACES]
+
+
+def pieces_b(place):
+    return list(zip(windows_of(place)[0][1:], (CHUNK, BOTH)))
+
+
+def product(pieces, smooth_ref, right_ref, left_ref):
     at = 0
-    for first, size in zip(windows_of(place)[0], WINDOWS):
+    for first, size in pieces:
         for i in range((size + 8) // HALF):
             build_rows(smooth_ref, first // HALF + i, left_ref, at)
             at += HALF
@@ -139,12 +147,9 @@
     )
 
 
-def emit(place, prod_ref, out_ref):
-    skip = windows_of(place)[1]
-    at, base, group, tail = 0, 0, 0, 2 * CHUNK
-    for number, size in enumerate(WINDOWS):
-        if number == 1:
-            base, group, tail = LAST, 0, LAST + REST
+def emit(sizes, at, skip, prod_ref, out_ref):
+    base, group, tail = 0, 0, 2 * sum(sizes)
+    for size in sizes:
         for half in range(2):
             rows = pl.ds(pl.multiple_of(at + skip, 8), size)
             out_ref[base : base + size, :] = prod_ref[rows, half * LANES : (half + 1) * LANES]
@@ -158,28 +163,38 @@
         at += size + 8
 
 
+def emit_a(prod_ref, out_refs):
+    for number, (place, ref) in enumerate(zip(PLACES, out_refs)):
+        emit((CHUNK,), number * (CHUNK + 8), windows_of(place)[1], prod_ref, ref)
+
+
+def emit_b(place, prod_ref, out_ref):
+    emit((CHUNK, BOTH), 0, windows_of(place)[1], prod_ref, out_ref)
+
+
 def begin_kernel(place, smooth_ref, right_ref, out_ref, left_ref):
-    out_ref[...] = product(place, smooth_ref, right_ref, left_ref)
-
-
-def finish_kernel(place, part_ref, smooth_ref, right_ref, out_ref, left_ref, prod_ref):
-    prod_ref[...] = part_ref[...] + product(place, smooth_ref, right_ref, left_ref)
-    emit(place, prod_ref, out_ref)
+    out_ref[...] = product(pieces_b(place) if place else pieces_a(), smooth_ref, right_ref, left_ref)
+
+
+def finish_a_kernel(place, part_ref, smooth_ref, right_ref, *refs):
+    left_ref, prod_ref = refs[4:]
+    prod_ref[...] = part_ref[...] + product(pieces_a(), smooth_ref, right_ref, left_ref)
+    emit_a(prod_ref, refs[:4])
+
+
+def finish_b_kernel(place, part_ref, smooth_ref, right_ref, out_ref, left_ref, prod_ref):
+    prod_ref[...] = part_ref[...] + product(pieces_b(place), smooth_ref, right_ref, left_ref)
+    emit_b(place, prod_ref, out_ref)
 
 
 def gram_kernel(place, own_ref, own_right_ref, other_ref, other_right_ref, out_ref, left_ref, prod_ref):
-    prod_ref[...] = product(place, own_ref, own_right_ref, left_ref)
-    prod_ref[...] += product(place, other_ref, other_right_ref, left_ref)
-    emit(place, prod_ref, out_ref)
+    prod_ref[...] = product(pieces_b(place), own_ref, own_right_ref, left_ref)
+    prod_ref[...] += product(pieces_b(place), other_ref, other_right_ref, left_ref)
+    emit_b(place, prod_ref, out_ref)
 
 
 def add_kernel(a_ref, b_ref, out_ref):
     out_ref[...] = a_ref[...] + b_ref[...]
-
-
-def cut_kernel(a_ref, b_ref, far_ref, rest_ref):
-    far_ref[...] = a_ref[0:LAST, :] + b_ref[0:LAST, :]
-    rest_ref[...] = a_ref[LAST:SENT, :] + b_ref[LAST:SENT, :]
 
 
 def split_kernel(a_ref, b_ref, own_ref, near_ref, cross_ref):
@@ -249,16 +264,17 @@
 
 
 def gram(kernel, place, out_shape, *operands):
-    scratch = [pltpu.VMEM((BUILT, BLOCK), jnp.bfloat16), pltpu.VMEM((BUILT, COLS_OUT), jnp.float32)]
+    built = BUILT_B if place else BUILT_A
+    scratch = [pltpu.VMEM((built, BLOCK), jnp.bfloat16), pltpu.VMEM((built, COLS_OUT), jnp.float32)]
     return pl.pallas_call(
         functools.partial(kernel, place),
-        out_shape=jax.ShapeDtypeStruct(out_shape, jnp.float32),
+        out_shape=out_shape,
         in_specs=[VMEM] * len(operands),
-        out_specs=VMEM,
+        out_specs=jax.tree.map(lambda _: VMEM, out_shape),
         scratch_shapes=scratch[:1] if kernel is begin_kernel else scratch,
         compiler_params=params(12),
         cost_estimate=cost(1, SHARE),
-        name="gram_" + place,
+        name="gram_" + (place or "a"),
     )(*operands)
 
 
@@ -271,19 +287,6 @@
         compiler_params=params(4),
         cost_estimate=cost(share, SHARE),
         name="add",
-    )(a, b)
-
-
-def cut(a, b):
-    shapes = ((LAST, LANES), (SENT - LAST, LANES))
-    return pl.pallas_call(
-        cut_kernel,
-        out_shape=[jax.ShapeDtypeStruct(shape, a.dtype) for shape in shapes],
-        in_specs=[VMEM] * 2,
-        out_specs=[VMEM] * 2,
-        compiler_params=params(4),
-        cost_estimate=cost(1, SHARE),
-        name="cut",
     )(a, b)
 
 
@@ -330,31 +333,40 @@
         name="smooth",
     )(coef, near, far[1], far[2], far[3])
     other = swap_cores(own)
+    def array(*shape):
+        return jax.ShapeDtypeStruct(shape, f32)
+
     own_right = right_of(own)
-    begun = gram(begin_kernel, "far", (BUILT, COLS_OUT), own, own_right)
+    begun_a = gram(begin_kernel, None, array(BUILT_A, COLS_OUT), own, own_right)
+    begun_a, own, own_right = lax.optimization_barrier((begun_a, own, own_right))
+    begun_b = gram(begin_kernel, "far", array(BUILT_B, COLS_OUT), own, own_right)
     other_right = right_of(other)
-    sent = (SENT, LANES)
-    parts = {"far": gram(finish_kernel, "far", sent, begun, other, other_right)}
+    chunk, sent = array(LAST, LANES), array(SENT, LANES)
+    far_a, cross_a, near_a, own_a = gram(finish_a_kernel, None, [chunk] * 4, begun_a, other, other_right)
+    begun_b, far_a = lax.optimization_barrier((begun_b, far_a))
+    far_b = gram(finish_b_kernel, "far", sent, begun_b, other, other_right)
     both = (own, own_right, other, other_right)
-    parts["cross"] = gram(gram_kernel, "cross", sent, *both)
-    both, parts["cross"] = lax.optimization_barrier((both, parts["cross"]))
-    parts["near"] = gram(gram_kernel, "near", sent, *both)
-    parts["own"] = gram(gram_kernel, "own", sent, *both)
-    two_back = hop(parts["far"], "y", 0)
-    from_cross = hop(parts["cross"], "y", 1)
-    near_far, near_rest = cut(parts["near"], two_back)
-    from_near_far, from_near_rest = hop(near_far, "y", 0), hop(near_rest, "y", 0)
-    sum_far, sum_rest = cut(parts["own"], from_cross)
-    two_back = hop(add(sum_far, from_near_far, 1 << 30), "z_hi", 0)
+    cross_b = gram(gram_kernel, "cross", sent, *both)
+    both, cross_b = lax.optimization_barrier((both, cross_b))
+    near_b = gram(gram_kernel, "near", sent, *both)
+    own_b = gram(gram_kernel, "own", sent, *both)
+
+    two_back = hop(far_a, "y", 0)
+    from_cross = hop(cross_a, "y", 1)
+    from_near = hop(add(near_a, two_back, 1 << 31), "y", 0)
+    two_back = hop(add(add(own_a, from_cross), from_near, 1 << 30), "z_hi", 0)
+    two_back_b = hop(far_b, "y", 0)
+    from_cross = hop(cross_b, "y", 1)
+    from_near = hop(add(near_b, two_back_b), "y", 0)
     kept, near, cross = pl.pallas_call(
         split_kernel,
-        out_shape=[jax.ShapeDtypeStruct((LAST, LANES), f32)] * 3,
+        out_shape=[chunk] * 3,
         in_specs=[VMEM] * 2,
         out_specs=[VMEM] * 3,
         compiler_params=params(8),
         cost_estimate=cost(1, SHARE),
         name="split",
-    )(sum_rest, from_near_rest)
+    )(add(own_b, from_cross), from_near)
     from_cross = hop(cross, "z_hi", 1)
     from_near = hop(add(near, two_back), "z_hi", 0)
     return pl.pallas_call(

time: 60 us -> 62 us (1.033)
  the two profiles are of different devices: /device:TPU:6 before, /device:TPU:1 now
where the time goes in v7:
time: 62 us; the launch traced here: 61.8 us
  starting transfers between devices  33.1 us (53%)
  waiting for transfers between devices  17.7 us (29%)
  Pallas kernels  8.6 us (14%)
  local copies, waits for them, and re-layouts  1.96 us (3%)
    ppermute x9, starting transfers between devices, hop(): return lax.ppermute(value, 'hor', pairs)  18.6 us
    ppermute x9, waiting for transfers between devices, hop(): return lax.ppermute(value, 'hor', pairs)  7.48 us
    ppermute x4, waiting for transfers between devices, shift_lev(): return lax.ppermute(value, 'lev', pairs)  6.7 us
    all_to_all x1, starting transfers between devices, on_device(): lists = lax.all_to_all(repeated, 'lev', 0, 0, tiled=True)  6.33 us
    pallas_call x7, Pallas kernels, gram(): pl.pallas_call(functools.partial(kernel, place), out_shape=out_shape, in_...  5.85 us
    ppermute x1, starting transfers between devices, swap_cores(): return lax.ppermute(value, 'hor', [(i, i ^ 1) for i in range(N_HOR)])  4.72 us
    all_to_all x1, waiting for transfers between devices, on_device(): lists = lax.all_to_all(repeated, 'lev', 0, 0, tiled=True)  3.47 us
    ppermute x4, starting transfers between devices, shift_lev(): return lax.ppermute(value, 'lev', pairs)  3.4 us
  transfers between devices with their start and end apart: 15, of which 8 were waited for; matrix products, arithmetic and copies ran while one was open for 0% of the time, Pallas kernels for 9%

profile of v7, /device:TPU:1, one launch (start us, length us, event | category | flops | bytes accessed | tf_op | source)
XLA Modules:
  0.0 61.8 jit_solution(4559922301398239480)
XLA Ops:
  0.0 0.7 %copy-done.1 = s32[1,128]{1,0:T(1,128)S(1)} copy-done((s32[1,128]{1,0:T(1,128)S(1)}, s32[1,128]{1,0:T(1,128)}, u32[]{:S(2)}) %copy-start.1) | copy-done | bytes 536
  0.7 0.6 repeat.1
  1.3 6.3 %all-to-all-start = ((s32[8,1,128]{2,1,0:T(1,128)}), s32[8,1,128]{2,1,0:T(1,128)S(1)}, u32[]{:S(2)}, u32[]{:S(2)}) async-start(s32[8,1,128]{2,1,0:T(1,128)} %repeat.1), calls=%async_computation | async-start | bytes 8192 | tf_op jit(solution)/shard_map/all_to_all | solution.py:304
  7.7 1.2 %copy-done = f32[4,4,16384]{2,1,0:T(4,128)S(1)} copy-done((f32[4,4,16384]{2,1,0:T(4,128)S(1)}, f32[4,4,16384]{2,1,0:T(4,128)}, u32[]{:S(2)}) %copy-start) | copy-done | bytes 1048600
  9.0 3.5 %all-to-all-done.index_ref = s32[8,1,128]{2,1,0:T(1,128)S(1)} async-done(((s32[8,1,128]{2,1,0:T(1,128)}), s32[8,1,128]{2,1,0:T(1,128)S(1)}, u32[]{:S(2)}, u32[]{:S(2)}) %all-to-all-start) | async-done | bytes 4128 | tf_op jit(solution)/shard_map/all_to_all | solution.py:304
  12.9 0.4 collective-permute-start
  13.3 2.8 %collective-permute-done = f32[16,1024]{1,0:T(8,128)S(1)} collective-permute-done((f32[16,1024]{1,0:T(8,128)S(1)}, f32[16,1024]{1,0:T(8,128)S(1)}, u32[]{:S(2)}, u32[]{:S(2)}) %collective-permute-start) | collective-permute-done | bytes 65568 | tf_op jit(solution)/shard_map/ppermute | solution.py:37
  16.5 1.8 %collective-permute-start.2 = (f32[2,16,1024]{2,1,0:T(8,128)S(1)}, f32[2,16,1024]{2,1,0:T(8,128)S(1)}, u32[]{:S(2)}, u32[]{:S(2)}) collective-permute-start(f32[2,16,1024]{2,1,0:T(8,128)S(1)} %pad_maximum_fusion.w0_ref), channel_id=1, source_target_pairs={{0,64},{32,96},{64,0},{96,32},{128,192},{160,224},{192,128},{224,1... | collective-permute-start | bytes 393224 | tf_op jit(solution)/shard_map/ppermute | solution.py:37
  18.3 0.9 %collective-permute-start.3 = (f32[2,16,1024]{2,1,0:T(8,128)S(1)}, f32[2,16,1024]{2,1,0:T(8,128)S(1)}, u32[]{:S(2)}, u32[]{:S(2)}) collective-permute-start(f32[2,16,1024]{2,1,0:T(8,128)S(1)} %pad_maximum_fusion.w0_ref), channel_id=1, source_target_pairs={{0,96},{32,0},{64,32},{96,64},{128,224},{160,128},{192,160},{224,1... | collective-permute-start | bytes 393224 | tf_op jit(solution)/shard_map/ppermute | solution.py:37
  19.3 3.3 %collective-permute-done.1.w1_ref = f32[2,16,1024]{2,1,0:T(8,128)S(1)} collective-permute-done((f32[2,16,1024]{2,1,0:T(8,128)S(1)}, f32[2,16,1024]{2,1,0:T(8,128)S(1)}, u32[]{:S(2)}, u32[]{:S(2)}) %collective-permute-start.1) | collective-permute-done | bytes 131104 | tf_op jit(solution)/shard_map/ppermute | solution.py:37
  22.6 0.6 %collective-permute-done.3.w3_ref = f32[2,16,1024]{2,1,0:T(8,128)S(1)} collective-permute-done((f32[2,16,1024]{2,1,0:T(8,128)S(1)}, f32[2,16,1024]{2,1,0:T(8,128)S(1)}, u32[]{:S(2)}, u32[]{:S(2)}) %collective-permute-start.3) | collective-permute-done | bytes 131104 | tf_op jit(solution)/shard_map/ppermute | solution.py:37
  23.6 4.7 %collective-permute-start.4 = (f32[128,1024]{1,0:T(8,128)S(1)}, f32[128,1024]{1,0:T(8,128)S(1)}, u32[]{:S(2)}, u32[]{:S(2)}) collective-permute-start(f32[128,1024]{1,0:T(8,128)S(1)} %smooth.1.smooth_ref.own_ref), channel_id=1, source_target_pairs={{0,1},{1,0},{2,3},{3,2},{4,5},{5,4},{6,7},{7,6},{8,9},{9,8},{10,11... | collective-permute-start | bytes 1572872 | tf_op jit(solution)/shard_map/ppermute | solution.py:41
  28.6 0.7 %gram_a.2.part_ref = f32[320,272]{1,0:T(8,128)S(1)} custom-call(f32[128,1024]{1,0:T(8,128)S(1)} %smooth.1.smooth_ref.own_ref, bf16[272,1024]{1,0:T(8,128)(2,1)S(1)} %right.2.right_ref.own_right_ref), custom_call_target="tpu_custom_call" | custom-call | flops 1 | bytes 262144 | tf_op jit(solution)/shard_map/gram_a/pallas_call | solution.py:269
  29.3 0.5 gram_far.2.part_ref
  30.1 0.9 %gram_a.3 = (f32[160,128]{1,0:T(8,128)S(1)}, f32[160,128]{1,0:T(8,128)S(1)}, f32[160,128]{1,0:T(8,128)S(1)}, f32[160,128]{1,0:T(8,128)S(1)}) custom-call(f32[320,272]{1,0:T(8,128)S(1)} %gram_a.2.part_ref, f32[128,1024]{1,0:T(8,128)S(1)} %collective-permute-done.4.smooth_ref.other_ref, bf16[272,1024]{1,0:T(8,128)(2,1)S(1)} %right.3.other_right_ref.right_ref), custom_call_target="tpu_custom_call" | custom-call | flops 1 | bytes 262144 | tf_op jit(solution)/shard_map/gram_a/pallas_call | solution.py:269
  31.0 2.8 %collective-permute-start.10 = (f32[160,128]{1,0:T(8,128)S(1)}, f32[160,128]{1,0:T(8,128)S(1)}, u32[]{:S(2)}, u32[]{:S(2)}) collective-permute-start(f32[160,128]{1,0:T(8,128)S(1)} %get-tuple-element.38), channel_id=1, source_target_pairs={{0,2},{1,7},{2,4},{3,1},{4,6},{5,3},{6,0},{7,5},{8,10},{9,15},{10,... | collective-permute-start | bytes 245768 | tf_op jit(solution)/shard_map/ppermute | solution.py:54
  33.8 0.5 collective-permute-start.9
  34.3 0.7 %gram_far.3 = f32[448,128]{1,0:T(8,128)S(1)} custom-call(f32[224,272]{1,0:T(8,128)S(1)} %gram_far.2.part_ref, f32[128,1024]{1,0:T(8,128)S(1)} %collective-permute-done.4.smooth_ref.other_ref, bf16[272,1024]{1,0:T(8,128)(2,1)S(1)} %right.3.other_right_ref.right_ref), custom_call_target="tpu_custom_call" | custom-call | flops 1 | bytes 262144 | tf_op jit(solution)/shard_map/gram_far/pallas_call | solution.py:269
  35.0 1.5 %collective-permute-start.6 = (f32[448,128]{1,0:T(8,128)S(1)}, f32[448,128]{1,0:T(8,128)S(1)}, u32[]{:S(2)}, u32[]{:S(2)}) collective-permute-start(f32[448,128]{1,0:T(8,128)S(1)} %gram_far.3), channel_id=1, source_target_pairs={{0,2},{1,7},{2,4},{3,1},{4,6},{5,3},{6,0},{7,5},{8,10},{9,15},{10,... | collective-permute-start | bytes 688136 | tf_op jit(solution)/shard_map/ppermute | solution.py:54
  36.6 1.8 %collective-permute-start.11 = (f32[160,128]{1,0:T(8,128)S(1)}, f32[160,128]{1,0:T(8,128)S(1)}, u32[]{:S(2)}, u32[]{:S(2)}) collective-permute-start(f32[160,128]{1,0:T(8,128)S(1)} %add.22), channel_id=1, source_target_pairs={{0,2},{1,7},{2,4},{3,1},{4,6},{5,3},{6,0},{7,5},{8,10},{9,15},{10,... | collective-permute-start | bytes 245768 | tf_op jit(solution)/shard_map/ppermute | solution.py:54
  38.4 1.0 %gram_cross.1 = f32[448,128]{1,0:T(8,128)S(1)} custom-call(f32[128,1024]{1,0:T(8,128)S(1)} %smooth.1.smooth_ref.own_ref, bf16[272,1024]{1,0:T(8,128)(2,1)S(1)} %right.2.right_ref.own_right_ref, f32[128,1024]{1,0:T(8,128)S(1)} %collective-permute-done.4.smooth_ref.other_ref, bf16[272,1024]{1,0:T(8,128)(2,1)S(1)} %right.3.other_right_ref.right_ref), custom_call_target="tpu_custom_call" | custom-call | flops 1 | bytes 262144 | tf_op jit(solution)/shard_map/gram_cross/pallas_call | solution.py:269
  39.4 1.9 %collective-permute-start.5 = (f32[448,128]{1,0:T(8,128)S(1)}, f32[448,128]{1,0:T(8,128)S(1)}, u32[]{:S(2)}, u32[]{:S(2)}) collective-permute-start(f32[448,128]{1,0:T(8,128)S(1)} %gram_cross.1), channel_id=1, source_target_pairs={{0,3},{1,6},{2,5},{3,0},{4,7},{5,2},{6,1},{7,4},{8,11},{9,14},{10,... | collective-permute-start | bytes 688136 | tf_op jit(solution)/shard_map/ppermute | solution.py:54
  41.3 1.0 %gram_near.1.a_ref = f32[448,128]{1,0:T(8,128)S(1)} custom-call(f32[128,1024]{1,0:T(8,128)S(1)} %smooth.1.smooth_ref.own_ref, bf16[272,1024]{1,0:T(8,128)(2,1)S(1)} %right.2.right_ref.own_right_ref, f32[128,1024]{1,0:T(8,128)S(1)} %collective-permute-done.4.smooth_ref.other_ref, bf16[272,1024]{1,0:T(8,128)(2,1)S(1)} %right.3.other_right_ref.right_ref), custom_call_target="tpu_custom_call" | custom-call | flops 1 | bytes 262144 | tf_op jit(solution)/shard_map/gram_near/pallas_call | solution.py:269
  42.3 0.4 collective-permute-start.7
  42.8 5.2 %collective-permute-start.12 = (f32[160,128]{1,0:T(8,128)S(1)}, f32[160,128]{1,0:T(8,128)S(1)}, u32[]{:S(2)}, u32[]{:S(2)}) collective-permute-start(f32[160,128]{1,0:T(8,128)S(1)} %add.23), channel_id=1, source_target_pairs={{0,8},{1,25},{2,10},{3,27},{4,12},{5,29},{6,14},{7,31},{8,16},{9,1... | collective-permute-start | bytes 245768 | tf_op jit(solution)/shard_map/ppermute | solution.py:54
  48.0 1.0 %gram_own.1.a_ref = f32[448,128]{1,0:T(8,128)S(1)} custom-call(f32[128,1024]{1,0:T(8,128)S(1)} %smooth.1.smooth_ref.own_ref, bf16[272,1024]{1,0:T(8,128)(2,1)S(1)} %right.2.right_ref.own_right_ref, f32[128,1024]{1,0:T(8,128)S(1)} %collective-permute-done.4.smooth_ref.other_ref, bf16[272,1024]{1,0:T(8,128)(2,1)S(1)} %right.3.other_right_ref.right_ref), custom_call_target="tpu_custom_call" | custom-call | flops 1 | bytes 262144 | tf_op jit(solution)/shard_map/gram_own/pallas_call | solution.py:269
  49.1 1.1 %collective-permute-done.12.b_ref = f32[160,128]{1,0:T(8,128)S(1)} collective-permute-done((f32[160,128]{1,0:T(8,128)S(1)}, f32[160,128]{1,0:T(8,128)S(1)}, u32[]{:S(2)}, u32[]{:S(2)}) %collective-permute-start.12) | collective-permute-done | bytes 81952 | tf_op jit(solution)/shard_map/ppermute | solution.py:54
  50.2 4.1 %collective-permute-start.13 = (f32[160,128]{1,0:T(8,128)S(1)}, f32[160,128]{1,0:T(8,128)S(1)}, u32[]{:S(2)}, u32[]{:S(2)}) collective-permute-start(f32[160,128]{1,0:T(8,128)S(1)} %add.24), channel_id=1, source_target_pairs={{0,8},{1,25},{2,10},{3,27},{4,12},{5,29},{6,14},{7,31},{8,16},{9,1... | collective-permute-start | bytes 245768 | tf_op jit(solution)/shard_map/ppermute | solution.py:54
  54.3 0.4 collective-permute-start.8
  54.7 1.7 %collective-permute-done.13.t2_ref = f32[160,128]{1,0:T(8,128)S(1)} collective-permute-done((f32[160,128]{1,0:T(8,128)S(1)}, f32[160,128]{1,0:T(8,128)S(1)}, u32[]{:S(2)}, u32[]{:S(2)}) %collective-permute-start.13) | collective-permute-done | bytes 81952 | tf_op jit(solution)/shard_map/ppermute | solution.py:54
  56.5 4.6 %collective-permute-done.8.t1_ref = f32[160,128]{1,0:T(8,128)S(1)} collective-permute-done((f32[160,128]{1,0:T(8,128)S(1)}, f32[160,128]{1,0:T(8,128)S(1)}, u32[]{:S(2)}, u32[]{:S(2)}) %collective-permute-start.8) | collective-permute-done | bytes 81952 | tf_op jit(solution)/shard_map/ppermute | solution.py:54
  61.1 0.7 %final.1 = f32[68,272]{1,0:T(8,128)} custom-call(f32[160,128]{1,0:T(8,128)S(1)} %get-tuple-element.32.t0_ref, f32[160,128]{1,0:T(8,128)S(1)} %collective-permute-done.8.t1_ref, f32[160,128]{1,0:T(8,128)S(1)} %collective-permute-done.13.t2_ref), custom_call_target="tpu_custom_call" | custom-call | flops 1 | bytes 262144 | tf_op jit(solution)/shard_map/final/pallas_call | solution.py:372
  (34 shorter events, 2.3 us)
Async XLA Ops:
  0.0 0.7 %copy-start.1 = (s32[1,128]{1,0:T(1,128)S(1)}, s32[1,128]{1,0:T(1,128)}, u32[]{:S(2)}) copy-start(s32[1,128]{1,0:T(1,128)} %index_ref.1) | copy-start | bytes 1540
  1.3 6.3 %copy-start.2 = (f32[32]{0:T(128)S(1)}, f32[32]{0:T(128)}, u32[]{:S(2)}) copy-start(f32[32]{0:T(128)} %param.6) | copy-start | bytes 388
  1.3 6.3 %copy-start.3 = (s32[31]{0:T(128)S(1)}, s32[31]{0:T(128)}, u32[]{:S(2)}) copy-start(s32[31]{0:T(128)} %param.7) | copy-start | bytes 376
  1.3 11.3 %all-to-all-start = ((s32[8,1,128]{2,1,0:T(1,128)}), s32[8,1,128]{2,1,0:T(1,128)S(1)}, u32[]{:S(2)}, u32[]{:S(2)}) async-start(s32[8,1,128]{2,1,0:T(1,128)} %repeat.1), calls=%async_computation | async-start | bytes 8192 | tf_op jit(solution)/shard_map/all_to_all | solution.py:304
  7.7 1.2 %copy-start = (f32[4,4,16384]{2,1,0:T(4,128)S(1)}, f32[4,4,16384]{2,1,0:T(4,128)}, u32[]{:S(2)}) copy-start(f32[4,4,16384]{2,1,0:T(4,128)} %slab_ref.1) | copy-start | bytes 3145732
  12.9 3.2 %collective-permute-start = (f32[16,1024]{1,0:T(8,128)S(1)}, f32[16,1024]{1,0:T(8,128)S(1)}, u32[]{:S(2)}, u32[]{:S(2)}) collective-permute-start(f32[16,1024]{1,0:T(8,128)S(1)} %pick.1), channel_id=1, source_target_pairs={{0,128},{32,160},{64,192},{96,224},{128,0},{160,32},{192,64},{224,... | collective-permute-start | bytes 196616 | tf_op jit(solution)/shard_map/ppermute | solution.py:37
  16.1 6.5 %collective-permute-start.1 = (f32[2,16,1024]{2,1,0:T(8,128)S(1)}, f32[2,16,1024]{2,1,0:T(8,128)S(1)}, u32[]{:S(2)}, u32[]{:S(2)}) collective-permute-start(f32[2,16,1024]{2,1,0:T(8,128)S(1)} %pad_maximum_fusion.w0_ref), channel_id=1, source_target_pairs={{0,32},{32,64},{64,96},{96,0},{128,160},{160,192},{192,224},{224,1... | collective-permute-start | bytes 393224 | tf_op jit(solution)/shard_map/ppermute | solution.py:37
  16.5 6.2 %collective-permute-start.2 = (f32[2,16,1024]{2,1,0:T(8,128)S(1)}, f32[2,16,1024]{2,1,0:T(8,128)S(1)}, u32[]{:S(2)}, u32[]{:S(2)}) collective-permute-start(f32[2,16,1024]{2,1,0:T(8,128)S(1)} %pad_maximum_fusion.w0_ref), channel_id=1, source_target_pairs={{0,64},{32,96},{64,0},{96,32},{128,192},{160,224},{192,128},{224,1... | collective-permute-start | bytes 393224 | tf_op jit(solution)/shard_map/ppermute | solution.py:37
  18.3 5.0 %collective-permute-start.3 = (f32[2,16,1024]{2,1,0:T(8,128)S(1)}, f32[2,16,1024]{2,1,0:T(8,128)S(1)}, u32[]{:S(2)}, u32[]{:S(2)}) collective-permute-start(f32[2,16,1024]{2,1,0:T(8,128)S(1)} %pad_maximum_fusion.w0_ref), channel_id=1, source_target_pairs={{0,96},{32,0},{64,32},{96,64},{128,224},{160,128},{192,160},{224,1... | collective-permute-start | bytes 393224 | tf_op jit(solution)/shard_map/ppermute | solution.py:37
  23.6 6.3 %collective-permute-start.4 = (f32[128,1024]{1,0:T(8,128)S(1)}, f32[128,1024]{1,0:T(8,128)S(1)}, u32[]{:S(2)}, u32[]{:S(2)}) collective-permute-start(f32[128,1024]{1,0:T(8,128)S(1)} %smooth.1.smooth_ref.own_ref), channel_id=1, source_target_pairs={{0,1},{1,0},{2,3},{3,2},{4,5},{5,4},{6,7},{7,6},{8,9},{9,8},{10,11... | collective-permute-start | bytes 1572872 | tf_op jit(solution)/shard_map/ppermute | solution.py:41
  31.0 5.5 %collective-permute-start.10 = (f32[160,128]{1,0:T(8,128)S(1)}, f32[160,128]{1,0:T(8,128)S(1)}, u32[]{:S(2)}, u32[]{:S(2)}) collective-permute-start(f32[160,128]{1,0:T(8,128)S(1)} %get-tuple-element.38), channel_id=1, source_target_pairs={{0,2},{1,7},{2,4},{3,1},{4,6},{5,3},{6,0},{7,5},{8,10},{9,15},{10,... | collective-permute-start | bytes 245768 | tf_op jit(solution)/shard_map/ppermute | solution.py:54
  33.8 8.9 %collective-permute-start.9 = (f32[160,128]{1,0:T(8,128)S(1)}, f32[160,128]{1,0:T(8,128)S(1)}, u32[]{:S(2)}, u32[]{:S(2)}) collective-permute-start(f32[160,128]{1,0:T(8,128)S(1)} %get-tuple-element.36), channel_id=1, source_target_pairs={{0,3},{1,6},{2,5},{3,0},{4,7},{5,2},{6,1},{7,4},{8,11},{9,14},{10,... | collective-permute-start | bytes 245768 | tf_op jit(solution)/shard_map/ppermute | solution.py:54
  35.0 7.3 %collective-permute-start.6 = (f32[448,128]{1,0:T(8,128)S(1)}, f32[448,128]{1,0:T(8,128)S(1)}, u32[]{:S(2)}, u32[]{:S(2)}) collective-permute-start(f32[448,128]{1,0:T(8,128)S(1)} %gram_far.3), channel_id=1, source_target_pairs={{0,2},{1,7},{2,4},{3,1},{4,6},{5,3},{6,0},{7,5},{8,10},{9,15},{10,... | collective-permute-start | bytes 688136 | tf_op jit(solution)/shard_map/ppermute | solution.py:54
  36.6 6.2 %collective-permute-start.11 = (f32[160,128]{1,0:T(8,128)S(1)}, f32[160,128]{1,0:T(8,128)S(1)}, u32[]{:S(2)}, u32[]{:S(2)}) collective-permute-start(f32[160,128]{1,0:T(8,128)S(1)} %add.22), channel_id=1, source_target_pairs={{0,2},{1,7},{2,4},{3,1},{4,6},{5,3},{6,0},{7,5},{8,10},{9,15},{10,... | collective-permute-start | bytes 245768 | tf_op jit(solution)/shard_map/ppermute | solution.py:54
  39.4 9.6 %collective-permute-start.5 = (f32[448,128]{1,0:T(8,128)S(1)}, f32[448,128]{1,0:T(8,128)S(1)}, u32[]{:S(2)}, u32[]{:S(2)}) collective-permute-start(f32[448,128]{1,0:T(8,128)S(1)} %gram_cross.1), channel_id=1, source_target_pairs={{0,3},{1,6},{2,5},{3,0},{4,7},{5,2},{6,1},{7,4},{8,11},{9,14},{10,... | collective-permute-start | bytes 688136 | tf_op jit(solution)/shard_map/ppermute | solution.py:54
  42.3 6.7 %collective-permute-start.7 = (f32[448,128]{1,0:T(8,128)S(1)}, f32[448,128]{1,0:T(8,128)S(1)}, u32[]{:S(2)}, u32[]{:S(2)}) collective-permute-start(f32[448,128]{1,0:T(8,128)S(1)} %add.20), channel_id=1, source_target_pairs={{0,2},{1,7},{2,4},{3,1},{4,6},{5,3},{6,0},{7,5},{8,10},{9,15},{10,... | collective-permute-start | bytes 688136 | tf_op jit(solution)/shard_map/ppermute | solution.py:54
  42.8 7.5 %collective-permute-start.12 = (f32[160,128]{1,0:T(8,128)S(1)}, f32[160,128]{1,0:T(8,128)S(1)}, u32[]{:S(2)}, u32[]{:S(2)}) collective-permute-start(f32[160,128]{1,0:T(8,128)S(1)} %add.23), channel_id=1, source_target_pairs={{0,8},{1,25},{2,10},{3,27},{4,12},{5,29},{6,14},{7,31},{8,16},{9,1... | collective-permute-start | bytes 245768 | tf_op jit(solution)/shard_map/ppermute | solution.py:54
  50.2 6.2 %collective-permute-start.13 = (f32[160,128]{1,0:T(8,128)S(1)}, f32[160,128]{1,0:T(8,128)S(1)}, u32[]{:S(2)}, u32[]{:S(2)}) collective-permute-start(f32[160,128]{1,0:T(8,128)S(1)} %add.24), channel_id=1, source_target_pairs={{0,8},{1,25},{2,10},{3,27},{4,12},{5,29},{6,14},{7,31},{8,16},{9,1... | collective-permute-start | bytes 245768 | tf_op jit(solution)/shard_map/ppermute | solution.py:54
  54.3 6.7 %collective-permute-start.8 = (f32[160,128]{1,0:T(8,128)S(1)}, f32[160,128]{1,0:T(8,128)S(1)}, u32[]{:S(2)}, u32[]{:S(2)}) collective-permute-start(f32[160,128]{1,0:T(8,128)S(1)} %get-tuple-element.33), channel_id=1, source_target_pairs={{0,9},{1,24},{2,11},{3,26},{4,13},{5,28},{6,15},{7,30},{8,17},{9,0... | collective-permute-start | bytes 245768 | tf_op jit(solution)/shard_map/ppermute | solution.py:54

commit v8 on v6

--- a/solution.py
+++ b/solution.py
@@ -207,12 +207,12 @@
         ref[2 * CHUNK + 8 : LAST, :] = two
 
 
-def final_kernel(t0_ref, t1_ref, t2_ref, out_ref):
+def final_kernel(kept_ref, near_ref, out_ref):
     odd = lax.axis_index("hor") % 2 == 1
     scale = 1.0 / (BLOCK * N_HOR)
 
     def total(rows):
-        return (t0_ref[rows, :] + t1_ref[rows, :]) + t2_ref[rows, :]
+        return kept_ref[rows, :] + near_ref[rows, :]
 
     def place(value):
         return jnp.where(odd, value[CHUNK - ROWS_OUT : CHUNK], value[0:ROWS_OUT]) * scale
@@ -342,6 +342,7 @@
     parts["own"] = gram(gram_kernel, "own", sent, *both)
     two_back = hop(parts["far"], "y", 0)
     from_cross = hop(parts["cross"], "y", 1)
+    parts["near"], parts["own"] = lax.optimization_barrier((parts["near"], parts["own"]))
     near_far, near_rest = cut(parts["near"], two_back)
     from_near_far, from_near_rest = hop(near_far, "y", 0), hop(near_rest, "y", 0)
     sum_far, sum_rest = cut(parts["own"], from_cross)
@@ -356,16 +357,17 @@
         name="split",
     )(sum_rest, from_near_rest)
     from_cross = hop(cross, "z_hi", 1)
+    kept = add(kept, from_cross)
     from_near = hop(add(near, two_back), "z_hi", 0)
     return pl.pallas_call(
         final_kernel,
         out_shape=jax.ShapeDtypeStruct((ROWS_OUT, COLS_OUT), f32),
-        in_specs=[VMEM] * 3,
+        in_specs=[VMEM] * 2,
         out_specs=VMEM,
         compiler_params=params(8),
         cost_estimate=cost(1, SHARE),
         name="final",
-    )(kept, from_cross, from_near)
+    )(kept, from_near)
 
 
 def solution(mesh):

time: 60 us -> 60 us (level)
  no operation moved by 1% of the time
where the time goes in v8:
time: 60 us; the launch traced here: 59.8 us
  waiting for transfers between devices  29.4 us (49%)
  starting transfers between devices  20.2 us (34%)
  Pallas kernels  7.91 us (13%)
  local copies, waits for them, and re-layouts  1.96 us (3%)
    ppermute x7, waiting for transfers between devices, hop(): return lax.ppermute(value, 'hor', pairs)  15.9 us
    ppermute x4, waiting for transfers between devices, shift_lev(): return lax.ppermute(value, 'lev', pairs)  9.91 us
    ppermute x7, starting transfers between devices, hop(): return lax.ppermute(value, 'hor', pairs)  9.58 us
    all_to_all x1, starting transfers between devices, on_device(): lists = lax.all_to_all(repeated, 'lev', 0, 0, tiled=True)  6.26 us
    pallas_call x5, Pallas kernels, gram(): pl.pallas_call(functools.partial(kernel, place), out_shape=jax.ShapeDtype...  5.14 us
    ppermute x4, starting transfers between devices, shift_lev(): return lax.ppermute(value, 'lev', pairs)  4.23 us
    all_to_all x1, waiting for transfers between devices, on_device(): lists = lax.all_to_all(repeated, 'lev', 0, 0, tiled=True)  2.57 us
    unnamed x8, local copies, waits for them, and re-layouts  1.89 us
  transfers between devices with their start and end apart: 13, of which 10 were waited for; matrix products, arithmetic and copies ran while one was open for 1% of the time, Pallas kernels for 8%

profile of v8, /device:TPU:6, one launch (start us, length us, event | category | flops | bytes accessed | tf_op | source)
XLA Modules:
  0.0 59.8 jit_solution(695838223127698257)
XLA Ops:
  0.0 0.7 %copy-done.1 = s32[1,128]{1,0:T(1,128)S(1)} copy-done((s32[1,128]{1,0:T(1,128)S(1)}, s32[1,128]{1,0:T(1,128)}, u32[]{:S(2)}) %copy-start.1) | copy-done | bytes 536
  0.7 0.6 repeat.1
  1.3 6.3 %all-to-all-start = ((s32[8,1,128]{2,1,0:T(1,128)}), s32[8,1,128]{2,1,0:T(1,128)S(1)}, u32[]{:S(2)}, u32[]{:S(2)}) async-start(s32[8,1,128]{2,1,0:T(1,128)} %repeat.1), calls=%async_computation | async-start | bytes 8192 | tf_op jit(solution)/shard_map/all_to_all | solution.py:301
  7.6 1.2 %copy-done = f32[4,4,16384]{2,1,0:T(4,128)S(1)} copy-done((f32[4,4,16384]{2,1,0:T(4,128)S(1)}, f32[4,4,16384]{2,1,0:T(4,128)}, u32[]{:S(2)}) %copy-start) | copy-done | bytes 1048600
  9.0 2.6 %all-to-all-done.index_ref = s32[8,1,128]{2,1,0:T(1,128)S(1)} async-done(((s32[8,1,128]{2,1,0:T(1,128)}), s32[8,1,128]{2,1,0:T(1,128)S(1)}, u32[]{:S(2)}, u32[]{:S(2)}) %all-to-all-start) | async-done | bytes 4128 | tf_op jit(solution)/shard_map/all_to_all | solution.py:301
  11.5 0.4 pick.1
  11.9 0.7 %collective-permute-start = (f32[16,1024]{1,0:T(8,128)S(1)}, f32[16,1024]{1,0:T(8,128)S(1)}, u32[]{:S(2)}, u32[]{:S(2)}) collective-permute-start(f32[16,1024]{1,0:T(8,128)S(1)} %pick.1), channel_id=1, source_target_pairs={{0,128},{32,160},{64,192},{96,224},{128,0},{160,32},{192,64},{224,... | collective-permute-start | bytes 196616 | tf_op jit(solution)/shard_map/ppermute | solution.py:37
  12.6 3.6 %collective-permute-done = f32[16,1024]{1,0:T(8,128)S(1)} collective-permute-done((f32[16,1024]{1,0:T(8,128)S(1)}, f32[16,1024]{1,0:T(8,128)S(1)}, u32[]{:S(2)}, u32[]{:S(2)}) %collective-permute-start) | collective-permute-done | bytes 65568 | tf_op jit(solution)/shard_map/ppermute | solution.py:37
  16.3 2.1 %collective-permute-start.1 = (f32[2,16,1024]{2,1,0:T(8,128)S(1)}, f32[2,16,1024]{2,1,0:T(8,128)S(1)}, u32[]{:S(2)}, u32[]{:S(2)}) collective-permute-start(f32[2,16,1024]{2,1,0:T(8,128)S(1)} %pad_maximum_fusion.w0_ref), channel_id=1, source_target_pairs={{0,32},{32,64},{64,96},{96,0},{128,160},{160,192},{192,224},{224,1... | collective-permute-start | bytes 393224 | tf_op jit(solution)/shard_map/ppermute | solution.py:37
  18.4 0.6 collective-permute-start.2
  19.0 0.9 %collective-permute-start.3 = (f32[2,16,1024]{2,1,0:T(8,128)S(1)}, f32[2,16,1024]{2,1,0:T(8,128)S(1)}, u32[]{:S(2)}, u32[]{:S(2)}) collective-permute-start(f32[2,16,1024]{2,1,0:T(8,128)S(1)} %pad_maximum_fusion.w0_ref), channel_id=1, source_target_pairs={{0,96},{32,0},{64,32},{96,64},{128,224},{160,128},{192,160},{224,1... | collective-permute-start | bytes 393224 | tf_op jit(solution)/shard_map/ppermute | solution.py:37
  20.0 2.3 %collective-permute-done.1.w1_ref = f32[2,16,1024]{2,1,0:T(8,128)S(1)} collective-permute-done((f32[2,16,1024]{2,1,0:T(8,128)S(1)}, f32[2,16,1024]{2,1,0:T(8,128)S(1)}, u32[]{:S(2)}, u32[]{:S(2)}) %collective-permute-start.1) | collective-permute-done | bytes 131104 | tf_op jit(solution)/shard_map/ppermute | solution.py:37
  22.4 2.7 %collective-permute-done.2.w2_ref = f32[2,16,1024]{2,1,0:T(8,128)S(1)} collective-permute-done((f32[2,16,1024]{2,1,0:T(8,128)S(1)}, f32[2,16,1024]{2,1,0:T(8,128)S(1)}, u32[]{:S(2)}, u32[]{:S(2)}) %collective-permute-start.2) | collective-permute-done | bytes 131104 | tf_op jit(solution)/shard_map/ppermute | solution.py:37
  25.0 1.3 %collective-permute-done.3.w3_ref = f32[2,16,1024]{2,1,0:T(8,128)S(1)} collective-permute-done((f32[2,16,1024]{2,1,0:T(8,128)S(1)}, f32[2,16,1024]{2,1,0:T(8,128)S(1)}, u32[]{:S(2)}, u32[]{:S(2)}) %collective-permute-start.3) | collective-permute-done | bytes 131104 | tf_op jit(solution)/shard_map/ppermute | solution.py:37
  26.4 0.3 smooth.1.smooth_ref.own_ref
  27.0 0.7 %gram_far.2.part_ref = f32[304,272]{1,0:T(8,128)S(1)} custom-call(f32[128,1024]{1,0:T(8,128)S(1)} %smooth.1.smooth_ref.own_ref, bf16[272,1024]{1,0:T(8,128)(2,1)S(1)} %right.2.own_right_ref.right_ref), custom_call_target="tpu_custom_call" | custom-call | flops 1 | bytes 262144 | tf_op jit(solution)/shard_map/gram_far/pallas_call | solution.py:253
  27.7 1.0 %collective-permute-done.4.smooth_ref.other_ref = f32[128,1024]{1,0:T(8,128)S(1)} collective-permute-done((f32[128,1024]{1,0:T(8,128)S(1)}, f32[128,1024]{1,0:T(8,128)S(1)}, u32[]{:S(2)}, u32[]{:S(2)}) %collective-permute-start.4) | collective-permute-done | bytes 524320 | tf_op jit(solution)/shard_map/ppermute | solution.py:41
  28.9 0.9 %gram_far.3 = f32[608,128]{1,0:T(8,128)S(1)} custom-call(f32[304,272]{1,0:T(8,128)S(1)} %gram_far.2.part_ref, f32[128,1024]{1,0:T(8,128)S(1)} %collective-permute-done.4.smooth_ref.other_ref, bf16[272,1024]{1,0:T(8,128)(2,1)S(1)} %right.3.other_right_ref.right_ref), custom_call_target="tpu_custom_call" | custom-call | flops 1 | bytes 262144 | tf_op jit(solution)/shard_map/gram_far/pallas_call | solution.py:253
  29.8 1.6 %collective-permute-start.6 = (f32[608,128]{1,0:T(8,128)S(1)}, f32[608,128]{1,0:T(8,128)S(1)}, u32[]{:S(2)}, u32[]{:S(2)}) collective-permute-start(f32[608,128]{1,0:T(8,128)S(1)} %gram_far.3), channel_id=1, source_target_pairs={{0,2},{1,7},{2,4},{3,1},{4,6},{5,3},{6,0},{7,5},{8,10},{9,15},{10,... | collective-permute-start | bytes 933896 | tf_op jit(solution)/shard_map/ppermute | solution.py:54
  31.4 1.2 %gram_cross.1 = f32[608,128]{1,0:T(8,128)S(1)} custom-call(f32[128,1024]{1,0:T(8,128)S(1)} %smooth.1.smooth_ref.own_ref, bf16[272,1024]{1,0:T(8,128)(2,1)S(1)} %right.2.own_right_ref.right_ref, f32[128,1024]{1,0:T(8,128)S(1)} %collective-permute-done.4.smooth_ref.other_ref, bf16[272,1024]{1,0:T(8,128)(2,1)S(1)} %right.3.other_right_ref.right_ref), custom_call_target="tpu_custom_call" | custom-call | flops 1 | bytes 262144 | tf_op jit(solution)/shard_map/gram_cross/pallas_call | solution.py:253
  32.7 1.2 %gram_own.1.a_ref = f32[608,128]{1,0:T(8,128)S(1)} custom-call(f32[128,1024]{1,0:T(8,128)S(1)} %smooth.1.smooth_ref.own_ref, bf16[272,1024]{1,0:T(8,128)(2,1)S(1)} %right.2.own_right_ref.right_ref, f32[128,1024]{1,0:T(8,128)S(1)} %collective-permute-done.4.smooth_ref.other_ref, bf16[272,1024]{1,0:T(8,128)(2,1)S(1)} %right.3.other_right_ref.right_ref), custom_call_target="tpu_custom_call" | custom-call | flops 1 | bytes 262144 | tf_op jit(solution)/shard_map/gram_own/pallas_call | solution.py:253
  33.9 1.2 %gram_near.1.a_ref = f32[608,128]{1,0:T(8,128)S(1)} custom-call(f32[128,1024]{1,0:T(8,128)S(1)} %smooth.1.smooth_ref.own_ref, bf16[272,1024]{1,0:T(8,128)(2,1)S(1)} %right.2.own_right_ref.right_ref, f32[128,1024]{1,0:T(8,128)S(1)} %collective-permute-done.4.smooth_ref.other_ref, bf16[272,1024]{1,0:T(8,128)(2,1)S(1)} %right.3.other_right_ref.right_ref), custom_call_target="tpu_custom_call" | custom-call | flops 1 | bytes 262144 | tf_op jit(solution)/shard_map/gram_near/pallas_call | solution.py:253
  35.1 2.8 %collective-permute-done.6.b_ref = f32[608,128]{1,0:T(8,128)S(1)} collective-permute-done((f32[608,128]{1,0:T(8,128)S(1)}, f32[608,128]{1,0:T(8,128)S(1)}, u32[]{:S(2)}, u32[]{:S(2)}) %collective-permute-start.6) | collective-permute-done | bytes 311328 | tf_op jit(solution)/shard_map/ppermute | solution.py:54
  38.0 0.4 collective-permute-start.9
  38.4 1.6 %collective-permute-start.7 = (f32[448,128]{1,0:T(8,128)S(1)}, f32[448,128]{1,0:T(8,128)S(1)}, u32[]{:S(2)}, u32[]{:S(2)}) collective-permute-start(f32[448,128]{1,0:T(8,128)S(1)} %get-tuple-element.27), channel_id=1, source_target_pairs={{0,2},{1,7},{2,4},{3,1},{4,6},{5,3},{6,0},{7,5},{8,10},{9,15},{10,... | collective-permute-start | bytes 688136 | tf_op jit(solution)/shard_map/ppermute | solution.py:54
  40.0 3.7 %collective-permute-done.9.b_ref = f32[160,128]{1,0:T(8,128)S(1)} collective-permute-done((f32[160,128]{1,0:T(8,128)S(1)}, f32[160,128]{1,0:T(8,128)S(1)}, u32[]{:S(2)}, u32[]{:S(2)}) %collective-permute-start.9) | collective-permute-done | bytes 81952 | tf_op jit(solution)/shard_map/ppermute | solution.py:54
  43.7 3.4 %collective-permute-start.10 = (f32[160,128]{1,0:T(8,128)S(1)}, f32[160,128]{1,0:T(8,128)S(1)}, u32[]{:S(2)}, u32[]{:S(2)}) collective-permute-start(f32[160,128]{1,0:T(8,128)S(1)} %add.17), channel_id=1, source_target_pairs={{0,8},{1,25},{2,10},{3,27},{4,12},{5,29},{6,14},{7,31},{8,16},{9,1... | collective-permute-start | bytes 245768 | tf_op jit(solution)/shard_map/ppermute | solution.py:54
  47.1 0.8 %collective-permute-start.8 = (f32[160,128]{1,0:T(8,128)S(1)}, f32[160,128]{1,0:T(8,128)S(1)}, u32[]{:S(2)}, u32[]{:S(2)}) collective-permute-start(f32[160,128]{1,0:T(8,128)S(1)} %get-tuple-element.29), channel_id=1, source_target_pairs={{0,9},{1,24},{2,11},{3,26},{4,13},{5,28},{6,15},{7,30},{8,17},{9,0... | collective-permute-start | bytes 245768 | tf_op jit(solution)/shard_map/ppermute | solution.py:54
  47.9 3.7 %collective-permute-done.10.b_ref = f32[160,128]{1,0:T(8,128)S(1)} collective-permute-done((f32[160,128]{1,0:T(8,128)S(1)}, f32[160,128]{1,0:T(8,128)S(1)}, u32[]{:S(2)}, u32[]{:S(2)}) %collective-permute-start.10) | collective-permute-done | bytes 81952 | tf_op jit(solution)/shard_map/ppermute | solution.py:54
  51.6 1.8 %collective-permute-start.11 = (f32[160,128]{1,0:T(8,128)S(1)}, f32[160,128]{1,0:T(8,128)S(1)}, u32[]{:S(2)}, u32[]{:S(2)}) collective-permute-start(f32[160,128]{1,0:T(8,128)S(1)} %add.18), channel_id=1, source_target_pairs={{0,8},{1,25},{2,10},{3,27},{4,12},{5,29},{6,14},{7,31},{8,16},{9,1... | collective-permute-start | bytes 245768 | tf_op jit(solution)/shard_map/ppermute | solution.py:54
  53.4 5.7 %collective-permute-done.11.near_ref = f32[160,128]{1,0:T(8,128)S(1)} collective-permute-done((f32[160,128]{1,0:T(8,128)S(1)}, f32[160,128]{1,0:T(8,128)S(1)}, u32[]{:S(2)}, u32[]{:S(2)}) %collective-permute-start.11) | collective-permute-done | bytes 81952 | tf_op jit(solution)/shard_map/ppermute | solution.py:54
  59.1 0.7 %final.1 = f32[68,272]{1,0:T(8,128)} custom-call(f32[160,128]{1,0:T(8,128)S(1)} %add.16.kept_ref, f32[160,128]{1,0:T(8,128)S(1)} %collective-permute-done.11.near_ref), custom_call_target="tpu_custom_call" | custom-call | flops 1 | bytes 262144 | tf_op jit(solution)/shard_map/final/pallas_call | solution.py:362
  (27 shorter events, 1.4 us)
Async XLA Ops:
  0.0 0.7 %copy-start.1 = (s32[1,128]{1,0:T(1,128)S(1)}, s32[1,128]{1,0:T(1,128)}, u32[]{:S(2)}) copy-start(s32[1,128]{1,0:T(1,128)} %index_ref.1) | copy-start | bytes 1540
  1.3 6.3 %copy-start.2 = (f32[32]{0:T(128)S(1)}, f32[32]{0:T(128)}, u32[]{:S(2)}) copy-start(f32[32]{0:T(128)} %param.6) | copy-start | bytes 388
  1.3 6.3 %copy-start.3 = (s32[31]{0:T(128)S(1)}, s32[31]{0:T(128)}, u32[]{:S(2)}) copy-start(s32[31]{0:T(128)} %param.7) | copy-start | bytes 376
  1.3 10.3 %all-to-all-start = ((s32[8,1,128]{2,1,0:T(1,128)}), s32[8,1,128]{2,1,0:T(1,128)S(1)}, u32[]{:S(2)}, u32[]{:S(2)}) async-start(s32[8,1,128]{2,1,0:T(1,128)} %repeat.1), calls=%async_computation | async-start | bytes 8192 | tf_op jit(solution)/shard_map/all_to_all | solution.py:301
  7.6 1.2 %copy-start = (f32[4,4,16384]{2,1,0:T(4,128)S(1)}, f32[4,4,16384]{2,1,0:T(4,128)}, u32[]{:S(2)}) copy-start(f32[4,4,16384]{2,1,0:T(4,128)} %slab_ref.1) | copy-start | bytes 3145732
  11.9 4.4 %collective-permute-start = (f32[16,1024]{1,0:T(8,128)S(1)}, f32[16,1024]{1,0:T(8,128)S(1)}, u32[]{:S(2)}, u32[]{:S(2)}) collective-permute-start(f32[16,1024]{1,0:T(8,128)S(1)} %pick.1), channel_id=1, source_target_pairs={{0,128},{32,160},{64,192},{96,224},{128,0},{160,32},{192,64},{224,... | collective-permute-start | bytes 196616 | tf_op jit(solution)/shard_map/ppermute | solution.py:37
  16.3 6.1 %collective-permute-start.1 = (f32[2,16,1024]{2,1,0:T(8,128)S(1)}, f32[2,16,1024]{2,1,0:T(8,128)S(1)}, u32[]{:S(2)}, u32[]{:S(2)}) collective-permute-start(f32[2,16,1024]{2,1,0:T(8,128)S(1)} %pad_maximum_fusion.w0_ref), channel_id=1, source_target_pairs={{0,32},{32,64},{64,96},{96,0},{128,160},{160,192},{192,224},{224,1... | collective-permute-start | bytes 393224 | tf_op jit(solution)/shard_map/ppermute | solution.py:37
  18.4 6.6 %collective-permute-start.2 = (f32[2,16,1024]{2,1,0:T(8,128)S(1)}, f32[2,16,1024]{2,1,0:T(8,128)S(1)}, u32[]{:S(2)}, u32[]{:S(2)}) collective-permute-start(f32[2,16,1024]{2,1,0:T(8,128)S(1)} %pad_maximum_fusion.w0_ref), channel_id=1, source_target_pairs={{0,64},{32,96},{64,0},{96,32},{128,192},{160,224},{192,128},{224,1... | collective-permute-start | bytes 393224 | tf_op jit(solution)/shard_map/ppermute | solution.py:37
  19.0 7.3 %collective-permute-start.3 = (f32[2,16,1024]{2,1,0:T(8,128)S(1)}, f32[2,16,1024]{2,1,0:T(8,128)S(1)}, u32[]{:S(2)}, u32[]{:S(2)}) collective-permute-start(f32[2,16,1024]{2,1,0:T(8,128)S(1)} %pad_maximum_fusion.w0_ref), channel_id=1, source_target_pairs={{0,96},{32,0},{64,32},{96,64},{128,224},{160,128},{192,160},{224,1... | collective-permute-start | bytes 393224 | tf_op jit(solution)/shard_map/ppermute | solution.py:37
  26.7 2.0 %collective-permute-start.4 = (f32[128,1024]{1,0:T(8,128)S(1)}, f32[128,1024]{1,0:T(8,128)S(1)}, u32[]{:S(2)}, u32[]{:S(2)}) collective-permute-start(f32[128,1024]{1,0:T(8,128)S(1)} %smooth.1.smooth_ref.own_ref), channel_id=1, source_target_pairs={{0,1},{1,0},{2,3},{3,2},{4,5},{5,4},{6,7},{7,6},{8,9},{9,8},{10,11... | collective-permute-start | bytes 1572872 | tf_op jit(solution)/shard_map/ppermute | solution.py:41
  29.8 8.1 %collective-permute-start.6 = (f32[608,128]{1,0:T(8,128)S(1)}, f32[608,128]{1,0:T(8,128)S(1)}, u32[]{:S(2)}, u32[]{:S(2)}) collective-permute-start(f32[608,128]{1,0:T(8,128)S(1)} %gram_far.3), channel_id=1, source_target_pairs={{0,2},{1,7},{2,4},{3,1},{4,6},{5,3},{6,0},{7,5},{8,10},{9,15},{10,... | collective-permute-start | bytes 933896 | tf_op jit(solution)/shard_map/ppermute | solution.py:54
  32.6 7.4 %collective-permute-start.5 = (f32[608,128]{1,0:T(8,128)S(1)}, f32[608,128]{1,0:T(8,128)S(1)}, u32[]{:S(2)}, u32[]{:S(2)}) collective-permute-start(f32[608,128]{1,0:T(8,128)S(1)} %gram_cross.1), channel_id=1, source_target_pairs={{0,3},{1,6},{2,5},{3,0},{4,7},{5,2},{6,1},{7,4},{8,11},{9,14},{10,... | collective-permute-start | bytes 933896 | tf_op jit(solution)/shard_map/ppermute | solution.py:54
  38.0 5.7 %collective-permute-start.9 = (f32[160,128]{1,0:T(8,128)S(1)}, f32[160,128]{1,0:T(8,128)S(1)}, u32[]{:S(2)}, u32[]{:S(2)}) collective-permute-start(f32[160,128]{1,0:T(8,128)S(1)} %get-tuple-element.32), channel_id=1, source_target_pairs={{0,2},{1,7},{2,4},{3,1},{4,6},{5,3},{6,0},{7,5},{8,10},{9,15},{10,... | collective-permute-start | bytes 245768 | tf_op jit(solution)/shard_map/ppermute | solution.py:54
  38.4 8.7 %collective-permute-start.7 = (f32[448,128]{1,0:T(8,128)S(1)}, f32[448,128]{1,0:T(8,128)S(1)}, u32[]{:S(2)}, u32[]{:S(2)}) collective-permute-start(f32[448,128]{1,0:T(8,128)S(1)} %get-tuple-element.27), channel_id=1, source_target_pairs={{0,2},{1,7},{2,4},{3,1},{4,6},{5,3},{6,0},{7,5},{8,10},{9,15},{10,... | collective-permute-start | bytes 688136 | tf_op jit(solution)/shard_map/ppermute | solution.py:54
  43.7 7.9 %collective-permute-start.10 = (f32[160,128]{1,0:T(8,128)S(1)}, f32[160,128]{1,0:T(8,128)S(1)}, u32[]{:S(2)}, u32[]{:S(2)}) collective-permute-start(f32[160,128]{1,0:T(8,128)S(1)} %add.17), channel_id=1, source_target_pairs={{0,8},{1,25},{2,10},{3,27},{4,12},{5,29},{6,14},{7,31},{8,16},{9,1... | collective-permute-start | bytes 245768 | tf_op jit(solution)/shard_map/ppermute | solution.py:54
  47.1 6.2 %collective-permute-start.8 = (f32[160,128]{1,0:T(8,128)S(1)}, f32[160,128]{1,0:T(8,128)S(1)}, u32[]{:S(2)}, u32[]{:S(2)}) collective-permute-start(f32[160,128]{1,0:T(8,128)S(1)} %get-tuple-element.29), channel_id=1, source_target_pairs={{0,9},{1,24},{2,11},{3,26},{4,13},{5,28},{6,15},{7,30},{8,17},{9,0... | collective-permute-start | bytes 245768 | tf_op jit(solution)/shard_map/ppermute | solution.py:54
  51.6 7.5 %collective-permute-start.11 = (f32[160,128]{1,0:T(8,128)S(1)}, f32[160,128]{1,0:T(8,128)S(1)}, u32[]{:S(2)}, u32[]{:S(2)}) collective-permute-start(f32[160,128]{1,0:T(8,128)S(1)} %add.18), channel_id=1, source_target_pairs={{0,8},{1,25},{2,10},{3,27},{4,12},{5,29},{6,14},{7,31},{8,16},{9,1... | collective-permute-start | bytes 245768 | tf_op jit(solution)/shard_map/ppermute | solution.py:54

commit v9 on v6

--- a/solution.py
+++ b/solution.py
@@ -207,12 +207,12 @@
         ref[2 * CHUNK + 8 : LAST, :] = two
 
 
-def final_kernel(t0_ref, t1_ref, t2_ref, out_ref):
+def final_kernel(kept_ref, near_ref, cross_ref, out_ref):
     odd = lax.axis_index("hor") % 2 == 1
     scale = 1.0 / (BLOCK * N_HOR)
 
     def total(rows):
-        return (t0_ref[rows, :] + t1_ref[rows, :]) + t2_ref[rows, :]
+        return (kept_ref[rows, :] + near_ref[rows, :]) + cross_ref[rows, :]
 
     def place(value):
         return jnp.where(odd, value[CHUNK - ROWS_OUT : CHUNK], value[0:ROWS_OUT]) * scale
@@ -342,10 +342,12 @@
     parts["own"] = gram(gram_kernel, "own", sent, *both)
     two_back = hop(parts["far"], "y", 0)
     from_cross = hop(parts["cross"], "y", 1)
+    parts["near"], parts["own"] = lax.optimization_barrier((parts["near"], parts["own"]))
     near_far, near_rest = cut(parts["near"], two_back)
     from_near_far, from_near_rest = hop(near_far, "y", 0), hop(near_rest, "y", 0)
     sum_far, sum_rest = cut(parts["own"], from_cross)
-    two_back = hop(add(sum_far, from_near_far, 1 << 30), "z_hi", 0)
+    straight = [(i, (i + N_HOR // 2) % N_HOR) for i in range(N_HOR)]
+    from_far = lax.ppermute(add(sum_far, from_near_far, 1 << 30), "hor", straight)
     kept, near, cross = pl.pallas_call(
         split_kernel,
         out_shape=[jax.ShapeDtypeStruct((LAST, LANES), f32)] * 3,
@@ -355,8 +357,9 @@
         cost_estimate=cost(1, SHARE),
         name="split",
     )(sum_rest, from_near_rest)
+    from_near = hop(near, "z_hi", 0)
     from_cross = hop(cross, "z_hi", 1)
-    from_near = hop(add(near, two_back), "z_hi", 0)
+    kept = add(kept, from_far, 1 << 30)
     return pl.pallas_call(
         final_kernel,
         out_shape=jax.ShapeDtypeStruct((ROWS_OUT, COLS_OUT), f32),
@@ -365,7 +368,7 @@
         compiler_params=params(8),
         cost_estimate=cost(1, SHARE),
         name="final",
-    )(kept, from_cross, from_near)
+    )(kept, from_near, from_cross)
 
 
 def solution(mesh):

time: 60 us -> 59.7 us (level)
  the two profiles are of different devices: /device:TPU:6 before, /device:TPU:1 now
where the time goes in v9:
time: 59.7 us; the launch traced here: 59.5 us
  starting transfers between devices  33.5 us (56%)
  waiting for transfers between devices  15.7 us (26%)
  Pallas kernels  7.87 us (13%)
  local copies, waits for them, and re-layouts  1.96 us (3%)
    ppermute x6, starting transfers between devices, hop(): return lax.ppermute(value, 'hor', pairs)  13 us
    ppermute x4, waiting for transfers between devices, shift_lev(): return lax.ppermute(value, 'lev', pairs)  6.7 us
    all_to_all x1, starting transfers between devices, on_device(): lists = lax.all_to_all(repeated, 'lev', 0, 0, tiled=True)  6.33 us
    ppermute x1, starting transfers between devices, on_device(): lax.ppermute(add(sum_far, from_near_far, 1 << 30), 'hor', straight)  6.1 us
    pallas_call x5, Pallas kernels, gram(): pl.pallas_call(functools.partial(kernel, place), out_shape=jax.ShapeDtype...  5.13 us
    ppermute x6, waiting for transfers between devices, hop(): return lax.ppermute(value, 'hor', pairs)  4.89 us
    ppermute x1, starting transfers between devices, swap_cores(): return lax.ppermute(value, 'hor', [(i, i ^ 1) for i in range(N_HOR)])  4.72 us
    all_to_all x1, waiting for transfers between devices, on_device(): lists = lax.all_to_all(repeated, 'lev', 0, 0, tiled=True)  3.47 us
  transfers between devices with their start and end apart: 13, of which 8 were waited for; matrix products, arithmetic and copies ran while one was open for 1% of the time, Pallas kernels for 8%

profile of v9, /device:TPU:1, one launch (start us, length us, event | category | flops | bytes accessed | tf_op | source)
XLA Modules:
  0.0 59.5 jit_solution(7850309978694981442)
XLA Ops:
  0.0 0.7 %copy-done.1 = s32[1,128]{1,0:T(1,128)S(1)} copy-done((s32[1,128]{1,0:T(1,128)S(1)}, s32[1,128]{1,0:T(1,128)}, u32[]{:S(2)}) %copy-start.1) | copy-done | bytes 536
  0.7 0.6 repeat.1
  1.3 6.3 %all-to-all-start = ((s32[8,1,128]{2,1,0:T(1,128)}), s32[8,1,128]{2,1,0:T(1,128)S(1)}, u32[]{:S(2)}, u32[]{:S(2)}) async-start(s32[8,1,128]{2,1,0:T(1,128)} %repeat.1), calls=%async_computation | async-start | bytes 8192 | tf_op jit(solution)/shard_map/all_to_all | solution.py:301
  7.7 1.2 %copy-done = f32[4,4,16384]{2,1,0:T(4,128)S(1)} copy-done((f32[4,4,16384]{2,1,0:T(4,128)S(1)}, f32[4,4,16384]{2,1,0:T(4,128)}, u32[]{:S(2)}) %copy-start) | copy-done | bytes 1048600
  9.0 3.5 %all-to-all-done.index_ref = s32[8,1,128]{2,1,0:T(1,128)S(1)} async-done(((s32[8,1,128]{2,1,0:T(1,128)}), s32[8,1,128]{2,1,0:T(1,128)S(1)}, u32[]{:S(2)}, u32[]{:S(2)}) %all-to-all-start) | async-done | bytes 4128 | tf_op jit(solution)/shard_map/all_to_all | solution.py:301
  12.5 0.4 pick.1
  12.9 0.4 collective-permute-start
  13.3 2.8 %collective-permute-done = f32[16,1024]{1,0:T(8,128)S(1)} collective-permute-done((f32[16,1024]{1,0:T(8,128)S(1)}, f32[16,1024]{1,0:T(8,128)S(1)}, u32[]{:S(2)}, u32[]{:S(2)}) %collective-permute-start) | collective-permute-done | bytes 65568 | tf_op jit(solution)/shard_map/ppermute | solution.py:37
  16.1 0.4 collective-permute-start.1
  16.5 1.8 %collective-permute-start.2 = (f32[2,16,1024]{2,1,0:T(8,128)S(1)}, f32[2,16,1024]{2,1,0:T(8,128)S(1)}, u32[]{:S(2)}, u32[]{:S(2)}) collective-permute-start(f32[2,16,1024]{2,1,0:T(8,128)S(1)} %pad_maximum_fusion.w0_ref), channel_id=1, source_target_pairs={{0,64},{32,96},{64,0},{96,32},{128,192},{160,224},{192,128},{224,1... | collective-permute-start | bytes 393224 | tf_op jit(solution)/shard_map/ppermute | solution.py:37
  18.3 0.9 %collective-permute-start.3 = (f32[2,16,1024]{2,1,0:T(8,128)S(1)}, f32[2,16,1024]{2,1,0:T(8,128)S(1)}, u32[]{:S(2)}, u32[]{:S(2)}) collective-permute-start(f32[2,16,1024]{2,1,0:T(8,128)S(1)} %pad_maximum_fusion.w0_ref), channel_id=1, source_target_pairs={{0,96},{32,0},{64,32},{96,64},{128,224},{160,128},{192,160},{224,1... | collective-permute-start | bytes 393224 | tf_op jit(solution)/shard_map/ppermute | solution.py:37
  19.3 3.3 %collective-permute-done.1.w1_ref = f32[2,16,1024]{2,1,0:T(8,128)S(1)} collective-permute-done((f32[2,16,1024]{2,1,0:T(8,128)S(1)}, f32[2,16,1024]{2,1,0:T(8,128)S(1)}, u32[]{:S(2)}, u32[]{:S(2)}) %collective-permute-start.1) | collective-permute-done | bytes 131104 | tf_op jit(solution)/shard_map/ppermute | solution.py:37
  22.6 0.6 %collective-permute-done.3.w3_ref = f32[2,16,1024]{2,1,0:T(8,128)S(1)} collective-permute-done((f32[2,16,1024]{2,1,0:T(8,128)S(1)}, f32[2,16,1024]{2,1,0:T(8,128)S(1)}, u32[]{:S(2)}, u32[]{:S(2)}) %collective-permute-start.3) | collective-permute-done | bytes 131104 | tf_op jit(solution)/shard_map/ppermute | solution.py:37
  23.3 0.3 smooth.1.smooth_ref.own_ref
  23.6 4.7 %collective-permute-start.4 = (f32[128,1024]{1,0:T(8,128)S(1)}, f32[128,1024]{1,0:T(8,128)S(1)}, u32[]{:S(2)}, u32[]{:S(2)}) collective-permute-start(f32[128,1024]{1,0:T(8,128)S(1)} %smooth.1.smooth_ref.own_ref), channel_id=1, source_target_pairs={{0,1},{1,0},{2,3},{3,2},{4,5},{5,4},{6,7},{7,6},{8,9},{9,8},{10,11... | collective-permute-start | bytes 1572872 | tf_op jit(solution)/shard_map/ppermute | solution.py:41
  28.4 0.2 right.2.own_right_ref.right_ref
  28.6 0.7 %gram_far.2.part_ref = f32[304,272]{1,0:T(8,128)S(1)} custom-call(f32[128,1024]{1,0:T(8,128)S(1)} %smooth.1.smooth_ref.own_ref, bf16[272,1024]{1,0:T(8,128)(2,1)S(1)} %right.2.own_right_ref.right_ref), custom_call_target="tpu_custom_call" | custom-call | flops 1 | bytes 262144 | tf_op jit(solution)/shard_map/gram_far/pallas_call | solution.py:253
  29.3 0.6 %collective-permute-done.4.smooth_ref.other_ref = f32[128,1024]{1,0:T(8,128)S(1)} collective-permute-done((f32[128,1024]{1,0:T(8,128)S(1)}, f32[128,1024]{1,0:T(8,128)S(1)}, u32[]{:S(2)}, u32[]{:S(2)}) %collective-permute-start.4) | collective-permute-done | bytes 524320 | tf_op jit(solution)/shard_map/ppermute | solution.py:41
  30.1 0.9 %gram_far.3 = f32[608,128]{1,0:T(8,128)S(1)} custom-call(f32[304,272]{1,0:T(8,128)S(1)} %gram_far.2.part_ref, f32[128,1024]{1,0:T(8,128)S(1)} %collective-permute-done.4.smooth_ref.other_ref, bf16[272,1024]{1,0:T(8,128)(2,1)S(1)} %right.3.other_right_ref.right_ref), custom_call_target="tpu_custom_call" | custom-call | flops 1 | bytes 262144 | tf_op jit(solution)/shard_map/gram_far/pallas_call | solution.py:253
  31.0 2.8 %collective-permute-start.6 = (f32[608,128]{1,0:T(8,128)S(1)}, f32[608,128]{1,0:T(8,128)S(1)}, u32[]{:S(2)}, u32[]{:S(2)}) collective-permute-start(f32[608,128]{1,0:T(8,128)S(1)} %gram_far.3), channel_id=1, source_target_pairs={{0,2},{1,7},{2,4},{3,1},{4,6},{5,3},{6,0},{7,5},{8,10},{9,15},{10,... | collective-permute-start | bytes 933896 | tf_op jit(solution)/shard_map/ppermute | solution.py:54
  33.8 1.2 %gram_cross.1 = f32[608,128]{1,0:T(8,128)S(1)} custom-call(f32[128,1024]{1,0:T(8,128)S(1)} %smooth.1.smooth_ref.own_ref, bf16[272,1024]{1,0:T(8,128)(2,1)S(1)} %right.2.own_right_ref.right_ref, f32[128,1024]{1,0:T(8,128)S(1)} %collective-permute-done.4.smooth_ref.other_ref, bf16[272,1024]{1,0:T(8,128)(2,1)S(1)} %right.3.other_right_ref.right_ref), custom_call_target="tpu_custom_call" | custom-call | flops 1 | bytes 262144 | tf_op jit(solution)/shard_map/gram_cross/pallas_call | solution.py:253
  35.0 0.5 collective-permute-start.5
  35.5 1.2 %gram_own.1.a_ref = f32[608,128]{1,0:T(8,128)S(1)} custom-call(f32[128,1024]{1,0:T(8,128)S(1)} %smooth.1.smooth_ref.own_ref, bf16[272,1024]{1,0:T(8,128)(2,1)S(1)} %right.2.own_right_ref.right_ref, f32[128,1024]{1,0:T(8,128)S(1)} %collective-permute-done.4.smooth_ref.other_ref, bf16[272,1024]{1,0:T(8,128)(2,1)S(1)} %right.3.other_right_ref.right_ref), custom_call_target="tpu_custom_call" | custom-call | flops 1 | bytes 262144 | tf_op jit(solution)/shard_map/gram_own/pallas_call | solution.py:253
  36.7 1.2 %gram_near.1.a_ref = f32[608,128]{1,0:T(8,128)S(1)} custom-call(f32[128,1024]{1,0:T(8,128)S(1)} %smooth.1.smooth_ref.own_ref, bf16[272,1024]{1,0:T(8,128)(2,1)S(1)} %right.2.own_right_ref.right_ref, f32[128,1024]{1,0:T(8,128)S(1)} %collective-permute-done.4.smooth_ref.other_ref, bf16[272,1024]{1,0:T(8,128)(2,1)S(1)} %right.3.other_right_ref.right_ref), custom_call_target="tpu_custom_call" | custom-call | flops 1 | bytes 262144 | tf_op jit(solution)/shard_map/gram_near/pallas_call | solution.py:253
  37.9 2.9 %collective-permute-start.8 = (f32[160,128]{1,0:T(8,128)S(1)}, f32[160,128]{1,0:T(8,128)S(1)}, u32[]{:S(2)}, u32[]{:S(2)}) collective-permute-start(f32[160,128]{1,0:T(8,128)S(1)} %get-tuple-element.30), channel_id=1, source_target_pairs={{0,2},{1,7},{2,4},{3,1},{4,6},{5,3},{6,0},{7,5},{8,10},{9,15},{10,... | collective-permute-start | bytes 245768 | tf_op jit(solution)/shard_map/ppermute | solution.py:54
  40.9 1.7 %collective-permute-done.5.b_ref = f32[608,128]{1,0:T(8,128)S(1)} collective-permute-done((f32[608,128]{1,0:T(8,128)S(1)}, f32[608,128]{1,0:T(8,128)S(1)}, u32[]{:S(2)}, u32[]{:S(2)}) %collective-permute-start.5) | collective-permute-done | bytes 311328 | tf_op jit(solution)/shard_map/ppermute | solution.py:54
  42.7 6.1 %collective-permute-start.9 = (f32[160,128]{1,0:T(8,128)S(1)}, f32[160,128]{1,0:T(8,128)S(1)}, u32[]{:S(2)}, u32[]{:S(2)}) collective-permute-start(f32[160,128]{1,0:T(8,128)S(1)} %add.15), channel_id=1, source_target_pairs={{0,16},{1,17},{2,18},{3,19},{4,20},{5,21},{6,22},{7,23},{8,24},{9,... | collective-permute-start | bytes 245768 | tf_op jit(solution)/shard_map/ppermute | solution.py:350
  48.9 2.4 %collective-permute-start.10 = (f32[160,128]{1,0:T(8,128)S(1)}, f32[160,128]{1,0:T(8,128)S(1)}, u32[]{:S(2)}, u32[]{:S(2)}) collective-permute-start(f32[160,128]{1,0:T(8,128)S(1)} %get-tuple-element.31), channel_id=1, source_target_pairs={{0,8},{1,25},{2,10},{3,27},{4,12},{5,29},{6,14},{7,31},{8,16},{9,1... | collective-permute-start | bytes 245768 | tf_op jit(solution)/shard_map/ppermute | solution.py:54
  51.2 4.3 %collective-permute-start.11 = (f32[160,128]{1,0:T(8,128)S(1)}, f32[160,128]{1,0:T(8,128)S(1)}, u32[]{:S(2)}, u32[]{:S(2)}) collective-permute-start(f32[160,128]{1,0:T(8,128)S(1)} %get-tuple-element.32), channel_id=1, source_target_pairs={{0,9},{1,24},{2,11},{3,26},{4,13},{5,28},{6,15},{7,30},{8,17},{9,0... | collective-permute-start | bytes 245768 | tf_op jit(solution)/shard_map/ppermute | solution.py:54
  55.5 0.2 collective-permute-done.10.near_ref
  55.8 3.0 %collective-permute-done.11.cross_ref = f32[160,128]{1,0:T(8,128)S(1)} collective-permute-done((f32[160,128]{1,0:T(8,128)S(1)}, f32[160,128]{1,0:T(8,128)S(1)}, u32[]{:S(2)}, u32[]{:S(2)}) %collective-permute-start.11) | collective-permute-done | bytes 81952 | tf_op jit(solution)/shard_map/ppermute | solution.py:54
  58.8 0.7 %final.1 = f32[68,272]{1,0:T(8,128)} custom-call(f32[160,128]{1,0:T(8,128)S(1)} %add.16.kept_ref, f32[160,128]{1,0:T(8,128)S(1)} %collective-permute-done.10.near_ref, f32[160,128]{1,0:T(8,128)S(1)} %collective-permute-done.11.cross_ref), custom_call_target="tpu_custom_call" | custom-call | flops 1 | bytes 262144 | tf_op jit(solution)/shard_map/final/pallas_call | solution.py:363
  (26 shorter events, 1.0 us)
Async XLA Ops:
  0.0 0.7 %copy-start.1 = (s32[1,128]{1,0:T(1,128)S(1)}, s32[1,128]{1,0:T(1,128)}, u32[]{:S(2)}) copy-start(s32[1,128]{1,0:T(1,128)} %index_ref.1) | copy-start | bytes 1540
  1.3 6.3 %copy-start.2 = (f32[32]{0:T(128)S(1)}, f32[32]{0:T(128)}, u32[]{:S(2)}) copy-start(f32[32]{0:T(128)} %param.6) | copy-start | bytes 388
  1.3 6.3 %copy-start.3 = (s32[31]{0:T(128)S(1)}, s32[31]{0:T(128)}, u32[]{:S(2)}) copy-start(s32[31]{0:T(128)} %param.7) | copy-start | bytes 376
  1.3 11.3 %all-to-all-start = ((s32[8,1,128]{2,1,0:T(1,128)}), s32[8,1,128]{2,1,0:T(1,128)S(1)}, u32[]{:S(2)}, u32[]{:S(2)}) async-start(s32[8,1,128]{2,1,0:T(1,128)} %repeat.1), calls=%async_computation | async-start | bytes 8192 | tf_op jit(solution)/shard_map/all_to_all | solution.py:301
  7.7 1.2 %copy-start = (f32[4,4,16384]{2,1,0:T(4,128)S(1)}, f32[4,4,16384]{2,1,0:T(4,128)}, u32[]{:S(2)}) copy-start(f32[4,4,16384]{2,1,0:T(4,128)} %slab_ref.1) | copy-start | bytes 3145732
  12.9 3.2 %collective-permute-start = (f32[16,1024]{1,0:T(8,128)S(1)}, f32[16,1024]{1,0:T(8,128)S(1)}, u32[]{:S(2)}, u32[]{:S(2)}) collective-permute-start(f32[16,1024]{1,0:T(8,128)S(1)} %pick.1), channel_id=1, source_target_pairs={{0,128},{32,160},{64,192},{96,224},{128,0},{160,32},{192,64},{224,... | collective-permute-start | bytes 196616 | tf_op jit(solution)/shard_map/ppermute | solution.py:37
  16.1 6.5 %collective-permute-start.1 = (f32[2,16,1024]{2,1,0:T(8,128)S(1)}, f32[2,16,1024]{2,1,0:T(8,128)S(1)}, u32[]{:S(2)}, u32[]{:S(2)}) collective-permute-start(f32[2,16,1024]{2,1,0:T(8,128)S(1)} %pad_maximum_fusion.w0_ref), channel_id=1, source_target_pairs={{0,32},{32,64},{64,96},{96,0},{128,160},{160,192},{192,224},{224,1... | collective-permute-start | bytes 393224 | tf_op jit(solution)/shard_map/ppermute | solution.py:37
  16.5 6.2 %collective-permute-start.2 = (f32[2,16,1024]{2,1,0:T(8,128)S(1)}, f32[2,16,1024]{2,1,0:T(8,128)S(1)}, u32[]{:S(2)}, u32[]{:S(2)}) collective-permute-start(f32[2,16,1024]{2,1,0:T(8,128)S(1)} %pad_maximum_fusion.w0_ref), channel_id=1, source_target_pairs={{0,64},{32,96},{64,0},{96,32},{128,192},{160,224},{192,128},{224,1... | collective-permute-start | bytes 393224 | tf_op jit(solution)/shard_map/ppermute | solution.py:37
  18.3 5.0 %collective-permute-start.3 = (f32[2,16,1024]{2,1,0:T(8,128)S(1)}, f32[2,16,1024]{2,1,0:T(8,128)S(1)}, u32[]{:S(2)}, u32[]{:S(2)}) collective-permute-start(f32[2,16,1024]{2,1,0:T(8,128)S(1)} %pad_maximum_fusion.w0_ref), channel_id=1, source_target_pairs={{0,96},{32,0},{64,32},{96,64},{128,224},{160,128},{192,160},{224,1... | collective-permute-start | bytes 393224 | tf_op jit(solution)/shard_map/ppermute | solution.py:37
  23.6 6.3 %collective-permute-start.4 = (f32[128,1024]{1,0:T(8,128)S(1)}, f32[128,1024]{1,0:T(8,128)S(1)}, u32[]{:S(2)}, u32[]{:S(2)}) collective-permute-start(f32[128,1024]{1,0:T(8,128)S(1)} %smooth.1.smooth_ref.own_ref), channel_id=1, source_target_pairs={{0,1},{1,0},{2,3},{3,2},{4,5},{5,4},{6,7},{7,6},{8,9},{9,8},{10,11... | collective-permute-start | bytes 1572872 | tf_op jit(solution)/shard_map/ppermute | solution.py:41
  31.0 6.9 %collective-permute-start.6 = (f32[608,128]{1,0:T(8,128)S(1)}, f32[608,128]{1,0:T(8,128)S(1)}, u32[]{:S(2)}, u32[]{:S(2)}) collective-permute-start(f32[608,128]{1,0:T(8,128)S(1)} %gram_far.3), channel_id=1, source_target_pairs={{0,2},{1,7},{2,4},{3,1},{4,6},{5,3},{6,0},{7,5},{8,10},{9,15},{10,... | collective-permute-start | bytes 933896 | tf_op jit(solution)/shard_map/ppermute | solution.py:54
  35.0 7.6 %collective-permute-start.5 = (f32[608,128]{1,0:T(8,128)S(1)}, f32[608,128]{1,0:T(8,128)S(1)}, u32[]{:S(2)}, u32[]{:S(2)}) collective-permute-start(f32[608,128]{1,0:T(8,128)S(1)} %gram_cross.1), channel_id=1, source_target_pairs={{0,3},{1,6},{2,5},{3,0},{4,7},{5,2},{6,1},{7,4},{8,11},{9,14},{10,... | collective-permute-start | bytes 933896 | tf_op jit(solution)/shard_map/ppermute | solution.py:54
  37.9 4.7 %collective-permute-start.8 = (f32[160,128]{1,0:T(8,128)S(1)}, f32[160,128]{1,0:T(8,128)S(1)}, u32[]{:S(2)}, u32[]{:S(2)}) collective-permute-start(f32[160,128]{1,0:T(8,128)S(1)} %get-tuple-element.30), channel_id=1, source_target_pairs={{0,2},{1,7},{2,4},{3,1},{4,6},{5,3},{6,0},{7,5},{8,10},{9,15},{10,... | collective-permute-start | bytes 245768 | tf_op jit(solution)/shard_map/ppermute | solution.py:54
  40.8 7.9 %collective-permute-start.7 = (f32[448,128]{1,0:T(8,128)S(1)}, f32[448,128]{1,0:T(8,128)S(1)}, u32[]{:S(2)}, u32[]{:S(2)}) collective-permute-start(f32[448,128]{1,0:T(8,128)S(1)} %get-tuple-element.27), channel_id=1, source_target_pairs={{0,2},{1,7},{2,4},{3,1},{4,6},{5,3},{6,0},{7,5},{8,10},{9,15},{10,... | collective-permute-start | bytes 688136 | tf_op jit(solution)/shard_map/ppermute | solution.py:54
  42.7 12.9 %collective-permute-start.9 = (f32[160,128]{1,0:T(8,128)S(1)}, f32[160,128]{1,0:T(8,128)S(1)}, u32[]{:S(2)}, u32[]{:S(2)}) collective-permute-start(f32[160,128]{1,0:T(8,128)S(1)} %add.15), channel_id=1, source_target_pairs={{0,16},{1,17},{2,18},{3,19},{4,20},{5,21},{6,22},{7,23},{8,24},{9,... | collective-permute-start | bytes 245768 | tf_op jit(solution)/shard_map/ppermute | solution.py:350
  48.9 6.9 %collective-permute-start.10 = (f32[160,128]{1,0:T(8,128)S(1)}, f32[160,128]{1,0:T(8,128)S(1)}, u32[]{:S(2)}, u32[]{:S(2)}) collective-permute-start(f32[160,128]{1,0:T(8,128)S(1)} %get-tuple-element.31), channel_id=1, source_target_pairs={{0,8},{1,25},{2,10},{3,27},{4,12},{5,29},{6,14},{7,31},{8,16},{9,1... | collective-permute-start | bytes 245768 | tf_op jit(solution)/shard_map/ppermute | solution.py:54
  51.2 7.5 %collective-permute-start.11 = (f32[160,128]{1,0:T(8,128)S(1)}, f32[160,128]{1,0:T(8,128)S(1)}, u32[]{:S(2)}, u32[]{:S(2)}) collective-permute-start(f32[160,128]{1,0:T(8,128)S(1)} %get-tuple-element.32), channel_id=1, source_target_pairs={{0,9},{1,24},{2,11},{3,26},{4,13},{5,28},{6,15},{7,30},{8,17},{9,0... | collective-permute-start | bytes 245768 | tf_op jit(solution)/shard_map/ppermute | solution.py:54

commit v10 on v8

--- a/solution.py
+++ b/solution.py
@@ -139,12 +139,15 @@
     )
 
 
-def emit(place, prod_ref, out_ref):
+def emit(place, prod_ref, out_refs):
     skip = windows_of(place)[1]
     at, base, group, tail = 0, 0, 0, 2 * CHUNK
+    out_ref = out_refs[0]
     for number, size in enumerate(WINDOWS):
         if number == 1:
             base, group, tail = LAST, 0, LAST + REST
+            if len(out_refs) == 2:
+                out_ref, base, tail = out_refs[1], 0, REST
         for half in range(2):
             rows = pl.ds(pl.multiple_of(at + skip, 8), size)
             out_ref[base : base + size, :] = prod_ref[rows, half * LANES : (half + 1) * LANES]
@@ -162,15 +165,17 @@
     out_ref[...] = product(place, smooth_ref, right_ref, left_ref)
 
 
-def finish_kernel(place, part_ref, smooth_ref, right_ref, out_ref, left_ref, prod_ref):
+def finish_kernel(place, part_ref, smooth_ref, right_ref, *refs):
+    left_ref, prod_ref = refs[-2:]
     prod_ref[...] = part_ref[...] + product(place, smooth_ref, right_ref, left_ref)
-    emit(place, prod_ref, out_ref)
-
-
-def gram_kernel(place, own_ref, own_right_ref, other_ref, other_right_ref, out_ref, left_ref, prod_ref):
+    emit(place, prod_ref, refs[:-2])
+
+
+def gram_kernel(place, own_ref, own_right_ref, other_ref, other_right_ref, *refs):
+    left_ref, prod_ref = refs[-2:]
     prod_ref[...] = product(place, own_ref, own_right_ref, left_ref)
     prod_ref[...] += product(place, other_ref, other_right_ref, left_ref)
-    emit(place, prod_ref, out_ref)
+    emit(place, prod_ref, refs[:-2])
 
 
 def add_kernel(a_ref, b_ref, out_ref):
@@ -248,13 +253,13 @@
     )(smoothed)
 
 
-def gram(kernel, place, out_shape, *operands):
+def gram(kernel, place, out_shapes, *operands):
     scratch = [pltpu.VMEM((BUILT, BLOCK), jnp.bfloat16), pltpu.VMEM((BUILT, COLS_OUT), jnp.float32)]
     return pl.pallas_call(
         functools.partial(kernel, place),
-        out_shape=jax.ShapeDtypeStruct(out_shape, jnp.float32),
+        out_shape=[jax.ShapeDtypeStruct(shape, jnp.float32) for shape in out_shapes],
         in_specs=[VMEM] * len(operands),
-        out_specs=VMEM,
+        out_specs=[VMEM] * len(out_shapes),
         scratch_shapes=scratch[:1] if kernel is begin_kernel else scratch,
         compiler_params=params(12),
         cost_estimate=cost(1, SHARE),
@@ -331,22 +336,22 @@
     )(coef, near, far[1], far[2], far[3])
     other = swap_cores(own)
     own_right = right_of(own)
-    begun = gram(begin_kernel, "far", (BUILT, COLS_OUT), own, own_right)
+    (begun,) = gram(begin_kernel, "far", [(BUILT, COLS_OUT)], own, own_right)
     other_right = right_of(other)
-    sent = (SENT, LANES)
-    parts = {"far": gram(finish_kernel, "far", sent, begun, other, other_right)}
+    whole, apart = [(SENT, LANES)], [(LAST, LANES), (SENT - LAST, LANES)]
+    far_far, far_rest = gram(finish_kernel, "far", apart, begun, other, other_right)
     both = (own, own_right, other, other_right)
-    parts["cross"] = gram(gram_kernel, "cross", sent, *both)
-    both, parts["cross"] = lax.optimization_barrier((both, parts["cross"]))
-    parts["near"] = gram(gram_kernel, "near", sent, *both)
-    parts["own"] = gram(gram_kernel, "own", sent, *both)
-    two_back = hop(parts["far"], "y", 0)
-    from_cross = hop(parts["cross"], "y", 1)
-    parts["near"], parts["own"] = lax.optimization_barrier((parts["near"], parts["own"]))
-    near_far, near_rest = cut(parts["near"], two_back)
+    (crossing,) = gram(gram_kernel, "cross", whole, *both)
+    both, crossing = lax.optimization_barrier((both, crossing))
+    near_far, near_rest = gram(gram_kernel, "near", apart, *both)
+    (own_part,) = gram(gram_kernel, "own", whole, *both)
+    two_back_far, two_back_rest = hop(far_far, "y", 0), hop(far_rest, "y", 0)
+    from_cross = hop(crossing, "y", 1)
+    near_far = add(near_far, two_back_far, 1 << 31)
+    near_rest = add(near_rest, two_back_rest)
     from_near_far, from_near_rest = hop(near_far, "y", 0), hop(near_rest, "y", 0)
-    sum_far, sum_rest = cut(parts["own"], from_cross)
-    two_back = hop(add(sum_far, from_near_far, 1 << 30), "z_hi", 0)
+    sum_far, sum_rest = cut(own_part, from_cross)
+    two_back = hop(add(sum_far, from_near_far, 1 << 31), "z_hi", 0)
     kept, near, cross = pl.pallas_call(
         split_kernel,
         out_shape=[jax.ShapeDtypeStruct((LAST, LANES), f32)] * 3,

time: 60 us -> 64.1 us (1.068)
  the two profiles are of different devices: /device:TPU:6 before, /device:TPU:1 now
where the time goes in v10:
time: 64.1 us; the launch traced here: 63.9 us
  starting transfers between devices  36.9 us (58%)
  waiting for transfers between devices  16.8 us (26%)
  Pallas kernels  7.87 us (12%)
  local copies, waits for them, and re-layouts  1.96 us (3%)
    ppermute x8, starting transfers between devices, hop(): return lax.ppermute(value, 'hor', pairs)  22.4 us
    ppermute x4, waiting for transfers between devices, shift_lev(): return lax.ppermute(value, 'lev', pairs)  6.7 us
    all_to_all x1, starting transfers between devices, on_device(): lists = lax.all_to_all(repeated, 'lev', 0, 0, tiled=True)  6.33 us
    ppermute x8, waiting for transfers between devices, hop(): return lax.ppermute(value, 'hor', pairs)  5.93 us
    pallas_call x5, Pallas kernels, gram(): pl.pallas_call(functools.partial(kernel, place), out_shape=[jax.ShapeDtyp...  5.12 us
    ppermute x1, starting transfers between devices, swap_cores(): return lax.ppermute(value, 'hor', [(i, i ^ 1) for i in range(N_HOR)])  4.72 us
    all_to_all x1, waiting for transfers between devices, on_device(): lists = lax.all_to_all(repeated, 'lev', 0, 0, tiled=True)  3.47 us
    ppermute x4, starting transfers between devices, shift_lev(): return lax.ppermute(value, 'lev', pairs)  3.4 us
  transfers between devices with their start and end apart: 14, of which 8 were waited for; matrix products, arithmetic and copies ran while one was open for 0% of the time, Pallas kernels for 8%

profile of v10, /device:TPU:1, one launch (start us, length us, event | category | flops | bytes accessed | tf_op | source)
XLA Modules:
  0.0 63.9 jit_solution(6105231338532815555)
XLA Ops:
  0.0 0.7 %copy-done.1 = s32[1,128]{1,0:T(1,128)S(1)} copy-done((s32[1,128]{1,0:T(1,128)S(1)}, s32[1,128]{1,0:T(1,128)}, u32[]{:S(2)}) %copy-start.1) | copy-done | bytes 536
  0.7 0.6 repeat.1
  1.3 6.3 %all-to-all-start = ((s32[8,1,128]{2,1,0:T(1,128)}), s32[8,1,128]{2,1,0:T(1,128)S(1)}, u32[]{:S(2)}, u32[]{:S(2)}) async-start(s32[8,1,128]{2,1,0:T(1,128)} %repeat.1), calls=%async_computation | async-start | bytes 8192 | tf_op jit(solution)/shard_map/all_to_all | solution.py:306
  7.7 1.2 %copy-done = f32[4,4,16384]{2,1,0:T(4,128)S(1)} copy-done((f32[4,4,16384]{2,1,0:T(4,128)S(1)}, f32[4,4,16384]{2,1,0:T(4,128)}, u32[]{:S(2)}) %copy-start) | copy-done | bytes 1048600
  9.0 3.5 %all-to-all-done.index_ref = s32[8,1,128]{2,1,0:T(1,128)S(1)} async-done(((s32[8,1,128]{2,1,0:T(1,128)}), s32[8,1,128]{2,1,0:T(1,128)S(1)}, u32[]{:S(2)}, u32[]{:S(2)}) %all-to-all-start) | async-done | bytes 4128 | tf_op jit(solution)/shard_map/all_to_all | solution.py:306
  12.5 0.4 pick.1
  12.9 0.4 collective-permute-start
  13.3 2.8 %collective-permute-done = f32[16,1024]{1,0:T(8,128)S(1)} collective-permute-done((f32[16,1024]{1,0:T(8,128)S(1)}, f32[16,1024]{1,0:T(8,128)S(1)}, u32[]{:S(2)}, u32[]{:S(2)}) %collective-permute-start) | collective-permute-done | bytes 65568 | tf_op jit(solution)/shard_map/ppermute | solution.py:37
  16.1 0.4 collective-permute-start.1
  16.5 1.8 %collective-permute-start.2 = (f32[2,16,1024]{2,1,0:T(8,128)S(1)}, f32[2,16,1024]{2,1,0:T(8,128)S(1)}, u32[]{:S(2)}, u32[]{:S(2)}) collective-permute-start(f32[2,16,1024]{2,1,0:T(8,128)S(1)} %pad_maximum_fusion.w0_ref), channel_id=1, source_target_pairs={{0,64},{32,96},{64,0},{96,32},{128,192},{160,224},{192,128},{224,1... | collective-permute-start | bytes 393224 | tf_op jit(solution)/shard_map/ppermute | solution.py:37
  18.3 0.9 %collective-permute-start.3 = (f32[2,16,1024]{2,1,0:T(8,128)S(1)}, f32[2,16,1024]{2,1,0:T(8,128)S(1)}, u32[]{:S(2)}, u32[]{:S(2)}) collective-permute-start(f32[2,16,1024]{2,1,0:T(8,128)S(1)} %pad_maximum_fusion.w0_ref), channel_id=1, source_target_pairs={{0,96},{32,0},{64,32},{96,64},{128,224},{160,128},{192,160},{224,1... | collective-permute-start | bytes 393224 | tf_op jit(solution)/shard_map/ppermute | solution.py:37
  19.3 3.3 %collective-permute-done.1.w1_ref = f32[2,16,1024]{2,1,0:T(8,128)S(1)} collective-permute-done((f32[2,16,1024]{2,1,0:T(8,128)S(1)}, f32[2,16,1024]{2,1,0:T(8,128)S(1)}, u32[]{:S(2)}, u32[]{:S(2)}) %collective-permute-start.1) | collective-permute-done | bytes 131104 | tf_op jit(solution)/shard_map/ppermute | solution.py:37
  22.6 0.6 collective-permute-done.3.w3_ref
  23.6 4.7 %collective-permute-start.4 = (f32[128,1024]{1,0:T(8,128)S(1)}, f32[128,1024]{1,0:T(8,128)S(1)}, u32[]{:S(2)}, u32[]{:S(2)}) collective-permute-start(f32[128,1024]{1,0:T(8,128)S(1)} %smooth.1.smooth_ref.own_ref), channel_id=1, source_target_pairs={{0,1},{1,0},{2,3},{3,2},{4,5},{5,4},{6,7},{7,6},{8,9},{9,8},{10,11... | collective-permute-start | bytes 1572872 | tf_op jit(solution)/shard_map/ppermute | solution.py:41
  28.6 0.7 %gram_far.2.part_ref = f32[304,272]{1,0:T(8,128)S(1)} custom-call(f32[128,1024]{1,0:T(8,128)S(1)} %smooth.1.smooth_ref.own_ref, bf16[272,1024]{1,0:T(8,128)(2,1)S(1)} %right.2.own_right_ref.right_ref), custom_call_target="tpu_custom_call" | custom-call | flops 1 | bytes 262144 | tf_op jit(solution)/shard_map/gram_far/pallas_call | solution.py:258
  29.3 0.6 %collective-permute-done.4.smooth_ref.other_ref = f32[128,1024]{1,0:T(8,128)S(1)} collective-permute-done((f32[128,1024]{1,0:T(8,128)S(1)}, f32[128,1024]{1,0:T(8,128)S(1)}, u32[]{:S(2)}, u32[]{:S(2)}) %collective-permute-start.4) | collective-permute-done | bytes 524320 | tf_op jit(solution)/shard_map/ppermute | solution.py:41
  30.1 0.8 %gram_far.3 = (f32[160,128]{1,0:T(8,128)S(1)}, f32[448,128]{1,0:T(8,128)S(1)}) custom-call(f32[304,272]{1,0:T(8,128)S(1)} %gram_far.2.part_ref, f32[128,1024]{1,0:T(8,128)S(1)} %collective-permute-done.4.smooth_ref.other_ref, bf16[272,1024]{1,0:T(8,128)(2,1)S(1)} %right.3.other_right_ref.right_ref), custom_call_target="tpu_custom_call" | custom-call | flops 1 | bytes 262144 | tf_op jit(solution)/shard_map/gram_far/pallas_call | solution.py:258
  31.0 2.8 %collective-permute-start.9 = (f32[160,128]{1,0:T(8,128)S(1)}, f32[160,128]{1,0:T(8,128)S(1)}, u32[]{:S(2)}, u32[]{:S(2)}) collective-permute-start(f32[160,128]{1,0:T(8,128)S(1)} %get-tuple-element.32), channel_id=1, source_target_pairs={{0,2},{1,7},{2,4},{3,1},{4,6},{5,3},{6,0},{7,5},{8,10},{9,15},{10,... | collective-permute-start | bytes 245768 | tf_op jit(solution)/shard_map/ppermute | solution.py:54
  33.8 1.2 %gram_cross.1 = f32[608,128]{1,0:T(8,128)S(1)} custom-call(f32[128,1024]{1,0:T(8,128)S(1)} %smooth.1.smooth_ref.own_ref, bf16[272,1024]{1,0:T(8,128)(2,1)S(1)} %right.2.own_right_ref.right_ref, f32[128,1024]{1,0:T(8,128)S(1)} %collective-permute-done.4.smooth_ref.other_ref, bf16[272,1024]{1,0:T(8,128)(2,1)S(1)} %right.3.other_right_ref.right_ref), custom_call_target="tpu_custom_call" | custom-call | flops 1 | bytes 262144 | tf_op jit(solution)/shard_map/gram_cross/pallas_call | solution.py:258
  35.0 0.5 collective-permute-start.5
  35.5 1.6 %collective-permute-start.6 = (f32[448,128]{1,0:T(8,128)S(1)}, f32[448,128]{1,0:T(8,128)S(1)}, u32[]{:S(2)}, u32[]{:S(2)}) collective-permute-start(f32[448,128]{1,0:T(8,128)S(1)} %get-tuple-element.26), channel_id=1, source_target_pairs={{0,2},{1,7},{2,4},{3,1},{4,6},{5,3},{6,0},{7,5},{8,10},{9,15},{10,... | collective-permute-start | bytes 688136 | tf_op jit(solution)/shard_map/ppermute | solution.py:54
  37.1 1.2 %gram_near.1 = (f32[160,128]{1,0:T(8,128)S(1)}, f32[448,128]{1,0:T(8,128)S(1)}) custom-call(f32[128,1024]{1,0:T(8,128)S(1)} %smooth.1.smooth_ref.own_ref, bf16[272,1024]{1,0:T(8,128)(2,1)S(1)} %right.2.own_right_ref.right_ref, f32[128,1024]{1,0:T(8,128)S(1)} %collective-permute-done.4.smooth_ref.other_ref, bf16[272,1024]{1,0:T(8,128)(2,1)S(1)} %right.3.other_right_ref.right_ref), custom_call_target="tpu_custom_call" | custom-call | flops 1 | bytes 262144 | tf_op jit(solution)/shard_map/gram_near/pallas_call | solution.py:258
  38.3 0.7 %collective-permute-start.10 = (f32[160,128]{1,0:T(8,128)S(1)}, f32[160,128]{1,0:T(8,128)S(1)}, u32[]{:S(2)}, u32[]{:S(2)}) collective-permute-start(f32[160,128]{1,0:T(8,128)S(1)} %add.20), channel_id=1, source_target_pairs={{0,2},{1,7},{2,4},{3,1},{4,6},{5,3},{6,0},{7,5},{8,10},{9,15},{10,... | collective-permute-start | bytes 245768 | tf_op jit(solution)/shard_map/ppermute | solution.py:54
  39.0 1.2 %gram_own.1.a_ref = f32[608,128]{1,0:T(8,128)S(1)} custom-call(f32[128,1024]{1,0:T(8,128)S(1)} %smooth.1.smooth_ref.own_ref, bf16[272,1024]{1,0:T(8,128)(2,1)S(1)} %right.2.own_right_ref.right_ref, f32[128,1024]{1,0:T(8,128)S(1)} %collective-permute-done.4.smooth_ref.other_ref, bf16[272,1024]{1,0:T(8,128)(2,1)S(1)} %right.3.other_right_ref.right_ref), custom_call_target="tpu_custom_call" | custom-call | flops 1 | bytes 262144 | tf_op jit(solution)/shard_map/gram_own/pallas_call | solution.py:258
  40.1 2.2 %collective-permute-done.6.b_ref = f32[448,128]{1,0:T(8,128)S(1)} collective-permute-done((f32[448,128]{1,0:T(8,128)S(1)}, f32[448,128]{1,0:T(8,128)S(1)}, u32[]{:S(2)}, u32[]{:S(2)}) %collective-permute-start.6) | collective-permute-done | bytes 229408 | tf_op jit(solution)/shard_map/ppermute | solution.py:54
  42.4 2.6 %collective-permute-start.7 = (f32[448,128]{1,0:T(8,128)S(1)}, f32[448,128]{1,0:T(8,128)S(1)}, u32[]{:S(2)}, u32[]{:S(2)}) collective-permute-start(f32[448,128]{1,0:T(8,128)S(1)} %add.18), channel_id=1, source_target_pairs={{0,2},{1,7},{2,4},{3,1},{4,6},{5,3},{6,0},{7,5},{8,10},{9,15},{10,... | collective-permute-start | bytes 688136 | tf_op jit(solution)/shard_map/ppermute | solution.py:54
  45.1 5.2 %collective-permute-start.11 = (f32[160,128]{1,0:T(8,128)S(1)}, f32[160,128]{1,0:T(8,128)S(1)}, u32[]{:S(2)}, u32[]{:S(2)}) collective-permute-start(f32[160,128]{1,0:T(8,128)S(1)} %add.21), channel_id=1, source_target_pairs={{0,8},{1,25},{2,10},{3,27},{4,12},{5,29},{6,14},{7,31},{8,16},{9,1... | collective-permute-start | bytes 245768 | tf_op jit(solution)/shard_map/ppermute | solution.py:54
  50.4 7.8 %collective-permute-start.8 = (f32[160,128]{1,0:T(8,128)S(1)}, f32[160,128]{1,0:T(8,128)S(1)}, u32[]{:S(2)}, u32[]{:S(2)}) collective-permute-start(f32[160,128]{1,0:T(8,128)S(1)} %get-tuple-element.28), channel_id=1, source_target_pairs={{0,9},{1,24},{2,11},{3,26},{4,13},{5,28},{6,15},{7,30},{8,17},{9,0... | collective-permute-start | bytes 245768 | tf_op jit(solution)/shard_map/ppermute | solution.py:54
  58.2 1.3 %collective-permute-start.12 = (f32[160,128]{1,0:T(8,128)S(1)}, f32[160,128]{1,0:T(8,128)S(1)}, u32[]{:S(2)}, u32[]{:S(2)}) collective-permute-start(f32[160,128]{1,0:T(8,128)S(1)} %add.22), channel_id=1, source_target_pairs={{0,8},{1,25},{2,10},{3,27},{4,12},{5,29},{6,14},{7,31},{8,16},{9,1... | collective-permute-start | bytes 245768 | tf_op jit(solution)/shard_map/ppermute | solution.py:54
  59.5 1.9 %collective-permute-done.8.b_ref = f32[160,128]{1,0:T(8,128)S(1)} collective-permute-done((f32[160,128]{1,0:T(8,128)S(1)}, f32[160,128]{1,0:T(8,128)S(1)}, u32[]{:S(2)}, u32[]{:S(2)}) %collective-permute-start.8) | collective-permute-done | bytes 81952 | tf_op jit(solution)/shard_map/ppermute | solution.py:54
  61.3 1.8 %collective-permute-done.12.near_ref = f32[160,128]{1,0:T(8,128)S(1)} collective-permute-done((f32[160,128]{1,0:T(8,128)S(1)}, f32[160,128]{1,0:T(8,128)S(1)}, u32[]{:S(2)}, u32[]{:S(2)}) %collective-permute-start.12) | collective-permute-done | bytes 81952 | tf_op jit(solution)/shard_map/ppermute | solution.py:54
  63.2 0.7 %final.1 = f32[68,272]{1,0:T(8,128)} custom-call(f32[160,128]{1,0:T(8,128)S(1)} %add.19.kept_ref, f32[160,128]{1,0:T(8,128)S(1)} %collective-permute-done.12.near_ref), custom_call_target="tpu_custom_call" | custom-call | flops 1 | bytes 262144 | tf_op jit(solution)/shard_map/final/pallas_call | solution.py:367
  (30 shorter events, 1.5 us)
Async XLA Ops:
  0.0 0.7 %copy-start.1 = (s32[1,128]{1,0:T(1,128)S(1)}, s32[1,128]{1,0:T(1,128)}, u32[]{:S(2)}) copy-start(s32[1,128]{1,0:T(1,128)} %index_ref.1) | copy-start | bytes 1540
  1.3 6.3 %copy-start.2 = (f32[32]{0:T(128)S(1)}, f32[32]{0:T(128)}, u32[]{:S(2)}) copy-start(f32[32]{0:T(128)} %param.6) | copy-start | bytes 388
  1.3 6.3 %copy-start.3 = (s32[31]{0:T(128)S(1)}, s32[31]{0:T(128)}, u32[]{:S(2)}) copy-start(s32[31]{0:T(128)} %param.7) | copy-start | bytes 376
  1.3 11.3 %all-to-all-start = ((s32[8,1,128]{2,1,0:T(1,128)}), s32[8,1,128]{2,1,0:T(1,128)S(1)}, u32[]{:S(2)}, u32[]{:S(2)}) async-start(s32[8,1,128]{2,1,0:T(1,128)} %repeat.1), calls=%async_computation | async-start | bytes 8192 | tf_op jit(solution)/shard_map/all_to_all | solution.py:306
  7.7 1.2 %copy-start = (f32[4,4,16384]{2,1,0:T(4,128)S(1)}, f32[4,4,16384]{2,1,0:T(4,128)}, u32[]{:S(2)}) copy-start(f32[4,4,16384]{2,1,0:T(4,128)} %slab_ref.1) | copy-start | bytes 3145732
  12.9 3.2 %collective-permute-start = (f32[16,1024]{1,0:T(8,128)S(1)}, f32[16,1024]{1,0:T(8,128)S(1)}, u32[]{:S(2)}, u32[]{:S(2)}) collective-permute-start(f32[16,1024]{1,0:T(8,128)S(1)} %pick.1), channel_id=1, source_target_pairs={{0,128},{32,160},{64,192},{96,224},{128,0},{160,32},{192,64},{224,... | collective-permute-start | bytes 196616 | tf_op jit(solution)/shard_map/ppermute | solution.py:37
  16.1 6.5 %collective-permute-start.1 = (f32[2,16,1024]{2,1,0:T(8,128)S(1)}, f32[2,16,1024]{2,1,0:T(8,128)S(1)}, u32[]{:S(2)}, u32[]{:S(2)}) collective-permute-start(f32[2,16,1024]{2,1,0:T(8,128)S(1)} %pad_maximum_fusion.w0_ref), channel_id=1, source_target_pairs={{0,32},{32,64},{64,96},{96,0},{128,160},{160,192},{192,224},{224,1... | collective-permute-start | bytes 393224 | tf_op jit(solution)/shard_map/ppermute | solution.py:37
  16.5 6.2 %collective-permute-start.2 = (f32[2,16,1024]{2,1,0:T(8,128)S(1)}, f32[2,16,1024]{2,1,0:T(8,128)S(1)}, u32[]{:S(2)}, u32[]{:S(2)}) collective-permute-start(f32[2,16,1024]{2,1,0:T(8,128)S(1)} %pad_maximum_fusion.w0_ref), channel_id=1, source_target_pairs={{0,64},{32,96},{64,0},{96,32},{128,192},{160,224},{192,128},{224,1... | collective-permute-start | bytes 393224 | tf_op jit(solution)/shard_map/ppermute | solution.py:37
  18.3 5.0 %collective-permute-start.3 = (f32[2,16,1024]{2,1,0:T(8,128)S(1)}, f32[2,16,1024]{2,1,0:T(8,128)S(1)}, u32[]{:S(2)}, u32[]{:S(2)}) collective-permute-start(f32[2,16,1024]{2,1,0:T(8,128)S(1)} %pad_maximum_fusion.w0_ref), channel_id=1, source_target_pairs={{0,96},{32,0},{64,32},{96,64},{128,224},{160,128},{192,160},{224,1... | collective-permute-start | bytes 393224 | tf_op jit(solution)/shard_map/ppermute | solution.py:37
  23.6 6.3 %collective-permute-start.4 = (f32[128,1024]{1,0:T(8,128)S(1)}, f32[128,1024]{1,0:T(8,128)S(1)}, u32[]{:S(2)}, u32[]{:S(2)}) collective-permute-start(f32[128,1024]{1,0:T(8,128)S(1)} %smooth.1.smooth_ref.own_ref), channel_id=1, source_target_pairs={{0,1},{1,0},{2,3},{3,2},{4,5},{5,4},{6,7},{7,6},{8,9},{9,8},{10,11... | collective-permute-start | bytes 1572872 | tf_op jit(solution)/shard_map/ppermute | solution.py:41
  31.0 7.3 %collective-permute-start.9 = (f32[160,128]{1,0:T(8,128)S(1)}, f32[160,128]{1,0:T(8,128)S(1)}, u32[]{:S(2)}, u32[]{:S(2)}) collective-permute-start(f32[160,128]{1,0:T(8,128)S(1)} %get-tuple-element.32), channel_id=1, source_target_pairs={{0,2},{1,7},{2,4},{3,1},{4,6},{5,3},{6,0},{7,5},{8,10},{9,15},{10,... | collective-permute-start | bytes 245768 | tf_op jit(solution)/shard_map/ppermute | solution.py:54
  35.0 10.1 %collective-permute-start.5 = (f32[608,128]{1,0:T(8,128)S(1)}, f32[608,128]{1,0:T(8,128)S(1)}, u32[]{:S(2)}, u32[]{:S(2)}) collective-permute-start(f32[608,128]{1,0:T(8,128)S(1)} %gram_cross.1), channel_id=1, source_target_pairs={{0,3},{1,6},{2,5},{3,0},{4,7},{5,2},{6,1},{7,4},{8,11},{9,14},{10,... | collective-permute-start | bytes 933896 | tf_op jit(solution)/shard_map/ppermute | solution.py:54
  35.5 6.9 %collective-permute-start.6 = (f32[448,128]{1,0:T(8,128)S(1)}, f32[448,128]{1,0:T(8,128)S(1)}, u32[]{:S(2)}, u32[]{:S(2)}) collective-permute-start(f32[448,128]{1,0:T(8,128)S(1)} %get-tuple-element.26), channel_id=1, source_target_pairs={{0,2},{1,7},{2,4},{3,1},{4,6},{5,3},{6,0},{7,5},{8,10},{9,15},{10,... | collective-permute-start | bytes 688136 | tf_op jit(solution)/shard_map/ppermute | solution.py:54
  38.3 6.8 %collective-permute-start.10 = (f32[160,128]{1,0:T(8,128)S(1)}, f32[160,128]{1,0:T(8,128)S(1)}, u32[]{:S(2)}, u32[]{:S(2)}) collective-permute-start(f32[160,128]{1,0:T(8,128)S(1)} %add.20), channel_id=1, source_target_pairs={{0,2},{1,7},{2,4},{3,1},{4,6},{5,3},{6,0},{7,5},{8,10},{9,15},{10,... | collective-permute-start | bytes 245768 | tf_op jit(solution)/shard_map/ppermute | solution.py:54
  42.4 7.9 %collective-permute-start.7 = (f32[448,128]{1,0:T(8,128)S(1)}, f32[448,128]{1,0:T(8,128)S(1)}, u32[]{:S(2)}, u32[]{:S(2)}) collective-permute-start(f32[448,128]{1,0:T(8,128)S(1)} %add.18), channel_id=1, source_target_pairs={{0,2},{1,7},{2,4},{3,1},{4,6},{5,3},{6,0},{7,5},{8,10},{9,15},{10,... | collective-permute-start | bytes 688136 | tf_op jit(solution)/shard_map/ppermute | solution.py:54
  45.1 13.1 %collective-permute-start.11 = (f32[160,128]{1,0:T(8,128)S(1)}, f32[160,128]{1,0:T(8,128)S(1)}, u32[]{:S(2)}, u32[]{:S(2)}) collective-permute-start(f32[160,128]{1,0:T(8,128)S(1)} %add.21), channel_id=1, source_target_pairs={{0,8},{1,25},{2,10},{3,27},{4,12},{5,29},{6,14},{7,31},{8,16},{9,1... | collective-permute-start | bytes 245768 | tf_op jit(solution)/shard_map/ppermute | solution.py:54
  50.4 10.9 %collective-permute-start.8 = (f32[160,128]{1,0:T(8,128)S(1)}, f32[160,128]{1,0:T(8,128)S(1)}, u32[]{:S(2)}, u32[]{:S(2)}) collective-permute-start(f32[160,128]{1,0:T(8,128)S(1)} %get-tuple-element.28), channel_id=1, source_target_pairs={{0,9},{1,24},{2,11},{3,26},{4,13},{5,28},{6,15},{7,30},{8,17},{9,0... | collective-permute-start | bytes 245768 | tf_op jit(solution)/shard_map/ppermute | solution.py:54
  58.2 5.0 %collective-permute-start.12 = (f32[160,128]{1,0:T(8,128)S(1)}, f32[160,128]{1,0:T(8,128)S(1)}, u32[]{:S(2)}, u32[]{:S(2)}) collective-permute-start(f32[160,128]{1,0:T(8,128)S(1)} %add.22), channel_id=1, source_target_pairs={{0,8},{1,25},{2,10},{3,27},{4,12},{5,29},{6,14},{7,31},{8,16},{9,1... | collective-permute-start | bytes 245768 | tf_op jit(solution)/shard_map/ppermute | solution.py:54

commit v11 on v6

--- a/solution.py
+++ b/solution.py
@@ -78,7 +78,7 @@
             out_ref[rows, group * SAMP : (group + 1) * SAMP] = total
 
 
-def smooth_kernel(coef_ref, w0_ref, w1_ref, w2_ref, w3_ref, out_ref, raw_ref):
+def smooth_kernel(coef_ref, w0_ref, w2_ref, w1_ref, w3_ref, out_ref, raw_ref):
     x = lax.axis_index("lev") % N_X
     for step, ref in enumerate((w0_ref, w1_ref, w2_ref, w3_ref)):
         source = lax.rem(x - step + N_X, N_X)
@@ -295,7 +295,7 @@
         out_shape=jax.ShapeDtypeStruct((N_LEV, 1, SAMP), jnp.int32),
         in_specs=[VMEM],
         out_specs=VMEM,
-        compiler_params=params(1),
+        compiler_params=params(60),
         name="repeat",
     )(sample_index)
     lists = lax.all_to_all(repeated, "lev", 0, 0, tiled=True)
@@ -328,7 +328,7 @@
         scratch_shapes=[pltpu.VMEM((N_LEV, 4 * SLOTS, BLOCK), f32)],
         compiler_params=params(16),
         name="smooth",
-    )(coef, near, far[1], far[2], far[3])
+    )(coef, near, far[2], far[1], far[3])
     other = swap_cores(own)
     own_right = right_of(own)
     begun = gram(begin_kernel, "far", (BUILT, COLS_OUT), own, own_right)

time: 60 us -> 59.5 us (level)
  waiting for transfers between devices: 29.4 us -> 28.3 us
  local copies, waits for them, and re-layouts: 1.96 us -> 1.3 us
  Pallas kernels: 7.89 us -> 8.54 us
  starting transfers between devices: 20.2 us -> 20.8 us
    ppermute x4, waiting for transfers between devices: 9.91 us -> 8.77 us  [shift_lev(): return lax.ppermute(value, 'lev', pairs)]
    unnamed x8 -> x6, local copies, waits for them, and re-layouts: 1.89 us -> 1.23 us
    pallas_call x1, Pallas kernels: 0.59 us -> 1.25 us  [on_device(): pl.pallas_call(repeat_kernel, out_shape=jax.ShapeDtypeStruct((N_LEV, 1, S...]
    ppermute x4, starting transfers between devices: 4.23 us -> 4.84 us  [shift_lev(): return lax.ppermute(value, 'lev', pairs)]
where the time goes in v11:
time: 59.5 us; the launch traced here: 59.3 us
  waiting for transfers between devices  28.3 us (48%)
  starting transfers between devices  20.8 us (35%)
  Pallas kernels  8.54 us (14%)
  local copies, waits for them, and re-layouts  1.3 us (2%)
    ppermute x7, waiting for transfers between devices, hop(): return lax.ppermute(value, 'hor', pairs)  15.9 us
    ppermute x7, starting transfers between devices, hop(): return lax.ppermute(value, 'hor', pairs)  9.58 us
    ppermute x4, waiting for transfers between devices, shift_lev(): return lax.ppermute(value, 'lev', pairs)  8.77 us
    all_to_all x1, starting transfers between devices, on_device(): lists = lax.all_to_all(repeated, 'lev', 0, 0, tiled=True)  6.26 us
    pallas_call x5, Pallas kernels, gram(): pl.pallas_call(functools.partial(kernel, place), out_shape=jax.ShapeDtype...  5.12 us
    ppermute x4, starting transfers between devices, shift_lev(): return lax.ppermute(value, 'lev', pairs)  4.84 us
    all_to_all x1, waiting for transfers between devices, on_device(): lists = lax.all_to_all(repeated, 'lev', 0, 0, tiled=True)  2.57 us
    pallas_call x1, Pallas kernels, on_device(): pl.pallas_call(repeat_kernel, out_shape=jax.ShapeDtypeStruct((N_LEV, 1, S...  1.25 us
  transfers between devices with their start and end apart: 13, of which 10 were waited for; matrix products, arithmetic and copies ran while one was open for 1% of the time, Pallas kernels for 8%

profile of v11, /device:TPU:6, one launch (start us, length us, event | category | flops | bytes accessed | tf_op | source)
XLA Modules:
  0.0 59.3 jit_solution(7496025730778905090)
XLA Ops:
  0.0 1.2 %repeat.1 = s32[8,1,128]{2,1,0:T(1,128)} custom-call(s32[1,128]{1,0:T(1,128)} %index_ref.1), custom_call_target="tpu_custom_call" | custom-call | tf_op jit(solution)/shard_map/repeat/pallas_call | solution.py:293
  1.3 6.3 %all-to-all-start = ((s32[8,1,128]{2,1,0:T(1,128)}), s32[8,1,128]{2,1,0:T(1,128)S(1)}, u32[]{:S(2)}, u32[]{:S(2)}) async-start(s32[8,1,128]{2,1,0:T(1,128)} %repeat.1), calls=%async_computation | async-start | bytes 8192 | tf_op jit(solution)/shard_map/all_to_all | solution.py:301
  7.6 1.2 %copy-done = f32[4,4,16384]{2,1,0:T(4,128)S(1)} copy-done((f32[4,4,16384]{2,1,0:T(4,128)S(1)}, f32[4,4,16384]{2,1,0:T(4,128)}, u32[]{:S(2)}) %copy-start) | copy-done | bytes 1048600
  9.0 2.6 %all-to-all-done.index_ref = s32[8,1,128]{2,1,0:T(1,128)S(1)} async-done(((s32[8,1,128]{2,1,0:T(1,128)}), s32[8,1,128]{2,1,0:T(1,128)S(1)}, u32[]{:S(2)}, u32[]{:S(2)}) %all-to-all-start) | async-done | bytes 4128 | tf_op jit(solution)/shard_map/all_to_all | solution.py:301
  11.5 0.4 pick.1
  11.9 0.7 %collective-permute-start = (f32[16,1024]{1,0:T(8,128)S(1)}, f32[16,1024]{1,0:T(8,128)S(1)}, u32[]{:S(2)}, u32[]{:S(2)}) collective-permute-start(f32[16,1024]{1,0:T(8,128)S(1)} %pick.1), channel_id=1, source_target_pairs={{0,128},{32,160},{64,192},{96,224},{128,0},{160,32},{192,64},{224,... | collective-permute-start | bytes 196616 | tf_op jit(solution)/shard_map/ppermute | solution.py:37
  12.6 3.6 %collective-permute-done = f32[16,1024]{1,0:T(8,128)S(1)} collective-permute-done((f32[16,1024]{1,0:T(8,128)S(1)}, f32[16,1024]{1,0:T(8,128)S(1)}, u32[]{:S(2)}, u32[]{:S(2)}) %collective-permute-start) | collective-permute-done | bytes 65568 | tf_op jit(solution)/shard_map/ppermute | solution.py:37
  16.3 2.2 %collective-permute-start.1 = (f32[2,16,1024]{2,1,0:T(8,128)S(1)}, f32[2,16,1024]{2,1,0:T(8,128)S(1)}, u32[]{:S(2)}, u32[]{:S(2)}) collective-permute-start(f32[2,16,1024]{2,1,0:T(8,128)S(1)} %pad_maximum_fusion.w0_ref), channel_id=1, source_target_pairs={{0,64},{32,96},{64,0},{96,32},{128,192},{160,224},{192,128},{224,1... | collective-permute-start | bytes 393224 | tf_op jit(solution)/shard_map/ppermute | solution.py:37
  18.4 1.2 %collective-permute-start.2 = (f32[2,16,1024]{2,1,0:T(8,128)S(1)}, f32[2,16,1024]{2,1,0:T(8,128)S(1)}, u32[]{:S(2)}, u32[]{:S(2)}) collective-permute-start(f32[2,16,1024]{2,1,0:T(8,128)S(1)} %pad_maximum_fusion.w0_ref), channel_id=1, source_target_pairs={{0,32},{32,64},{64,96},{96,0},{128,160},{160,192},{192,224},{224,1... | collective-permute-start | bytes 393224 | tf_op jit(solution)/shard_map/ppermute | solution.py:37
  19.6 0.9 %collective-permute-start.3 = (f32[2,16,1024]{2,1,0:T(8,128)S(1)}, f32[2,16,1024]{2,1,0:T(8,128)S(1)}, u32[]{:S(2)}, u32[]{:S(2)}) collective-permute-start(f32[2,16,1024]{2,1,0:T(8,128)S(1)} %pad_maximum_fusion.w0_ref), channel_id=1, source_target_pairs={{0,96},{32,0},{64,32},{96,64},{128,224},{160,128},{192,160},{224,1... | collective-permute-start | bytes 393224 | tf_op jit(solution)/shard_map/ppermute | solution.py:37
  20.6 2.3 %collective-permute-done.1.w2_ref = f32[2,16,1024]{2,1,0:T(8,128)S(1)} collective-permute-done((f32[2,16,1024]{2,1,0:T(8,128)S(1)}, f32[2,16,1024]{2,1,0:T(8,128)S(1)}, u32[]{:S(2)}, u32[]{:S(2)}) %collective-permute-start.1) | collective-permute-done | bytes 131104 | tf_op jit(solution)/shard_map/ppermute | solution.py:37
  22.9 0.7 %collective-permute-done.2.w1_ref = f32[2,16,1024]{2,1,0:T(8,128)S(1)} collective-permute-done((f32[2,16,1024]{2,1,0:T(8,128)S(1)}, f32[2,16,1024]{2,1,0:T(8,128)S(1)}, u32[]{:S(2)}, u32[]{:S(2)}) %collective-permute-start.2) | collective-permute-done | bytes 131104 | tf_op jit(solution)/shard_map/ppermute | solution.py:37
  23.6 2.1 %collective-permute-done.3.w3_ref = f32[2,16,1024]{2,1,0:T(8,128)S(1)} collective-permute-done((f32[2,16,1024]{2,1,0:T(8,128)S(1)}, f32[2,16,1024]{2,1,0:T(8,128)S(1)}, u32[]{:S(2)}, u32[]{:S(2)}) %collective-permute-start.3) | collective-permute-done | bytes 131104 | tf_op jit(solution)/shard_map/ppermute | solution.py:37
  25.9 0.3 smooth.1.smooth_ref.own_ref
  26.3 0.2 right.2.own_right_ref.right_ref
  26.5 0.7 %gram_far.2.part_ref = f32[304,272]{1,0:T(8,128)S(1)} custom-call(f32[128,1024]{1,0:T(8,128)S(1)} %smooth.1.smooth_ref.own_ref, bf16[272,1024]{1,0:T(8,128)(2,1)S(1)} %right.2.own_right_ref.right_ref), custom_call_target="tpu_custom_call" | custom-call | flops 1 | bytes 262144 | tf_op jit(solution)/shard_map/gram_far/pallas_call | solution.py:253
  27.2 1.0 %collective-permute-done.4.smooth_ref.other_ref = f32[128,1024]{1,0:T(8,128)S(1)} collective-permute-done((f32[128,1024]{1,0:T(8,128)S(1)}, f32[128,1024]{1,0:T(8,128)S(1)}, u32[]{:S(2)}, u32[]{:S(2)}) %collective-permute-start.4) | collective-permute-done | bytes 524320 | tf_op jit(solution)/shard_map/ppermute | solution.py:41
  28.4 0.9 %gram_far.3 = f32[608,128]{1,0:T(8,128)S(1)} custom-call(f32[304,272]{1,0:T(8,128)S(1)} %gram_far.2.part_ref, f32[128,1024]{1,0:T(8,128)S(1)} %collective-permute-done.4.smooth_ref.other_ref, bf16[272,1024]{1,0:T(8,128)(2,1)S(1)} %right.3.other_right_ref.right_ref), custom_call_target="tpu_custom_call" | custom-call | flops 1 | bytes 262144 | tf_op jit(solution)/shard_map/gram_far/pallas_call | solution.py:253
  29.2 1.6 %collective-permute-start.6 = (f32[608,128]{1,0:T(8,128)S(1)}, f32[608,128]{1,0:T(8,128)S(1)}, u32[]{:S(2)}, u32[]{:S(2)}) collective-permute-start(f32[608,128]{1,0:T(8,128)S(1)} %gram_far.3), channel_id=1, source_target_pairs={{0,2},{1,7},{2,4},{3,1},{4,6},{5,3},{6,0},{7,5},{8,10},{9,15},{10,... | collective-permute-start | bytes 933896 | tf_op jit(solution)/shard_map/ppermute | solution.py:54
  30.9 1.2 %gram_cross.1 = f32[608,128]{1,0:T(8,128)S(1)} custom-call(f32[128,1024]{1,0:T(8,128)S(1)} %smooth.1.smooth_ref.own_ref, bf16[272,1024]{1,0:T(8,128)(2,1)S(1)} %right.2.own_right_ref.right_ref, f32[128,1024]{1,0:T(8,128)S(1)} %collective-permute-done.4.smooth_ref.other_ref, bf16[272,1024]{1,0:T(8,128)(2,1)S(1)} %right.3.other_right_ref.right_ref), custom_call_target="tpu_custom_call" | custom-call | flops 1 | bytes 262144 | tf_op jit(solution)/shard_map/gram_cross/pallas_call | solution.py:253
  32.2 1.2 %gram_near.1.a_ref = f32[608,128]{1,0:T(8,128)S(1)} custom-call(f32[128,1024]{1,0:T(8,128)S(1)} %smooth.1.smooth_ref.own_ref, bf16[272,1024]{1,0:T(8,128)(2,1)S(1)} %right.2.own_right_ref.right_ref, f32[128,1024]{1,0:T(8,128)S(1)} %collective-permute-done.4.smooth_ref.other_ref, bf16[272,1024]{1,0:T(8,128)(2,1)S(1)} %right.3.other_right_ref.right_ref), custom_call_target="tpu_custom_call" | custom-call | flops 1 | bytes 262144 | tf_op jit(solution)/shard_map/gram_near/pallas_call | solution.py:253
  33.4 4.0 %collective-permute-done.6.b_ref = f32[608,128]{1,0:T(8,128)S(1)} collective-permute-done((f32[608,128]{1,0:T(8,128)S(1)}, f32[608,128]{1,0:T(8,128)S(1)}, u32[]{:S(2)}, u32[]{:S(2)}) %collective-permute-start.6) | collective-permute-done | bytes 311328 | tf_op jit(solution)/shard_map/ppermute | solution.py:54
  37.4 0.5 collective-permute-start.9
  37.9 1.6 %collective-permute-start.7 = (f32[448,128]{1,0:T(8,128)S(1)}, f32[448,128]{1,0:T(8,128)S(1)}, u32[]{:S(2)}, u32[]{:S(2)}) collective-permute-start(f32[448,128]{1,0:T(8,128)S(1)} %get-tuple-element.23), channel_id=1, source_target_pairs={{0,2},{1,7},{2,4},{3,1},{4,6},{5,3},{6,0},{7,5},{8,10},{9,15},{10,... | collective-permute-start | bytes 688136 | tf_op jit(solution)/shard_map/ppermute | solution.py:54
  39.4 1.2 %gram_own.1.a_ref = f32[608,128]{1,0:T(8,128)S(1)} custom-call(f32[128,1024]{1,0:T(8,128)S(1)} %smooth.1.smooth_ref.own_ref, bf16[272,1024]{1,0:T(8,128)(2,1)S(1)} %right.2.own_right_ref.right_ref, f32[128,1024]{1,0:T(8,128)S(1)} %collective-permute-done.4.smooth_ref.other_ref, bf16[272,1024]{1,0:T(8,128)(2,1)S(1)} %right.3.other_right_ref.right_ref), custom_call_target="tpu_custom_call" | custom-call | flops 1 | bytes 262144 | tf_op jit(solution)/shard_map/gram_own/pallas_call | solution.py:253
  40.7 2.5 %collective-permute-done.9.b_ref = f32[160,128]{1,0:T(8,128)S(1)} collective-permute-done((f32[160,128]{1,0:T(8,128)S(1)}, f32[160,128]{1,0:T(8,128)S(1)}, u32[]{:S(2)}, u32[]{:S(2)}) %collective-permute-start.9) | collective-permute-done | bytes 81952 | tf_op jit(solution)/shard_map/ppermute | solution.py:54
  43.2 3.3 %collective-permute-start.10 = (f32[160,128]{1,0:T(8,128)S(1)}, f32[160,128]{1,0:T(8,128)S(1)}, u32[]{:S(2)}, u32[]{:S(2)}) collective-permute-start(f32[160,128]{1,0:T(8,128)S(1)} %add.15), channel_id=1, source_target_pairs={{0,8},{1,25},{2,10},{3,27},{4,12},{5,29},{6,14},{7,31},{8,16},{9,1... | collective-permute-start | bytes 245768 | tf_op jit(solution)/shard_map/ppermute | solution.py:54
  46.6 0.8 %collective-permute-start.8 = (f32[160,128]{1,0:T(8,128)S(1)}, f32[160,128]{1,0:T(8,128)S(1)}, u32[]{:S(2)}, u32[]{:S(2)}) collective-permute-start(f32[160,128]{1,0:T(8,128)S(1)} %get-tuple-element.25), channel_id=1, source_target_pairs={{0,9},{1,24},{2,11},{3,26},{4,13},{5,28},{6,15},{7,30},{8,17},{9,0... | collective-permute-start | bytes 245768 | tf_op jit(solution)/shard_map/ppermute | solution.py:54
  47.4 3.7 %collective-permute-done.10.b_ref = f32[160,128]{1,0:T(8,128)S(1)} collective-permute-done((f32[160,128]{1,0:T(8,128)S(1)}, f32[160,128]{1,0:T(8,128)S(1)}, u32[]{:S(2)}, u32[]{:S(2)}) %collective-permute-start.10) | collective-permute-done | bytes 81952 | tf_op jit(solution)/shard_map/ppermute | solution.py:54
  51.1 1.7 %collective-permute-start.11 = (f32[160,128]{1,0:T(8,128)S(1)}, f32[160,128]{1,0:T(8,128)S(1)}, u32[]{:S(2)}, u32[]{:S(2)}) collective-permute-start(f32[160,128]{1,0:T(8,128)S(1)} %add.16), channel_id=1, source_target_pairs={{0,8},{1,25},{2,10},{3,27},{4,12},{5,29},{6,14},{7,31},{8,16},{9,1... | collective-permute-start | bytes 245768 | tf_op jit(solution)/shard_map/ppermute | solution.py:54
  52.8 5.8 %collective-permute-done.11.t2_ref = f32[160,128]{1,0:T(8,128)S(1)} collective-permute-done((f32[160,128]{1,0:T(8,128)S(1)}, f32[160,128]{1,0:T(8,128)S(1)}, u32[]{:S(2)}, u32[]{:S(2)}) %collective-permute-start.11) | collective-permute-done | bytes 81952 | tf_op jit(solution)/shard_map/ppermute | solution.py:54
  58.6 0.7 %final.1 = f32[68,272]{1,0:T(8,128)} custom-call(f32[160,128]{1,0:T(8,128)S(1)} %get-tuple-element.24.t0_ref, f32[160,128]{1,0:T(8,128)S(1)} %collective-permute-done.8.t1_ref, f32[160,128]{1,0:T(8,128)S(1)} %collective-permute-done.11.t2_ref), custom_call_target="tpu_custom_call" | custom-call | flops 1 | bytes 262144 | tf_op jit(solution)/shard_map/final/pallas_call | solution.py:360
  (24 shorter events, 1.1 us)
Async XLA Ops:
  1.2 6.3 %copy-start.1 = (f32[32]{0:T(128)S(1)}, f32[32]{0:T(128)}, u32[]{:S(2)}) copy-start(f32[32]{0:T(128)} %param.6) | copy-start | bytes 388
  1.3 6.3 %copy-start.2 = (s32[31]{0:T(128)S(1)}, s32[31]{0:T(128)}, u32[]{:S(2)}) copy-start(s32[31]{0:T(128)} %param.7) | copy-start | bytes 376
  1.3 10.3 %all-to-all-start = ((s32[8,1,128]{2,1,0:T(1,128)}), s32[8,1,128]{2,1,0:T(1,128)S(1)}, u32[]{:S(2)}, u32[]{:S(2)}) async-start(s32[8,1,128]{2,1,0:T(1,128)} %repeat.1), calls=%async_computation | async-start | bytes 8192 | tf_op jit(solution)/shard_map/all_to_all | solution.py:301
  7.6 1.2 %copy-start = (f32[4,4,16384]{2,1,0:T(4,128)S(1)}, f32[4,4,16384]{2,1,0:T(4,128)}, u32[]{:S(2)}) copy-start(f32[4,4,16384]{2,1,0:T(4,128)} %slab_ref.1) | copy-start | bytes 3145732
  11.9 4.4 %collective-permute-start = (f32[16,1024]{1,0:T(8,128)S(1)}, f32[16,1024]{1,0:T(8,128)S(1)}, u32[]{:S(2)}, u32[]{:S(2)}) collective-permute-start(f32[16,1024]{1,0:T(8,128)S(1)} %pick.1), channel_id=1, source_target_pairs={{0,128},{32,160},{64,192},{96,224},{128,0},{160,32},{192,64},{224,... | collective-permute-start | bytes 196616 | tf_op jit(solution)/shard_map/ppermute | solution.py:37
  16.3 6.6 %collective-permute-start.1 = (f32[2,16,1024]{2,1,0:T(8,128)S(1)}, f32[2,16,1024]{2,1,0:T(8,128)S(1)}, u32[]{:S(2)}, u32[]{:S(2)}) collective-permute-start(f32[2,16,1024]{2,1,0:T(8,128)S(1)} %pad_maximum_fusion.w0_ref), channel_id=1, source_target_pairs={{0,64},{32,96},{64,0},{96,32},{128,192},{160,224},{192,128},{224,1... | collective-permute-start | bytes 393224 | tf_op jit(solution)/shard_map/ppermute | solution.py:37
  18.4 5.2 %collective-permute-start.2 = (f32[2,16,1024]{2,1,0:T(8,128)S(1)}, f32[2,16,1024]{2,1,0:T(8,128)S(1)}, u32[]{:S(2)}, u32[]{:S(2)}) collective-permute-start(f32[2,16,1024]{2,1,0:T(8,128)S(1)} %pad_maximum_fusion.w0_ref), channel_id=1, source_target_pairs={{0,32},{32,64},{64,96},{96,0},{128,160},{160,192},{192,224},{224,1... | collective-permute-start | bytes 393224 | tf_op jit(solution)/shard_map/ppermute | solution.py:37
  19.6 6.2 %collective-permute-start.3 = (f32[2,16,1024]{2,1,0:T(8,128)S(1)}, f32[2,16,1024]{2,1,0:T(8,128)S(1)}, u32[]{:S(2)}, u32[]{:S(2)}) collective-permute-start(f32[2,16,1024]{2,1,0:T(8,128)S(1)} %pad_maximum_fusion.w0_ref), channel_id=1, source_target_pairs={{0,96},{32,0},{64,32},{96,64},{128,224},{160,128},{192,160},{224,1... | collective-permute-start | bytes 393224 | tf_op jit(solution)/shard_map/ppermute | solution.py:37
  26.2 2.0 %collective-permute-start.4 = (f32[128,1024]{1,0:T(8,128)S(1)}, f32[128,1024]{1,0:T(8,128)S(1)}, u32[]{:S(2)}, u32[]{:S(2)}) collective-permute-start(f32[128,1024]{1,0:T(8,128)S(1)} %smooth.1.smooth_ref.own_ref), channel_id=1, source_target_pairs={{0,1},{1,0},{2,3},{3,2},{4,5},{5,4},{6,7},{7,6},{8,9},{9,8},{10,11... | collective-permute-start | bytes 1572872 | tf_op jit(solution)/shard_map/ppermute | solution.py:41
  29.2 8.1 %collective-permute-start.6 = (f32[608,128]{1,0:T(8,128)S(1)}, f32[608,128]{1,0:T(8,128)S(1)}, u32[]{:S(2)}, u32[]{:S(2)}) collective-permute-start(f32[608,128]{1,0:T(8,128)S(1)} %gram_far.3), channel_id=1, source_target_pairs={{0,2},{1,7},{2,4},{3,1},{4,6},{5,3},{6,0},{7,5},{8,10},{9,15},{10,... | collective-permute-start | bytes 933896 | tf_op jit(solution)/shard_map/ppermute | solution.py:54
  32.1 8.5 %collective-permute-start.5 = (f32[608,128]{1,0:T(8,128)S(1)}, f32[608,128]{1,0:T(8,128)S(1)}, u32[]{:S(2)}, u32[]{:S(2)}) collective-permute-start(f32[608,128]{1,0:T(8,128)S(1)} %gram_cross.1), channel_id=1, source_target_pairs={{0,3},{1,6},{2,5},{3,0},{4,7},{5,2},{6,1},{7,4},{8,11},{9,14},{10,... | collective-permute-start | bytes 933896 | tf_op jit(solution)/shard_map/ppermute | solution.py:54
  37.4 5.7 %collective-permute-start.9 = (f32[160,128]{1,0:T(8,128)S(1)}, f32[160,128]{1,0:T(8,128)S(1)}, u32[]{:S(2)}, u32[]{:S(2)}) collective-permute-start(f32[160,128]{1,0:T(8,128)S(1)} %get-tuple-element.28), channel_id=1, source_target_pairs={{0,2},{1,7},{2,4},{3,1},{4,6},{5,3},{6,0},{7,5},{8,10},{9,15},{10,... | collective-permute-start | bytes 245768 | tf_op jit(solution)/shard_map/ppermute | solution.py:54
  37.9 8.6 %collective-permute-start.7 = (f32[448,128]{1,0:T(8,128)S(1)}, f32[448,128]{1,0:T(8,128)S(1)}, u32[]{:S(2)}, u32[]{:S(2)}) collective-permute-start(f32[448,128]{1,0:T(8,128)S(1)} %get-tuple-element.23), channel_id=1, source_target_pairs={{0,2},{1,7},{2,4},{3,1},{4,6},{5,3},{6,0},{7,5},{8,10},{9,15},{10,... | collective-permute-start | bytes 688136 | tf_op jit(solution)/shard_map/ppermute | solution.py:54
  43.2 7.9 %collective-permute-start.10 = (f32[160,128]{1,0:T(8,128)S(1)}, f32[160,128]{1,0:T(8,128)S(1)}, u32[]{:S(2)}, u32[]{:S(2)}) collective-permute-start(f32[160,128]{1,0:T(8,128)S(1)} %add.15), channel_id=1, source_target_pairs={{0,8},{1,25},{2,10},{3,27},{4,12},{5,29},{6,14},{7,31},{8,16},{9,1... | collective-permute-start | bytes 245768 | tf_op jit(solution)/shard_map/ppermute | solution.py:54
  46.6 6.2 %collective-permute-start.8 = (f32[160,128]{1,0:T(8,128)S(1)}, f32[160,128]{1,0:T(8,128)S(1)}, u32[]{:S(2)}, u32[]{:S(2)}) collective-permute-start(f32[160,128]{1,0:T(8,128)S(1)} %get-tuple-element.25), channel_id=1, source_target_pairs={{0,9},{1,24},{2,11},{3,26},{4,13},{5,28},{6,15},{7,30},{8,17},{9,0... | collective-permute-start | bytes 245768 | tf_op jit(solution)/shard_map/ppermute | solution.py:54
  51.1 7.5 %collective-permute-start.11 = (f32[160,128]{1,0:T(8,128)S(1)}, f32[160,128]{1,0:T(8,128)S(1)}, u32[]{:S(2)}, u32[]{:S(2)}) collective-permute-start(f32[160,128]{1,0:T(8,128)S(1)} %add.16), channel_id=1, source_target_pairs={{0,8},{1,25},{2,10},{3,27},{4,12},{5,29},{6,14},{7,31},{8,16},{9,1... | collective-permute-start | bytes 245768 | tf_op jit(solution)/shard_map/ppermute | solution.py:54

commit v12 on v11

--- a/solution.py
+++ b/solution.py
@@ -108,7 +108,7 @@
     out_ref[at : at + HALF, :] = rows.astype(jnp.bfloat16)
 
 
-def right_kernel(smooth_ref, out_ref):
+def build_right(smooth_ref, out_ref):
     lev = lax.axis_index("lev")
     for i in range(COLS_OUT // HALF):
         build_rows(smooth_ref, lev * (COLS_OUT // HALF) + i, out_ref, i * HALF)
@@ -158,11 +158,13 @@
         at += size + 8
 
 
-def begin_kernel(place, smooth_ref, right_ref, out_ref, left_ref):
+def begin_kernel(place, smooth_ref, out_ref, right_ref, left_ref):
+    build_right(smooth_ref, right_ref)
     out_ref[...] = product(place, smooth_ref, right_ref, left_ref)
 
 
-def finish_kernel(place, part_ref, smooth_ref, right_ref, out_ref, left_ref, prod_ref):
+def finish_kernel(place, part_ref, smooth_ref, out_ref, right_ref, left_ref, prod_ref):
+    build_right(smooth_ref, right_ref)
     prod_ref[...] = part_ref[...] + product(place, smooth_ref, right_ref, left_ref)
     emit(place, prod_ref, out_ref)
 
@@ -236,25 +238,13 @@
     return jnp.broadcast_to(coef[:, None], (3 * LEV, LANES))
 
 
-def right_of(smoothed):
-    return pl.pallas_call(
-        right_kernel,
-        out_shape=jax.ShapeDtypeStruct((COLS_OUT, BLOCK), jnp.bfloat16),
-        in_specs=[VMEM],
-        out_specs=VMEM,
-        compiler_params=params(4),
-        cost_estimate=cost(1, SHARE),
-        name="right",
-    )(smoothed)
-
-
 def gram(kernel, place, out_shape, *operands):
     scratch = [pltpu.VMEM((BUILT, BLOCK), jnp.bfloat16), pltpu.VMEM((BUILT, COLS_OUT), jnp.float32)]
     return pl.pallas_call(
         functools.partial(kernel, place),
-        out_shape=jax.ShapeDtypeStruct(out_shape, jnp.float32),
+        out_shape=out_shape,
         in_specs=[VMEM] * len(operands),
-        out_specs=VMEM,
+        out_specs=jax.tree.map(lambda _: VMEM, out_shape),
         scratch_shapes=scratch[:1] if kernel is begin_kernel else scratch,
         compiler_params=params(12),
         cost_estimate=cost(1, SHARE),
@@ -330,11 +320,11 @@
         name="smooth",
     )(coef, near, far[2], far[1], far[3])
     other = swap_cores(own)
-    own_right = right_of(own)
-    begun = gram(begin_kernel, "far", (BUILT, COLS_OUT), own, own_right)
-    other_right = right_of(other)
-    sent = (SENT, LANES)
-    parts = {"far": gram(finish_kernel, "far", sent, begun, other, other_right)}
+    right = jax.ShapeDtypeStruct((COLS_OUT, BLOCK), jnp.bfloat16)
+    begun, own_right = gram(begin_kernel, "far", [jax.ShapeDtypeStruct((BUILT, COLS_OUT), f32), right], own)
+    sent = jax.ShapeDtypeStruct((SENT, LANES), f32)
+    far, other_right = gram(finish_kernel, "far", [sent, right], begun, other)
+    parts = {"far": far}
     both = (own, own_right, other, other_right)
     parts["cross"] = gram(gram_kernel, "cross", sent, *both)
     both, parts["cross"] = lax.optimization_barrier((both, parts["cross"]))

time: 59.5 us -> 59.8 us (level)
    pallas_call x7 -> x5, Pallas kernels: 5.57 us -> 5.6 us  [gram(): pl.pallas_call(functools.partial(kernel, place), out_shape=out_shape, in_...]
  transfers between devices with their start and end apart: 13 -> 13, of which waited for: 10 -> 9; matrix products, arithmetic and copies ran while one was open for 1% -> 1% of each run, Pallas kernels for 8% -> 8%
where the time goes in v12:
time: 59.8 us; the launch traced here: 59.6 us
  waiting for transfers between devices  28.5 us (48%)
  starting transfers between devices  20.8 us (35%)
  Pallas kernels  8.56 us (14%)
  local copies, waits for them, and re-layouts  1.3 us (2%)
    ppermute x7, waiting for transfers between devices, hop(): return lax.ppermute(value, 'hor', pairs)  15.9 us
    ppermute x7, starting transfers between devices, hop(): return lax.ppermute(value, 'hor', pairs)  9.59 us
    ppermute x4, waiting for transfers between devices, shift_lev(): return lax.ppermute(value, 'lev', pairs)  9.07 us
    all_to_all x1, starting transfers between devices, on_device(): lists = lax.all_to_all(repeated, 'lev', 0, 0, tiled=True)  6.26 us
    pallas_call x5, Pallas kernels, gram(): pl.pallas_call(functools.partial(kernel, place), out_shape=out_shape, in_...  5.6 us
    ppermute x4, starting transfers between devices, shift_lev(): return lax.ppermute(value, 'lev', pairs)  4.83 us
    all_to_all x1, waiting for transfers between devices, on_device(): lists = lax.all_to_all(repeated, 'lev', 0, 0, tiled=True)  2.57 us
    pallas_call x1, Pallas kernels, on_device(): pl.pallas_call(repeat_kernel, out_shape=jax.ShapeDtypeStruct((N_LEV, 1, S...  1.25 us
  transfers between devices with their start and end apart: 13, of which 9 were waited for; matrix products, arithmetic and copies ran while one was open for 1% of the time, Pallas kernels for 8%

profile of v12, /device:TPU:6, one launch (start us, length us, event | category | flops | bytes accessed | tf_op | source)
XLA Modules:
  0.0 59.6 jit_solution(10153474112271080831)
XLA Ops:
  0.0 1.2 %repeat.1 = s32[8,1,128]{2,1,0:T(1,128)} custom-call(s32[1,128]{1,0:T(1,128)} %index_ref.1), custom_call_target="tpu_custom_call" | custom-call | tf_op jit(solution)/shard_map/repeat/pallas_call | solution.py:283
  1.3 6.3 %all-to-all-start = ((s32[8,1,128]{2,1,0:T(1,128)}), s32[8,1,128]{2,1,0:T(1,128)S(1)}, u32[]{:S(2)}, u32[]{:S(2)}) async-start(s32[8,1,128]{2,1,0:T(1,128)} %repeat.1), calls=%async_computation | async-start | bytes 8192 | tf_op jit(solution)/shard_map/all_to_all | solution.py:291
  7.6 1.2 %copy-done = f32[4,4,16384]{2,1,0:T(4,128)S(1)} copy-done((f32[4,4,16384]{2,1,0:T(4,128)S(1)}, f32[4,4,16384]{2,1,0:T(4,128)}, u32[]{:S(2)}) %copy-start) | copy-done | bytes 1048600
  8.8 0.1 stage.1.slab_ref
  9.0 2.6 %all-to-all-done.index_ref = s32[8,1,128]{2,1,0:T(1,128)S(1)} async-done(((s32[8,1,128]{2,1,0:T(1,128)}), s32[8,1,128]{2,1,0:T(1,128)S(1)}, u32[]{:S(2)}, u32[]{:S(2)}) %all-to-all-start) | async-done | bytes 4128 | tf_op jit(solution)/shard_map/all_to_all | solution.py:291
  11.5 0.4 pick.1
  11.9 0.7 %collective-permute-start = (f32[16,1024]{1,0:T(8,128)S(1)}, f32[16,1024]{1,0:T(8,128)S(1)}, u32[]{:S(2)}, u32[]{:S(2)}) collective-permute-start(f32[16,1024]{1,0:T(8,128)S(1)} %pick.1), channel_id=1, source_target_pairs={{0,128},{32,160},{64,192},{96,224},{128,0},{160,32},{192,64},{224,... | collective-permute-start | bytes 196616 | tf_op jit(solution)/shard_map/ppermute | solution.py:37
  12.6 3.6 %collective-permute-done = f32[16,1024]{1,0:T(8,128)S(1)} collective-permute-done((f32[16,1024]{1,0:T(8,128)S(1)}, f32[16,1024]{1,0:T(8,128)S(1)}, u32[]{:S(2)}, u32[]{:S(2)}) %collective-permute-start) | collective-permute-done | bytes 65568 | tf_op jit(solution)/shard_map/ppermute | solution.py:37
  16.3 0.6 %collective-permute-start.3 = (f32[2,16,1024]{2,1,0:T(8,128)S(1)}, f32[2,16,1024]{2,1,0:T(8,128)S(1)}, u32[]{:S(2)}, u32[]{:S(2)}) collective-permute-start(f32[2,16,1024]{2,1,0:T(8,128)S(1)} %pad_maximum_fusion.w0_ref), channel_id=1, source_target_pairs={{0,96},{32,0},{64,32},{96,64},{128,224},{160,128},{192,160},{224,1... | collective-permute-start | bytes 393224 | tf_op jit(solution)/shard_map/ppermute | solution.py:37
  16.9 2.7 %collective-permute-start.2 = (f32[2,16,1024]{2,1,0:T(8,128)S(1)}, f32[2,16,1024]{2,1,0:T(8,128)S(1)}, u32[]{:S(2)}, u32[]{:S(2)}) collective-permute-start(f32[2,16,1024]{2,1,0:T(8,128)S(1)} %pad_maximum_fusion.w0_ref), channel_id=1, source_target_pairs={{0,32},{32,64},{64,96},{96,0},{128,160},{160,192},{192,224},{224,1... | collective-permute-start | bytes 393224 | tf_op jit(solution)/shard_map/ppermute | solution.py:37
  19.6 0.9 %collective-permute-start.1 = (f32[2,16,1024]{2,1,0:T(8,128)S(1)}, f32[2,16,1024]{2,1,0:T(8,128)S(1)}, u32[]{:S(2)}, u32[]{:S(2)}) collective-permute-start(f32[2,16,1024]{2,1,0:T(8,128)S(1)} %pad_maximum_fusion.w0_ref), channel_id=1, source_target_pairs={{0,64},{32,96},{64,0},{96,32},{128,192},{160,224},{192,128},{224,1... | collective-permute-start | bytes 393224 | tf_op jit(solution)/shard_map/ppermute | solution.py:37
  20.6 2.6 %collective-permute-done.3.w3_ref = f32[2,16,1024]{2,1,0:T(8,128)S(1)} collective-permute-done((f32[2,16,1024]{2,1,0:T(8,128)S(1)}, f32[2,16,1024]{2,1,0:T(8,128)S(1)}, u32[]{:S(2)}, u32[]{:S(2)}) %collective-permute-start.3) | collective-permute-done | bytes 131104 | tf_op jit(solution)/shard_map/ppermute | solution.py:37
  23.2 2.9 %collective-permute-done.1.w2_ref = f32[2,16,1024]{2,1,0:T(8,128)S(1)} collective-permute-done((f32[2,16,1024]{2,1,0:T(8,128)S(1)}, f32[2,16,1024]{2,1,0:T(8,128)S(1)}, u32[]{:S(2)}, u32[]{:S(2)}) %collective-permute-start.1) | collective-permute-done | bytes 131104 | tf_op jit(solution)/shard_map/ppermute | solution.py:37
  26.1 0.3 smooth.1.smooth_ref.own_ref
  26.5 0.1 collective-permute-start.4
  26.6 0.9 %gram_far.2 = (f32[304,272]{1,0:T(8,128)S(1)}, bf16[272,1024]{1,0:T(8,128)(2,1)S(1)}) custom-call(f32[128,1024]{1,0:T(8,128)S(1)} %smooth.1.smooth_ref.own_ref), custom_call_target="tpu_custom_call" | custom-call | flops 1 | bytes 262144 | tf_op jit(solution)/shard_map/gram_far/pallas_call | solution.py:243
  27.5 1.0 %collective-permute-done.4.smooth_ref.other_ref = f32[128,1024]{1,0:T(8,128)S(1)} collective-permute-done((f32[128,1024]{1,0:T(8,128)S(1)}, f32[128,1024]{1,0:T(8,128)S(1)}, u32[]{:S(2)}, u32[]{:S(2)}) %collective-permute-start.4) | collective-permute-done | bytes 524320 | tf_op jit(solution)/shard_map/ppermute | solution.py:41
  28.5 1.1 %gram_far.3 = (f32[608,128]{1,0:T(8,128)S(1)}, bf16[272,1024]{1,0:T(8,128)(2,1)S(1)}) custom-call(f32[304,272]{1,0:T(8,128)S(1)} %get-tuple-element.22.part_ref, f32[128,1024]{1,0:T(8,128)S(1)} %collective-permute-done.4.smooth_ref.other_ref), custom_call_target="tpu_custom_call" | custom-call | flops 1 | bytes 262144 | tf_op jit(solution)/shard_map/gram_far/pallas_call | solution.py:243
  29.5 1.6 %collective-permute-start.6 = (f32[608,128]{1,0:T(8,128)S(1)}, f32[608,128]{1,0:T(8,128)S(1)}, u32[]{:S(2)}, u32[]{:S(2)}) collective-permute-start(f32[608,128]{1,0:T(8,128)S(1)} %get-tuple-element.30), channel_id=1, source_target_pairs={{0,2},{1,7},{2,4},{3,1},{4,6},{5,3},{6,0},{7,5},{8,10},{9,15},{10,... | collective-permute-start | bytes 933896 | tf_op jit(solution)/shard_map/ppermute | solution.py:54
  31.1 1.2 %gram_cross.1 = f32[608,128]{1,0:T(8,128)S(1)} custom-call(f32[128,1024]{1,0:T(8,128)S(1)} %smooth.1.smooth_ref.own_ref, bf16[272,1024]{1,0:T(8,128)(2,1)S(1)} %get-tuple-element.25.own_right_ref, f32[128,1024]{1,0:T(8,128)S(1)} %collective-permute-done.4.smooth_ref.other_ref, bf16[272,1024]{1,0:T(8,128)(2,1)S(1)} %get-tuple-element.27.other_right_ref), custom_call_target="tpu_custom_call" | custom-call | flops 1 | bytes 262144 | tf_op jit(solution)/shard_map/gram_cross/pallas_call | solution.py:243
  32.4 1.2 %gram_near.1.a_ref = f32[608,128]{1,0:T(8,128)S(1)} custom-call(f32[128,1024]{1,0:T(8,128)S(1)} %smooth.1.smooth_ref.own_ref, bf16[272,1024]{1,0:T(8,128)(2,1)S(1)} %get-tuple-element.25.own_right_ref, f32[128,1024]{1,0:T(8,128)S(1)} %collective-permute-done.4.smooth_ref.other_ref, bf16[272,1024]{1,0:T(8,128)(2,1)S(1)} %get-tuple-element.27.other_right_ref), custom_call_target="tpu_custom_call" | custom-call | flops 1 | bytes 262144 | tf_op jit(solution)/shard_map/gram_near/pallas_call | solution.py:243
  33.7 4.0 %collective-permute-done.6.b_ref = f32[608,128]{1,0:T(8,128)S(1)} collective-permute-done((f32[608,128]{1,0:T(8,128)S(1)}, f32[608,128]{1,0:T(8,128)S(1)}, u32[]{:S(2)}, u32[]{:S(2)}) %collective-permute-start.6) | collective-permute-done | bytes 311328 | tf_op jit(solution)/shard_map/ppermute | solution.py:54
  37.7 0.4 collective-permute-start.9
  38.2 1.6 %collective-permute-start.7 = (f32[448,128]{1,0:T(8,128)S(1)}, f32[448,128]{1,0:T(8,128)S(1)}, u32[]{:S(2)}, u32[]{:S(2)}) collective-permute-start(f32[448,128]{1,0:T(8,128)S(1)} %get-tuple-element.31), channel_id=1, source_target_pairs={{0,2},{1,7},{2,4},{3,1},{4,6},{5,3},{6,0},{7,5},{8,10},{9,15},{10,... | collective-permute-start | bytes 688136 | tf_op jit(solution)/shard_map/ppermute | solution.py:54
  39.7 1.2 %gram_own.1.a_ref = f32[608,128]{1,0:T(8,128)S(1)} custom-call(f32[128,1024]{1,0:T(8,128)S(1)} %smooth.1.smooth_ref.own_ref, bf16[272,1024]{1,0:T(8,128)(2,1)S(1)} %get-tuple-element.25.own_right_ref, f32[128,1024]{1,0:T(8,128)S(1)} %collective-permute-done.4.smooth_ref.other_ref, bf16[272,1024]{1,0:T(8,128)(2,1)S(1)} %get-tuple-element.27.other_right_ref), custom_call_target="tpu_custom_call" | custom-call | flops 1 | bytes 262144 | tf_op jit(solution)/shard_map/gram_own/pallas_call | solution.py:243
  41.0 2.5 %collective-permute-done.9.b_ref = f32[160,128]{1,0:T(8,128)S(1)} collective-permute-done((f32[160,128]{1,0:T(8,128)S(1)}, f32[160,128]{1,0:T(8,128)S(1)}, u32[]{:S(2)}, u32[]{:S(2)}) %collective-permute-start.9) | collective-permute-done | bytes 81952 | tf_op jit(solution)/shard_map/ppermute | solution.py:54
  43.5 3.3 %collective-permute-start.10 = (f32[160,128]{1,0:T(8,128)S(1)}, f32[160,128]{1,0:T(8,128)S(1)}, u32[]{:S(2)}, u32[]{:S(2)}) collective-permute-start(f32[160,128]{1,0:T(8,128)S(1)} %add.15), channel_id=1, source_target_pairs={{0,8},{1,25},{2,10},{3,27},{4,12},{5,29},{6,14},{7,31},{8,16},{9,1... | collective-permute-start | bytes 245768 | tf_op jit(solution)/shard_map/ppermute | solution.py:54
  46.9 0.8 %collective-permute-start.8 = (f32[160,128]{1,0:T(8,128)S(1)}, f32[160,128]{1,0:T(8,128)S(1)}, u32[]{:S(2)}, u32[]{:S(2)}) collective-permute-start(f32[160,128]{1,0:T(8,128)S(1)} %get-tuple-element.33), channel_id=1, source_target_pairs={{0,9},{1,24},{2,11},{3,26},{4,13},{5,28},{6,15},{7,30},{8,17},{9,0... | collective-permute-start | bytes 245768 | tf_op jit(solution)/shard_map/ppermute | solution.py:54
  47.7 3.7 %collective-permute-done.10.b_ref = f32[160,128]{1,0:T(8,128)S(1)} collective-permute-done((f32[160,128]{1,0:T(8,128)S(1)}, f32[160,128]{1,0:T(8,128)S(1)}, u32[]{:S(2)}, u32[]{:S(2)}) %collective-permute-start.10) | collective-permute-done | bytes 81952 | tf_op jit(solution)/shard_map/ppermute | solution.py:54
  51.4 1.7 %collective-permute-start.11 = (f32[160,128]{1,0:T(8,128)S(1)}, f32[160,128]{1,0:T(8,128)S(1)}, u32[]{:S(2)}, u32[]{:S(2)}) collective-permute-start(f32[160,128]{1,0:T(8,128)S(1)} %add.16), channel_id=1, source_target_pairs={{0,8},{1,25},{2,10},{3,27},{4,12},{5,29},{6,14},{7,31},{8,16},{9,1... | collective-permute-start | bytes 245768 | tf_op jit(solution)/shard_map/ppermute | solution.py:54
  53.1 5.8 %collective-permute-done.11.t2_ref = f32[160,128]{1,0:T(8,128)S(1)} collective-permute-done((f32[160,128]{1,0:T(8,128)S(1)}, f32[160,128]{1,0:T(8,128)S(1)}, u32[]{:S(2)}, u32[]{:S(2)}) %collective-permute-start.11) | collective-permute-done | bytes 81952 | tf_op jit(solution)/shard_map/ppermute | solution.py:54
  58.9 0.7 %final.1 = f32[68,272]{1,0:T(8,128)} custom-call(f32[160,128]{1,0:T(8,128)S(1)} %get-tuple-element.32.t0_ref, f32[160,128]{1,0:T(8,128)S(1)} %collective-permute-done.8.t1_ref, f32[160,128]{1,0:T(8,128)S(1)} %collective-permute-done.11.t2_ref), custom_call_target="tpu_custom_call" | custom-call | flops 1 | bytes 262144 | tf_op jit(solution)/shard_map/final/pallas_call | solution.py:350
  (22 shorter events, 0.7 us)
Async XLA Ops:
  1.2 6.3 %copy-start.1 = (f32[32]{0:T(128)S(1)}, f32[32]{0:T(128)}, u32[]{:S(2)}) copy-start(f32[32]{0:T(128)} %param.6) | copy-start | bytes 388
  1.3 6.3 %copy-start.2 = (s32[31]{0:T(128)S(1)}, s32[31]{0:T(128)}, u32[]{:S(2)}) copy-start(s32[31]{0:T(128)} %param.7) | copy-start | bytes 376
  1.3 10.3 %all-to-all-start = ((s32[8,1,128]{2,1,0:T(1,128)}), s32[8,1,128]{2,1,0:T(1,128)S(1)}, u32[]{:S(2)}, u32[]{:S(2)}) async-start(s32[8,1,128]{2,1,0:T(1,128)} %repeat.1), calls=%async_computation | async-start | bytes 8192 | tf_op jit(solution)/shard_map/all_to_all | solution.py:291
  7.6 1.2 %copy-start = (f32[4,4,16384]{2,1,0:T(4,128)S(1)}, f32[4,4,16384]{2,1,0:T(4,128)}, u32[]{:S(2)}) copy-start(f32[4,4,16384]{2,1,0:T(4,128)} %slab_ref.1) | copy-start | bytes 3145732
  11.9 4.4 %collective-permute-start = (f32[16,1024]{1,0:T(8,128)S(1)}, f32[16,1024]{1,0:T(8,128)S(1)}, u32[]{:S(2)}, u32[]{:S(2)}) collective-permute-start(f32[16,1024]{1,0:T(8,128)S(1)} %pick.1), channel_id=1, source_target_pairs={{0,128},{32,160},{64,192},{96,224},{128,0},{160,32},{192,64},{224,... | collective-permute-start | bytes 196616 | tf_op jit(solution)/shard_map/ppermute | solution.py:37
  16.3 6.9 %collective-permute-start.3 = (f32[2,16,1024]{2,1,0:T(8,128)S(1)}, f32[2,16,1024]{2,1,0:T(8,128)S(1)}, u32[]{:S(2)}, u32[]{:S(2)}) collective-permute-start(f32[2,16,1024]{2,1,0:T(8,128)S(1)} %pad_maximum_fusion.w0_ref), channel_id=1, source_target_pairs={{0,96},{32,0},{64,32},{96,64},{128,224},{160,128},{192,160},{224,1... | collective-permute-start | bytes 393224 | tf_op jit(solution)/shard_map/ppermute | solution.py:37
  16.9 6.3 %collective-permute-start.2 = (f32[2,16,1024]{2,1,0:T(8,128)S(1)}, f32[2,16,1024]{2,1,0:T(8,128)S(1)}, u32[]{:S(2)}, u32[]{:S(2)}) collective-permute-start(f32[2,16,1024]{2,1,0:T(8,128)S(1)} %pad_maximum_fusion.w0_ref), channel_id=1, source_target_pairs={{0,32},{32,64},{64,96},{96,0},{128,160},{160,192},{192,224},{224,1... | collective-permute-start | bytes 393224 | tf_op jit(solution)/shard_map/ppermute | solution.py:37
  19.6 6.5 %collective-permute-start.1 = (f32[2,16,1024]{2,1,0:T(8,128)S(1)}, f32[2,16,1024]{2,1,0:T(8,128)S(1)}, u32[]{:S(2)}, u32[]{:S(2)}) collective-permute-start(f32[2,16,1024]{2,1,0:T(8,128)S(1)} %pad_maximum_fusion.w0_ref), channel_id=1, source_target_pairs={{0,64},{32,96},{64,0},{96,32},{128,192},{160,224},{192,128},{224,1... | collective-permute-start | bytes 393224 | tf_op jit(solution)/shard_map/ppermute | solution.py:37
  26.5 2.0 %collective-permute-start.4 = (f32[128,1024]{1,0:T(8,128)S(1)}, f32[128,1024]{1,0:T(8,128)S(1)}, u32[]{:S(2)}, u32[]{:S(2)}) collective-permute-start(f32[128,1024]{1,0:T(8,128)S(1)} %smooth.1.smooth_ref.own_ref), channel_id=1, source_target_pairs={{0,1},{1,0},{2,3},{3,2},{4,5},{5,4},{6,7},{7,6},{8,9},{9,8},{10,11... | collective-permute-start | bytes 1572872 | tf_op jit(solution)/shard_map/ppermute | solution.py:41
  29.5 8.1 %collective-permute-start.6 = (f32[608,128]{1,0:T(8,128)S(1)}, f32[608,128]{1,0:T(8,128)S(1)}, u32[]{:S(2)}, u32[]{:S(2)}) collective-permute-start(f32[608,128]{1,0:T(8,128)S(1)} %get-tuple-element.30), channel_id=1, source_target_pairs={{0,2},{1,7},{2,4},{3,1},{4,6},{5,3},{6,0},{7,5},{8,10},{9,15},{10,... | collective-permute-start | bytes 933896 | tf_op jit(solution)/shard_map/ppermute | solution.py:54
  32.4 8.6 %collective-permute-start.5 = (f32[608,128]{1,0:T(8,128)S(1)}, f32[608,128]{1,0:T(8,128)S(1)}, u32[]{:S(2)}, u32[]{:S(2)}) collective-permute-start(f32[608,128]{1,0:T(8,128)S(1)} %gram_cross.1), channel_id=1, source_target_pairs={{0,3},{1,6},{2,5},{3,0},{4,7},{5,2},{6,1},{7,4},{8,11},{9,14},{10,... | collective-permute-start | bytes 933896 | tf_op jit(solution)/shard_map/ppermute | solution.py:54
  37.7 5.7 %collective-permute-start.9 = (f32[160,128]{1,0:T(8,128)S(1)}, f32[160,128]{1,0:T(8,128)S(1)}, u32[]{:S(2)}, u32[]{:S(2)}) collective-permute-start(f32[160,128]{1,0:T(8,128)S(1)} %get-tuple-element.36), channel_id=1, source_target_pairs={{0,2},{1,7},{2,4},{3,1},{4,6},{5,3},{6,0},{7,5},{8,10},{9,15},{10,... | collective-permute-start | bytes 245768 | tf_op jit(solution)/shard_map/ppermute | solution.py:54
  38.2 8.6 %collective-permute-start.7 = (f32[448,128]{1,0:T(8,128)S(1)}, f32[448,128]{1,0:T(8,128)S(1)}, u32[]{:S(2)}, u32[]{:S(2)}) collective-permute-start(f32[448,128]{1,0:T(8,128)S(1)} %get-tuple-element.31), channel_id=1, source_target_pairs={{0,2},{1,7},{2,4},{3,1},{4,6},{5,3},{6,0},{7,5},{8,10},{9,15},{10,... | collective-permute-start | bytes 688136 | tf_op jit(solution)/shard_map/ppermute | solution.py:54
  43.5 7.9 %collective-permute-start.10 = (f32[160,128]{1,0:T(8,128)S(1)}, f32[160,128]{1,0:T(8,128)S(1)}, u32[]{:S(2)}, u32[]{:S(2)}) collective-permute-start(f32[160,128]{1,0:T(8,128)S(1)} %add.15), channel_id=1, source_target_pairs={{0,8},{1,25},{2,10},{3,27},{4,12},{5,29},{6,14},{7,31},{8,16},{9,1... | collective-permute-start | bytes 245768 | tf_op jit(solution)/shard_map/ppermute | solution.py:54
  46.9 6.2 %collective-permute-start.8 = (f32[160,128]{1,0:T(8,128)S(1)}, f32[160,128]{1,0:T(8,128)S(1)}, u32[]{:S(2)}, u32[]{:S(2)}) collective-permute-start(f32[160,128]{1,0:T(8,128)S(1)} %get-tuple-element.33), channel_id=1, source_target_pairs={{0,9},{1,24},{2,11},{3,26},{4,13},{5,28},{6,15},{7,30},{8,17},{9,0... | collective-permute-start | bytes 245768 | tf_op jit(solution)/shard_map/ppermute | solution.py:54
  51.4 7.5 %collective-permute-start.11 = (f32[160,128]{1,0:T(8,128)S(1)}, f32[160,128]{1,0:T(8,128)S(1)}, u32[]{:S(2)}, u32[]{:S(2)}) collective-permute-start(f32[160,128]{1,0:T(8,128)S(1)} %add.16), channel_id=1, source_target_pairs={{0,8},{1,25},{2,10},{3,27},{4,12},{5,29},{6,14},{7,31},{8,16},{9,1... | collective-permute-start | bytes 245768 | tf_op jit(solution)/shard_map/ppermute | solution.py:54

commit v13 on v12

--- a/solution.py
+++ b/solution.py
@@ -78,7 +78,7 @@
             out_ref[rows, group * SAMP : (group + 1) * SAMP] = total
 
 
-def smooth_kernel(coef_ref, w0_ref, w2_ref, w1_ref, w3_ref, out_ref, raw_ref):
+def smooth_kernel(coef_ref, w0_ref, w3_ref, w1_ref, w2_ref, out_ref, raw_ref):
     x = lax.axis_index("lev") % N_X
     for step, ref in enumerate((w0_ref, w1_ref, w2_ref, w3_ref)):
         source = lax.rem(x - step + N_X, N_X)
@@ -318,7 +318,7 @@
         scratch_shapes=[pltpu.VMEM((N_LEV, 4 * SLOTS, BLOCK), f32)],
         compiler_params=params(16),
         name="smooth",
-    )(coef, near, far[2], far[1], far[3])
+    )(coef, near, far[3], far[1], far[2])
     other = swap_cores(own)
     right = jax.ShapeDtypeStruct((COLS_OUT, BLOCK), jnp.bfloat16)
     begun, own_right = gram(begin_kernel, "far", [jax.ShapeDtypeStruct((BUILT, COLS_OUT), f32), right], own)

time: 59.8 us -> 59.5 us (level)
  transfers between devices with their start and end apart: 13 -> 13, of which waited for: 9 -> 10; matrix products, arithmetic and copies ran while one was open for 1% -> 1% of each run, Pallas kernels for 8% -> 8%
where the time goes in v13:
time: 59.5 us; the launch traced here: 59.3 us
  waiting for transfers between devices  28.2 us (47%)
  starting transfers between devices  20.8 us (35%)
  Pallas kernels  8.57 us (14%)
  local copies, waits for them, and re-layouts  1.3 us (2%)
    ppermute x7, waiting for transfers between devices, hop(): return lax.ppermute(value, 'hor', pairs)  15.9 us
    ppermute x7, starting transfers between devices, hop(): return lax.ppermute(value, 'hor', pairs)  9.59 us
    ppermute x4, waiting for transfers between devices, shift_lev(): return lax.ppermute(value, 'lev', pairs)  8.77 us
    all_to_all x1, starting transfers between devices, on_device(): lists = lax.all_to_all(repeated, 'lev', 0, 0, tiled=True)  6.26 us
    pallas_call x5, Pallas kernels, gram(): pl.pallas_call(functools.partial(kernel, place), out_shape=out_shape, in_...  5.61 us
    ppermute x4, starting transfers between devices, shift_lev(): return lax.ppermute(value, 'lev', pairs)  4.84 us
    all_to_all x1, waiting for transfers between devices, on_device(): lists = lax.all_to_all(repeated, 'lev', 0, 0, tiled=True)  2.57 us
    pallas_call x1, Pallas kernels, on_device(): pl.pallas_call(repeat_kernel, out_shape=jax.ShapeDtypeStruct((N_LEV, 1, S...  1.25 us
  transfers between devices with their start and end apart: 13, of which 10 were waited for; matrix products, arithmetic and copies ran while one was open for 1% of the time, Pallas kernels for 8%

profile of v13, /device:TPU:6, one launch (start us, length us, event | category | flops | bytes accessed | tf_op | source)
XLA Modules:
  0.0 59.3 jit_solution(16553644821097953297)
XLA Ops:
  0.0 1.2 %repeat.1 = s32[8,1,128]{2,1,0:T(1,128)} custom-call(s32[1,128]{1,0:T(1,128)} %index_ref.1), custom_call_target="tpu_custom_call" | custom-call | tf_op jit(solution)/shard_map/repeat/pallas_call | solution.py:283
  1.3 6.3 %all-to-all-start = ((s32[8,1,128]{2,1,0:T(1,128)}), s32[8,1,128]{2,1,0:T(1,128)S(1)}, u32[]{:S(2)}, u32[]{:S(2)}) async-start(s32[8,1,128]{2,1,0:T(1,128)} %repeat.1), calls=%async_computation | async-start | bytes 8192 | tf_op jit(solution)/shard_map/all_to_all | solution.py:291
  7.6 1.2 %copy-done = f32[4,4,16384]{2,1,0:T(4,128)S(1)} copy-done((f32[4,4,16384]{2,1,0:T(4,128)S(1)}, f32[4,4,16384]{2,1,0:T(4,128)}, u32[]{:S(2)}) %copy-start) | copy-done | bytes 1048600
  8.8 0.1 stage.1.slab_ref
  9.0 2.6 %all-to-all-done.index_ref = s32[8,1,128]{2,1,0:T(1,128)S(1)} async-done(((s32[8,1,128]{2,1,0:T(1,128)}), s32[8,1,128]{2,1,0:T(1,128)S(1)}, u32[]{:S(2)}, u32[]{:S(2)}) %all-to-all-start) | async-done | bytes 4128 | tf_op jit(solution)/shard_map/all_to_all | solution.py:291
  11.5 0.4 pick.1
  11.9 0.7 %collective-permute-start = (f32[16,1024]{1,0:T(8,128)S(1)}, f32[16,1024]{1,0:T(8,128)S(1)}, u32[]{:S(2)}, u32[]{:S(2)}) collective-permute-start(f32[16,1024]{1,0:T(8,128)S(1)} %pick.1), channel_id=1, source_target_pairs={{0,128},{32,160},{64,192},{96,224},{128,0},{160,32},{192,64},{224,... | collective-permute-start | bytes 196616 | tf_op jit(solution)/shard_map/ppermute | solution.py:37
  12.6 3.6 %collective-permute-done = f32[16,1024]{1,0:T(8,128)S(1)} collective-permute-done((f32[16,1024]{1,0:T(8,128)S(1)}, f32[16,1024]{1,0:T(8,128)S(1)}, u32[]{:S(2)}, u32[]{:S(2)}) %collective-permute-start) | collective-permute-done | bytes 65568 | tf_op jit(solution)/shard_map/ppermute | solution.py:37
  16.3 2.2 %collective-permute-start.3 = (f32[2,16,1024]{2,1,0:T(8,128)S(1)}, f32[2,16,1024]{2,1,0:T(8,128)S(1)}, u32[]{:S(2)}, u32[]{:S(2)}) collective-permute-start(f32[2,16,1024]{2,1,0:T(8,128)S(1)} %pad_maximum_fusion.w0_ref), channel_id=1, source_target_pairs={{0,64},{32,96},{64,0},{96,32},{128,192},{160,224},{192,128},{224,1... | collective-permute-start | bytes 393224 | tf_op jit(solution)/shard_map/ppermute | solution.py:37
  18.4 1.2 %collective-permute-start.2 = (f32[2,16,1024]{2,1,0:T(8,128)S(1)}, f32[2,16,1024]{2,1,0:T(8,128)S(1)}, u32[]{:S(2)}, u32[]{:S(2)}) collective-permute-start(f32[2,16,1024]{2,1,0:T(8,128)S(1)} %pad_maximum_fusion.w0_ref), channel_id=1, source_target_pairs={{0,32},{32,64},{64,96},{96,0},{128,160},{160,192},{192,224},{224,1... | collective-permute-start | bytes 393224 | tf_op jit(solution)/shard_map/ppermute | solution.py:37
  19.6 0.9 %collective-permute-start.1 = (f32[2,16,1024]{2,1,0:T(8,128)S(1)}, f32[2,16,1024]{2,1,0:T(8,128)S(1)}, u32[]{:S(2)}, u32[]{:S(2)}) collective-permute-start(f32[2,16,1024]{2,1,0:T(8,128)S(1)} %pad_maximum_fusion.w0_ref), channel_id=1, source_target_pairs={{0,96},{32,0},{64,32},{96,64},{128,224},{160,128},{192,160},{224,1... | collective-permute-start | bytes 393224 | tf_op jit(solution)/shard_map/ppermute | solution.py:37
  20.6 2.3 %collective-permute-done.3.w2_ref = f32[2,16,1024]{2,1,0:T(8,128)S(1)} collective-permute-done((f32[2,16,1024]{2,1,0:T(8,128)S(1)}, f32[2,16,1024]{2,1,0:T(8,128)S(1)}, u32[]{:S(2)}, u32[]{:S(2)}) %collective-permute-start.3) | collective-permute-done | bytes 131104 | tf_op jit(solution)/shard_map/ppermute | solution.py:37
  22.9 0.7 %collective-permute-done.2.w1_ref = f32[2,16,1024]{2,1,0:T(8,128)S(1)} collective-permute-done((f32[2,16,1024]{2,1,0:T(8,128)S(1)}, f32[2,16,1024]{2,1,0:T(8,128)S(1)}, u32[]{:S(2)}, u32[]{:S(2)}) %collective-permute-start.2) | collective-permute-done | bytes 131104 | tf_op jit(solution)/shard_map/ppermute | solution.py:37
  23.6 2.1 %collective-permute-done.1.w3_ref = f32[2,16,1024]{2,1,0:T(8,128)S(1)} collective-permute-done((f32[2,16,1024]{2,1,0:T(8,128)S(1)}, f32[2,16,1024]{2,1,0:T(8,128)S(1)}, u32[]{:S(2)}, u32[]{:S(2)}) %collective-permute-start.1) | collective-permute-done | bytes 131104 | tf_op jit(solution)/shard_map/ppermute | solution.py:37
  25.9 0.3 smooth.1.smooth_ref.own_ref
  26.3 0.9 %gram_far.2 = (f32[304,272]{1,0:T(8,128)S(1)}, bf16[272,1024]{1,0:T(8,128)(2,1)S(1)}) custom-call(f32[128,1024]{1,0:T(8,128)S(1)} %smooth.1.smooth_ref.own_ref), custom_call_target="tpu_custom_call" | custom-call | flops 1 | bytes 262144 | tf_op jit(solution)/shard_map/gram_far/pallas_call | solution.py:243
  27.2 1.0 %collective-permute-done.4.smooth_ref.other_ref = f32[128,1024]{1,0:T(8,128)S(1)} collective-permute-done((f32[128,1024]{1,0:T(8,128)S(1)}, f32[128,1024]{1,0:T(8,128)S(1)}, u32[]{:S(2)}, u32[]{:S(2)}) %collective-permute-start.4) | collective-permute-done | bytes 524320 | tf_op jit(solution)/shard_map/ppermute | solution.py:41
  28.2 1.1 %gram_far.3 = (f32[608,128]{1,0:T(8,128)S(1)}, bf16[272,1024]{1,0:T(8,128)(2,1)S(1)}) custom-call(f32[304,272]{1,0:T(8,128)S(1)} %get-tuple-element.22.part_ref, f32[128,1024]{1,0:T(8,128)S(1)} %collective-permute-done.4.smooth_ref.other_ref), custom_call_target="tpu_custom_call" | custom-call | flops 1 | bytes 262144 | tf_op jit(solution)/shard_map/gram_far/pallas_call | solution.py:243
  29.2 1.6 %collective-permute-start.6 = (f32[608,128]{1,0:T(8,128)S(1)}, f32[608,128]{1,0:T(8,128)S(1)}, u32[]{:S(2)}, u32[]{:S(2)}) collective-permute-start(f32[608,128]{1,0:T(8,128)S(1)} %get-tuple-element.30), channel_id=1, source_target_pairs={{0,2},{1,7},{2,4},{3,1},{4,6},{5,3},{6,0},{7,5},{8,10},{9,15},{10,... | collective-permute-start | bytes 933896 | tf_op jit(solution)/shard_map/ppermute | solution.py:54
  30.9 1.2 %gram_cross.1 = f32[608,128]{1,0:T(8,128)S(1)} custom-call(f32[128,1024]{1,0:T(8,128)S(1)} %smooth.1.smooth_ref.own_ref, bf16[272,1024]{1,0:T(8,128)(2,1)S(1)} %get-tuple-element.25.own_right_ref, f32[128,1024]{1,0:T(8,128)S(1)} %collective-permute-done.4.smooth_ref.other_ref, bf16[272,1024]{1,0:T(8,128)(2,1)S(1)} %get-tuple-element.27.other_right_ref), custom_call_target="tpu_custom_call" | custom-call | flops 1 | bytes 262144 | tf_op jit(solution)/shard_map/gram_cross/pallas_call | solution.py:243
  32.2 1.2 %gram_near.1.a_ref = f32[608,128]{1,0:T(8,128)S(1)} custom-call(f32[128,1024]{1,0:T(8,128)S(1)} %smooth.1.smooth_ref.own_ref, bf16[272,1024]{1,0:T(8,128)(2,1)S(1)} %get-tuple-element.25.own_right_ref, f32[128,1024]{1,0:T(8,128)S(1)} %collective-permute-done.4.smooth_ref.other_ref, bf16[272,1024]{1,0:T(8,128)(2,1)S(1)} %get-tuple-element.27.other_right_ref), custom_call_target="tpu_custom_call" | custom-call | flops 1 | bytes 262144 | tf_op jit(solution)/shard_map/gram_near/pallas_call | solution.py:243
  33.4 4.0 %collective-permute-done.6.b_ref = f32[608,128]{1,0:T(8,128)S(1)} collective-permute-done((f32[608,128]{1,0:T(8,128)S(1)}, f32[608,128]{1,0:T(8,128)S(1)}, u32[]{:S(2)}, u32[]{:S(2)}) %collective-permute-start.6) | collective-permute-done | bytes 311328 | tf_op jit(solution)/shard_map/ppermute | solution.py:54
  37.4 0.4 collective-permute-start.9
  37.9 1.6 %collective-permute-start.7 = (f32[448,128]{1,0:T(8,128)S(1)}, f32[448,128]{1,0:T(8,128)S(1)}, u32[]{:S(2)}, u32[]{:S(2)}) collective-permute-start(f32[448,128]{1,0:T(8,128)S(1)} %get-tuple-element.31), channel_id=1, source_target_pairs={{0,2},{1,7},{2,4},{3,1},{4,6},{5,3},{6,0},{7,5},{8,10},{9,15},{10,... | collective-permute-start | bytes 688136 | tf_op jit(solution)/shard_map/ppermute | solution.py:54
  39.4 1.2 %gram_own.1.a_ref = f32[608,128]{1,0:T(8,128)S(1)} custom-call(f32[128,1024]{1,0:T(8,128)S(1)} %smooth.1.smooth_ref.own_ref, bf16[272,1024]{1,0:T(8,128)(2,1)S(1)} %get-tuple-element.25.own_right_ref, f32[128,1024]{1,0:T(8,128)S(1)} %collective-permute-done.4.smooth_ref.other_ref, bf16[272,1024]{1,0:T(8,128)(2,1)S(1)} %get-tuple-element.27.other_right_ref), custom_call_target="tpu_custom_call" | custom-call | flops 1 | bytes 262144 | tf_op jit(solution)/shard_map/gram_own/pallas_call | solution.py:243
  40.7 2.5 %collective-permute-done.9.b_ref = f32[160,128]{1,0:T(8,128)S(1)} collective-permute-done((f32[160,128]{1,0:T(8,128)S(1)}, f32[160,128]{1,0:T(8,128)S(1)}, u32[]{:S(2)}, u32[]{:S(2)}) %collective-permute-start.9) | collective-permute-done | bytes 81952 | tf_op jit(solution)/shard_map/ppermute | solution.py:54
  43.2 3.3 %collective-permute-start.10 = (f32[160,128]{1,0:T(8,128)S(1)}, f32[160,128]{1,0:T(8,128)S(1)}, u32[]{:S(2)}, u32[]{:S(2)}) collective-permute-start(f32[160,128]{1,0:T(8,128)S(1)} %add.15), channel_id=1, source_target_pairs={{0,8},{1,25},{2,10},{3,27},{4,12},{5,29},{6,14},{7,31},{8,16},{9,1... | collective-permute-start | bytes 245768 | tf_op jit(solution)/shard_map/ppermute | solution.py:54
  46.6 0.8 %collective-permute-start.8 = (f32[160,128]{1,0:T(8,128)S(1)}, f32[160,128]{1,0:T(8,128)S(1)}, u32[]{:S(2)}, u32[]{:S(2)}) collective-permute-start(f32[160,128]{1,0:T(8,128)S(1)} %get-tuple-element.33), channel_id=1, source_target_pairs={{0,9},{1,24},{2,11},{3,26},{4,13},{5,28},{6,15},{7,30},{8,17},{9,0... | collective-permute-start | bytes 245768 | tf_op jit(solution)/shard_map/ppermute | solution.py:54
  47.4 3.7 %collective-permute-done.10.b_ref = f32[160,128]{1,0:T(8,128)S(1)} collective-permute-done((f32[160,128]{1,0:T(8,128)S(1)}, f32[160,128]{1,0:T(8,128)S(1)}, u32[]{:S(2)}, u32[]{:S(2)}) %collective-permute-start.10) | collective-permute-done | bytes 81952 | tf_op jit(solution)/shard_map/ppermute | solution.py:54
  51.1 1.7 %collective-permute-start.11 = (f32[160,128]{1,0:T(8,128)S(1)}, f32[160,128]{1,0:T(8,128)S(1)}, u32[]{:S(2)}, u32[]{:S(2)}) collective-permute-start(f32[160,128]{1,0:T(8,128)S(1)} %add.16), channel_id=1, source_target_pairs={{0,8},{1,25},{2,10},{3,27},{4,12},{5,29},{6,14},{7,31},{8,16},{9,1... | collective-permute-start | bytes 245768 | tf_op jit(solution)/shard_map/ppermute | solution.py:54
  52.8 5.8 %collective-permute-done.11.t2_ref = f32[160,128]{1,0:T(8,128)S(1)} collective-permute-done((f32[160,128]{1,0:T(8,128)S(1)}, f32[160,128]{1,0:T(8,128)S(1)}, u32[]{:S(2)}, u32[]{:S(2)}) %collective-permute-start.11) | collective-permute-done | bytes 81952 | tf_op jit(solution)/shard_map/ppermute | solution.py:54
  58.6 0.7 %final.1 = f32[68,272]{1,0:T(8,128)} custom-call(f32[160,128]{1,0:T(8,128)S(1)} %get-tuple-element.32.t0_ref, f32[160,128]{1,0:T(8,128)S(1)} %collective-permute-done.8.t1_ref, f32[160,128]{1,0:T(8,128)S(1)} %collective-permute-done.11.t2_ref), custom_call_target="tpu_custom_call" | custom-call | flops 1 | bytes 262144 | tf_op jit(solution)/shard_map/final/pallas_call | solution.py:350
  (22 shorter events, 0.8 us)
Async XLA Ops:
  1.2 6.3 %copy-start.1 = (f32[32]{0:T(128)S(1)}, f32[32]{0:T(128)}, u32[]{:S(2)}) copy-start(f32[32]{0:T(128)} %param.6) | copy-start | bytes 388
  1.3 6.3 %copy-start.2 = (s32[31]{0:T(128)S(1)}, s32[31]{0:T(128)}, u32[]{:S(2)}) copy-start(s32[31]{0:T(128)} %param.7) | copy-start | bytes 376
  1.3 10.3 %all-to-all-start = ((s32[8,1,128]{2,1,0:T(1,128)}), s32[8,1,128]{2,1,0:T(1,128)S(1)}, u32[]{:S(2)}, u32[]{:S(2)}) async-start(s32[8,1,128]{2,1,0:T(1,128)} %repeat.1), calls=%async_computation | async-start | bytes 8192 | tf_op jit(solution)/shard_map/all_to_all | solution.py:291
  7.6 1.2 %copy-start = (f32[4,4,16384]{2,1,0:T(4,128)S(1)}, f32[4,4,16384]{2,1,0:T(4,128)}, u32[]{:S(2)}) copy-start(f32[4,4,16384]{2,1,0:T(4,128)} %slab_ref.1) | copy-start | bytes 3145732
  11.9 4.4 %collective-permute-start = (f32[16,1024]{1,0:T(8,128)S(1)}, f32[16,1024]{1,0:T(8,128)S(1)}, u32[]{:S(2)}, u32[]{:S(2)}) collective-permute-start(f32[16,1024]{1,0:T(8,128)S(1)} %pick.1), channel_id=1, source_target_pairs={{0,128},{32,160},{64,192},{96,224},{128,0},{160,32},{192,64},{224,... | collective-permute-start | bytes 196616 | tf_op jit(solution)/shard_map/ppermute | solution.py:37
  16.3 6.6 %collective-permute-start.3 = (f32[2,16,1024]{2,1,0:T(8,128)S(1)}, f32[2,16,1024]{2,1,0:T(8,128)S(1)}, u32[]{:S(2)}, u32[]{:S(2)}) collective-permute-start(f32[2,16,1024]{2,1,0:T(8,128)S(1)} %pad_maximum_fusion.w0_ref), channel_id=1, source_target_pairs={{0,64},{32,96},{64,0},{96,32},{128,192},{160,224},{192,128},{224,1... | collective-permute-start | bytes 393224 | tf_op jit(solution)/shard_map/ppermute | solution.py:37
  18.4 5.2 %collective-permute-start.2 = (f32[2,16,1024]{2,1,0:T(8,128)S(1)}, f32[2,16,1024]{2,1,0:T(8,128)S(1)}, u32[]{:S(2)}, u32[]{:S(2)}) collective-permute-start(f32[2,16,1024]{2,1,0:T(8,128)S(1)} %pad_maximum_fusion.w0_ref), channel_id=1, source_target_pairs={{0,32},{32,64},{64,96},{96,0},{128,160},{160,192},{192,224},{224,1... | collective-permute-start | bytes 393224 | tf_op jit(solution)/shard_map/ppermute | solution.py:37
  19.6 6.2 %collective-permute-start.1 = (f32[2,16,1024]{2,1,0:T(8,128)S(1)}, f32[2,16,1024]{2,1,0:T(8,128)S(1)}, u32[]{:S(2)}, u32[]{:S(2)}) collective-permute-start(f32[2,16,1024]{2,1,0:T(8,128)S(1)} %pad_maximum_fusion.w0_ref), channel_id=1, source_target_pairs={{0,96},{32,0},{64,32},{96,64},{128,224},{160,128},{192,160},{224,1... | collective-permute-start | bytes 393224 | tf_op jit(solution)/shard_map/ppermute | solution.py:37
  26.2 2.0 %collective-permute-start.4 = (f32[128,1024]{1,0:T(8,128)S(1)}, f32[128,1024]{1,0:T(8,128)S(1)}, u32[]{:S(2)}, u32[]{:S(2)}) collective-permute-start(f32[128,1024]{1,0:T(8,128)S(1)} %smooth.1.smooth_ref.own_ref), channel_id=1, source_target_pairs={{0,1},{1,0},{2,3},{3,2},{4,5},{5,4},{6,7},{7,6},{8,9},{9,8},{10,11... | collective-permute-start | bytes 1572872 | tf_op jit(solution)/shard_map/ppermute | solution.py:41
  29.2 8.1 %collective-permute-start.6 = (f32[608,128]{1,0:T(8,128)S(1)}, f32[608,128]{1,0:T(8,128)S(1)}, u32[]{:S(2)}, u32[]{:S(2)}) collective-permute-start(f32[608,128]{1,0:T(8,128)S(1)} %get-tuple-element.30), channel_id=1, source_target_pairs={{0,2},{1,7},{2,4},{3,1},{4,6},{5,3},{6,0},{7,5},{8,10},{9,15},{10,... | collective-permute-start | bytes 933896 | tf_op jit(solution)/shard_map/ppermute | solution.py:54
  32.1 8.6 %collective-permute-start.5 = (f32[608,128]{1,0:T(8,128)S(1)}, f32[608,128]{1,0:T(8,128)S(1)}, u32[]{:S(2)}, u32[]{:S(2)}) collective-permute-start(f32[608,128]{1,0:T(8,128)S(1)} %gram_cross.1), channel_id=1, source_target_pairs={{0,3},{1,6},{2,5},{3,0},{4,7},{5,2},{6,1},{7,4},{8,11},{9,14},{10,... | collective-permute-start | bytes 933896 | tf_op jit(solution)/shard_map/ppermute | solution.py:54
  37.4 5.7 %collective-permute-start.9 = (f32[160,128]{1,0:T(8,128)S(1)}, f32[160,128]{1,0:T(8,128)S(1)}, u32[]{:S(2)}, u32[]{:S(2)}) collective-permute-start(f32[160,128]{1,0:T(8,128)S(1)} %get-tuple-element.36), channel_id=1, source_target_pairs={{0,2},{1,7},{2,4},{3,1},{4,6},{5,3},{6,0},{7,5},{8,10},{9,15},{10,... | collective-permute-start | bytes 245768 | tf_op jit(solution)/shard_map/ppermute | solution.py:54
  37.9 8.6 %collective-permute-start.7 = (f32[448,128]{1,0:T(8,128)S(1)}, f32[448,128]{1,0:T(8,128)S(1)}, u32[]{:S(2)}, u32[]{:S(2)}) collective-permute-start(f32[448,128]{1,0:T(8,128)S(1)} %get-tuple-element.31), channel_id=1, source_target_pairs={{0,2},{1,7},{2,4},{3,1},{4,6},{5,3},{6,0},{7,5},{8,10},{9,15},{10,... | collective-permute-start | bytes 688136 | tf_op jit(solution)/shard_map/ppermute | solution.py:54
  43.2 7.9 %collective-permute-start.10 = (f32[160,128]{1,0:T(8,128)S(1)}, f32[160,128]{1,0:T(8,128)S(1)}, u32[]{:S(2)}, u32[]{:S(2)}) collective-permute-start(f32[160,128]{1,0:T(8,128)S(1)} %add.15), channel_id=1, source_target_pairs={{0,8},{1,25},{2,10},{3,27},{4,12},{5,29},{6,14},{7,31},{8,16},{9,1... | collective-permute-start | bytes 245768 | tf_op jit(solution)/shard_map/ppermute | solution.py:54
  46.6 6.2 %collective-permute-start.8 = (f32[160,128]{1,0:T(8,128)S(1)}, f32[160,128]{1,0:T(8,128)S(1)}, u32[]{:S(2)}, u32[]{:S(2)}) collective-permute-start(f32[160,128]{1,0:T(8,128)S(1)} %get-tuple-element.33), channel_id=1, source_target_pairs={{0,9},{1,24},{2,11},{3,26},{4,13},{5,28},{6,15},{7,30},{8,17},{9,0... | collective-permute-start | bytes 245768 | tf_op jit(solution)/shard_map/ppermute | solution.py:54
  51.1 7.5 %collective-permute-start.11 = (f32[160,128]{1,0:T(8,128)S(1)}, f32[160,128]{1,0:T(8,128)S(1)}, u32[]{:S(2)}, u32[]{:S(2)}) collective-permute-start(f32[160,128]{1,0:T(8,128)S(1)} %add.16), channel_id=1, source_target_pairs={{0,8},{1,25},{2,10},{3,27},{4,12},{5,29},{6,14},{7,31},{8,16},{9,1... | collective-permute-start | bytes 245768 | tf_op jit(solution)/shard_map/ppermute | solution.py:54

commit v14 on v13

--- a/solution.py
+++ b/solution.py
@@ -209,12 +209,12 @@
         ref[2 * CHUNK + 8 : LAST, :] = two
 
 
-def final_kernel(t0_ref, t1_ref, t2_ref, out_ref):
+def final_kernel(kept_ref, near_ref, out_ref):
     odd = lax.axis_index("hor") % 2 == 1
     scale = 1.0 / (BLOCK * N_HOR)
 
     def total(rows):
-        return (t0_ref[rows, :] + t1_ref[rows, :]) + t2_ref[rows, :]
+        return kept_ref[rows, :] + near_ref[rows, :]
 
     def place(value):
         return jnp.where(odd, value[CHUNK - ROWS_OUT : CHUNK], value[0:ROWS_OUT]) * scale
@@ -332,6 +332,7 @@
     parts["own"] = gram(gram_kernel, "own", sent, *both)
     two_back = hop(parts["far"], "y", 0)
     from_cross = hop(parts["cross"], "y", 1)
+    parts["near"], parts["own"] = lax.optimization_barrier((parts["near"], parts["own"]))
     near_far, near_rest = cut(parts["near"], two_back)
     from_near_far, from_near_rest = hop(near_far, "y", 0), hop(near_rest, "y", 0)
     sum_far, sum_rest = cut(parts["own"], from_cross)
@@ -346,16 +347,17 @@
         name="split",
     )(sum_rest, from_near_rest)
     from_cross = hop(cross, "z_hi", 1)
+    kept = add(kept, from_cross)
     from_near = hop(add(near, two_back), "z_hi", 0)
     return pl.pallas_call(
         final_kernel,
         out_shape=jax.ShapeDtypeStruct((ROWS_OUT, COLS_OUT), f32),
-        in_specs=[VMEM] * 3,
+        in_specs=[VMEM] * 2,
         out_specs=VMEM,
         compiler_params=params(8),
         cost_estimate=cost(1, SHARE),
         name="final",
-    )(kept, from_cross, from_near)
+    )(kept, from_near)
 
 
 def solution(mesh):

time: 59.5 us -> 59.5 us (level)
  no operation moved by 1% of the time
where the time goes in v14:
time: 59.5 us; the launch traced here: 59.3 us
  waiting for transfers between devices  28.2 us (47%)
  starting transfers between devices  20.8 us (35%)
  Pallas kernels  8.58 us (14%)
  local copies, waits for them, and re-layouts  1.3 us (2%)
    ppermute x7, waiting for transfers between devices, hop(): return lax.ppermute(value, 'hor', pairs)  15.9 us
    ppermute x7, starting transfers between devices, hop(): return lax.ppermute(value, 'hor', pairs)  9.6 us
    ppermute x4, waiting for transfers between devices, shift_lev(): return lax.ppermute(value, 'lev', pairs)  8.77 us
    all_to_all x1, starting transfers between devices, on_device(): lists = lax.all_to_all(repeated, 'lev', 0, 0, tiled=True)  6.26 us
    pallas_call x5, Pallas kernels, gram(): pl.pallas_call(functools.partial(kernel, place), out_shape=out_shape, in_...  5.61 us
    ppermute x4, starting transfers between devices, shift_lev(): return lax.ppermute(value, 'lev', pairs)  4.84 us
    all_to_all x1, waiting for transfers between devices, on_device(): lists = lax.all_to_all(repeated, 'lev', 0, 0, tiled=True)  2.57 us
    pallas_call x1, Pallas kernels, on_device(): pl.pallas_call(repeat_kernel, out_shape=jax.ShapeDtypeStruct((N_LEV, 1, S...  1.25 us
  transfers between devices with their start and end apart: 13, of which 10 were waited for; matrix products, arithmetic and copies ran while one was open for 1% of the time, Pallas kernels for 8%

profile of v14, /device:TPU:6, one launch (start us, length us, event | category | flops | bytes accessed | tf_op | source)
XLA Modules:
  0.0 59.3 jit_solution(9392341574863869592)
XLA Ops:
  0.0 1.2 %repeat.1 = s32[8,1,128]{2,1,0:T(1,128)} custom-call(s32[1,128]{1,0:T(1,128)} %index_ref.1), custom_call_target="tpu_custom_call" | custom-call | tf_op jit(solution)/shard_map/repeat/pallas_call | solution.py:283
  1.3 6.3 %all-to-all-start = ((s32[8,1,128]{2,1,0:T(1,128)}), s32[8,1,128]{2,1,0:T(1,128)S(1)}, u32[]{:S(2)}, u32[]{:S(2)}) async-start(s32[8,1,128]{2,1,0:T(1,128)} %repeat.1), calls=%async_computation | async-start | bytes 8192 | tf_op jit(solution)/shard_map/all_to_all | solution.py:291
  7.6 1.2 %copy-done = f32[4,4,16384]{2,1,0:T(4,128)S(1)} copy-done((f32[4,4,16384]{2,1,0:T(4,128)S(1)}, f32[4,4,16384]{2,1,0:T(4,128)}, u32[]{:S(2)}) %copy-start) | copy-done | bytes 1048600
  8.8 0.1 stage.1.slab_ref
  9.0 2.6 %all-to-all-done.index_ref = s32[8,1,128]{2,1,0:T(1,128)S(1)} async-done(((s32[8,1,128]{2,1,0:T(1,128)}), s32[8,1,128]{2,1,0:T(1,128)S(1)}, u32[]{:S(2)}, u32[]{:S(2)}) %all-to-all-start) | async-done | bytes 4128 | tf_op jit(solution)/shard_map/all_to_all | solution.py:291
  11.5 0.4 pick.1
  11.9 0.7 %collective-permute-start = (f32[16,1024]{1,0:T(8,128)S(1)}, f32[16,1024]{1,0:T(8,128)S(1)}, u32[]{:S(2)}, u32[]{:S(2)}) collective-permute-start(f32[16,1024]{1,0:T(8,128)S(1)} %pick.1), channel_id=1, source_target_pairs={{0,128},{32,160},{64,192},{96,224},{128,0},{160,32},{192,64},{224,... | collective-permute-start | bytes 196616 | tf_op jit(solution)/shard_map/ppermute | solution.py:37
  12.6 3.6 %collective-permute-done = f32[16,1024]{1,0:T(8,128)S(1)} collective-permute-done((f32[16,1024]{1,0:T(8,128)S(1)}, f32[16,1024]{1,0:T(8,128)S(1)}, u32[]{:S(2)}, u32[]{:S(2)}) %collective-permute-start) | collective-permute-done | bytes 65568 | tf_op jit(solution)/shard_map/ppermute | solution.py:37
  16.3 2.2 %collective-permute-start.3 = (f32[2,16,1024]{2,1,0:T(8,128)S(1)}, f32[2,16,1024]{2,1,0:T(8,128)S(1)}, u32[]{:S(2)}, u32[]{:S(2)}) collective-permute-start(f32[2,16,1024]{2,1,0:T(8,128)S(1)} %pad_maximum_fusion.w0_ref), channel_id=1, source_target_pairs={{0,64},{32,96},{64,0},{96,32},{128,192},{160,224},{192,128},{224,1... | collective-permute-start | bytes 393224 | tf_op jit(solution)/shard_map/ppermute | solution.py:37
  18.4 1.2 %collective-permute-start.2 = (f32[2,16,1024]{2,1,0:T(8,128)S(1)}, f32[2,16,1024]{2,1,0:T(8,128)S(1)}, u32[]{:S(2)}, u32[]{:S(2)}) collective-permute-start(f32[2,16,1024]{2,1,0:T(8,128)S(1)} %pad_maximum_fusion.w0_ref), channel_id=1, source_target_pairs={{0,32},{32,64},{64,96},{96,0},{128,160},{160,192},{192,224},{224,1... | collective-permute-start | bytes 393224 | tf_op jit(solution)/shard_map/ppermute | solution.py:37
  19.6 0.9 %collective-permute-start.1 = (f32[2,16,1024]{2,1,0:T(8,128)S(1)}, f32[2,16,1024]{2,1,0:T(8,128)S(1)}, u32[]{:S(2)}, u32[]{:S(2)}) collective-permute-start(f32[2,16,1024]{2,1,0:T(8,128)S(1)} %pad_maximum_fusion.w0_ref), channel_id=1, source_target_pairs={{0,96},{32,0},{64,32},{96,64},{128,224},{160,128},{192,160},{224,1... | collective-permute-start | bytes 393224 | tf_op jit(solution)/shard_map/ppermute | solution.py:37
  20.6 2.3 %collective-permute-done.3.w2_ref = f32[2,16,1024]{2,1,0:T(8,128)S(1)} collective-permute-done((f32[2,16,1024]{2,1,0:T(8,128)S(1)}, f32[2,16,1024]{2,1,0:T(8,128)S(1)}, u32[]{:S(2)}, u32[]{:S(2)}) %collective-permute-start.3) | collective-permute-done | bytes 131104 | tf_op jit(solution)/shard_map/ppermute | solution.py:37
  22.9 0.7 %collective-permute-done.2.w1_ref = f32[2,16,1024]{2,1,0:T(8,128)S(1)} collective-permute-done((f32[2,16,1024]{2,1,0:T(8,128)S(1)}, f32[2,16,1024]{2,1,0:T(8,128)S(1)}, u32[]{:S(2)}, u32[]{:S(2)}) %collective-permute-start.2) | collective-permute-done | bytes 131104 | tf_op jit(solution)/shard_map/ppermute | solution.py:37
  23.6 2.1 %collective-permute-done.1.w3_ref = f32[2,16,1024]{2,1,0:T(8,128)S(1)} collective-permute-done((f32[2,16,1024]{2,1,0:T(8,128)S(1)}, f32[2,16,1024]{2,1,0:T(8,128)S(1)}, u32[]{:S(2)}, u32[]{:S(2)}) %collective-permute-start.1) | collective-permute-done | bytes 131104 | tf_op jit(solution)/shard_map/ppermute | solution.py:37
  25.9 0.3 smooth.1.smooth_ref.own_ref
  26.3 0.9 %gram_far.2 = (f32[304,272]{1,0:T(8,128)S(1)}, bf16[272,1024]{1,0:T(8,128)(2,1)S(1)}) custom-call(f32[128,1024]{1,0:T(8,128)S(1)} %smooth.1.smooth_ref.own_ref), custom_call_target="tpu_custom_call" | custom-call | flops 1 | bytes 262144 | tf_op jit(solution)/shard_map/gram_far/pallas_call | solution.py:243
  27.2 1.0 %collective-permute-done.4.smooth_ref.other_ref = f32[128,1024]{1,0:T(8,128)S(1)} collective-permute-done((f32[128,1024]{1,0:T(8,128)S(1)}, f32[128,1024]{1,0:T(8,128)S(1)}, u32[]{:S(2)}, u32[]{:S(2)}) %collective-permute-start.4) | collective-permute-done | bytes 524320 | tf_op jit(solution)/shard_map/ppermute | solution.py:41
  28.2 1.1 %gram_far.3 = (f32[608,128]{1,0:T(8,128)S(1)}, bf16[272,1024]{1,0:T(8,128)(2,1)S(1)}) custom-call(f32[304,272]{1,0:T(8,128)S(1)} %get-tuple-element.24.part_ref, f32[128,1024]{1,0:T(8,128)S(1)} %collective-permute-done.4.smooth_ref.other_ref), custom_call_target="tpu_custom_call" | custom-call | flops 1 | bytes 262144 | tf_op jit(solution)/shard_map/gram_far/pallas_call | solution.py:243
  29.2 1.6 %collective-permute-start.6 = (f32[608,128]{1,0:T(8,128)S(1)}, f32[608,128]{1,0:T(8,128)S(1)}, u32[]{:S(2)}, u32[]{:S(2)}) collective-permute-start(f32[608,128]{1,0:T(8,128)S(1)} %get-tuple-element.34), channel_id=1, source_target_pairs={{0,2},{1,7},{2,4},{3,1},{4,6},{5,3},{6,0},{7,5},{8,10},{9,15},{10,... | collective-permute-start | bytes 933896 | tf_op jit(solution)/shard_map/ppermute | solution.py:54
  30.9 1.2 %gram_cross.1 = f32[608,128]{1,0:T(8,128)S(1)} custom-call(f32[128,1024]{1,0:T(8,128)S(1)} %smooth.1.smooth_ref.own_ref, bf16[272,1024]{1,0:T(8,128)(2,1)S(1)} %get-tuple-element.27.own_right_ref, f32[128,1024]{1,0:T(8,128)S(1)} %collective-permute-done.4.smooth_ref.other_ref, bf16[272,1024]{1,0:T(8,128)(2,1)S(1)} %get-tuple-element.29.other_right_ref), custom_call_target="tpu_custom_call" | custom-call | flops 1 | bytes 262144 | tf_op jit(solution)/shard_map/gram_cross/pallas_call | solution.py:243
  32.2 1.2 %gram_own.1.a_ref = f32[608,128]{1,0:T(8,128)S(1)} custom-call(f32[128,1024]{1,0:T(8,128)S(1)} %smooth.1.smooth_ref.own_ref, bf16[272,1024]{1,0:T(8,128)(2,1)S(1)} %get-tuple-element.27.own_right_ref, f32[128,1024]{1,0:T(8,128)S(1)} %collective-permute-done.4.smooth_ref.other_ref, bf16[272,1024]{1,0:T(8,128)(2,1)S(1)} %get-tuple-element.29.other_right_ref), custom_call_target="tpu_custom_call" | custom-call | flops 1 | bytes 262144 | tf_op jit(solution)/shard_map/gram_own/pallas_call | solution.py:243
  33.3 1.2 %gram_near.1.a_ref = f32[608,128]{1,0:T(8,128)S(1)} custom-call(f32[128,1024]{1,0:T(8,128)S(1)} %smooth.1.smooth_ref.own_ref, bf16[272,1024]{1,0:T(8,128)(2,1)S(1)} %get-tuple-element.27.own_right_ref, f32[128,1024]{1,0:T(8,128)S(1)} %collective-permute-done.4.smooth_ref.other_ref, bf16[272,1024]{1,0:T(8,128)(2,1)S(1)} %get-tuple-element.29.other_right_ref), custom_call_target="tpu_custom_call" | custom-call | flops 1 | bytes 262144 | tf_op jit(solution)/shard_map/gram_near/pallas_call | solution.py:243
  34.6 2.8 %collective-permute-done.6.b_ref = f32[608,128]{1,0:T(8,128)S(1)} collective-permute-done((f32[608,128]{1,0:T(8,128)S(1)}, f32[608,128]{1,0:T(8,128)S(1)}, u32[]{:S(2)}, u32[]{:S(2)}) %collective-permute-start.6) | collective-permute-done | bytes 311328 | tf_op jit(solution)/shard_map/ppermute | solution.py:54
  37.4 0.4 collective-permute-start.9
  37.9 1.6 %collective-permute-start.7 = (f32[448,128]{1,0:T(8,128)S(1)}, f32[448,128]{1,0:T(8,128)S(1)}, u32[]{:S(2)}, u32[]{:S(2)}) collective-permute-start(f32[448,128]{1,0:T(8,128)S(1)} %get-tuple-element.35), channel_id=1, source_target_pairs={{0,2},{1,7},{2,4},{3,1},{4,6},{5,3},{6,0},{7,5},{8,10},{9,15},{10,... | collective-permute-start | bytes 688136 | tf_op jit(solution)/shard_map/ppermute | solution.py:54
  39.5 3.7 %collective-permute-done.9.b_ref = f32[160,128]{1,0:T(8,128)S(1)} collective-permute-done((f32[160,128]{1,0:T(8,128)S(1)}, f32[160,128]{1,0:T(8,128)S(1)}, u32[]{:S(2)}, u32[]{:S(2)}) %collective-permute-start.9) | collective-permute-done | bytes 81952 | tf_op jit(solution)/shard_map/ppermute | solution.py:54
  43.2 3.4 %collective-permute-start.10 = (f32[160,128]{1,0:T(8,128)S(1)}, f32[160,128]{1,0:T(8,128)S(1)}, u32[]{:S(2)}, u32[]{:S(2)}) collective-permute-start(f32[160,128]{1,0:T(8,128)S(1)} %add.17), channel_id=1, source_target_pairs={{0,8},{1,25},{2,10},{3,27},{4,12},{5,29},{6,14},{7,31},{8,16},{9,1... | collective-permute-start | bytes 245768 | tf_op jit(solution)/shard_map/ppermute | solution.py:54
  46.6 0.8 %collective-permute-start.8 = (f32[160,128]{1,0:T(8,128)S(1)}, f32[160,128]{1,0:T(8,128)S(1)}, u32[]{:S(2)}, u32[]{:S(2)}) collective-permute-start(f32[160,128]{1,0:T(8,128)S(1)} %get-tuple-element.37), channel_id=1, source_target_pairs={{0,9},{1,24},{2,11},{3,26},{4,13},{5,28},{6,15},{7,30},{8,17},{9,0... | collective-permute-start | bytes 245768 | tf_op jit(solution)/shard_map/ppermute | solution.py:54
  47.4 3.7 %collective-permute-done.10.b_ref = f32[160,128]{1,0:T(8,128)S(1)} collective-permute-done((f32[160,128]{1,0:T(8,128)S(1)}, f32[160,128]{1,0:T(8,128)S(1)}, u32[]{:S(2)}, u32[]{:S(2)}) %collective-permute-start.10) | collective-permute-done | bytes 81952 | tf_op jit(solution)/shard_map/ppermute | solution.py:54
  51.1 1.7 %collective-permute-start.11 = (f32[160,128]{1,0:T(8,128)S(1)}, f32[160,128]{1,0:T(8,128)S(1)}, u32[]{:S(2)}, u32[]{:S(2)}) collective-permute-start(f32[160,128]{1,0:T(8,128)S(1)} %add.18), channel_id=1, source_target_pairs={{0,8},{1,25},{2,10},{3,27},{4,12},{5,29},{6,14},{7,31},{8,16},{9,1... | collective-permute-start | bytes 245768 | tf_op jit(solution)/shard_map/ppermute | solution.py:54
  52.8 5.7 %collective-permute-done.11.near_ref = f32[160,128]{1,0:T(8,128)S(1)} collective-permute-done((f32[160,128]{1,0:T(8,128)S(1)}, f32[160,128]{1,0:T(8,128)S(1)}, u32[]{:S(2)}, u32[]{:S(2)}) %collective-permute-start.11) | collective-permute-done | bytes 81952 | tf_op jit(solution)/shard_map/ppermute | solution.py:54
  58.6 0.7 %final.1 = f32[68,272]{1,0:T(8,128)} custom-call(f32[160,128]{1,0:T(8,128)S(1)} %add.16.kept_ref, f32[160,128]{1,0:T(8,128)S(1)} %collective-permute-done.11.near_ref), custom_call_target="tpu_custom_call" | custom-call | flops 1 | bytes 262144 | tf_op jit(solution)/shard_map/final/pallas_call | solution.py:352
  (23 shorter events, 0.8 us)
Async XLA Ops:
  1.2 6.3 %copy-start.1 = (f32[32]{0:T(128)S(1)}, f32[32]{0:T(128)}, u32[]{:S(2)}) copy-start(f32[32]{0:T(128)} %param.6) | copy-start | bytes 388
  1.3 6.3 %copy-start.2 = (s32[31]{0:T(128)S(1)}, s32[31]{0:T(128)}, u32[]{:S(2)}) copy-start(s32[31]{0:T(128)} %param.7) | copy-start | bytes 376
  1.3 10.3 %all-to-all-start = ((s32[8,1,128]{2,1,0:T(1,128)}), s32[8,1,128]{2,1,0:T(1,128)S(1)}, u32[]{:S(2)}, u32[]{:S(2)}) async-start(s32[8,1,128]{2,1,0:T(1,128)} %repeat.1), calls=%async_computation | async-start | bytes 8192 | tf_op jit(solution)/shard_map/all_to_all | solution.py:291
  7.6 1.2 %copy-start = (f32[4,4,16384]{2,1,0:T(4,128)S(1)}, f32[4,4,16384]{2,1,0:T(4,128)}, u32[]{:S(2)}) copy-start(f32[4,4,16384]{2,1,0:T(4,128)} %slab_ref.1) | copy-start | bytes 3145732
  11.9 4.4 %collective-permute-start = (f32[16,1024]{1,0:T(8,128)S(1)}, f32[16,1024]{1,0:T(8,128)S(1)}, u32[]{:S(2)}, u32[]{:S(2)}) collective-permute-start(f32[16,1024]{1,0:T(8,128)S(1)} %pick.1), channel_id=1, source_target_pairs={{0,128},{32,160},{64,192},{96,224},{128,0},{160,32},{192,64},{224,... | collective-permute-start | bytes 196616 | tf_op jit(solution)/shard_map/ppermute | solution.py:37
  16.3 6.6 %collective-permute-start.3 = (f32[2,16,1024]{2,1,0:T(8,128)S(1)}, f32[2,16,1024]{2,1,0:T(8,128)S(1)}, u32[]{:S(2)}, u32[]{:S(2)}) collective-permute-start(f32[2,16,1024]{2,1,0:T(8,128)S(1)} %pad_maximum_fusion.w0_ref), channel_id=1, source_target_pairs={{0,64},{32,96},{64,0},{96,32},{128,192},{160,224},{192,128},{224,1... | collective-permute-start | bytes 393224 | tf_op jit(solution)/shard_map/ppermute | solution.py:37
  18.4 5.2 %collective-permute-start.2 = (f32[2,16,1024]{2,1,0:T(8,128)S(1)}, f32[2,16,1024]{2,1,0:T(8,128)S(1)}, u32[]{:S(2)}, u32[]{:S(2)}) collective-permute-start(f32[2,16,1024]{2,1,0:T(8,128)S(1)} %pad_maximum_fusion.w0_ref), channel_id=1, source_target_pairs={{0,32},{32,64},{64,96},{96,0},{128,160},{160,192},{192,224},{224,1... | collective-permute-start | bytes 393224 | tf_op jit(solution)/shard_map/ppermute | solution.py:37
  19.6 6.2 %collective-permute-start.1 = (f32[2,16,1024]{2,1,0:T(8,128)S(1)}, f32[2,16,1024]{2,1,0:T(8,128)S(1)}, u32[]{:S(2)}, u32[]{:S(2)}) collective-permute-start(f32[2,16,1024]{2,1,0:T(8,128)S(1)} %pad_maximum_fusion.w0_ref), channel_id=1, source_target_pairs={{0,96},{32,0},{64,32},{96,64},{128,224},{160,128},{192,160},{224,1... | collective-permute-start | bytes 393224 | tf_op jit(solution)/shard_map/ppermute | solution.py:37
  26.2 2.0 %collective-permute-start.4 = (f32[128,1024]{1,0:T(8,128)S(1)}, f32[128,1024]{1,0:T(8,128)S(1)}, u32[]{:S(2)}, u32[]{:S(2)}) collective-permute-start(f32[128,1024]{1,0:T(8,128)S(1)} %smooth.1.smooth_ref.own_ref), channel_id=1, source_target_pairs={{0,1},{1,0},{2,3},{3,2},{4,5},{5,4},{6,7},{7,6},{8,9},{9,8},{10,11... | collective-permute-start | bytes 1572872 | tf_op jit(solution)/shard_map/ppermute | solution.py:41
  29.2 8.1 %collective-permute-start.6 = (f32[608,128]{1,0:T(8,128)S(1)}, f32[608,128]{1,0:T(8,128)S(1)}, u32[]{:S(2)}, u32[]{:S(2)}) collective-permute-start(f32[608,128]{1,0:T(8,128)S(1)} %get-tuple-element.34), channel_id=1, source_target_pairs={{0,2},{1,7},{2,4},{3,1},{4,6},{5,3},{6,0},{7,5},{8,10},{9,15},{10,... | collective-permute-start | bytes 933896 | tf_op jit(solution)/shard_map/ppermute | solution.py:54
  32.1 7.4 %collective-permute-start.5 = (f32[608,128]{1,0:T(8,128)S(1)}, f32[608,128]{1,0:T(8,128)S(1)}, u32[]{:S(2)}, u32[]{:S(2)}) collective-permute-start(f32[608,128]{1,0:T(8,128)S(1)} %gram_cross.1), channel_id=1, source_target_pairs={{0,3},{1,6},{2,5},{3,0},{4,7},{5,2},{6,1},{7,4},{8,11},{9,14},{10,... | collective-permute-start | bytes 933896 | tf_op jit(solution)/shard_map/ppermute | solution.py:54
  37.4 5.7 %collective-permute-start.9 = (f32[160,128]{1,0:T(8,128)S(1)}, f32[160,128]{1,0:T(8,128)S(1)}, u32[]{:S(2)}, u32[]{:S(2)}) collective-permute-start(f32[160,128]{1,0:T(8,128)S(1)} %get-tuple-element.40), channel_id=1, source_target_pairs={{0,2},{1,7},{2,4},{3,1},{4,6},{5,3},{6,0},{7,5},{8,10},{9,15},{10,... | collective-permute-start | bytes 245768 | tf_op jit(solution)/shard_map/ppermute | solution.py:54
  37.9 8.6 %collective-permute-start.7 = (f32[448,128]{1,0:T(8,128)S(1)}, f32[448,128]{1,0:T(8,128)S(1)}, u32[]{:S(2)}, u32[]{:S(2)}) collective-permute-start(f32[448,128]{1,0:T(8,128)S(1)} %get-tuple-element.35), channel_id=1, source_target_pairs={{0,2},{1,7},{2,4},{3,1},{4,6},{5,3},{6,0},{7,5},{8,10},{9,15},{10,... | collective-permute-start | bytes 688136 | tf_op jit(solution)/shard_map/ppermute | solution.py:54
  43.2 7.9 %collective-permute-start.10 = (f32[160,128]{1,0:T(8,128)S(1)}, f32[160,128]{1,0:T(8,128)S(1)}, u32[]{:S(2)}, u32[]{:S(2)}) collective-permute-start(f32[160,128]{1,0:T(8,128)S(1)} %add.17), channel_id=1, source_target_pairs={{0,8},{1,25},{2,10},{3,27},{4,12},{5,29},{6,14},{7,31},{8,16},{9,1... | collective-permute-start | bytes 245768 | tf_op jit(solution)/shard_map/ppermute | solution.py:54
  46.6 6.2 %collective-permute-start.8 = (f32[160,128]{1,0:T(8,128)S(1)}, f32[160,128]{1,0:T(8,128)S(1)}, u32[]{:S(2)}, u32[]{:S(2)}) collective-permute-start(f32[160,128]{1,0:T(8,128)S(1)} %get-tuple-element.37), channel_id=1, source_target_pairs={{0,9},{1,24},{2,11},{3,26},{4,13},{5,28},{6,15},{7,30},{8,17},{9,0... | collective-permute-start | bytes 245768 | tf_op jit(solution)/shard_map/ppermute | solution.py:54
  51.1 7.5 %collective-permute-start.11 = (f32[160,128]{1,0:T(8,128)S(1)}, f32[160,128]{1,0:T(8,128)S(1)}, u32[]{:S(2)}, u32[]{:S(2)}) collective-permute-start(f32[160,128]{1,0:T(8,128)S(1)} %add.18), channel_id=1, source_target_pairs={{0,8},{1,25},{2,10},{3,27},{4,12},{5,29},{6,14},{7,31},{8,16},{9,1... | collective-permute-start | bytes 245768 | tf_op jit(solution)/shard_map/ppermute | solution.py:54
